TPU v7x, 256 devices: a whole 4x4x8 slice. The times are simulated.
256 devices in a mesh: seq: 32 (over y, z_hi, core), sub: 8 (over z_lo, x).
Axes of the slice: x: 4, y: 4, z: 8 (z_hi: 4, z_lo: 2; z = z_hi * 2 + z_lo), core: 2. Of those that a mesh axis runs over, the one named last changes fastest.
Arguments:
- tokens: bfloat16 [32768, 1024], P(('seq', 'sub')), may hold values from -6 to 6
- cotangent: bfloat16 [32768, 1024], P(('seq', 'sub')), may hold values from -6 to 6
- fine_qkv: bfloat16 [1024, 3, 1024], replicated, may hold values from -0.1875 to 0.1875
- fine_out: bfloat16 [1024, 1024], replicated, may hold values from -0.1875 to 0.1875
- coarse_qkv: bfloat16 [1024, 3, 1024], P(None, None, 'sub'), may hold values from -0.1875 to 0.1875
- coarse_out: bfloat16 [1024, 1024], P('sub'), may hold values from -0.5 to 0.5
Outputs:
- output: bfloat16 [32768, 1024], P(('seq', 'sub'))
- grad_tokens: bfloat16 [32768, 1024], P(('seq', 'sub'))
All inputs are finite; a program needn't handle non-finite values.
Results may differ from a plain program's by a relative error of at most 0.02.
Values may be sent and summed in bfloat16 or wider, within the bound.
No kernel may reach another device: no remote copies, remote signals or barrier semaphores. Data moves between devices by JAX's collectives and lax.ppermute only.
A program may use at most 128 MiB of HBM per device.

v0:
```python
import jax
import jax.numpy as jnp
from jax import lax
from jax.sharding import PartitionSpec as P

D = 1024
HEADS = 16
HEAD_DIM = 64
WINDOW = 512
POOL = 16


EPS = 1e-06


def from_behind(value, axis, steps):
    count = lax.axis_size(axis)
    first, last = (max(0, -steps), min(count, count - steps))
    return lax.ppermute(value, axis, [(source, source + steps) for source in range(first, last)])


def from_everyone(x, axis):
    peers = lax.axis_size(axis)
    return lax.all_to_all(jnp.broadcast_to(x[None], (peers, *x.shape)), axis, 0, 0, tiled=True)


def laid_out(pieces, dim):
    dims = list(pieces.shape[1:])
    dims[dim] *= pieces.shape[0]
    return jnp.moveaxis(pieces, 0, dim).reshape(dims)


def gathered_copies(x, axis, dim):
    pieces = from_everyone(x, axis)
    return laid_out(pieces, dim)


def split_up(x, dim, peers):
    before, after = (x.shape[:dim], x.shape[dim + 1 :])
    return jnp.moveaxis(x.reshape(*before, peers, -1, *after), dim, 0)


def sent_and_summed(x, axis, dim):
    peers = lax.axis_size(axis)
    pieces = lax.all_to_all(split_up(x, dim, peers), axis, 0, 0, tiled=True)
    return jnp.sum(pieces.astype(jnp.float32), axis=0)


def sent_together(arrays, axis, dim, along):
    both = jnp.concatenate(arrays, axis=along)
    filled, at, done = (lax.all_gather(both, axis, axis=dim, tiled=True), 0, [])
    for a in arrays:
        done.append(lax.slice_in_dim(filled, at, at + a.shape[along], axis=along))
        at += a.shape[along]
    return tuple(done)


def rms_rows(values):
    widened = values.astype(jnp.float32)
    factor = lax.rsqrt(jnp.mean(widened * widened, axis=-1, keepdims=True) + EPS)
    return (widened * factor, factor)


def norm_back(grad_rows, normed, factor):
    return factor * (grad_rows - normed * jnp.mean(normed * grad_rows, axis=-1, keepdims=True))


def project_rows(normed_b, weight):
    row_count = normed_b.shape[0]
    local_width = weight.shape[2]
    projected = jnp.dot(
        normed_b,
        weight.reshape(weight.shape[0], 3 * local_width),
        preferred_element_type=jnp.float32,
    )
    projected = projected.reshape(row_count, 3, local_width // HEAD_DIM, HEAD_DIM)
    query_unit, query_scale = rms_rows(projected[:, 0])
    key_unit, key_scale = rms_rows(projected[:, 1])
    return (query_unit, query_scale, key_unit, key_scale, projected[:, 2])


def contract_last(left, right):
    return lax.dot_general(
        left, right, (((1,), (1,)), ((), ())), preferred_element_type=jnp.float32
    )


def window_exp(query_blk, key_blk, first_pos):
    scores = jnp.einsum(
        "qhd,khd->hqk", query_blk, key_blk, preferred_element_type=jnp.float32
    ) * HEAD_DIM ** (-0.5)
    query_pos = lax.broadcasted_iota(jnp.int32, (query_blk.shape[0], key_blk.shape[0]), 0)
    key_pos = lax.broadcasted_iota(jnp.int32, (query_blk.shape[0], key_blk.shape[0]), 1)
    gap = WINDOW + query_pos - key_pos
    allowed = (gap >= 0) & (gap < WINDOW) & (first_pos - WINDOW + key_pos >= 0)
    return jnp.where(allowed[None], jnp.exp(scores), 0.0)


def send_down(rows, distance):
    return from_behind(rows, ("seq", "sub"), distance)


def send_up(rows, distance):
    return from_behind(rows.astype(jnp.bfloat16), ("seq", "sub"), -distance).astype(rows.dtype)


def gather_group(rows):
    return gathered_copies(rows, "sub", 0)


def sum_heads(rows):
    return sent_and_summed(rows.astype(jnp.bfloat16), "sub", 0)


def per_device(tokens, cotangent, fine_qkv, fine_out, coarse_qkv, coarse_out):
    row_count = tokens.shape[0]
    score_scale = HEAD_DIM ** (-0.5)
    lead_rows = POOL - 1
    tail_rows = min(WINDOW, row_count)
    hop_count = -(-WINDOW // row_count)
    margin = hop_count * tail_rows
    block_rows = min(row_count, 512)
    anchor = lax.axis_index(("seq", "sub")) * row_count
    normed_fine, scale_fine = rms_rows(tokens)
    query_unit1, query_scale1, key_unit1, key_scale1, value_raw1 = project_rows(
        normed_fine.astype(jnp.bfloat16), fine_qkv
    )
    query_one = query_unit1.astype(jnp.bfloat16)
    key_one = key_unit1.astype(jnp.bfloat16)
    value_one = value_raw1.astype(jnp.bfloat16)
    own_tail = jnp.stack([key_one.reshape(tail_rows, D), value_one.reshape(tail_rows, D)])
    earlier = []
    for distance in range(1, hop_count + 1):
        earlier.append(send_down(own_tail, distance))
    key_all = jnp.concatenate(
        [pieces[0] for pieces in earlier[::-1]] + [key_one.reshape(row_count, D)]
    ).reshape(margin + row_count, HEADS, HEAD_DIM)
    value_all = jnp.concatenate(
        [pieces[1] for pieces in earlier[::-1]] + [value_one.reshape(row_count, D)]
    ).reshape(margin + row_count, HEADS, HEAD_DIM)
    block_start = 0
    numer = window_exp(query_one, key_all, anchor + block_start)
    totals = jnp.sum(numer, axis=-1)
    probs_half = (numer / totals[:, :, None]).astype(jnp.bfloat16)
    attended_list = jnp.einsum(
        "hqk,khd->qhd", probs_half, value_all, preferred_element_type=jnp.float32
    ).astype(jnp.bfloat16)
    hidden = (
        tokens.astype(jnp.float32)
        + jnp.dot(attended_list.reshape(row_count, D), fine_out, preferred_element_type=jnp.float32)
    ).astype(jnp.bfloat16)
    carried_rows = send_down(hidden[row_count - lead_rows :], 1)
    shifted = jnp.concatenate([carried_rows, hidden[: row_count - lead_rows]])
    pooled = (
        shifted.reshape(row_count // POOL, POOL, D)
        .astype(jnp.float32)
        .mean(axis=1)
        .astype(jnp.bfloat16)
    )
    group_in = gather_group(pooled)
    group_size = group_in.shape[0]
    local_width = coarse_qkv.shape[2]
    local_heads = local_width // HEAD_DIM
    normed_coarse, scale_coarse = rms_rows(group_in)
    query_unit2, query_scale2, key_unit2, key_scale2, value_raw2 = project_rows(
        normed_coarse.astype(jnp.bfloat16), coarse_qkv
    )
    query_two = query_unit2.astype(jnp.bfloat16)
    key_two = key_unit2.astype(jnp.bfloat16)
    value_two = value_raw2.astype(jnp.bfloat16)
    every_key, every_value = sent_together(
        (key_two.reshape(group_size, local_width), value_two.reshape(group_size, local_width)),
        "seq",
        0,
        1,
    )
    coarse_len = every_key.shape[0]
    every_key = every_key.reshape(coarse_len, local_heads, HEAD_DIM)
    every_value = every_value.reshape(coarse_len, local_heads, HEAD_DIM)
    group_start = lax.axis_index("seq") * group_size
    query_pos = group_start + lax.broadcasted_iota(jnp.int32, (group_size, coarse_len), 0)
    key_pos = lax.broadcasted_iota(jnp.int32, (group_size, coarse_len), 1)
    scores_two = (
        jnp.einsum("qhd,khd->hqk", query_two, every_key, preferred_element_type=jnp.float32)
        * score_scale
    )
    numer_two = jnp.where((key_pos <= query_pos)[None], jnp.exp(scores_two), 0.0)
    totals_two = jnp.sum(numer_two, axis=-1)
    probs_full2 = numer_two / totals_two[:, :, None]
    probs_half2 = probs_full2.astype(jnp.bfloat16)
    attended_two = jnp.einsum(
        "hqk,khd->qhd", probs_half2, every_value, preferred_element_type=jnp.float32
    ).astype(jnp.bfloat16)
    mixed_rows = sum_heads(
        jnp.dot(
            attended_two.reshape(group_size, local_width),
            coarse_out,
            preferred_element_type=jnp.float32,
        )
    )
    coarse_state = (pooled.astype(jnp.float32) + mixed_rows).astype(jnp.bfloat16)
    output = (
        hidden.astype(jnp.float32) + jnp.repeat(coarse_state, POOL, axis=0).astype(jnp.float32)
    ).astype(jnp.bfloat16)
    grad_rows = cotangent.astype(jnp.float32)
    coarse_grad = grad_rows.reshape(row_count // POOL, POOL, D).sum(axis=1)
    group_grad = gather_group(coarse_grad.astype(jnp.bfloat16))
    grad_att2 = (
        contract_last(group_grad, coarse_out)
        .astype(jnp.bfloat16)
        .reshape(group_size, local_heads, HEAD_DIM)
    )
    deltas_two = jnp.sum(grad_att2.astype(jnp.float32) * attended_two.astype(jnp.float32), axis=-1)
    prob_grad2 = jnp.einsum(
        "qhd,khd->hqk", grad_att2, every_value, preferred_element_type=jnp.float32
    )
    dscore_two = (probs_full2 * (prob_grad2 - deltas_two.T[:, :, None])).astype(jnp.bfloat16)
    query_grad2 = (
        jnp.einsum("hqk,khd->qhd", dscore_two, every_key, preferred_element_type=jnp.float32)
        * score_scale
    )
    piece_query = gathered_copies(query_two.reshape(group_size, local_width), "seq", 0).reshape(
        -1, local_heads, HEAD_DIM
    )
    piece_grad = gathered_copies(grad_att2.reshape(group_size, local_width), "seq", 0).reshape(
        -1, local_heads, HEAD_DIM
    )
    piece_rows = piece_query.shape[0]
    scores = (
        jnp.einsum("qhd,khd->hqk", piece_query, key_two, preferred_element_type=jnp.float32)
        * score_scale
    )
    later_pos = lax.broadcasted_iota(jnp.int32, (piece_rows, group_size), 0)
    own_pos = group_start + lax.broadcasted_iota(jnp.int32, (piece_rows, group_size), 1)
    numer = jnp.where((own_pos <= later_pos)[None], jnp.exp(scores), 0.0)
    probs_full = (
        numer
        / gathered_copies(totals_two.T.astype(jnp.bfloat16), "seq", 0)
        .astype(jnp.float32)
        .T[:, :, None]
    )
    prob_grad = jnp.einsum(
        "qhd,khd->hqk", piece_grad, value_two, preferred_element_type=jnp.float32
    )
    dscore = (
        probs_full
        * (
            prob_grad
            - gathered_copies(deltas_two.astype(jnp.bfloat16), "seq", 0)
            .astype(deltas_two.dtype)
            .T[:, :, None]
        )
    ).astype(jnp.bfloat16)
    key_grad2 = (
        jnp.einsum("hqk,qhd->khd", dscore, piece_query, preferred_element_type=jnp.float32)
        * score_scale
    )
    value_grad2 = jnp.einsum(
        "hqk,qhd->khd",
        probs_full.astype(jnp.bfloat16),
        piece_grad,
        preferred_element_type=jnp.float32,
    )
    query_grad2 = norm_back(query_grad2, query_unit2, query_scale2)
    key_grad2 = norm_back(key_grad2, key_unit2, key_scale2)
    qkv_grad2 = (
        jnp.stack([query_grad2, key_grad2, value_grad2], axis=1)
        .astype(jnp.bfloat16)
        .reshape(group_size, 3 * local_width)
    )
    normed_grad2 = sum_heads(contract_last(qkv_grad2, coarse_qkv.reshape(D, 3 * local_width)))
    normed_own, scale_own = rms_rows(pooled)
    pooled_grad = coarse_grad + norm_back(normed_grad2, normed_own, scale_own)
    spread = jnp.repeat(pooled_grad / POOL, POOL, axis=0)
    incoming = send_up(spread[:lead_rows], 1)
    hidden_grad = grad_rows + jnp.concatenate([spread[lead_rows:], incoming])
    grad_att1 = (
        contract_last(hidden_grad.astype(jnp.bfloat16), fine_out)
        .astype(jnp.bfloat16)
        .reshape(row_count, HEADS, HEAD_DIM)
    )
    deltas_one = jnp.sum(grad_att1.astype(jnp.float32) * attended_list.astype(jnp.float32), axis=-1)
    key_grad_all = jnp.zeros((margin + row_count, HEADS, HEAD_DIM), jnp.float32)
    value_grad_all = jnp.zeros((margin + row_count, HEADS, HEAD_DIM), jnp.float32)
    block_start = 0
    low_key = block_start + margin - WINDOW
    numer = window_exp(query_one, key_all, anchor + block_start)
    probs_full = numer / totals[:, block_start : block_start + block_rows, None]
    prob_grad = jnp.einsum("qhd,khd->hqk", grad_att1, value_all, preferred_element_type=jnp.float32)
    dscore = (probs_full * (prob_grad - deltas_one.T[:, :, None])).astype(jnp.bfloat16)
    query_list = (
        jnp.einsum("hqk,khd->qhd", dscore, key_all, preferred_element_type=jnp.float32)
        * score_scale
    )
    key_grad_all = key_grad_all.at[low_key : low_key + WINDOW + block_rows].add(
        jnp.einsum("hqk,qhd->khd", dscore, query_one, preferred_element_type=jnp.float32)
        * score_scale
    )
    value_grad_all = value_grad_all.at[low_key : low_key + WINDOW + block_rows].add(
        jnp.einsum(
            "hqk,qhd->khd",
            probs_full.astype(jnp.bfloat16),
            grad_att1,
            preferred_element_type=jnp.float32,
        )
    )
    stacked = jnp.stack(
        [key_grad_all.reshape(margin + row_count, D), value_grad_all.reshape(margin + row_count, D)]
    )

    def halo_part(distance):
        return stacked[:, margin - distance * tail_rows : margin - (distance - 1) * tail_rows]

    arriving = send_up(halo_part(1), 1)
    for distance in range(2, hop_count + 1):
        arriving = arriving + send_up(halo_part(distance), distance)
    own_grads = stacked[:, margin:].at[:, row_count - tail_rows :].add(arriving)
    query_grad1 = norm_back(query_list, query_unit1, query_scale1)
    key_grad1 = norm_back(own_grads[0].reshape(row_count, HEADS, HEAD_DIM), key_unit1, key_scale1)
    value_grad1 = own_grads[1].reshape(row_count, HEADS, HEAD_DIM)
    qkv_grad1 = (
        jnp.stack([query_grad1, key_grad1, value_grad1], axis=1)
        .astype(jnp.bfloat16)
        .reshape(row_count, 3 * D)
    )
    normed_grad1 = contract_last(qkv_grad1, fine_qkv.reshape(D, 3 * D))
    grad_tokens = (hidden_grad + norm_back(normed_grad1, normed_fine, scale_fine)).astype(
        jnp.bfloat16
    )
    return (output, grad_tokens)


def solution(mesh):
    placed = (
        P(("seq", "sub"), None),
        P(("seq", "sub"), None),
        P(),
        P(),
        P(None, None, "sub"),
        P("sub", None),
    )
    return jax.shard_map(
        per_device,
        mesh=mesh,
        in_specs=placed,
        out_specs=(P(("seq", "sub"), None), P(("seq", "sub"), None)),
        check_vma=False,
    )
```

profile of v0, /device:TPU:4, one launch (start us, length us, event | category | flops | bytes accessed | tf_op | source)
XLA Modules:
  0.0 340.0 jit_solution(17694499258041698001)
XLA Ops:
  8.4 8.7 %copy.54 = bf16[1024,3,1024]{0,2,1:T(8,128)(2,1)} copy(bf16[1024,3,1024]{2,0,1:T(8,128)(2,1)} %param.20) | data formatting | bytes 12582912 | tf_op args[2]
  17.1 4.7 %fusion.60 = f32[128,3,16,64]{0,3,2,1:T(8,128)S(1)} fusion(bf16[3,16,64,1024]{3,2,1,0:T(8,128)(2,1)} %bitcast.208, bf16[128,1024]{1,0:T(8,128)(2,1)S(1)} %copy-done.5, f32[128]{0:T(128)S(1)} %add_rsqrt_fusion.6), kind=kOutput, calls=%fused_computation.102 | convolution fusion | flops 805699584 | bytes 8126976 | tf_op jit(solution)/shard_map/dot_general | solution.py:71
  23.2 4.6 %collective-permute-start.1 = (bf16[2,128,1024]{1,2,0:T(8,128)(2,1)S(1)}, bf16[2,128,1024]{1,2,0:T(8,128)(2,1)}, u32[]{:S(2)}, u32[]{:S(2)}) collective-permute-start(bf16[2,128,1024]{1,2,0:T(8,128)(2,1)S(1)} %pad_maximum_fusion.2), channel_id=1, source_target_pairs={{0,3},{1,4},{2,5},{3,6},{4,7},{5,8},{6,9},{7,10},{8,11},{9,12},{10... | collective-permute-start | bytes 1572872 | tf_op jit(solution)/shard_map/ppermute | solution.py:19
  36.1 3.2 collective-permute-done.1
  40.4 26.0 %collective-permute-done = bf16[2,128,1024]{1,2,0:T(8,128)(2,1)} collective-permute-done((bf16[2,128,1024]{1,2,0:T(8,128)(2,1)S(1)}, bf16[2,128,1024]{1,2,0:T(8,128)(2,1)}, u32[]{:S(2)}, u32[]{:S(2)}) %collective-permute-start) | collective-permute-done | bytes 524320 | tf_op jit(solution)/shard_map/ppermute | solution.py:19
  74.6 18.5 %collective-permute-start.4 = (bf16[15,1024]{1,0:T(8,128)(2,1)}, bf16[15,1024]{1,0:T(8,128)(2,1)}, u32[]{:S(2)}, u32[]{:S(2)}) collective-permute-start(bf16[15,1024]{1,0:T(8,128)(2,1)} %slice.182), channel_id=1, source_target_pairs={{0,1},{1,2},{2,3},{3,4},{4,5},{5,6},{6,7},{7,8},{8,9},{9,10},{10,1... | collective-permute-start | bytes 92168 | tf_op jit(solution)/shard_map/ppermute | solution.py:19
  94.5 6.8 %all-to-all-start.2 = ((bf16[8,8,1024]{2,1,0:T(8,128)(2,1)}), bf16[8,8,1024]{2,1,0:T(8,128)(2,1)S(1)}, u32[]{:S(2)}, u32[]{:S(2)}) async-start(bf16[8,8,1024]{2,1,0:T(8,128)(2,1)} %broadcast_in_dim.62), calls=%async_computation.2 | async-start | bytes 262144 | tf_op jit(solution)/shard_map/all_to_all | solution.py:24
  106.0 5.9 %all-to-all-start = ((bf16[8,8,1024]{2,1,0:T(8,128)(2,1)}), bf16[8,8,1024]{2,1,0:T(8,128)(2,1)S(1)}, u32[]{:S(2)}, u32[]{:S(2)}) async-start(bf16[8,8,1024]{2,1,0:T(8,128)(2,1)} %broadcast_in_dim.58), calls=%async_computation | async-start | bytes 262144 | tf_op jit(solution)/shard_map/all_to_all | solution.py:24
  117.5 10.7 %all-to-all-start.5 = ((bf16[32,64,128]{2,1,0:T(8,128)(2,1)}), bf16[32,64,128]{2,1,0:T(8,128)(2,1)}, u32[]{:S(2)}, u32[]{:S(2)}) async-start(bf16[32,64,128]{2,1,0:T(8,128)(2,1)} %broadcast_in_dim.67), calls=%async_computation.5 | async-start | bytes 1048576 | tf_op jit(solution)/shard_map/all_to_all | solution.py:24
  135.0 12.1 %all-to-all-done.5 = bf16[32,64,128]{2,1,0:T(8,128)(2,1)} async-done(((bf16[32,64,128]{2,1,0:T(8,128)(2,1)}), bf16[32,64,128]{2,1,0:T(8,128)(2,1)}, u32[]{:S(2)}, u32[]{:S(2)}) %all-to-all-start.5) | async-done | bytes 524320 | tf_op jit(solution)/shard_map/all_to_all | solution.py:24
  148.1 4.8 %all-to-all-start.3 = ((bf16[32,64,128]{2,1,0:T(8,128)(2,1)}), bf16[32,64,128]{2,1,0:T(8,128)(2,1)}, u32[]{:S(2)}, u32[]{:S(2)}) async-start(bf16[32,64,128]{2,1,0:T(8,128)(2,1)} %broadcast_in_dim.63), calls=%async_computation.3 | async-start | bytes 1048576 | tf_op jit(solution)/shard_map/all_to_all | solution.py:24
  154.7 3.2 reshape.455
  157.9 3.6 %copy.79 = bf16[2048,2,64]{0,2,1:T(8,128)(2,1)} copy(bf16[2048,2,64]{2,1,0:T(2,128)(2,1)} %reshape.455) | data formatting | bytes 1048576 | tf_op jit(solution)/shard_map/reshape;reshape | solution.py:225
  161.4 10.2 %all-to-all-done.3 = bf16[32,64,128]{2,1,0:T(8,128)(2,1)} async-done(((bf16[32,64,128]{2,1,0:T(8,128)(2,1)}), bf16[32,64,128]{2,1,0:T(8,128)(2,1)}, u32[]{:S(2)}, u32[]{:S(2)}) %all-to-all-start.3) | async-done | bytes 524320 | tf_op jit(solution)/shard_map/all_to_all | solution.py:24
  174.8 3.6 %copy.78 = bf16[2048,2,64]{0,2,1:T(8,128)(2,1)} copy(bf16[2048,2,64]{2,1,0:T(2,128)(2,1)} %reshape.454) | data formatting | bytes 1048576 | tf_op jit(solution)/shard_map/reshape;reshape | solution.py:222
  178.4 15.6 %all-gather.2.cloned.1.call-done = bf16[2048,256]{1,0:T(8,128)(2,1)} async-done(((bf16[64,256]{1,0:T(8,128)(2,1)}), bf16[2048,256]{1,0:T(8,128)(2,1)}) %all-gather.2.cloned.1.call-update) | async-done | bytes 1048592 | tf_op jit(solution)/shard_map/all_gather | solution.py:51
  203.5 6.0 %all-to-all-start.4 = ((bf16[32,64,2]{1,2,0:T(2,128)(2,1)}), bf16[32,64,2]{1,2,0:T(2,128)(2,1)S(1)}, u32[]{:S(2)}, u32[]{:S(2)}) async-start(bf16[32,64,2]{1,2,0:T(2,128)(2,1)} %broadcast_in_dim.66), calls=%async_computation.4 | async-start | bytes 32768 | tf_op jit(solution)/shard_map/all_to_all | solution.py:24
  212.2 7.0 %all-to-all-done.4 = bf16[32,64,2]{1,2,0:T(2,128)(2,1)S(1)} async-done(((bf16[32,64,2]{1,2,0:T(2,128)(2,1)}), bf16[32,64,2]{1,2,0:T(2,128)(2,1)S(1)}, u32[]{:S(2)}, u32[]{:S(2)}) %all-to-all-start.4) | async-done | bytes 8224 | tf_op jit(solution)/shard_map/all_to_all | solution.py:24
  219.9 3.8 %all-to-all-start.6 = ((bf16[32,64,2]{1,2,0:T(2,128)(2,1)}), bf16[32,64,2]{1,2,0:T(2,128)(2,1)S(1)}, u32[]{:S(2)}, u32[]{:S(2)}) async-start(bf16[32,64,2]{1,2,0:T(2,128)(2,1)} %broadcast_in_dim.68), calls=%async_computation.6 | async-start | bytes 32768 | tf_op jit(solution)/shard_map/all_to_all | solution.py:24
  223.8 9.7 %all-to-all-done.6 = bf16[32,64,2]{1,2,0:T(2,128)(2,1)S(1)} async-done(((bf16[32,64,2]{1,2,0:T(2,128)(2,1)}), bf16[32,64,2]{1,2,0:T(2,128)(2,1)S(1)}, u32[]{:S(2)}, u32[]{:S(2)}) %all-to-all-start.6) | async-done | bytes 8224 | tf_op jit(solution)/shard_map/all_to_all | solution.py:24
  233.4 4.8 %all-to-all-start.1 = ((bf16[8,8,1024]{2,1,0:T(8,128)(2,1)}), bf16[8,8,1024]{2,1,0:T(8,128)(2,1)S(1)}, u32[]{:S(2)}, u32[]{:S(2)}) async-start(bf16[8,8,1024]{2,1,0:T(8,128)(2,1)} %fusion.24), calls=%async_computation.1 | async-start | bytes 262144 | tf_op jit(solution)/shard_map/all_to_all | solution.py:45
  243.7 3.4 multiply_reduce_fusion.5
  251.0 5.7 %all-to-all-start.7 = ((bf16[8,8,1024]{2,1,0:T(8,128)(2,1)}), bf16[8,8,1024]{2,1,0:T(8,128)(2,1)S(1)}, u32[]{:S(2)}, u32[]{:S(2)}) async-start(bf16[8,8,1024]{2,1,0:T(8,128)(2,1)} %fusion.23), calls=%async_computation.7 | async-start | bytes 262144 | tf_op jit(solution)/shard_map/all_to_all | solution.py:45
  257.3 3.4 all-to-all-done.7
  261.8 3.7 %collective-permute-start.5 = (bf16[15,1024]{1,0:T(8,128)(2,1)S(1)}, bf16[15,1024]{1,0:T(8,128)(2,1)S(1)}, u32[]{:S(2)}, u32[]{:S(2)}) collective-permute-start(bf16[15,1024]{1,0:T(8,128)(2,1)S(1)} %slice.246), channel_id=1, source_target_pairs={{1,0},{2,1},{3,2},{4,3},{5,4},{6,5},{7,6},{8,7},{9,8},{10,9},{11,1... | collective-permute-start | bytes 92168 | tf_op jit(solution)/shard_map/ppermute | solution.py:19
  269.9 3.5 %fusion.12 = f32[16,64,640]{2,1,0:T(8,128)S(1)} fusion(bf16[128,16,64]{0,2,1:T(8,128)(2,1)S(1)} %bitcast.225, f32[16,128,640]{2,1,0:T(8,128)} %copy-done.32, f32[16,128]{1,0:T(8,128)} %copy-done.33, pred[128,640]{1,0:T(8,128)(4,1)S(1)} %copy-done.23), kind=kOutput, calls=%fused_computation.22 | convolution fusion | flops 173015040 | bytes 8216576 | tf_op jit(solution)/shard_map/hqk,qhd->khd/dot_general | solution.py:300
  273.5 3.8 %multiply_convert_fusion = bf16[16,128,640]{2,1,0:T(8,128)(2,1)S(1)} fusion(f32[16,128]{1,0:T(8,128)S(1)} %bitcast.248, bf16[128,16,64]{0,2,1:T(8,128)(2,1)S(1)} %bitcast.226, bf16[640,16,64]{0,2,1:T(8,128)(2,1)S(1)} %copy-done.25, f32[16,128]{1,0:T(8,128)S(1)} %copy-done.34, f32[16,128,640]{2,1,0:T(8,128)} %copy-done.32, pred[128,640]{1,0:T(8,128)(4,1)S(1)} %copy-done.23), kind=kOutput, calls=%fused_computation.4 | convolution fusion | flops 175636480 | bytes 9535488 | tf_op jit(solution)/shard_map/qhd,khd->hqk/dot_general | solution.py:289
  278.7 3.7 %collective-permute-start.6 = (bf16[2,128,1024]{1,2,0:T(8,128)(2,1)S(1)}, bf16[2,128,1024]{1,2,0:T(8,128)(2,1)S(1)}, u32[]{:S(2)}, u32[]{:S(2)}) collective-permute-start(bf16[2,128,1024]{1,2,0:T(8,128)(2,1)S(1)} %get-tuple-element.72), channel_id=1, source_target_pairs={{1,0},{2,1},{3,2},{4,3},{5,4},{6,5},{7,6},{8,7},{9,8},{10,9},{11,1... | collective-permute-start | bytes 1572872 | tf_op jit(solution)/shard_map/ppermute | solution.py:19
  289.4 3.9 %collective-permute-done.6 = bf16[2,128,1024]{1,2,0:T(8,128)(2,1)S(1)} collective-permute-done((bf16[2,128,1024]{1,2,0:T(8,128)(2,1)S(1)}, bf16[2,128,1024]{1,2,0:T(8,128)(2,1)S(1)}, u32[]{:S(2)}, u32[]{:S(2)}) %collective-permute-start.6) | collective-permute-done | bytes 524320 | tf_op jit(solution)/shard_map/ppermute | solution.py:19
  293.3 5.0 %collective-permute-done.9 = bf16[2,128,1024]{1,2,0:T(8,128)(2,1)S(1)} collective-permute-done((bf16[2,128,1024]{1,2,0:T(8,128)(2,1)S(1)}, bf16[2,128,1024]{1,2,0:T(8,128)(2,1)S(1)}, u32[]{:S(2)}, u32[]{:S(2)}) %collective-permute-start.9) | collective-permute-done | bytes 524320 | tf_op jit(solution)/shard_map/ppermute | solution.py:19
  298.2 13.1 %collective-permute-done.8 = bf16[2,128,1024]{1,2,0:T(8,128)(2,1)S(1)} collective-permute-done((bf16[2,128,1024]{1,2,0:T(8,128)(2,1)S(1)}, bf16[2,128,1024]{1,2,0:T(8,128)(2,1)S(1)}, u32[]{:S(2)}, u32[]{:S(2)}) %collective-permute-start.8) | collective-permute-done | bytes 524320 | tf_op jit(solution)/shard_map/ppermute | solution.py:19
  311.3 18.3 %collective-permute-done.7 = bf16[2,128,1024]{1,2,0:T(8,128)(2,1)S(1)} collective-permute-done((bf16[2,128,1024]{1,2,0:T(8,128)(2,1)S(1)}, bf16[2,128,1024]{1,2,0:T(8,128)(2,1)S(1)}, u32[]{:S(2)}, u32[]{:S(2)}) %collective-permute-start.7) | collective-permute-done | bytes 524320 | tf_op jit(solution)/shard_map/ppermute | solution.py:19
  (203 shorter events, 84.0 us)
Async XLA Ops:
  7.2 66.2 %copy-start = (bf16[1024,1024]{1,0:T(8,128)(2,1)S(1)}, bf16[1024,1024]{1,0:T(8,128)(2,1)}, u32[]{:S(2)}) copy-start(bf16[1024,1024]{1,0:T(8,128)(2,1)} %param.21) | copy-start | bytes 6291460
  23.1 46.2 %copy-start.18 = (f32[128,16]{0,1:T(8,128)}, f32[128,16]{0,1:T(8,128)S(1)}, u32[]{:S(2)}) copy-start(f32[128,16]{0,1:T(8,128)S(1)} %get-tuple-element.102) | copy-start | bytes 24580
  23.1 46.3 %copy-start.20 = (f32[128,16]{0,1:T(8,128)}, f32[128,16]{0,1:T(8,128)S(1)}, u32[]{:S(2)}) copy-start(f32[128,16]{0,1:T(8,128)S(1)} %get-tuple-element.101) | copy-start | bytes 24580
  23.2 16.1 %collective-permute-start.1 = (bf16[2,128,1024]{1,2,0:T(8,128)(2,1)S(1)}, bf16[2,128,1024]{1,2,0:T(8,128)(2,1)}, u32[]{:S(2)}, u32[]{:S(2)}) collective-permute-start(bf16[2,128,1024]{1,2,0:T(8,128)(2,1)S(1)} %pad_maximum_fusion.2), channel_id=1, source_target_pairs={{0,3},{1,4},{2,5},{3,6},{4,7},{5,8},{6,9},{7,10},{8,11},{9,12},{10... | collective-permute-start | bytes 1572872 | tf_op jit(solution)/shard_map/ppermute | solution.py:19
  27.8 41.0 %collective-permute-start.3 = (bf16[2,128,1024]{1,2,0:T(8,128)(2,1)S(1)}, bf16[2,128,1024]{1,2,0:T(8,128)(2,1)S(1)}, u32[]{:S(2)}, u32[]{:S(2)}) collective-permute-start(bf16[2,128,1024]{1,2,0:T(8,128)(2,1)S(1)} %pad_maximum_fusion.2), channel_id=1, source_target_pairs={{0,1},{1,2},{2,3},{3,4},{4,5},{5,6},{6,7},{7,8},{8,9},{9,10},{10,1... | collective-permute-start | bytes 1572872 | tf_op jit(solution)/shard_map/ppermute | solution.py:19
  30.5 37.2 %collective-permute-start.2 = (bf16[2,128,1024]{1,2,0:T(8,128)(2,1)S(1)}, bf16[2,128,1024]{1,2,0:T(8,128)(2,1)}, u32[]{:S(2)}, u32[]{:S(2)}) collective-permute-start(bf16[2,128,1024]{1,2,0:T(8,128)(2,1)S(1)} %pad_maximum_fusion.2), channel_id=1, source_target_pairs={{0,2},{1,3},{2,4},{3,5},{4,6},{5,7},{6,8},{7,9},{8,10},{9,11},{10,... | collective-permute-start | bytes 1572872 | tf_op jit(solution)/shard_map/ppermute | solution.py:19
  33.6 32.8 %collective-permute-start = (bf16[2,128,1024]{1,2,0:T(8,128)(2,1)S(1)}, bf16[2,128,1024]{1,2,0:T(8,128)(2,1)}, u32[]{:S(2)}, u32[]{:S(2)}) collective-permute-start(bf16[2,128,1024]{1,2,0:T(8,128)(2,1)S(1)} %pad_maximum_fusion.2), channel_id=1, source_target_pairs={{0,4},{1,5},{2,6},{3,7},{4,8},{5,9},{6,10},{7,11},{8,12},{9,13},{1... | collective-permute-start | bytes 1572872 | tf_op jit(solution)/shard_map/ppermute | solution.py:19
  36.1 34.9 %copy-start.22 = (pred[128,640]{1,0:T(8,128)(4,1)}, pred[128,640]{1,0:T(8,128)(4,1)S(1)}, u32[]{:S(2)}) copy-start(pred[128,640]{1,0:T(8,128)(4,1)S(1)} %fusion.54) | copy-start | bytes 245764
  40.4 28.5 %copy-start.3 = (f32[128,3,16,64]{0,3,2,1:T(8,128)S(1)}, f32[128,3,16,64]{0,3,2,1:T(8,128)}, u32[]{:S(2)}) copy-start(f32[128,3,16,64]{0,3,2,1:T(8,128)} %copy-done.2) | copy-start | bytes 4718596
  73.9 43.7 %copy-start.8 = (bf16[128,1024]{1,0:T(8,128)(2,1)}, bf16[128,1024]{1,0:T(8,128)(2,1)S(1)}, u32[]{:S(2)}) copy-start(bf16[128,1024]{1,0:T(8,128)(2,1)S(1)} %fusion.22) | copy-start | bytes 786436
  74.6 28.2 %collective-permute-start.4 = (bf16[15,1024]{1,0:T(8,128)(2,1)}, bf16[15,1024]{1,0:T(8,128)(2,1)}, u32[]{:S(2)}, u32[]{:S(2)}) collective-permute-start(bf16[15,1024]{1,0:T(8,128)(2,1)} %slice.182), channel_id=1, source_target_pairs={{0,1},{1,2},{2,3},{3,4},{4,5},{5,6},{6,7},{7,8},{8,9},{9,10},{10,1... | collective-permute-start | bytes 92168 | tf_op jit(solution)/shard_map/ppermute | solution.py:19
  94.5 10.8 %all-to-all-start.2 = ((bf16[8,8,1024]{2,1,0:T(8,128)(2,1)}), bf16[8,8,1024]{2,1,0:T(8,128)(2,1)S(1)}, u32[]{:S(2)}, u32[]{:S(2)}) async-start(bf16[8,8,1024]{2,1,0:T(8,128)(2,1)} %broadcast_in_dim.62), calls=%async_computation.2 | async-start | bytes 262144 | tf_op jit(solution)/shard_map/all_to_all | solution.py:24
  106.0 9.9 %all-to-all-start = ((bf16[8,8,1024]{2,1,0:T(8,128)(2,1)}), bf16[8,8,1024]{2,1,0:T(8,128)(2,1)S(1)}, u32[]{:S(2)}, u32[]{:S(2)}) async-start(bf16[8,8,1024]{2,1,0:T(8,128)(2,1)} %broadcast_in_dim.58), calls=%async_computation | async-start | bytes 262144 | tf_op jit(solution)/shard_map/all_to_all | solution.py:24
  117.5 29.6 %all-to-all-start.5 = ((bf16[32,64,128]{2,1,0:T(8,128)(2,1)}), bf16[32,64,128]{2,1,0:T(8,128)(2,1)}, u32[]{:S(2)}, u32[]{:S(2)}) async-start(bf16[32,64,128]{2,1,0:T(8,128)(2,1)} %broadcast_in_dim.67), calls=%async_computation.5 | async-start | bytes 1048576 | tf_op jit(solution)/shard_map/all_to_all | solution.py:24
  128.2 65.8 %all-gather.2.cloned.1.call-start = ((), (), s32[]{:S(2)}) async-start(), calls=%async_computation.8 | async-start | bytes 1081344 | tf_op jit(solution)/shard_map/all_gather | solution.py:51
  134.9 65.5 %copy-start.27 = (f32[64,2]{0,1:T(2,128)}, f32[64,2]{0,1:T(2,128)S(1)}, u32[]{:S(2)}) copy-start(f32[64,2]{0,1:T(2,128)S(1)} %add_rsqrt_fusion.3) | copy-start | bytes 1540
  148.1 23.6 %all-to-all-start.3 = ((bf16[32,64,128]{2,1,0:T(8,128)(2,1)}), bf16[32,64,128]{2,1,0:T(8,128)(2,1)}, u32[]{:S(2)}, u32[]{:S(2)}) async-start(bf16[32,64,128]{2,1,0:T(8,128)(2,1)} %broadcast_in_dim.63), calls=%async_computation.3 | async-start | bytes 1048576 | tf_op jit(solution)/shard_map/all_to_all | solution.py:24
  154.7 54.9 %copy-start.26 = (bf16[64,128]{0,1:T(8,128)(2,1)}, bf16[64,128]{0,1:T(8,128)(2,1)S(1)}, u32[]{:S(2)}) copy-start(bf16[64,128]{0,1:T(8,128)(2,1)S(1)} %copy.62) | copy-start | bytes 49156
  202.9 30.6 %copy-start.30 = (f32[2,64]{1,0:T(2,128)}, f32[2,64]{1,0:T(2,128)S(1)}, u32[]{:S(2)}) copy-start(f32[2,64]{1,0:T(2,128)S(1)} %get-tuple-element.94) | copy-start | bytes 1540
  203.5 15.8 %all-to-all-start.4 = ((bf16[32,64,2]{1,2,0:T(2,128)(2,1)}), bf16[32,64,2]{1,2,0:T(2,128)(2,1)S(1)}, u32[]{:S(2)}, u32[]{:S(2)}) async-start(bf16[32,64,2]{1,2,0:T(2,128)(2,1)} %broadcast_in_dim.66), calls=%async_computation.4 | async-start | bytes 32768 | tf_op jit(solution)/shard_map/all_to_all | solution.py:24
  211.3 22.1 %copy-start.31 = (f32[64,2]{0,1:T(2,128)}, f32[64,2]{0,1:T(2,128)S(1)}, u32[]{:S(2)}) copy-start(f32[64,2]{0,1:T(2,128)S(1)} %get-tuple-element.96) | copy-start | bytes 1540
  219.9 13.6 %all-to-all-start.6 = ((bf16[32,64,2]{1,2,0:T(2,128)(2,1)}), bf16[32,64,2]{1,2,0:T(2,128)(2,1)S(1)}, u32[]{:S(2)}, u32[]{:S(2)}) async-start(bf16[32,64,2]{1,2,0:T(2,128)(2,1)} %broadcast_in_dim.68), calls=%async_computation.6 | async-start | bytes 32768 | tf_op jit(solution)/shard_map/all_to_all | solution.py:24
  233.4 17.6 %all-to-all-start.1 = ((bf16[8,8,1024]{2,1,0:T(8,128)(2,1)}), bf16[8,8,1024]{2,1,0:T(8,128)(2,1)S(1)}, u32[]{:S(2)}, u32[]{:S(2)}) async-start(bf16[8,8,1024]{2,1,0:T(8,128)(2,1)} %fusion.24), calls=%async_computation.1 | async-start | bytes 262144 | tf_op jit(solution)/shard_map/all_to_all | solution.py:45
  251.0 9.7 %all-to-all-start.7 = ((bf16[8,8,1024]{2,1,0:T(8,128)(2,1)}), bf16[8,8,1024]{2,1,0:T(8,128)(2,1)S(1)}, u32[]{:S(2)}, u32[]{:S(2)}) async-start(bf16[8,8,1024]{2,1,0:T(8,128)(2,1)} %fusion.23), calls=%async_computation.7 | async-start | bytes 262144 | tf_op jit(solution)/shard_map/all_to_all | solution.py:45
  261.8 5.9 %collective-permute-start.5 = (bf16[15,1024]{1,0:T(8,128)(2,1)S(1)}, bf16[15,1024]{1,0:T(8,128)(2,1)S(1)}, u32[]{:S(2)}, u32[]{:S(2)}) collective-permute-start(bf16[15,1024]{1,0:T(8,128)(2,1)S(1)} %slice.246), channel_id=1, source_target_pairs={{1,0},{2,1},{3,2},{4,3},{5,4},{6,5},{7,6},{8,7},{9,8},{10,9},{11,1... | collective-permute-start | bytes 92168 | tf_op jit(solution)/shard_map/ppermute | solution.py:19
  278.7 14.6 %collective-permute-start.6 = (bf16[2,128,1024]{1,2,0:T(8,128)(2,1)S(1)}, bf16[2,128,1024]{1,2,0:T(8,128)(2,1)S(1)}, u32[]{:S(2)}, u32[]{:S(2)}) collective-permute-start(bf16[2,128,1024]{1,2,0:T(8,128)(2,1)S(1)} %get-tuple-element.72), channel_id=1, source_target_pairs={{1,0},{2,1},{3,2},{4,3},{5,4},{6,5},{7,6},{8,7},{9,8},{10,9},{11,1... | collective-permute-start | bytes 1572872 | tf_op jit(solution)/shard_map/ppermute | solution.py:19
  282.4 15.8 %collective-permute-start.9 = (bf16[2,128,1024]{1,2,0:T(8,128)(2,1)S(1)}, bf16[2,128,1024]{1,2,0:T(8,128)(2,1)S(1)}, u32[]{:S(2)}, u32[]{:S(2)}) collective-permute-start(bf16[2,128,1024]{1,2,0:T(8,128)(2,1)S(1)} %get-tuple-element.73), channel_id=1, source_target_pairs={{4,0},{5,1},{6,2},{7,3},{8,4},{9,5},{10,6},{11,7},{12,8},{13,9},{1... | collective-permute-start | bytes 1572872 | tf_op jit(solution)/shard_map/ppermute | solution.py:19
  283.7 27.6 %collective-permute-start.8 = (bf16[2,128,1024]{1,2,0:T(8,128)(2,1)S(1)}, bf16[2,128,1024]{1,2,0:T(8,128)(2,1)S(1)}, u32[]{:S(2)}, u32[]{:S(2)}) collective-permute-start(bf16[2,128,1024]{1,2,0:T(8,128)(2,1)S(1)} %get-tuple-element.74), channel_id=1, source_target_pairs={{3,0},{4,1},{5,2},{6,3},{7,4},{8,5},{9,6},{10,7},{11,8},{12,9},{13... | collective-permute-start | bytes 1572872 | tf_op jit(solution)/shard_map/ppermute | solution.py:19
  285.0 44.7 %collective-permute-start.7 = (bf16[2,128,1024]{1,2,0:T(8,128)(2,1)S(1)}, bf16[2,128,1024]{1,2,0:T(8,128)(2,1)S(1)}, u32[]{:S(2)}, u32[]{:S(2)}) collective-permute-start(bf16[2,128,1024]{1,2,0:T(8,128)(2,1)S(1)} %get-tuple-element.75), channel_id=1, source_target_pairs={{2,0},{3,1},{4,2},{5,3},{6,4},{7,5},{8,6},{9,7},{10,8},{11,9},{12,... | collective-permute-start | bytes 1572872 | tf_op jit(solution)/shard_map/ppermute | solution.py:19
  288.2 42.5 %slice-start = ((s8[6291456]{0:T(1024)(128)(4,1)}), s8[2097152]{0:T(1024)(128)(4,1)S(1)}, s32[]{:S(2)}) async-start(s8[6291456]{0:T(1024)(128)(4,1)} %bitcast.209), calls=%async_computation.9 | async-start | bytes 4194304
  289.4 40.7 %copy-start.19 = (f32[128,16]{0,1:T(8,128)S(1)}, f32[128,16]{0,1:T(8,128)}, u32[]{:S(2)}) copy-start(f32[128,16]{0,1:T(8,128)} %copy-done.18) | copy-start | bytes 24580
  289.4 41.3 %slice-start.1 = ((s8[6291456]{0:T(1024)(128)(4,1)}), s8[4194304]{0:T(1024)(128)(4,1)S(1)}, s32[]{:S(2)}) async-start(s8[6291456]{0:T(1024)(128)(4,1)} %bitcast.209), calls=%async_computation.10 | async-start | bytes 8388608
  (24 other events, 135.5 us)
Sparse Core Ops, SparseCore 0:
  134.4 59.5 all-gather.1
where the time goes:
time: 342 us; the launch traced here: 340 us
  waiting for transfers between devices  133 us (39%)
  starting transfers between devices  92.1 us (27%)
  local copies, waits for them, and re-layouts  46.7 us (14%)
  matrix products  36 us (11%)
  other arithmetic  17.1 us (5%)
  between operations  15 us (4%)
    ppermute x10, waiting for transfers between devices, from_behind(): lax.ppermute(value, axis, [(source, source + steps) for source in range(f...  71.7 us
    ppermute x10, starting transfers between devices, from_behind(): lax.ppermute(value, axis, [(source, source + steps) for source in range(f...  43.6 us
    all_to_all x6, waiting for transfers between devices, from_everyone(): lax.all_to_all(jnp.broadcast_to(x[None], (peers, *x.shape)), axis, 0, 0,...  42.3 us
    all_to_all x6, starting transfers between devices, from_everyone(): lax.all_to_all(jnp.broadcast_to(x[None], (peers, *x.shape)), axis, 0, 0,...  38 us
    all_gather x1, waiting for transfers between devices, sent_together(): filled, at, done = (lax.all_gather(both, axis, axis=dim, tiled=True), 0, [])  15.6 us
    unnamed x84, local copies, waits for them, and re-layouts  13.1 us
    all_to_all x2, starting transfers between devices, sent_and_summed(): pieces = lax.all_to_all(split_up(x, dim, peers), axis, 0, 0, tiled=True)  10.5 us
  transfers between devices with their start and end apart: 19, of which 15 were waited for; matrix products, arithmetic and copies ran while one was open for 15% of the time, Pallas kernels for 0%

commit v1 on v0

v1 whole, which is shorter than its diff:
```python
import jax
import jax.numpy as jnp
from jax import lax
from jax.experimental import pallas as pl
from jax.experimental.pallas import tpu as pltpu
from jax.sharding import Mesh
from jax.sharding import PartitionSpec as P

D = 1024
HEADS = 16
HEAD_DIM = 64
WINDOW = 512
POOL = 16
EPS = 1e-06

LINE = ("y", "z_hi", "core", "z_lo", "x")
GROUP = ("core", "z_lo", "x")
FAR = ("y", "z_hi")

ROWS = 128
HALO = WINDOW
OWN_KEYS = HALO + ROWS
EXTRA = 16
ALL_KEYS = OWN_KEYS + EXTRA
QUERIES = EXTRA + ROWS
PAIR = 2 * HEAD_DIM
PAIRS = D // PAIR
COARSE = ROWS // POOL
SCALE = HEAD_DIM ** (-0.5)
NEG = -1e30

BF = jnp.bfloat16
F32 = jnp.float32


def shifted_by(value, steps):
    count = 1
    for name in LINE:
        count *= lax.axis_size(name)
    first, last = (max(0, -steps), min(count, count - steps))
    return lax.ppermute(value, LINE, [(source, source + steps) for source in range(first, last)])


def exchanged(pieces, axes):
    return lax.all_to_all(pieces, axes, 0, 0, tiled=True)


def last_last(left, right):
    return lax.dot_general(left, right, (((1,), (1,)), ((), ())), preferred_element_type=F32)


def first_first(left, right):
    return lax.dot_general(left, right, (((0,), (0,)), ((), ())), preferred_element_type=F32)


def plain(left, right):
    return jnp.dot(left, right, preferred_element_type=F32)


def low_lanes():
    return lax.broadcasted_iota(jnp.int32, (1, PAIR), 1) < HEAD_DIM


def pair_sums(values, low):
    low_sum = jnp.sum(jnp.where(low, values, 0.0), axis=-1, keepdims=True)
    high_sum = jnp.sum(jnp.where(low, 0.0, values), axis=-1, keepdims=True)
    return jnp.where(low, low_sum, high_sum)


def pair_norm(values, low):
    factor = lax.rsqrt(pair_sums(values * values, low) * (1.0 / HEAD_DIM) + EPS)
    return values * factor, factor


def pair_norm_back(grad, unit, factor, low):
    return factor * (grad - unit * (pair_sums(unit * grad, low) * (1.0 / HEAD_DIM)))


def row_norm(rows):
    factor = lax.rsqrt(jnp.mean(rows * rows, axis=-1, keepdims=True) + EPS)
    return rows * factor, factor


def row_norm_back(grad, normed, factor):
    return factor * (grad - normed * jnp.mean(normed * grad, axis=-1, keepdims=True))


def fine_forward_kernel(
    anchor_ref, t5, t4, t3, t2, t1, t0, cot_ref, w_ref, out_w_ref,
    q_ref, k_ref, v_ref, qf_ref, kf_ref, p_ref, att_ref, hid_ref, send_ref, cg_ref,
    normed, bias, acc,
):
    step = pl.program_id(0)
    anchor = anchor_ref[0]
    low = low_lanes()

    @pl.when(step == 0)
    def _():
        at = 0
        for ref in (t4, t3, t2, t1, t0, t5):
            rows = ref.shape[0]
            normed[at : at + rows, :] = row_norm(ref[...].astype(F32))[0].astype(BF)
            at += rows
        query_pos = lax.broadcasted_iota(jnp.int32, (QUERIES, ALL_KEYS), 0) - EXTRA
        column = lax.broadcasted_iota(jnp.int32, (QUERIES, ALL_KEYS), 1)
        key_pos = jnp.where(column < OWN_KEYS, column - HALO, column - (OWN_KEYS + HALO + EXTRA))
        gap = query_pos - key_pos
        allowed = (gap >= 0) & (gap < WINDOW) & (anchor + key_pos >= 0)
        bias[...] = jnp.where(allowed, 0.0, NEG)
        acc[...] = jnp.zeros_like(acc)

    query, q_factor = pair_norm(plain(normed[HALO - EXTRA : OWN_KEYS, :], w_ref[0]), low)
    both = plain(normed[...], jnp.concatenate([w_ref[1], w_ref[2]], axis=1))
    key, k_factor = pair_norm(both[:, :PAIR], low)
    value = both[:, PAIR:]
    key_b = key.astype(BF)
    q_ref[...] = query[EXTRA:].astype(BF)
    k_ref[...] = key_b[:OWN_KEYS]
    v_ref[...] = value[:OWN_KEYS].astype(BF)
    qf_ref[...] = q_factor[EXTRA:]
    kf_ref[...] = k_factor[:OWN_KEYS]
    attended = None
    for head, mask in enumerate((low, jnp.logical_not(low))):
        query_h = jnp.where(mask, query * SCALE, 0.0).astype(BF)
        numer = jnp.exp(last_last(query_h, key_b) + bias[...])
        total = jnp.sum(numer, axis=-1, keepdims=True)
        prob = (numer * (1.0 / jnp.where(total > 0.0, total, 1.0))).astype(BF)
        p_ref[head] = prob[EXTRA:, :OWN_KEYS]
        part = plain(prob, jnp.where(mask, value, 0.0).astype(BF))
        attended = part if attended is None else attended + part
    attended = attended.astype(BF)
    att_ref[...] = attended[EXTRA:]
    acc[...] += plain(attended, out_w_ref[...])

    @pl.when(step == PAIRS - 1)
    def _():
        before = t1[ROWS - EXTRA :, :].astype(F32) + acc[:EXTRA, :]
        before = jnp.where(anchor > 0, before, 0.0).astype(BF)
        own = (t0[...].astype(F32) + acc[EXTRA:, :]).astype(BF)
        hid_ref[...] = own
        chunk = lax.broadcasted_iota(jnp.int32, (COARSE, QUERIES), 0) * POOL
        row = lax.broadcasted_iota(jnp.int32, (COARSE, QUERIES), 1)
        member = jnp.where((row > chunk) & (row <= chunk + POOL), 1.0, 0.0).astype(BF)
        pooled = plain(member, jnp.concatenate([before, own], axis=0)) * (1.0 / POOL)
        chunk = lax.broadcasted_iota(jnp.int32, (COARSE, ROWS), 0) * POOL
        row = lax.broadcasted_iota(jnp.int32, (COARSE, ROWS), 1)
        member = jnp.where((row >= chunk) & (row < chunk + POOL), 1.0, 0.0).astype(BF)
        coarse_grad = plain(member, cot_ref[...])
        cg_ref[...] = coarse_grad
        message = jnp.concatenate([pooled, coarse_grad], axis=0).astype(BF)
        for peer in range(send_ref.shape[0]):
            send_ref[peer] = message


def coarse_project_kernel(got_ref, in_w_ref, out_w_ref, send_ref, factor_ref):
    low = low_lanes()
    rows = got_ref[...].astype(F32)
    count = rows.shape[0] * COARSE
    pooled = rows[:, :COARSE, :].reshape(count, D)
    coarse_grad = rows[:, COARSE:, :].reshape(count, D)
    normed = row_norm(pooled)[0].astype(BF)
    raw = plain(normed, in_w_ref[...]) + last_last(coarse_grad.astype(BF), out_w_ref[...])
    units, factors = [], []
    for tile in (raw[:, :PAIR], raw[:, PAIR:]):
        unit, factor = pair_norm(tile, low)
        units.append(jnp.where(low, unit, tile))
        factors.append(factor)
    message = jnp.concatenate(units, axis=1).astype(BF)
    factor_ref[...] = jnp.concatenate(factors, axis=1)
    for peer in range(send_ref.shape[0]):
        send_ref[peer] = message


def coarse_attention_kernel(
    start_ref, got_ref, factor_ref, in_w_ref, out_w_ref, send_ref, own_grad, left, right
):
    low = low_lanes()
    own_start = pl.multiple_of(start_ref[0], ROWS)
    length = got_ref.shape[0]
    block = 256
    chunk = 512

    left[...] = got_ref[:, :PAIR]
    right[...] = got_ref[:, PAIR:]
    own_left = left[pl.ds(own_start, ROWS), :]
    own_right = right[pl.ds(own_start, ROWS), :]
    zero = jnp.zeros((), BF)
    own_grad[...] = jnp.zeros_like(own_grad)

    def masked_halves(tile):
        wide = tile.astype(F32)
        return (
            jnp.where(low, wide * SCALE, 0.0).astype(BF),
            jnp.where(low, 0.0, wide).astype(BF),
        )

    def one_block(index, carry):
        first = pl.multiple_of(index * block, block)
        query, grad = masked_halves(left[pl.ds(first, block), :])
        query_pos = first + lax.broadcasted_iota(jnp.int32, (block, 1), 0)

        def one_chunk(at, sums):
            total, product = sums
            key_start = pl.multiple_of(at * chunk, chunk)
            keys = right[pl.ds(key_start, chunk), :]
            key_pos = key_start + lax.broadcasted_iota(jnp.int32, (1, chunk), 1)
            numer = jnp.where(key_pos <= query_pos, jnp.exp(last_last(query, keys)), 0.0)
            prob_grad = last_last(grad, keys)
            total = total + jnp.sum(numer, axis=-1, keepdims=True)
            product = product + jnp.sum(numer * prob_grad, axis=-1, keepdims=True)
            return total, product

        nothing = jnp.zeros((block, 1), F32)
        total, product = lax.fori_loop(0, index // (chunk // block) + 1, one_chunk, (nothing, nothing))
        inverse = 1.0 / total
        delta = product * inverse
        own_pos = own_start + lax.broadcasted_iota(jnp.int32, (1, ROWS), 1)
        numer = jnp.where(own_pos <= query_pos, jnp.exp(last_last(query, own_right)), 0.0)
        prob = numer * inverse
        score_grad = (prob * (last_last(grad, own_right) - delta)).astype(BF)
        own_grad[...] += first_first(score_grad, query) + first_first(prob.astype(BF), grad)
        return carry

    lax.fori_loop(own_start // block, length // block, one_block, 0)

    query, grad = masked_halves(own_left)
    query_pos = own_start + lax.broadcasted_iota(jnp.int32, (ROWS, 1), 0)
    key_pos = lax.broadcasted_iota(jnp.int32, (1, length), 1)
    keys = right[...]
    key_scaled, value = masked_halves(keys)
    numer = jnp.where(key_pos <= query_pos, jnp.exp(last_last(query, keys)), 0.0)
    prob_grad = last_last(grad, keys)
    inverse = 1.0 / jnp.sum(numer, axis=-1, keepdims=True)
    delta = jnp.sum(numer * prob_grad, axis=-1, keepdims=True) * inverse
    prob = numer * inverse
    score_grad = (prob * (prob_grad - delta)).astype(BF)
    mine = plain(score_grad, key_scaled) + plain(prob.astype(BF), value)

    parts = []
    for tile, unit, factor in (
        (mine, own_left, factor_ref[:, :PAIR]),
        (own_grad[...], own_right, factor_ref[:, PAIR:]),
    ):
        back = pair_norm_back(tile, unit.astype(F32), factor, low)
        parts.append(jnp.where(low, back, tile))
    parts = jnp.concatenate(parts, axis=1).astype(BF)
    peers = send_ref.shape[0]
    normed_grad = last_last(parts, in_w_ref[...]).reshape(peers, COARSE, D)
    mixed = plain(parts, out_w_ref[...]).reshape(peers, COARSE, D)
    send_ref[...] = jnp.concatenate([normed_grad, mixed], axis=1).astype(BF)


def coarse_finish_kernel(got_ref, pooled_ref, cg_ref, spread_ref, state_ref):
    summed = jnp.sum(got_ref[...].astype(F32), axis=0)
    pooled = pooled_ref[...].astype(F32)[:COARSE]
    normed, factor = row_norm(pooled)
    pooled_grad = cg_ref[...] + row_norm_back(summed[:COARSE], normed, factor)
    spread_ref[...] = pooled_grad * (1.0 / POOL)
    state_ref[...] = pooled + summed[COARSE:]


def fine_backward_kernel(
    cot_ref, spread_ref, next_ref, out_w_ref, w_ref, q_ref, k_ref, v_ref, qf_ref, kf_ref, p_ref,
    att_ref,
    h4, h3, h2, h1, own_ref, hg_ref,
    hidden_grad, acc,
):
    step = pl.program_id(0)
    low = low_lanes()

    @pl.when(step == 0)
    def _():
        block = (lax.broadcasted_iota(jnp.int32, (ROWS, 1), 0) + (POOL - 1)) // POOL
        added = jnp.zeros((ROWS, D), F32)
        for at in range(COARSE):
            added = jnp.where(block == at, spread_ref[at : at + 1, :], added)
        added = jnp.where(block == COARSE, next_ref[0:1, :], added)
        total = cot_ref[...].astype(F32) + added
        hg_ref[...] = total
        hidden_grad[...] = total.astype(BF)
        acc[...] = jnp.zeros_like(acc)

    att_grad = last_last(hidden_grad[...], out_w_ref[...]).astype(BF).astype(F32)
    delta_all = att_grad * att_ref[...].astype(F32)
    key = k_ref[...]
    value = v_ref[...]
    key_wide = key.astype(F32)
    query_wide = q_ref[...].astype(F32)
    query_grad = key_grad = value_grad = None
    for head, mask in enumerate((low, jnp.logical_not(low))):
        grad = jnp.where(mask, att_grad, 0.0).astype(BF)
        delta = jnp.sum(jnp.where(mask, delta_all, 0.0), axis=-1, keepdims=True)
        prob = p_ref[head]
        score_grad = (prob.astype(F32) * (last_last(grad, value) - delta)).astype(BF)
        dq = plain(score_grad, jnp.where(mask, key_wide * SCALE, 0.0).astype(BF))
        dk = first_first(score_grad, jnp.where(mask, query_wide * SCALE, 0.0).astype(BF))
        dv = first_first(prob, grad)
        if head == 0:
            query_grad, key_grad, value_grad = dq, dk, dv
        else:
            query_grad, key_grad, value_grad = query_grad + dq, key_grad + dk, value_grad + dv
    query_grad = pair_norm_back(query_grad, query_wide, qf_ref[...], low).astype(BF)
    key_grad = pair_norm_back(key_grad, key_wide, kf_ref[...], low).astype(BF)
    both = jnp.concatenate([key_grad, value_grad.astype(BF)], axis=1)
    acc[...] += last_last(both, jnp.concatenate([w_ref[1], w_ref[2]], axis=1))
    acc[HALO:, :] += last_last(query_grad, w_ref[0])

    @pl.when(step == PAIRS - 1)
    def _():
        for at, ref in enumerate((h4, h3, h2, h1)):
            ref[...] = acc[at * ROWS : (at + 1) * ROWS, :].astype(BF)
        own_ref[...] = acc[HALO:, :]


def fine_finish_kernel(own_ref, a1, a2, a3, a4, hg_ref, tokens_ref, out_ref):
    total = own_ref[...]
    for ref in (a1, a2, a3, a4):
        total = total + ref[...].astype(F32)
    normed, factor = row_norm(tokens_ref[...].astype(F32))
    out_ref[...] = (hg_ref[...] + row_norm_back(total, normed, factor)).astype(BF)


def whole(shape):
    return pl.BlockSpec(shape, lambda *_: (0,) * len(shape))


def pair_columns(rows):
    return pl.BlockSpec((rows, PAIR), lambda p: (0, p))


def shaped(shape, kind):
    return jax.ShapeDtypeStruct(shape, kind)


def params(mib):
    return pltpu.CompilerParams(vmem_limit_bytes=mib << 20)


def cost(flops, moved, exps=0):
    return pl.CostEstimate(flops=flops, bytes_accessed=moved, transcendentals=exps)


def per_device(tokens, cotangent, fine_qkv, fine_out, coarse_qkv, coarse_out):
    peers = 1
    for name in GROUP:
        peers *= lax.axis_size(name)
    groups = 1
    for name in FAR:
        groups *= lax.axis_size(name)
    core = lax.axis_index("core")
    scalar = pl.BlockSpec(memory_space=pltpu.SMEM)
    weights = jnp.transpose(fine_qkv, (1, 0, 2))
    coarse_all = jnp.transpose(coarse_qkv, (1, 0, 2))
    picked = jnp.where(core == 0, coarse_all[:, :, :HEAD_DIM], coarse_all[:, :, HEAD_DIM:])
    blank = jnp.zeros((D, HEAD_DIM), BF)
    coarse_in = jnp.concatenate([picked[0], blank, picked[1], picked[2]], axis=1)
    picked_out = jnp.where(core == 0, coarse_out[:HEAD_DIM], coarse_out[HEAD_DIM:])
    coarse_back = jnp.pad(picked_out, ((HEAD_DIM, PAIR), (0, 0)))

    t1, t2, t3, t4 = (shifted_by(tokens, steps) for steps in (1, 2, 3, 4))
    t5 = shifted_by(tokens[ROWS - EXTRA :], 5)
    anchor = (lax.axis_index(LINE) * ROWS).astype(jnp.int32).reshape(1)

    weight_block = pl.BlockSpec((3, D, PAIR), lambda p: (0, 0, p))
    out_block = pl.BlockSpec((PAIR, D), lambda p: (p, 0))
    query, key, value, q_factor, k_factor, probs, attended, hidden, message, coarse_grad = (
        pl.pallas_call(
            fine_forward_kernel,
            grid=(PAIRS,),
            in_specs=[scalar, whole((EXTRA, D))]
            + [whole((ROWS, D))] * 6
            + [weight_block, out_block],
            out_specs=[
                pair_columns(ROWS),
                pair_columns(OWN_KEYS),
                pair_columns(OWN_KEYS),
                pair_columns(ROWS),
                pair_columns(OWN_KEYS),
                pl.BlockSpec((2, ROWS, OWN_KEYS), lambda p: (p, 0, 0)),
                pair_columns(ROWS),
                whole((ROWS, D)),
                whole((peers, 2 * COARSE, D)),
                whole((COARSE, D)),
            ],
            out_shape=[
                shaped((ROWS, D), BF),
                shaped((OWN_KEYS, D), BF),
                shaped((OWN_KEYS, D), BF),
                shaped((ROWS, D), F32),
                shaped((OWN_KEYS, D), F32),
                shaped((HEADS, ROWS, OWN_KEYS), BF),
                shaped((ROWS, D), BF),
                shaped((ROWS, D), BF),
                shaped((peers, 2 * COARSE, D), BF),
                shaped((COARSE, D), F32),
            ],
            scratch_shapes=[
                pltpu.VMEM((ALL_KEYS, D), BF),
                pltpu.VMEM((QUERIES, ALL_KEYS), F32),
                pltpu.VMEM((QUERIES, D), F32),
            ],
            compiler_params=params(32),
            cost_estimate=cost(4_500_000_000, 20_000_000, 1_600_000),
            name="fine_forward",
        )(anchor, t5, t4, t3, t2, t1, tokens, cotangent, weights, fine_out)
    )
    gathered = exchanged(message, GROUP)
    group_rows = peers * COARSE
    coarse_send, coarse_factor = pl.pallas_call(
        coarse_project_kernel,
        out_shape=[
            shaped((groups, group_rows, 2 * PAIR), BF),
            shaped((group_rows, 2 * PAIR), F32),
        ],
        compiler_params=params(16),
        cost_estimate=cost(140_000_000, 3_000_000),
        name="coarse_project",
    )(gathered, coarse_in, coarse_back)
    everyone = exchanged(coarse_send, FAR).reshape(groups * group_rows, 2 * PAIR)
    own_start = (lax.axis_index(FAR) * group_rows).astype(jnp.int32).reshape(1)
    vmem = pl.BlockSpec(memory_space=pltpu.VMEM)
    partial = pl.pallas_call(
        coarse_attention_kernel,
        in_specs=[scalar] + [vmem] * 4,
        out_shape=shaped((peers, 2 * COARSE, D), BF),
        scratch_shapes=[
            pltpu.VMEM((group_rows, PAIR), F32),
            pltpu.VMEM((groups * group_rows, PAIR), BF),
            pltpu.VMEM((groups * group_rows, PAIR), BF),
        ],
        compiler_params=params(32),
        cost_estimate=cost(1_500_000_000, 3_000_000, 3_000_000),
        name="coarse_attention",
    )(own_start, everyone, coarse_factor, coarse_in, coarse_back)
    returned = exchanged(partial, GROUP)
    spread, state = pl.pallas_call(
        coarse_finish_kernel,
        out_shape=[shaped((COARSE, D), F32), shaped((COARSE, D), F32)],
        compiler_params=params(16),
        cost_estimate=cost(1_000_000, 1_000_000),
        name="coarse_finish",
    )(returned, message[0], coarse_grad)
    after = shifted_by(spread[0:1], -1)
    state = state.astype(BF)
    output = (
        hidden.astype(F32) + jnp.repeat(state, POOL, axis=0).astype(F32)
    ).astype(BF)
    h4, h3, h2, h1, own, hidden_grad = pl.pallas_call(
        fine_backward_kernel,
        grid=(PAIRS,),
        in_specs=[
            whole((ROWS, D)),
            whole((COARSE, D)),
            whole((1, D)),
            out_block,
            weight_block,
            pair_columns(ROWS),
            pair_columns(OWN_KEYS),
            pair_columns(OWN_KEYS),
            pair_columns(ROWS),
            pair_columns(OWN_KEYS),
            pl.BlockSpec((2, ROWS, OWN_KEYS), lambda p: (p, 0, 0)),
            pair_columns(ROWS),
        ],
        out_specs=[whole((ROWS, D))] * 6,
        out_shape=[shaped((ROWS, D), BF)] * 4 + [shaped((ROWS, D), F32)] * 2,
        scratch_shapes=[pltpu.VMEM((ROWS, D), BF), pltpu.VMEM((OWN_KEYS, D), F32)],
        compiler_params=params(32),
        cost_estimate=cost(5_000_000_000, 20_000_000),
        name="fine_backward",
    )(
        cotangent, spread, after, fine_out, weights, query, key, value, q_factor, k_factor, probs,
        attended,
    )
    a1, a2, a3, a4 = (
        shifted_by(rows, -steps) for rows, steps in ((h1, 1), (h2, 2), (h3, 3), (h4, 4))
    )
    grad_tokens = pl.pallas_call(
        fine_finish_kernel,
        out_shape=shaped((ROWS, D), BF),
        compiler_params=params(16),
        cost_estimate=cost(1_000_000, 3_000_000),
        name="fine_finish",
    )(own, a1, a2, a3, a4, hidden_grad, tokens)
    return (output, grad_tokens)


def solution(mesh):
    sizes = (4, 4, 2, 2, 4)
    fine_mesh = Mesh(mesh.devices.reshape(sizes), LINE)
    placed = (
        P(LINE, None),
        P(LINE, None),
        P(),
        P(),
        P(None, None, ("z_lo", "x")),
        P(("z_lo", "x"), None),
    )
    return jax.shard_map(
        per_device,
        mesh=fine_mesh,
        in_specs=placed,
        out_specs=(P(LINE, None), P(LINE, None)),
        check_vma=False,
    )
```

time: 342 us -> 211 us (0.62)
  the two profiles are of different devices: /device:TPU:4 before, /device:TPU:64 now
where the time goes in v1:
time: 211 us; the launch traced here: 208 us
  waiting for transfers between devices  73.6 us (35%)
  Pallas kernels  52.6 us (25%)
  starting transfers between devices  52.1 us (25%)
  local copies, waits for them, and re-layouts  26.3 us (12%)
  other arithmetic  2.77 us (1%)
    all_to_all x3, waiting for transfers between devices, exchanged(): return lax.all_to_all(pieces, axes, 0, 0, tiled=True)  46.4 us
    ppermute x10, starting transfers between devices, shifted_by(): lax.ppermute(value, LINE, [(source, source + steps) for source in range(f...  33.4 us
    ppermute x10, waiting for transfers between devices, shifted_by(): lax.ppermute(value, LINE, [(source, source + steps) for source in range(f...  27.2 us
    unnamed x42, local copies, waits for them, and re-layouts  24.6 us
    pallas_call x1, Pallas kernels, per_device(): pl.pallas_call(fine_forward_kernel, grid=(PAIRS,), in_specs=[scalar, whol...  19.9 us
    all_to_all x3, starting transfers between devices, exchanged(): return lax.all_to_all(pieces, axes, 0, 0, tiled=True)  18.7 us
    pallas_call x1, Pallas kernels, per_device(): pl.pallas_call(fine_backward_kernel, grid=(PAIRS,), in_specs=[whole((ROWS...  15.9 us
    pallas_call x1, Pallas kernels, per_device(): pl.pallas_call(coarse_attention_kernel, in_specs=[scalar] + [vmem] * 4, o...  13.9 us
  transfers between devices with their start and end apart: 13, of which 8 were waited for; matrix products, arithmetic and copies ran while one was open for 2% of the time, Pallas kernels for 0%

profile of v1, /device:TPU:64, one launch (start us, length us, event | category | flops | bytes accessed | tf_op | source)
XLA Modules:
  0.0 208.2 jit_solution(1182605990715034205)
XLA Ops:
  0.6 3.4 %collective-permute-start.4 = (bf16[128,1024]{1,0:T(8,128)(2,1)}, bf16[128,1024]{1,0:T(8,128)(2,1)S(1)}, u32[]{:S(2)}, u32[]{:S(2)}) collective-permute-start(bf16[128,1024]{1,0:T(8,128)(2,1)} %tokens_ref.1), channel_id=1, source_target_pairs={{0,1},{1,2},{2,3},{3,4},{4,5},{5,6},{6,7},{7,8},{8,9},{9,10},{10,1... | collective-permute-start | bytes 786440 | tf_op jit(solution)/shard_map/ppermute | solution.py:41
  4.0 4.6 %collective-permute-start.3 = (bf16[128,1024]{1,0:T(8,128)(2,1)}, bf16[128,1024]{1,0:T(8,128)(2,1)S(1)}, u32[]{:S(2)}, u32[]{:S(2)}) collective-permute-start(bf16[128,1024]{1,0:T(8,128)(2,1)} %tokens_ref.1), channel_id=1, source_target_pairs={{0,2},{1,3},{2,4},{3,5},{4,6},{5,7},{6,8},{7,9},{8,10},{9,11},{10,... | collective-permute-start | bytes 786440 | tf_op jit(solution)/shard_map/ppermute | solution.py:41
  8.7 4.7 %collective-permute-start.2 = (bf16[128,1024]{1,0:T(8,128)(2,1)}, bf16[128,1024]{1,0:T(8,128)(2,1)S(1)}, u32[]{:S(2)}, u32[]{:S(2)}) collective-permute-start(bf16[128,1024]{1,0:T(8,128)(2,1)} %tokens_ref.1), channel_id=1, source_target_pairs={{0,3},{1,4},{2,5},{3,6},{4,7},{5,8},{6,9},{7,10},{8,11},{9,12},{10... | collective-permute-start | bytes 786440 | tf_op jit(solution)/shard_map/ppermute | solution.py:41
  13.4 1.9 collective-permute-start.1
  16.1 2.5 %collective-permute-start = (bf16[16,1024]{1,0:T(8,128)(2,1)S(1)}, bf16[16,1024]{1,0:T(8,128)(2,1)S(1)}, u32[]{:S(2)}, u32[]{:S(2)}) collective-permute-start(bf16[16,1024]{1,0:T(8,128)(2,1)S(1)} %slice.30), channel_id=1, source_target_pairs={{0,5},{1,6},{2,7},{3,8},{4,9},{5,10},{6,11},{7,12},{8,13},{9,14},{... | collective-permute-start | bytes 98312 | tf_op jit(solution)/shard_map/ppermute | solution.py:41
  18.7 10.7 %collective-permute-done.t5 = bf16[16,1024]{1,0:T(8,128)(2,1)S(1)} collective-permute-done((bf16[16,1024]{1,0:T(8,128)(2,1)S(1)}, bf16[16,1024]{1,0:T(8,128)(2,1)S(1)}, u32[]{:S(2)}, u32[]{:S(2)}) %collective-permute-start) | collective-permute-done | bytes 32800 | tf_op jit(solution)/shard_map/ppermute | solution.py:41
  30.4 2.8 %copy-done.2 = bf16[1024,3,1024]{2,0,1:T(8,128)(2,1)S(1)} copy-done((bf16[1024,3,1024]{2,0,1:T(8,128)(2,1)S(1)}, bf16[1024,3,1024]{2,0,1:T(8,128)(2,1)}, u32[]{:S(2)}) %copy-start.2) | copy-done | bytes 6291480
  33.2 1.6 copy-done.4
  35.7 19.9 %fine_forward.1 = (bf16[128,1024]{1,0:T(8,128)(2,1)S(1)}, bf16[640,1024]{1,0:T(8,128)(2,1)S(1)}, bf16[640,1024]{1,0:T(8,128)(2,1)S(1)}, f32[128,1024]{1,0:T(8,12...) custom-call(s32[1]{0:T(128)} %bitcast.anchor_ref, ...), custom_call_target="tpu_custom_call" | custom-call | flops 4499999744 | bytes 20000000 | tf_op jit(solution)/shard_map/fine_forward/pallas_call | solution.py:367
  57.1 1.5 copy-done.10
  61.5 5.2 %all-to-all-start = ((bf16[16,16,1024]{2,1,0:T(8,128)(2,1)}), bf16[16,16,1024]{2,1,0:T(8,128)(2,1)S(1)}, u32[]{:S(2)}, u32[]{:S(2)}) async-start(bf16[16,16,1024]{2,1,0:T(8,128)(2,1)} %get-tuple-element.23), calls=%async_computation | async-start | bytes 1048576 | tf_op jit(solution)/shard_map/all_to_all | solution.py:45
  66.9 1.8 slice_select_fusion
  69.0 8.4 %all-to-all-done.got_ref = bf16[16,16,1024]{2,1,0:T(8,128)(2,1)S(1)} async-done(((bf16[16,16,1024]{2,1,0:T(8,128)(2,1)}), bf16[16,16,1024]{2,1,0:T(8,128)(2,1)S(1)}, u32[]{:S(2)}, u32[]{:S(2)}) %all-to-all-start) | async-done | bytes 524320 | tf_op jit(solution)/shard_map/all_to_all | solution.py:45
  77.4 1.6 coarse_project.1
  79.1 9.9 %all-to-all-start.1 = ((bf16[16,128,256]{2,1,0:T(8,128)(2,1)}), bf16[16,128,256]{2,1,0:T(8,128)(2,1)S(1)}, u32[]{:S(2)}, u32[]{:S(2)}) async-start(bf16[16,128,256]{2,1,0:T(8,128)(2,1)} %get-tuple-element.24), calls=%async_computation.1 | async-start | bytes 2097152 | tf_op jit(solution)/shard_map/all_to_all | solution.py:45
  88.9 28.1 %all-to-all-done.1 = bf16[16,128,256]{2,1,0:T(8,128)(2,1)S(1)} async-done(((bf16[16,128,256]{2,1,0:T(8,128)(2,1)}), bf16[16,128,256]{2,1,0:T(8,128)(2,1)S(1)}, u32[]{:S(2)}, u32[]{:S(2)}) %all-to-all-start.1) | async-done | bytes 1048608 | tf_op jit(solution)/shard_map/all_to_all | solution.py:45
  117.0 13.9 %coarse_attention.1 = bf16[16,16,1024]{2,1,0:T(8,128)(2,1)} custom-call(s32[1]{0:T(128)} %bitcast.2.start_ref, bf16[2048,256]{1,0:T(8,128)(2,1)S(1)} %bitcast.17, f32[128,256]{1,0:T(8,128)S(1)} %get-tuple-element.25.factor_ref, bf16[1024,256]{1,0:T(8,128)(2,1)S(1)} %pad_maximum_fusion.in_w_ref, bf16[256,1024]{1,0:T(8,128)(2,1)S(1)} %pad.4.out_w_ref), custom_call_target="tpu_custom_call" | custom-call | flops 1500000000 | bytes 3000000 | tf_op jit(solution)/shard_map/coarse_attention/pallas_call | solution.py:422
  130.9 3.6 %all-to-all-start.2 = ((bf16[16,16,1024]{2,1,0:T(8,128)(2,1)}), bf16[16,16,1024]{2,1,0:T(8,128)(2,1)S(1)}, u32[]{:S(2)}, u32[]{:S(2)}) async-start(bf16[16,16,1024]{2,1,0:T(8,128)(2,1)} %coarse_attention.1), calls=%async_computation.2 | async-start | bytes 1048576 | tf_op jit(solution)/shard_map/all_to_all | solution.py:45
  135.2 9.9 %all-to-all-done.2.got_ref = bf16[16,16,1024]{2,1,0:T(8,128)(2,1)S(1)} async-done(((bf16[16,16,1024]{2,1,0:T(8,128)(2,1)}), bf16[16,16,1024]{2,1,0:T(8,128)(2,1)S(1)}, u32[]{:S(2)}, u32[]{:S(2)}) %all-to-all-start.2) | async-done | bytes 524320 | tf_op jit(solution)/shard_map/all_to_all | solution.py:45
  145.3 3.1 %collective-permute-start.5 = (f32[1,1024]{1,0:T(1,128)S(1)}, f32[1,1024]{1,0:T(1,128)S(1)}, u32[]{:S(2)}, u32[]{:S(2)}) collective-permute-start(f32[1,1024]{1,0:T(1,128)S(1)} %slice.39), channel_id=1, source_target_pairs={{1,0},{2,1},{3,2},{4,3},{5,4},{6,5},{7,6},{8,7},{9,8},{10,9},{11,1... | collective-permute-start | bytes 12296 | tf_op jit(solution)/shard_map/ppermute | solution.py:41
  148.5 2.3 %collective-permute-done.5.next_ref = f32[1,1024]{1,0:T(1,128)S(1)} collective-permute-done((f32[1,1024]{1,0:T(1,128)S(1)}, f32[1,1024]{1,0:T(1,128)S(1)}, u32[]{:S(2)}, u32[]{:S(2)}) %collective-permute-start.5) | collective-permute-done | bytes 4128 | tf_op jit(solution)/shard_map/ppermute | solution.py:41
  150.8 2.8 %copy-done.3 = bf16[1024,3,1024]{2,0,1:T(8,128)(2,1)S(1)} copy-done((bf16[1024,3,1024]{2,0,1:T(8,128)(2,1)S(1)}, bf16[1024,3,1024]{2,0,1:T(8,128)(2,1)}, u32[]{:S(2)}) %copy-start.3) | copy-done | bytes 6291480
  153.6 1.6 copy-done.5
  155.2 1.7 copy-done.9
  156.9 1.7 copy-done.11
  163.2 15.9 %fine_backward.1 = (bf16[128,1024]{1,0:T(8,128)(2,1)S(1)}, bf16[128,1024]{1,0:T(8,128)(2,1)S(1)}, bf16[128,1024]{1,0:T(8,128)(2,1)S(1)}, bf16[128,1024]{1,0:T(8,...) custom-call(bf16[128,1024]{1,0:T(8,128)(2,1)S(1)} %copy-done.7, ...), custom_call_target="tpu_custom_call" | custom-call | flops 5000000000 | bytes 20000000 | tf_op jit(solution)/shard_map/fine_backward/pallas_call | solution.py:448
  179.1 4.7 %collective-permute-start.6 = (bf16[128,1024]{1,0:T(8,128)(2,1)S(1)}, bf16[128,1024]{1,0:T(8,128)(2,1)S(1)}, u32[]{:S(2)}, u32[]{:S(2)}) collective-permute-start(bf16[128,1024]{1,0:T(8,128)(2,1)S(1)} %get-tuple-element.37), channel_id=1, source_target_pairs={{1,0},{2,1},{3,2},{4,3},{5,4},{6,5},{7,6},{8,7},{9,8},{10,9},{11,1... | collective-permute-start | bytes 786440 | tf_op jit(solution)/shard_map/ppermute | solution.py:41
  183.8 1.9 collective-permute-start.7
  185.7 2.0 collective-permute-start.8
  187.7 4.5 %collective-permute-start.9 = (bf16[128,1024]{1,0:T(8,128)(2,1)S(1)}, bf16[128,1024]{1,0:T(8,128)(2,1)S(1)}, u32[]{:S(2)}, u32[]{:S(2)}) collective-permute-start(bf16[128,1024]{1,0:T(8,128)(2,1)S(1)} %get-tuple-element.40), channel_id=1, source_target_pairs={{4,0},{5,1},{6,2},{7,3},{8,4},{9,5},{10,6},{11,7},{12,8},{13,9},{1... | collective-permute-start | bytes 786440 | tf_op jit(solution)/shard_map/ppermute | solution.py:41
  193.0 8.7 %collective-permute-done.7.a2 = bf16[128,1024]{1,0:T(8,128)(2,1)S(1)} collective-permute-done((bf16[128,1024]{1,0:T(8,128)(2,1)S(1)}, bf16[128,1024]{1,0:T(8,128)(2,1)S(1)}, u32[]{:S(2)}, u32[]{:S(2)}) %collective-permute-start.7) | collective-permute-done | bytes 262176 | tf_op jit(solution)/shard_map/ppermute | solution.py:41
  202.3 4.8 %collective-permute-done.9.a4 = bf16[128,1024]{1,0:T(8,128)(2,1)S(1)} collective-permute-done((bf16[128,1024]{1,0:T(8,128)(2,1)S(1)}, bf16[128,1024]{1,0:T(8,128)(2,1)S(1)}, u32[]{:S(2)}, u32[]{:S(2)}) %collective-permute-start.9) | collective-permute-done | bytes 262176 | tf_op jit(solution)/shard_map/ppermute | solution.py:41
  (54 shorter events, 15.5 us)
Async XLA Ops:
  0.6 28.8 %collective-permute-start.4 = (bf16[128,1024]{1,0:T(8,128)(2,1)}, bf16[128,1024]{1,0:T(8,128)(2,1)S(1)}, u32[]{:S(2)}, u32[]{:S(2)}) collective-permute-start(bf16[128,1024]{1,0:T(8,128)(2,1)} %tokens_ref.1), channel_id=1, source_target_pairs={{0,1},{1,2},{2,3},{3,4},{4,5},{5,6},{6,7},{7,8},{8,9},{9,10},{10,1... | collective-permute-start | bytes 786440 | tf_op jit(solution)/shard_map/ppermute | solution.py:41
  4.0 25.4 %collective-permute-start.3 = (bf16[128,1024]{1,0:T(8,128)(2,1)}, bf16[128,1024]{1,0:T(8,128)(2,1)S(1)}, u32[]{:S(2)}, u32[]{:S(2)}) collective-permute-start(bf16[128,1024]{1,0:T(8,128)(2,1)} %tokens_ref.1), channel_id=1, source_target_pairs={{0,2},{1,3},{2,4},{3,5},{4,6},{5,7},{6,8},{7,9},{8,10},{9,11},{10,... | collective-permute-start | bytes 786440 | tf_op jit(solution)/shard_map/ppermute | solution.py:41
  8.7 20.7 %collective-permute-start.2 = (bf16[128,1024]{1,0:T(8,128)(2,1)}, bf16[128,1024]{1,0:T(8,128)(2,1)S(1)}, u32[]{:S(2)}, u32[]{:S(2)}) collective-permute-start(bf16[128,1024]{1,0:T(8,128)(2,1)} %tokens_ref.1), channel_id=1, source_target_pairs={{0,3},{1,4},{2,5},{3,6},{4,7},{5,8},{6,9},{7,10},{8,11},{9,12},{10... | collective-permute-start | bytes 786440 | tf_op jit(solution)/shard_map/ppermute | solution.py:41
  13.4 16.0 %collective-permute-start.1 = (bf16[128,1024]{1,0:T(8,128)(2,1)}, bf16[128,1024]{1,0:T(8,128)(2,1)S(1)}, u32[]{:S(2)}, u32[]{:S(2)}) collective-permute-start(bf16[128,1024]{1,0:T(8,128)(2,1)} %tokens_ref.1), channel_id=1, source_target_pairs={{0,4},{1,5},{2,6},{3,7},{4,8},{5,9},{6,10},{7,11},{8,12},{9,13},{1... | collective-permute-start | bytes 786440 | tf_op jit(solution)/shard_map/ppermute | solution.py:41
  16.1 13.3 %collective-permute-start = (bf16[16,1024]{1,0:T(8,128)(2,1)S(1)}, bf16[16,1024]{1,0:T(8,128)(2,1)S(1)}, u32[]{:S(2)}, u32[]{:S(2)}) collective-permute-start(bf16[16,1024]{1,0:T(8,128)(2,1)S(1)} %slice.30), channel_id=1, source_target_pairs={{0,5},{1,6},{2,7},{3,8},{4,9},{5,10},{6,11},{7,12},{8,13},{9,14},{... | collective-permute-start | bytes 98312 | tf_op jit(solution)/shard_map/ppermute | solution.py:41
  29.4 1.0 copy-start
  30.4 2.8 %copy-start.2 = (bf16[1024,3,1024]{2,0,1:T(8,128)(2,1)S(1)}, bf16[1024,3,1024]{2,0,1:T(8,128)(2,1)}, u32[]{:S(2)}) copy-start(bf16[1024,3,1024]{2,0,1:T(8,128)(2,1)} %param.8) | copy-start | bytes 18874372
  33.2 1.6 copy-start.4
  34.8 0.9 copy-start.6
  35.7 31.1 %copy-start.20 = (bf16[128,1024]{1,0:T(8,128)(2,1)S(1)}, bf16[128,1024]{1,0:T(8,128)(2,1)}, u32[]{:S(2)}) copy-start(bf16[128,1024]{1,0:T(8,128)(2,1)} %param.11) | copy-start | bytes 786436
  55.6 1.5 copy-start.8
  57.1 1.5 copy-start.10
  58.6 1.1 copy-start.12
  59.7 1.1 copy-start.14
  61.5 7.3 %copy-start.18 = (bf16[128,1024]{1,0:T(8,128)(2,1)}, bf16[128,1024]{1,0:T(8,128)(2,1)S(1)}, u32[]{:S(2)}) copy-start(bf16[128,1024]{1,0:T(8,128)(2,1)S(1)} %get-tuple-element.35.att_ref) | copy-start | bytes 786436
  61.5 15.9 %all-to-all-start = ((bf16[16,16,1024]{2,1,0:T(8,128)(2,1)}), bf16[16,16,1024]{2,1,0:T(8,128)(2,1)S(1)}, u32[]{:S(2)}, u32[]{:S(2)}) async-start(bf16[16,16,1024]{2,1,0:T(8,128)(2,1)} %get-tuple-element.23), calls=%async_computation | async-start | bytes 1048576 | tf_op jit(solution)/shard_map/all_to_all | solution.py:45
  79.1 38.0 %all-to-all-start.1 = ((bf16[16,128,256]{2,1,0:T(8,128)(2,1)}), bf16[16,128,256]{2,1,0:T(8,128)(2,1)S(1)}, u32[]{:S(2)}, u32[]{:S(2)}) async-start(bf16[16,128,256]{2,1,0:T(8,128)(2,1)} %get-tuple-element.24), calls=%async_computation.1 | async-start | bytes 2097152 | tf_op jit(solution)/shard_map/all_to_all | solution.py:45
  117.0 33.8 %copy-start.7 = (bf16[128,1024]{1,0:T(8,128)(2,1)S(1)}, bf16[128,1024]{1,0:T(8,128)(2,1)}, u32[]{:S(2)}) copy-start(bf16[128,1024]{1,0:T(8,128)(2,1)} %cot_ref.3) | copy-start | bytes 786436
  130.9 14.2 %all-to-all-start.2 = ((bf16[16,16,1024]{2,1,0:T(8,128)(2,1)}), bf16[16,16,1024]{2,1,0:T(8,128)(2,1)S(1)}, u32[]{:S(2)}, u32[]{:S(2)}) async-start(bf16[16,16,1024]{2,1,0:T(8,128)(2,1)} %coarse_attention.1), calls=%async_computation.2 | async-start | bytes 1048576 | tf_op jit(solution)/shard_map/all_to_all | solution.py:45
  145.3 5.5 %collective-permute-start.5 = (f32[1,1024]{1,0:T(1,128)S(1)}, f32[1,1024]{1,0:T(1,128)S(1)}, u32[]{:S(2)}, u32[]{:S(2)}) collective-permute-start(f32[1,1024]{1,0:T(1,128)S(1)} %slice.39), channel_id=1, source_target_pairs={{1,0},{2,1},{3,2},{4,3},{5,4},{6,5},{7,6},{8,7},{9,8},{10,9},{11,1... | collective-permute-start | bytes 12296 | tf_op jit(solution)/shard_map/ppermute | solution.py:41
  150.8 2.8 %copy-start.3 = (bf16[1024,3,1024]{2,0,1:T(8,128)(2,1)S(1)}, bf16[1024,3,1024]{2,0,1:T(8,128)(2,1)}, u32[]{:S(2)}) copy-start(bf16[1024,3,1024]{2,0,1:T(8,128)(2,1)} %param.8) | copy-start | bytes 18874372
  153.6 1.6 copy-start.5
  155.2 1.7 copy-start.9
  156.9 1.7 copy-start.11
  158.7 1.3 copy-start.13
  160.0 1.3 copy-start.15
  161.3 0.9 copy-start.17
  163.2 43.9 %copy-start.1 = (bf16[128,1024]{1,0:T(8,128)(2,1)S(1)}, bf16[128,1024]{1,0:T(8,128)(2,1)}, u32[]{:S(2)}) copy-start(bf16[128,1024]{1,0:T(8,128)(2,1)} %tokens_ref.1) | copy-start | bytes 786436
  179.1 13.8 %collective-permute-start.6 = (bf16[128,1024]{1,0:T(8,128)(2,1)S(1)}, bf16[128,1024]{1,0:T(8,128)(2,1)S(1)}, u32[]{:S(2)}, u32[]{:S(2)}) collective-permute-start(bf16[128,1024]{1,0:T(8,128)(2,1)S(1)} %get-tuple-element.37), channel_id=1, source_target_pairs={{1,0},{2,1},{3,2},{4,3},{5,4},{6,5},{7,6},{8,7},{9,8},{10,9},{11,1... | collective-permute-start | bytes 786440 | tf_op jit(solution)/shard_map/ppermute | solution.py:41
  183.8 17.8 %collective-permute-start.7 = (bf16[128,1024]{1,0:T(8,128)(2,1)S(1)}, bf16[128,1024]{1,0:T(8,128)(2,1)S(1)}, u32[]{:S(2)}, u32[]{:S(2)}) collective-permute-start(bf16[128,1024]{1,0:T(8,128)(2,1)S(1)} %get-tuple-element.38), channel_id=1, source_target_pairs={{2,0},{3,1},{4,2},{5,3},{6,4},{7,5},{8,6},{9,7},{10,8},{11,9},{12,... | collective-permute-start | bytes 786440 | tf_op jit(solution)/shard_map/ppermute | solution.py:41
  185.7 16.6 %collective-permute-start.8 = (bf16[128,1024]{1,0:T(8,128)(2,1)S(1)}, bf16[128,1024]{1,0:T(8,128)(2,1)S(1)}, u32[]{:S(2)}, u32[]{:S(2)}) collective-permute-start(bf16[128,1024]{1,0:T(8,128)(2,1)S(1)} %get-tuple-element.39), channel_id=1, source_target_pairs={{3,0},{4,1},{5,2},{6,3},{7,4},{8,5},{9,6},{10,7},{11,8},{12,9},{13... | collective-permute-start | bytes 786440 | tf_op jit(solution)/shard_map/ppermute | solution.py:41
  187.7 19.4 %collective-permute-start.9 = (bf16[128,1024]{1,0:T(8,128)(2,1)S(1)}, bf16[128,1024]{1,0:T(8,128)(2,1)S(1)}, u32[]{:S(2)}, u32[]{:S(2)}) collective-permute-start(bf16[128,1024]{1,0:T(8,128)(2,1)S(1)} %get-tuple-element.40), channel_id=1, source_target_pairs={{4,0},{5,1},{6,2},{7,3},{8,4},{9,5},{10,6},{11,7},{12,8},{13,9},{1... | collective-permute-start | bytes 786440 | tf_op jit(solution)/shard_map/ppermute | solution.py:41
  (2 other events, 1.7 us)

commit v2 on v1

v2 whole, which is shorter than its diff:
```python
import jax
import jax.numpy as jnp
from jax import lax
from jax.experimental import pallas as pl
from jax.experimental.pallas import tpu as pltpu
from jax.sharding import Mesh
from jax.sharding import PartitionSpec as P

D = 1024
HEADS = 16
HEAD_DIM = 64
WINDOW = 512
POOL = 16
EPS = 1e-06

LINE = ("y", "z_hi", "core", "z_lo", "x")
GROUP = ("core", "z_lo", "x")
FAR = ("y", "z_hi")

ROWS = 128
HALO = WINDOW
OWN_KEYS = HALO + ROWS
EXTRA = 16
ALL_KEYS = OWN_KEYS + EXTRA
QUERIES = EXTRA + ROWS
PAIR = 2 * HEAD_DIM
COARSE = ROWS // POOL
SCALE = HEAD_DIM ** (-0.5)
NEG = -1e30
VMEM_MIB = 32

BF = jnp.bfloat16
F32 = jnp.float32


def shifted_by(value, steps):
    count = 1
    for name in LINE:
        count *= lax.axis_size(name)
    first, last = (max(0, -steps), min(count, count - steps))
    return lax.ppermute(value, LINE, [(source, source + steps) for source in range(first, last)])


def exchanged(pieces, axes):
    return lax.all_to_all(pieces, axes, 0, 0, tiled=True)


def last_last(left, right):
    return lax.dot_general(left, right, (((1,), (1,)), ((), ())), preferred_element_type=F32)


def first_first(left, right):
    return lax.dot_general(left, right, (((0,), (0,)), ((), ())), preferred_element_type=F32)


def plain(left, right):
    return jnp.dot(left, right, preferred_element_type=F32)


def low_lanes():
    return lax.broadcasted_iota(jnp.int32, (1, PAIR), 1) < HEAD_DIM


def pair_sums(values, low):
    low_sum = jnp.sum(jnp.where(low, values, 0.0), axis=-1, keepdims=True)
    high_sum = jnp.sum(jnp.where(low, 0.0, values), axis=-1, keepdims=True)
    return jnp.where(low, low_sum, high_sum)


def pair_norm(values, low):
    factor = lax.rsqrt(pair_sums(values * values, low) * (1.0 / HEAD_DIM) + EPS)
    return values * factor, factor


def pair_norm_back(grad, unit, factor, low):
    return factor * (grad - unit * (pair_sums(unit * grad, low) * (1.0 / HEAD_DIM)))


def row_norm(rows):
    factor = lax.rsqrt(jnp.mean(rows * rows, axis=-1, keepdims=True) + EPS)
    return rows * factor, factor


def row_norm_back(grad, normed, factor):
    return factor * (grad - normed * jnp.mean(normed * grad, axis=-1, keepdims=True))


def fine_forward_kernel(
    anchor_ref, t5, t4, t3, t2, t1, t0, cot_ref, w_ref, out_w_ref,
    q_ref, k_ref, v_ref, qf_ref, kf_ref, p_ref, att_ref, hid_ref, send_ref, cg_ref,
    normed, bias, acc,
):
    step = pl.program_id(0)
    anchor = anchor_ref[0]
    low = low_lanes()

    @pl.when(step == 0)
    def _():
        at = 0
        for ref in (t4, t3, t2, t1, t0, t5):
            rows = ref.shape[0]
            normed[at : at + rows, :] = row_norm(ref[...].astype(F32))[0].astype(BF)
            at += rows
        row = lax.broadcasted_iota(jnp.int32, (2 * QUERIES, ALL_KEYS), 0)
        query_pos = jnp.where(row < QUERIES, row, row - QUERIES) - EXTRA
        column = lax.broadcasted_iota(jnp.int32, (2 * QUERIES, ALL_KEYS), 1)
        key_pos = jnp.where(column < OWN_KEYS, column - HALO, column - (OWN_KEYS + HALO + EXTRA))
        gap = query_pos - key_pos
        allowed = (gap >= 0) & (gap < WINDOW) & (anchor + key_pos >= 0)
        bias[...] = jnp.where(allowed, 0.0, NEG)
        acc[...] = jnp.zeros_like(acc)

    width = q_ref.shape[1]
    queries = plain(normed[HALO - EXTRA : OWN_KEYS, :], w_ref[0])
    both = plain(normed[...], jnp.concatenate([w_ref[1], w_ref[2]], axis=1))
    mixed = []
    for at in range(0, width, PAIR):
        here = slice(at, at + PAIR)
        query, q_factor = pair_norm(queries[:, here], low)
        key, k_factor = pair_norm(both[:, here], low)
        value = both[:, width + at : width + at + PAIR]
        key_b = key.astype(BF)
        q_ref[:, here] = query[EXTRA:].astype(BF)
        k_ref[:, here] = key_b[:OWN_KEYS]
        v_ref[:, here] = value[:OWN_KEYS].astype(BF)
        qf_ref[:, here] = q_factor[EXTRA:]
        kf_ref[:, here] = k_factor[:OWN_KEYS]
        scaled = query * SCALE
        stacked = jnp.concatenate([jnp.where(low, scaled, 0.0), jnp.where(low, 0.0, scaled)], axis=0)
        numer = jnp.exp(last_last(stacked.astype(BF), key_b) + bias[...])
        total = jnp.sum(numer, axis=-1, keepdims=True)
        prob = (numer * (1.0 / jnp.where(total > 0.0, total, 1.0))).astype(BF)
        p_ref[at // HEAD_DIM] = prob[EXTRA:QUERIES, :OWN_KEYS]
        p_ref[at // HEAD_DIM + 1] = prob[QUERIES + EXTRA :, :OWN_KEYS]
        twice = plain(prob, value.astype(BF))
        attended = jnp.where(low, twice[:QUERIES], twice[QUERIES:])
        attended = attended.astype(BF)
        att_ref[:, here] = attended[EXTRA:]
        mixed.append(attended)
    acc[...] += plain(jnp.concatenate(mixed, axis=1), out_w_ref[...])

    @pl.when(step == pl.num_programs(0) - 1)
    def _():
        before = t1[ROWS - EXTRA :, :].astype(F32) + acc[:EXTRA, :]
        before = jnp.where(anchor > 0, before, 0.0).astype(BF)
        own = (t0[...].astype(F32) + acc[EXTRA:, :]).astype(BF)
        hid_ref[...] = own
        chunk = lax.broadcasted_iota(jnp.int32, (COARSE, QUERIES), 0) * POOL
        row = lax.broadcasted_iota(jnp.int32, (COARSE, QUERIES), 1)
        member = jnp.where((row > chunk) & (row <= chunk + POOL), 1.0, 0.0).astype(BF)
        pooled = plain(member, jnp.concatenate([before, own], axis=0)) * (1.0 / POOL)
        chunk = lax.broadcasted_iota(jnp.int32, (COARSE, ROWS), 0) * POOL
        row = lax.broadcasted_iota(jnp.int32, (COARSE, ROWS), 1)
        member = jnp.where((row >= chunk) & (row < chunk + POOL), 1.0, 0.0).astype(BF)
        coarse_grad = plain(member, cot_ref[...])
        cg_ref[...] = coarse_grad
        message = jnp.concatenate([pooled, coarse_grad], axis=0).astype(BF)
        for peer in range(send_ref.shape[0]):
            send_ref[peer] = message


def coarse_project_kernel(got_ref, in_w_ref, out_w_ref, send_ref, factor_ref):
    low = low_lanes()
    rows = got_ref[...].astype(F32)
    count = rows.shape[0] * COARSE
    pooled = rows[:, :COARSE, :].reshape(count, D)
    coarse_grad = rows[:, COARSE:, :].reshape(count, D)
    normed = row_norm(pooled)[0].astype(BF)
    raw = plain(normed, in_w_ref[...]) + last_last(coarse_grad.astype(BF), out_w_ref[...])
    units, factors = [], []
    for tile in (raw[:, :PAIR], raw[:, PAIR:]):
        unit, factor = pair_norm(tile, low)
        units.append(jnp.where(low, unit, tile))
        factors.append(factor)
    message = jnp.concatenate(units, axis=1).astype(BF)
    factor_ref[...] = jnp.concatenate(factors, axis=1)
    for peer in range(send_ref.shape[0]):
        send_ref[peer] = message


def coarse_attention_kernel(start_ref, got_ref, factor_ref, in_w_ref, out_w_ref, send_ref, own_grad):
    low = low_lanes()
    own_start = pl.multiple_of(start_ref[0], ROWS)
    length = got_ref.shape[0]
    block = 512
    own_left = got_ref[pl.ds(own_start, ROWS), :PAIR]
    own_right = got_ref[pl.ds(own_start, ROWS), PAIR:]
    own_grad[...] = jnp.zeros_like(own_grad)

    def masked_halves(tile):
        wide = tile.astype(F32)
        return (
            jnp.where(low, wide * SCALE, 0.0).astype(BF),
            jnp.where(low, 0.0, wide).astype(BF),
        )

    def lane_partials(values):
        total = values[:, :PAIR]
        for at in range(PAIR, values.shape[1], PAIR):
            total = total + values[:, at : at + PAIR]
        return total

    def one_block(index, carry):
        first = pl.multiple_of(index * block, block)
        query, grad = masked_halves(got_ref[pl.ds(first, block), :PAIR])
        stacked = jnp.concatenate([query, grad], axis=0)

        def scored(keys):
            both = last_last(stacked, keys)
            return jnp.exp(both[:block]), both[block:]

        def one_chunk(at, sums):
            total, product = sums
            numer, prob_grad = scored(got_ref[pl.ds(pl.multiple_of(at * block, block), block), PAIR:])
            return total + lane_partials(numer), product + lane_partials(numer * prob_grad)

        nothing = jnp.zeros((block, PAIR), F32)
        total, product = lax.fori_loop(0, index, one_chunk, (nothing, nothing))
        numer, prob_grad = scored(got_ref[pl.ds(first, block), PAIR:])
        query_at = lax.broadcasted_iota(jnp.int32, (block, 1), 0)
        numer = jnp.where(lax.broadcasted_iota(jnp.int32, (1, block), 1) <= query_at, numer, 0.0)
        total = jnp.sum(total + lane_partials(numer), axis=-1, keepdims=True)
        product = jnp.sum(product + lane_partials(numer * prob_grad), axis=-1, keepdims=True)
        inverse = 1.0 / total
        delta = product * inverse
        own_pos = own_start + lax.broadcasted_iota(jnp.int32, (1, ROWS), 1)
        numer, prob_grad = scored(own_right)
        numer = jnp.where(own_pos <= query_at + first, numer, 0.0)
        prob = numer * inverse
        score_grad = (prob * (prob_grad - delta)).astype(BF)
        own_grad[...] += first_first(
            jnp.concatenate([score_grad, prob.astype(BF)], axis=0), stacked
        )
        return carry

    lax.fori_loop(own_start // block, length // block, one_block, 0)

    query, grad = masked_halves(own_left)
    query_pos = own_start + lax.broadcasted_iota(jnp.int32, (ROWS, 1), 0)
    key_pos = lax.broadcasted_iota(jnp.int32, (1, length), 1)
    keys = got_ref[:, PAIR:]
    key_scaled, value = masked_halves(keys)
    numer = jnp.where(key_pos <= query_pos, jnp.exp(last_last(query, keys)), 0.0)
    prob_grad = last_last(grad, keys)
    inverse = 1.0 / jnp.sum(numer, axis=-1, keepdims=True)
    delta = jnp.sum(numer * prob_grad, axis=-1, keepdims=True) * inverse
    prob = numer * inverse
    score_grad = (prob * (prob_grad - delta)).astype(BF)
    mine = plain(score_grad, key_scaled) + plain(prob.astype(BF), value)

    parts = []
    for tile, unit, factor in (
        (mine, own_left, factor_ref[:, :PAIR]),
        (own_grad[...], own_right, factor_ref[:, PAIR:]),
    ):
        back = pair_norm_back(tile, unit.astype(F32), factor, low)
        parts.append(jnp.where(low, back, tile))
    parts = jnp.concatenate(parts, axis=1).astype(BF)
    peers = send_ref.shape[0]
    normed_grad = last_last(parts, in_w_ref[...]).reshape(peers, COARSE, D)
    mixed = plain(parts, out_w_ref[...]).reshape(peers, COARSE, D)
    send_ref[...] = jnp.concatenate([normed_grad, mixed], axis=1).astype(BF)


def coarse_finish_kernel(got_ref, pooled_ref, cg_ref, spread_ref, state_ref):
    summed = jnp.sum(got_ref[...].astype(F32), axis=0)
    pooled = pooled_ref[...].astype(F32)[:COARSE]
    normed, factor = row_norm(pooled)
    pooled_grad = cg_ref[...] + row_norm_back(summed[:COARSE], normed, factor)
    spread_ref[...] = pooled_grad * (1.0 / POOL)
    state_ref[...] = pooled + summed[COARSE:]


def fine_backward_kernel(
    cot_ref, spread_ref, next_ref, out_w_ref, w_ref, q_ref, k_ref, v_ref, qf_ref, kf_ref, p_ref,
    att_ref,
    h4, h3, h2, h1, own_ref, hg_ref,
    hidden_grad, acc,
):
    step = pl.program_id(0)
    low = low_lanes()

    @pl.when(step == 0)
    def _():
        block = (lax.broadcasted_iota(jnp.int32, (ROWS, 1), 0) + (POOL - 1)) // POOL
        added = jnp.zeros((ROWS, D), F32)
        for at in range(COARSE):
            added = jnp.where(block == at, spread_ref[at : at + 1, :], added)
        added = jnp.where(block == COARSE, next_ref[0:1, :], added)
        total = cot_ref[...].astype(F32) + added
        hg_ref[...] = total
        hidden_grad[...] = total.astype(BF)
        acc[...] = jnp.zeros_like(acc)

    width = q_ref.shape[1]
    att_grads = last_last(hidden_grad[...], out_w_ref[...]).astype(BF).astype(F32)
    query_grads, key_grads, value_grads = [], [], []
    for at in range(0, width, PAIR):
        here = slice(at, at + PAIR)
        att_grad = att_grads[:, here]
        delta_all = att_grad * att_ref[:, here].astype(F32)
        value = v_ref[:, here]
        key_wide = k_ref[:, here].astype(F32)
        query_wide = q_ref[:, here].astype(F32)
        grad = jnp.concatenate(
            [jnp.where(low, att_grad, 0.0), jnp.where(low, 0.0, att_grad)], axis=0
        ).astype(BF)
        delta = jnp.sum(
            jnp.concatenate([jnp.where(low, delta_all, 0.0), jnp.where(low, 0.0, delta_all)], axis=0),
            axis=-1,
            keepdims=True,
        )
        scaled = query_wide * SCALE
        query = jnp.concatenate(
            [jnp.where(low, scaled, 0.0), jnp.where(low, 0.0, scaled)], axis=0
        ).astype(BF)
        first = at // HEAD_DIM
        prob = p_ref[first : first + 2].reshape(2 * ROWS, OWN_KEYS)
        score_grad = (prob.astype(F32) * (last_last(grad, value) - delta)).astype(BF)
        twice = plain(score_grad, (key_wide * SCALE).astype(BF))
        query_grad = jnp.where(low, twice[:ROWS], twice[ROWS:])
        key_grad = first_first(score_grad, query)
        value_grad = first_first(prob, grad)
        query_grads.append(pair_norm_back(query_grad, query_wide, qf_ref[:, here], low).astype(BF))
        key_grads.append(pair_norm_back(key_grad, key_wide, kf_ref[:, here], low).astype(BF))
        value_grads.append(value_grad.astype(BF))
    both = jnp.concatenate(key_grads + value_grads, axis=1)
    acc[...] += last_last(both, jnp.concatenate([w_ref[1], w_ref[2]], axis=1))
    acc[HALO:, :] += last_last(jnp.concatenate(query_grads, axis=1), w_ref[0])

    @pl.when(step == pl.num_programs(0) - 1)
    def _():
        for at, ref in enumerate((h4, h3, h2, h1)):
            ref[...] = acc[at * ROWS : (at + 1) * ROWS, :].astype(BF)
        own_ref[...] = acc[HALO:, :]


def fine_finish_kernel(own_ref, a1, a2, a3, a4, hg_ref, tokens_ref, out_ref):
    total = own_ref[...]
    for ref in (a1, a2, a3, a4):
        total = total + ref[...].astype(F32)
    normed, factor = row_norm(tokens_ref[...].astype(F32))
    out_ref[...] = (hg_ref[...] + row_norm_back(total, normed, factor)).astype(BF)


def whole(shape):
    return pl.BlockSpec(shape, lambda *_: (0,) * len(shape))


def columns(rows, width):
    return pl.BlockSpec((rows, width), lambda p: (0, p))


def shaped(shape, kind):
    return jax.ShapeDtypeStruct(shape, kind)


def params(mib):
    return pltpu.CompilerParams(vmem_limit_bytes=mib << 20)


def cost(flops, moved, exps=0):
    return pl.CostEstimate(flops=flops, bytes_accessed=moved, transcendentals=exps)


SCALAR = pl.BlockSpec(memory_space=pltpu.SMEM)
IN_VMEM = pl.BlockSpec(memory_space=pltpu.VMEM)
FORWARD_WIDTH = 2 * PAIR
BACKWARD_WIDTH = 2 * PAIR


def in_hbm(x):
    return pltpu.with_memory_space_constraint(x, pltpu.HBM)


def fine_forward(anchor, t5, t4, t3, t2, t1, tokens, cotangent, weights, fine_out, peers):
    width = FORWARD_WIDTH
    return pl.pallas_call(
        fine_forward_kernel,
        grid=(D // width,),
        in_specs=[SCALAR, whole((EXTRA, D))]
        + [whole((ROWS, D))] * 6
        + [
            pl.BlockSpec((3, D, width), lambda p: (0, 0, p)),
            pl.BlockSpec((width, D), lambda p: (p, 0)),
        ],
        out_specs=[
            columns(ROWS, width),
            columns(OWN_KEYS, width),
            columns(OWN_KEYS, width),
            columns(ROWS, width),
            columns(OWN_KEYS, width),
            pl.BlockSpec((width // HEAD_DIM, ROWS, OWN_KEYS), lambda p: (p, 0, 0)),
            columns(ROWS, width),
            whole((ROWS, D)),
            whole((peers, 2 * COARSE, D)),
            whole((COARSE, D)),
        ],
        out_shape=[
            pltpu.HBM((ROWS, D), BF),
            pltpu.HBM((OWN_KEYS, D), BF),
            pltpu.HBM((OWN_KEYS, D), BF),
            pltpu.HBM((ROWS, D), F32),
            pltpu.HBM((OWN_KEYS, D), F32),
            pltpu.HBM((HEADS, ROWS, OWN_KEYS), BF),
            pltpu.HBM((ROWS, D), BF),
            pltpu.HBM((ROWS, D), BF),
            shaped((peers, 2 * COARSE, D), BF),
            shaped((COARSE, D), F32),
        ],
        scratch_shapes=[
            pltpu.VMEM((ALL_KEYS, D), BF),
            pltpu.VMEM((2 * QUERIES, ALL_KEYS), F32),
            pltpu.VMEM((QUERIES, D), F32),
        ],
        compiler_params=params(VMEM_MIB),
        cost_estimate=cost(4_500_000_000, 20_000_000, 1_600_000),
        name="fine_forward",
    )(
        anchor, t5, t4, t3, t2, t1, in_hbm(tokens), in_hbm(cotangent), in_hbm(weights),
        in_hbm(fine_out),
    )


def coarse_project(gathered, coarse_in, coarse_back, groups):
    rows = gathered.shape[0] * COARSE
    return pl.pallas_call(
        coarse_project_kernel,
        out_shape=[shaped((groups, rows, 2 * PAIR), BF), shaped((rows, 2 * PAIR), F32)],
        compiler_params=params(VMEM_MIB),
        cost_estimate=cost(140_000_000, 3_000_000),
        name="coarse_project",
    )(gathered, coarse_in, coarse_back)


def coarse_attention(own_start, everyone, factor, coarse_in, coarse_back):
    rows = factor.shape[0]
    return pl.pallas_call(
        coarse_attention_kernel,
        in_specs=[SCALAR] + [IN_VMEM] * 4,
        out_shape=shaped((rows // COARSE, 2 * COARSE, D), BF),
        scratch_shapes=[pltpu.VMEM((rows, PAIR), F32)],
        compiler_params=params(VMEM_MIB),
        cost_estimate=cost(1_500_000_000, 3_000_000, 3_000_000),
        name="coarse_attention",
    )(own_start, everyone, factor, coarse_in, coarse_back)


def coarse_finish(returned, pooled, coarse_grad):
    return pl.pallas_call(
        coarse_finish_kernel,
        out_shape=[shaped((COARSE, D), F32), shaped((COARSE, D), F32)],
        compiler_params=params(VMEM_MIB),
        cost_estimate=cost(1_000_000, 1_000_000),
        name="coarse_finish",
    )(returned, pooled, coarse_grad)


def fine_backward(
    cotangent, spread, after, fine_out, weights, query, key, value, q_factor, k_factor, probs,
    attended,
):
    width = BACKWARD_WIDTH
    return pl.pallas_call(
        fine_backward_kernel,
        grid=(D // width,),
        in_specs=[
            whole((ROWS, D)),
            whole((COARSE, D)),
            whole((1, D)),
            pl.BlockSpec((width, D), lambda p: (p, 0)),
            pl.BlockSpec((3, D, width), lambda p: (0, 0, p)),
            columns(ROWS, width),
            columns(OWN_KEYS, width),
            columns(OWN_KEYS, width),
            columns(ROWS, width),
            columns(OWN_KEYS, width),
            pl.BlockSpec((width // HEAD_DIM, ROWS, OWN_KEYS), lambda p: (p, 0, 0)),
            columns(ROWS, width),
        ],
        out_specs=[whole((ROWS, D))] * 6,
        out_shape=[shaped((ROWS, D), BF)] * 4 + [shaped((ROWS, D), F32)] * 2,
        scratch_shapes=[pltpu.VMEM((ROWS, D), BF), pltpu.VMEM((OWN_KEYS, D), F32)],
        compiler_params=params(VMEM_MIB),
        cost_estimate=cost(5_000_000_000, 20_000_000),
        name="fine_backward",
    )(
        in_hbm(cotangent), spread, after,
        *(in_hbm(x) for x in (fine_out, weights, query, key, value, q_factor, k_factor, probs)),
        in_hbm(attended),
    )


def fine_finish(own, arrived, hidden_grad, tokens):
    return pl.pallas_call(
        fine_finish_kernel,
        out_shape=shaped((ROWS, D), BF),
        compiler_params=params(VMEM_MIB),
        cost_estimate=cost(1_000_000, 3_000_000),
        name="fine_finish",
    )(own, *arrived, hidden_grad, tokens)


def per_device(tokens, cotangent, fine_qkv, fine_out, coarse_qkv, coarse_out):
    peers = 1
    for name in GROUP:
        peers *= lax.axis_size(name)
    groups = 1
    for name in FAR:
        groups *= lax.axis_size(name)
    core = lax.axis_index("core")
    weights = jnp.transpose(fine_qkv, (1, 0, 2))
    coarse_all = jnp.transpose(coarse_qkv, (1, 0, 2))
    picked = jnp.where(core == 0, coarse_all[:, :, :HEAD_DIM], coarse_all[:, :, HEAD_DIM:])
    blank = jnp.zeros((D, HEAD_DIM), BF)
    coarse_in = jnp.concatenate([picked[0], blank, picked[1], picked[2]], axis=1)
    picked_out = jnp.where(core == 0, coarse_out[:HEAD_DIM], coarse_out[HEAD_DIM:])
    coarse_back = jnp.pad(picked_out, ((HEAD_DIM, PAIR), (0, 0)))

    t1, t2, t3, t4 = (shifted_by(tokens, steps) for steps in (1, 2, 3, 4))
    t5 = shifted_by(tokens[ROWS - EXTRA :], 5)
    anchor = (lax.axis_index(LINE) * ROWS).astype(jnp.int32).reshape(1)

    query, key, value, q_factor, k_factor, probs, attended, hidden, message, coarse_grad = (
        fine_forward(anchor, t5, t4, t3, t2, t1, tokens, cotangent, weights, fine_out, peers)
    )
    gathered = exchanged(message, GROUP)
    coarse_send, coarse_factor = coarse_project(gathered, coarse_in, coarse_back, groups)
    group_rows = coarse_factor.shape[0]
    everyone = exchanged(coarse_send, FAR).reshape(groups * group_rows, 2 * PAIR)
    own_start = (lax.axis_index(FAR) * group_rows).astype(jnp.int32).reshape(1)
    partial = coarse_attention(own_start, everyone, coarse_factor, coarse_in, coarse_back)
    returned = exchanged(partial, GROUP)
    spread, state = coarse_finish(returned, message[0], coarse_grad)
    after = shifted_by(spread[0:1], -1)
    output = (
        hidden.astype(F32) + jnp.repeat(state.astype(BF), POOL, axis=0).astype(F32)
    ).astype(BF)
    h4, h3, h2, h1, own, hidden_grad = fine_backward(
        cotangent, spread, after, fine_out, weights, query, key, value, q_factor, k_factor, probs,
        attended,
    )
    arrived = [shifted_by(rows, -steps) for rows, steps in ((h1, 1), (h2, 2), (h3, 3), (h4, 4))]
    return (output, fine_finish(own, arrived, hidden_grad, tokens))


def solution(mesh):
    sizes = (4, 4, 2, 2, 4)
    fine_mesh = Mesh(mesh.devices.reshape(sizes), LINE)
    placed = (
        P(LINE, None),
        P(LINE, None),
        P(),
        P(),
        P(None, None, ("z_lo", "x")),
        P(("z_lo", "x"), None),
    )
    return jax.shard_map(
        per_device,
        mesh=fine_mesh,
        in_specs=placed,
        out_specs=(P(LINE, None), P(LINE, None)),
        check_vma=False,
    )
```

time: 211 us -> 171 us (0.81)
  local copies, waits for them, and re-layouts: 26.3 us -> 1.74 us
  Pallas kernels: 52.6 us -> 37.6 us
    unnamed x42 -> x8, local copies, waits for them, and re-layouts: 24.6 us -> 0.02 us
    pallas_call x6, Pallas kernels: 52.6 us -> 37.6 us  [the longest x1 13 us: fine_forward(): pl.pallas_call(fine_forward_kernel, grid=(D // width,), in_specs=[SCALAR,...]
where the time goes in v2:
time: 171 us; the launch traced here: 169 us
  waiting for transfers between devices  75.1 us (44%)
  starting transfers between devices  52.2 us (31%)
  Pallas kernels  37.6 us (22%)
  local copies, waits for them, and re-layouts  1.74 us (1%)
    all_to_all x3, waiting for transfers between devices, exchanged(): return lax.all_to_all(pieces, axes, 0, 0, tiled=True)  47.9 us
    ppermute x10, starting transfers between devices, shifted_by(): lax.ppermute(value, LINE, [(source, source + steps) for source in range(f...  33.4 us
    ppermute x10, waiting for transfers between devices, shifted_by(): lax.ppermute(value, LINE, [(source, source + steps) for source in range(f...  27.2 us
    all_to_all x3, starting transfers between devices, exchanged(): return lax.all_to_all(pieces, axes, 0, 0, tiled=True)  18.8 us
    pallas_call x1, Pallas kernels, fine_forward(): pl.pallas_call(fine_forward_kernel, grid=(D // width,), in_specs=[SCALAR,...  13 us
    pallas_call x1, Pallas kernels, fine_backward(): pl.pallas_call(fine_backward_kernel, grid=(D // width,), in_specs=[whole(...  12.9 us
    pallas_call x1, Pallas kernels, coarse_attention(): pl.pallas_call(coarse_attention_kernel, in_specs=[SCALAR] + [IN_VMEM] * 4...  8.84 us
  transfers between devices with their start and end apart: 13, of which 8 were waited for; matrix products, arithmetic and copies ran while one was open for 2% of the time, Pallas kernels for 0%

profile of v2, /device:TPU:64, one launch (start us, length us, event | category | flops | bytes accessed | tf_op | source)
XLA Modules:
  0.0 168.8 jit_solution(3274683185460831343)
XLA Ops:
  0.6 3.4 %collective-permute-start.4 = (bf16[128,1024]{1,0:T(8,128)(2,1)}, bf16[128,1024]{1,0:T(8,128)(2,1)S(1)}, u32[]{:S(2)}, u32[]{:S(2)}) collective-permute-start(bf16[128,1024]{1,0:T(8,128)(2,1)} %tokens_ref.1), channel_id=1, source_target_pairs={{0,1},{1,2},{2,3},{3,4},{4,5},{5,6},{6,7},{7,8},{8,9},{9,10},{10,1... | collective-permute-start | bytes 786440 | tf_op jit(solution)/shard_map/ppermute | solution.py:41
  4.0 4.6 %collective-permute-start.3 = (bf16[128,1024]{1,0:T(8,128)(2,1)}, bf16[128,1024]{1,0:T(8,128)(2,1)S(1)}, u32[]{:S(2)}, u32[]{:S(2)}) collective-permute-start(bf16[128,1024]{1,0:T(8,128)(2,1)} %tokens_ref.1), channel_id=1, source_target_pairs={{0,2},{1,3},{2,4},{3,5},{4,6},{5,7},{6,8},{7,9},{8,10},{9,11},{10,... | collective-permute-start | bytes 786440 | tf_op jit(solution)/shard_map/ppermute | solution.py:41
  8.7 4.7 %collective-permute-start.2 = (bf16[128,1024]{1,0:T(8,128)(2,1)}, bf16[128,1024]{1,0:T(8,128)(2,1)S(1)}, u32[]{:S(2)}, u32[]{:S(2)}) collective-permute-start(bf16[128,1024]{1,0:T(8,128)(2,1)} %tokens_ref.1), channel_id=1, source_target_pairs={{0,3},{1,4},{2,5},{3,6},{4,7},{5,8},{6,9},{7,10},{8,11},{9,12},{10... | collective-permute-start | bytes 786440 | tf_op jit(solution)/shard_map/ppermute | solution.py:41
  13.4 1.9 %collective-permute-start.1 = (bf16[128,1024]{1,0:T(8,128)(2,1)}, bf16[128,1024]{1,0:T(8,128)(2,1)S(1)}, u32[]{:S(2)}, u32[]{:S(2)}) collective-permute-start(bf16[128,1024]{1,0:T(8,128)(2,1)} %tokens_ref.1), channel_id=1, source_target_pairs={{0,4},{1,5},{2,6},{3,7},{4,8},{5,9},{6,10},{7,11},{8,12},{9,13},{1... | collective-permute-start | bytes 786440 | tf_op jit(solution)/shard_map/ppermute | solution.py:41
  15.3 0.8 slice.30
  16.1 2.5 %collective-permute-start = (bf16[16,1024]{1,0:T(8,128)(2,1)S(1)}, bf16[16,1024]{1,0:T(8,128)(2,1)S(1)}, u32[]{:S(2)}, u32[]{:S(2)}) collective-permute-start(bf16[16,1024]{1,0:T(8,128)(2,1)S(1)} %slice.30), channel_id=1, source_target_pairs={{0,5},{1,6},{2,7},{3,8},{4,9},{5,10},{6,11},{7,12},{8,13},{9,14},{... | collective-permute-start | bytes 98312 | tf_op jit(solution)/shard_map/ppermute | solution.py:41
  18.7 10.7 %collective-permute-done.t5 = bf16[16,1024]{1,0:T(8,128)(2,1)S(1)} collective-permute-done((bf16[16,1024]{1,0:T(8,128)(2,1)S(1)}, bf16[16,1024]{1,0:T(8,128)(2,1)S(1)}, u32[]{:S(2)}, u32[]{:S(2)}) %collective-permute-start) | collective-permute-done | bytes 32800 | tf_op jit(solution)/shard_map/ppermute | solution.py:41
  29.4 13.0 %fine_forward.1 = (bf16[128,1024]{1,0:T(8,128)(2,1)}, bf16[640,1024]{1,0:T(8,128)(2,1)}, bf16[640,1024]{1,0:T(8,128)(2,1)}, f32[128,1024]{1,0:T(8,128)}, f32[640...) custom-call(s32[1]{0:T(128)} %bitcast.anchor_ref, ...), custom_call_target="tpu_custom_call" | custom-call | flops 4499999744 | bytes 20000000 | tf_op jit(solution)/shard_map/fine_forward/pallas_call | solution.py:378
  42.5 5.4 %all-to-all-start = ((bf16[16,16,1024]{2,1,0:T(8,128)(2,1)}), bf16[16,16,1024]{2,1,0:T(8,128)(2,1)S(1)}, u32[]{:S(2)}, u32[]{:S(2)}) async-start(bf16[16,16,1024]{2,1,0:T(8,128)(2,1)} %get-tuple-element.23), calls=%async_computation | async-start | bytes 1048576 | tf_op jit(solution)/shard_map/all_to_all | solution.py:45
  48.1 0.3 slice_select_fusion
  48.4 0.2 pad_maximum_fusion.in_w_ref
  48.6 9.9 %all-to-all-done.got_ref = bf16[16,16,1024]{2,1,0:T(8,128)(2,1)S(1)} async-done(((bf16[16,16,1024]{2,1,0:T(8,128)(2,1)}), bf16[16,16,1024]{2,1,0:T(8,128)(2,1)S(1)}, u32[]{:S(2)}, u32[]{:S(2)}) %all-to-all-start) | async-done | bytes 524320 | tf_op jit(solution)/shard_map/all_to_all | solution.py:45
  58.5 1.6 coarse_project.1
  60.2 9.9 %all-to-all-start.1 = ((bf16[16,128,256]{2,1,0:T(8,128)(2,1)}), bf16[16,128,256]{2,1,0:T(8,128)(2,1)S(1)}, u32[]{:S(2)}, u32[]{:S(2)}) async-start(bf16[16,128,256]{2,1,0:T(8,128)(2,1)} %get-tuple-element.24), calls=%async_computation.1 | async-start | bytes 2097152 | tf_op jit(solution)/shard_map/all_to_all | solution.py:45
  70.0 28.1 %all-to-all-done.1 = bf16[16,128,256]{2,1,0:T(8,128)(2,1)S(1)} async-done(((bf16[16,128,256]{2,1,0:T(8,128)(2,1)}), bf16[16,128,256]{2,1,0:T(8,128)(2,1)S(1)}, u32[]{:S(2)}, u32[]{:S(2)}) %all-to-all-start.1) | async-done | bytes 1048608 | tf_op jit(solution)/shard_map/all_to_all | solution.py:45
  98.1 8.8 %coarse_attention.1 = bf16[16,16,1024]{2,1,0:T(8,128)(2,1)} custom-call(s32[1]{0:T(128)} %bitcast.2.start_ref, bf16[2048,256]{1,0:T(8,128)(2,1)S(1)} %bitcast.17, f32[128,256]{1,0:T(8,128)S(1)} %get-tuple-element.25.factor_ref, bf16[1024,256]{1,0:T(8,128)(2,1)S(1)} %pad_maximum_fusion.in_w_ref, bf16[256,1024]{1,0:T(8,128)(2,1)S(1)} %pad.4.out_w_ref), custom_call_target="tpu_custom_call" | custom-call | flops 1500000000 | bytes 3000000 | tf_op jit(solution)/shard_map/coarse_attention/pallas_call | solution.py:438
  107.0 3.6 %all-to-all-start.2 = ((bf16[16,16,1024]{2,1,0:T(8,128)(2,1)}), bf16[16,16,1024]{2,1,0:T(8,128)(2,1)S(1)}, u32[]{:S(2)}, u32[]{:S(2)}) async-start(bf16[16,16,1024]{2,1,0:T(8,128)(2,1)} %coarse_attention.1), calls=%async_computation.2 | async-start | bytes 1048576 | tf_op jit(solution)/shard_map/all_to_all | solution.py:45
  110.6 0.8 slice_bitcast_fusion.3.pooled_ref
  111.3 9.9 %all-to-all-done.2.got_ref = bf16[16,16,1024]{2,1,0:T(8,128)(2,1)S(1)} async-done(((bf16[16,16,1024]{2,1,0:T(8,128)(2,1)}), bf16[16,16,1024]{2,1,0:T(8,128)(2,1)S(1)}, u32[]{:S(2)}, u32[]{:S(2)}) %all-to-all-start.2) | async-done | bytes 524320 | tf_op jit(solution)/shard_map/all_to_all | solution.py:45
  121.2 0.2 coarse_finish.1
  121.4 3.1 %collective-permute-start.5 = (f32[1,1024]{1,0:T(1,128)S(1)}, f32[1,1024]{1,0:T(1,128)S(1)}, u32[]{:S(2)}, u32[]{:S(2)}) collective-permute-start(f32[1,1024]{1,0:T(1,128)S(1)} %slice.39), channel_id=1, source_target_pairs={{1,0},{2,1},{3,2},{4,3},{5,4},{6,5},{7,6},{8,7},{9,8},{10,9},{11,1... | collective-permute-start | bytes 12296 | tf_op jit(solution)/shard_map/ppermute | solution.py:41
  124.5 2.3 %collective-permute-done.5.next_ref = f32[1,1024]{1,0:T(1,128)S(1)} collective-permute-done((f32[1,1024]{1,0:T(1,128)S(1)}, f32[1,1024]{1,0:T(1,128)S(1)}, u32[]{:S(2)}, u32[]{:S(2)}) %collective-permute-start.5) | collective-permute-done | bytes 4128 | tf_op jit(solution)/shard_map/ppermute | solution.py:41
  126.9 12.9 %fine_backward.1 = (bf16[128,1024]{1,0:T(8,128)(2,1)S(1)}, bf16[128,1024]{1,0:T(8,128)(2,1)S(1)}, bf16[128,1024]{1,0:T(8,128)(2,1)S(1)}, bf16[128,1024]{1,0:T(8,...) custom-call(bf16[128,1024]{1,0:T(8,128)(2,1)} %cot_ref.3, f32[8,1024]{1,0:T(8,128)S(1)} %get-tuple-element.28.spread_ref, ...), custom_call_target="tpu_custom_call" | custom-call | flops 5000000000 | bytes 20000000 | tf_op jit(solution)/shard_map/fine_backward/pallas_call | solution.py:464
  139.8 4.7 %collective-permute-start.6 = (bf16[128,1024]{1,0:T(8,128)(2,1)S(1)}, bf16[128,1024]{1,0:T(8,128)(2,1)S(1)}, u32[]{:S(2)}, u32[]{:S(2)}) collective-permute-start(bf16[128,1024]{1,0:T(8,128)(2,1)S(1)} %get-tuple-element.37), channel_id=1, source_target_pairs={{1,0},{2,1},{3,2},{4,3},{5,4},{6,5},{7,6},{8,7},{9,8},{10,9},{11,1... | collective-permute-start | bytes 786440 | tf_op jit(solution)/shard_map/ppermute | solution.py:41
  144.5 1.9 %collective-permute-start.7 = (bf16[128,1024]{1,0:T(8,128)(2,1)S(1)}, bf16[128,1024]{1,0:T(8,128)(2,1)S(1)}, u32[]{:S(2)}, u32[]{:S(2)}) collective-permute-start(bf16[128,1024]{1,0:T(8,128)(2,1)S(1)} %get-tuple-element.38), channel_id=1, source_target_pairs={{2,0},{3,1},{4,2},{5,3},{6,4},{7,5},{8,6},{9,7},{10,8},{11,9},{12,... | collective-permute-start | bytes 786440 | tf_op jit(solution)/shard_map/ppermute | solution.py:41
  146.4 1.9 %collective-permute-start.8 = (bf16[128,1024]{1,0:T(8,128)(2,1)S(1)}, bf16[128,1024]{1,0:T(8,128)(2,1)S(1)}, u32[]{:S(2)}, u32[]{:S(2)}) collective-permute-start(bf16[128,1024]{1,0:T(8,128)(2,1)S(1)} %get-tuple-element.39), channel_id=1, source_target_pairs={{3,0},{4,1},{5,2},{6,3},{7,4},{8,5},{9,6},{10,7},{11,8},{12,9},{13... | collective-permute-start | bytes 786440 | tf_op jit(solution)/shard_map/ppermute | solution.py:41
  148.4 4.5 %collective-permute-start.9 = (bf16[128,1024]{1,0:T(8,128)(2,1)S(1)}, bf16[128,1024]{1,0:T(8,128)(2,1)S(1)}, u32[]{:S(2)}, u32[]{:S(2)}) collective-permute-start(bf16[128,1024]{1,0:T(8,128)(2,1)S(1)} %get-tuple-element.40), channel_id=1, source_target_pairs={{4,0},{5,1},{6,2},{7,3},{8,4},{9,5},{10,6},{11,7},{12,8},{13,9},{1... | collective-permute-start | bytes 786440 | tf_op jit(solution)/shard_map/ppermute | solution.py:41
  152.9 0.8 fusion
  153.6 8.7 %collective-permute-done.7.a2 = bf16[128,1024]{1,0:T(8,128)(2,1)S(1)} collective-permute-done((bf16[128,1024]{1,0:T(8,128)(2,1)S(1)}, bf16[128,1024]{1,0:T(8,128)(2,1)S(1)}, u32[]{:S(2)}, u32[]{:S(2)}) %collective-permute-start.7) | collective-permute-done | bytes 262176 | tf_op jit(solution)/shard_map/ppermute | solution.py:41
  162.3 0.7 collective-permute-done.8.a3
  163.0 4.8 %collective-permute-done.9.a4 = bf16[128,1024]{1,0:T(8,128)(2,1)S(1)} collective-permute-done((bf16[128,1024]{1,0:T(8,128)(2,1)S(1)}, bf16[128,1024]{1,0:T(8,128)(2,1)S(1)}, u32[]{:S(2)}, u32[]{:S(2)}) %collective-permute-start.9) | collective-permute-done | bytes 262176 | tf_op jit(solution)/shard_map/ppermute | solution.py:41
  167.8 1.0 fine_finish.1
  (20 shorter events, 0.2 us)
Async XLA Ops:
  0.6 28.8 %collective-permute-start.4 = (bf16[128,1024]{1,0:T(8,128)(2,1)}, bf16[128,1024]{1,0:T(8,128)(2,1)S(1)}, u32[]{:S(2)}, u32[]{:S(2)}) collective-permute-start(bf16[128,1024]{1,0:T(8,128)(2,1)} %tokens_ref.1), channel_id=1, source_target_pairs={{0,1},{1,2},{2,3},{3,4},{4,5},{5,6},{6,7},{7,8},{8,9},{9,10},{10,1... | collective-permute-start | bytes 786440 | tf_op jit(solution)/shard_map/ppermute | solution.py:41
  4.0 25.4 %collective-permute-start.3 = (bf16[128,1024]{1,0:T(8,128)(2,1)}, bf16[128,1024]{1,0:T(8,128)(2,1)S(1)}, u32[]{:S(2)}, u32[]{:S(2)}) collective-permute-start(bf16[128,1024]{1,0:T(8,128)(2,1)} %tokens_ref.1), channel_id=1, source_target_pairs={{0,2},{1,3},{2,4},{3,5},{4,6},{5,7},{6,8},{7,9},{8,10},{9,11},{10,... | collective-permute-start | bytes 786440 | tf_op jit(solution)/shard_map/ppermute | solution.py:41
  8.7 20.7 %collective-permute-start.2 = (bf16[128,1024]{1,0:T(8,128)(2,1)}, bf16[128,1024]{1,0:T(8,128)(2,1)S(1)}, u32[]{:S(2)}, u32[]{:S(2)}) collective-permute-start(bf16[128,1024]{1,0:T(8,128)(2,1)} %tokens_ref.1), channel_id=1, source_target_pairs={{0,3},{1,4},{2,5},{3,6},{4,7},{5,8},{6,9},{7,10},{8,11},{9,12},{10... | collective-permute-start | bytes 786440 | tf_op jit(solution)/shard_map/ppermute | solution.py:41
  13.4 16.0 %collective-permute-start.1 = (bf16[128,1024]{1,0:T(8,128)(2,1)}, bf16[128,1024]{1,0:T(8,128)(2,1)S(1)}, u32[]{:S(2)}, u32[]{:S(2)}) collective-permute-start(bf16[128,1024]{1,0:T(8,128)(2,1)} %tokens_ref.1), channel_id=1, source_target_pairs={{0,4},{1,5},{2,6},{3,7},{4,8},{5,9},{6,10},{7,11},{8,12},{9,13},{1... | collective-permute-start | bytes 786440 | tf_op jit(solution)/shard_map/ppermute | solution.py:41
  16.1 13.3 %collective-permute-start = (bf16[16,1024]{1,0:T(8,128)(2,1)S(1)}, bf16[16,1024]{1,0:T(8,128)(2,1)S(1)}, u32[]{:S(2)}, u32[]{:S(2)}) collective-permute-start(bf16[16,1024]{1,0:T(8,128)(2,1)S(1)} %slice.30), channel_id=1, source_target_pairs={{0,5},{1,6},{2,7},{3,8},{4,9},{5,10},{6,11},{7,12},{8,13},{9,14},{... | collective-permute-start | bytes 98312 | tf_op jit(solution)/shard_map/ppermute | solution.py:41
  29.4 18.5 %copy-start.2 = (bf16[128,1024]{1,0:T(8,128)(2,1)S(1)}, bf16[128,1024]{1,0:T(8,128)(2,1)}, u32[]{:S(2)}) copy-start(bf16[128,1024]{1,0:T(8,128)(2,1)} %param.11) | copy-start | bytes 786436
  42.5 5.6 %copy-start.1 = (bf16[1024,3,128]{2,0,1:T(8,128)(2,1)S(1)}, bf16[1024,3,128]{2,0,1:T(8,128)(2,1)}, u32[]{:S(2)}) copy-start(bf16[1024,3,128]{2,0,1:T(8,128)(2,1)} %param.10) | copy-start | bytes 2359300
  42.5 16.1 %all-to-all-start = ((bf16[16,16,1024]{2,1,0:T(8,128)(2,1)}), bf16[16,16,1024]{2,1,0:T(8,128)(2,1)S(1)}, u32[]{:S(2)}, u32[]{:S(2)}) async-start(bf16[16,16,1024]{2,1,0:T(8,128)(2,1)} %get-tuple-element.23), calls=%async_computation | async-start | bytes 1048576 | tf_op jit(solution)/shard_map/all_to_all | solution.py:45
  60.2 38.0 %all-to-all-start.1 = ((bf16[16,128,256]{2,1,0:T(8,128)(2,1)}), bf16[16,128,256]{2,1,0:T(8,128)(2,1)S(1)}, u32[]{:S(2)}, u32[]{:S(2)}) async-start(bf16[16,128,256]{2,1,0:T(8,128)(2,1)} %get-tuple-element.24), calls=%async_computation.1 | async-start | bytes 2097152 | tf_op jit(solution)/shard_map/all_to_all | solution.py:45
  107.0 14.2 %all-to-all-start.2 = ((bf16[16,16,1024]{2,1,0:T(8,128)(2,1)}), bf16[16,16,1024]{2,1,0:T(8,128)(2,1)S(1)}, u32[]{:S(2)}, u32[]{:S(2)}) async-start(bf16[16,16,1024]{2,1,0:T(8,128)(2,1)} %coarse_attention.1), calls=%async_computation.2 | async-start | bytes 1048576 | tf_op jit(solution)/shard_map/all_to_all | solution.py:45
  121.4 5.5 %collective-permute-start.5 = (f32[1,1024]{1,0:T(1,128)S(1)}, f32[1,1024]{1,0:T(1,128)S(1)}, u32[]{:S(2)}, u32[]{:S(2)}) collective-permute-start(f32[1,1024]{1,0:T(1,128)S(1)} %slice.39), channel_id=1, source_target_pairs={{1,0},{2,1},{3,2},{4,3},{5,4},{6,5},{7,6},{8,7},{9,8},{10,9},{11,1... | collective-permute-start | bytes 12296 | tf_op jit(solution)/shard_map/ppermute | solution.py:41
  126.9 26.0 %copy-start.3 = (bf16[128,1024]{1,0:T(8,128)(2,1)S(1)}, bf16[128,1024]{1,0:T(8,128)(2,1)}, u32[]{:S(2)}) copy-start(bf16[128,1024]{1,0:T(8,128)(2,1)} %get-tuple-element.22) | copy-start | bytes 786436
  126.9 40.9 %copy-start = (bf16[128,1024]{1,0:T(8,128)(2,1)S(1)}, bf16[128,1024]{1,0:T(8,128)(2,1)}, u32[]{:S(2)}) copy-start(bf16[128,1024]{1,0:T(8,128)(2,1)} %tokens_ref.1) | copy-start | bytes 786436
  139.8 13.8 %collective-permute-start.6 = (bf16[128,1024]{1,0:T(8,128)(2,1)S(1)}, bf16[128,1024]{1,0:T(8,128)(2,1)S(1)}, u32[]{:S(2)}, u32[]{:S(2)}) collective-permute-start(bf16[128,1024]{1,0:T(8,128)(2,1)S(1)} %get-tuple-element.37), channel_id=1, source_target_pairs={{1,0},{2,1},{3,2},{4,3},{5,4},{6,5},{7,6},{8,7},{9,8},{10,9},{11,1... | collective-permute-start | bytes 786440 | tf_op jit(solution)/shard_map/ppermute | solution.py:41
  144.5 17.8 %collective-permute-start.7 = (bf16[128,1024]{1,0:T(8,128)(2,1)S(1)}, bf16[128,1024]{1,0:T(8,128)(2,1)S(1)}, u32[]{:S(2)}, u32[]{:S(2)}) collective-permute-start(bf16[128,1024]{1,0:T(8,128)(2,1)S(1)} %get-tuple-element.38), channel_id=1, source_target_pairs={{2,0},{3,1},{4,2},{5,3},{6,4},{7,5},{8,6},{9,7},{10,8},{11,9},{12,... | collective-permute-start | bytes 786440 | tf_op jit(solution)/shard_map/ppermute | solution.py:41
  146.4 16.6 %collective-permute-start.8 = (bf16[128,1024]{1,0:T(8,128)(2,1)S(1)}, bf16[128,1024]{1,0:T(8,128)(2,1)S(1)}, u32[]{:S(2)}, u32[]{:S(2)}) collective-permute-start(bf16[128,1024]{1,0:T(8,128)(2,1)S(1)} %get-tuple-element.39), channel_id=1, source_target_pairs={{3,0},{4,1},{5,2},{6,3},{7,4},{8,5},{9,6},{10,7},{11,8},{12,9},{13... | collective-permute-start | bytes 786440 | tf_op jit(solution)/shard_map/ppermute | solution.py:41
  148.4 19.4 %collective-permute-start.9 = (bf16[128,1024]{1,0:T(8,128)(2,1)S(1)}, bf16[128,1024]{1,0:T(8,128)(2,1)S(1)}, u32[]{:S(2)}, u32[]{:S(2)}) collective-permute-start(bf16[128,1024]{1,0:T(8,128)(2,1)S(1)} %get-tuple-element.40), channel_id=1, source_target_pairs={{4,0},{5,1},{6,2},{7,3},{8,4},{9,5},{10,6},{11,7},{12,8},{13,9},{1... | collective-permute-start | bytes 786440 | tf_op jit(solution)/shard_map/ppermute | solution.py:41

commit v3 on v2

--- a/solution.py
+++ b/solution.py
@@ -86,32 +86,42 @@
 
 
 def fine_forward_kernel(
-    anchor_ref, t5, t4, t3, t2, t1, t0, cot_ref, w_ref, out_w_ref,
+    place_ref, tail_ref, slots_ref, own_ref, cot_ref, w_ref, out_w_ref,
     q_ref, k_ref, v_ref, qf_ref, kf_ref, p_ref, att_ref, hid_ref, send_ref, cg_ref,
     normed, bias, acc,
 ):
     step = pl.program_id(0)
-    anchor = anchor_ref[0]
+    anchor = place_ref[0]
+    column_at = place_ref[1]
     low = low_lanes()
+    slots = slots_ref.shape[0]
+    nearest = lax.rem(column_at + (slots - 1), slots)
 
     @pl.when(step == 0)
     def _():
-        at = 0
-        for ref in (t4, t3, t2, t1, t0, t5):
-            rows = ref.shape[0]
-            normed[at : at + rows, :] = row_norm(ref[...].astype(F32))[0].astype(BF)
-            at += rows
+        for slot in range(slots):
+            at = slot * ROWS
+            normed[at : at + ROWS, :] = row_norm(slots_ref[slot].astype(F32))[0].astype(BF)
+        normed[HALO:OWN_KEYS, :] = row_norm(own_ref[...].astype(F32))[0].astype(BF)
+        normed[OWN_KEYS:, :] = row_norm(tail_ref[...].astype(F32))[0].astype(BF)
         row = lax.broadcasted_iota(jnp.int32, (2 * QUERIES, ALL_KEYS), 0)
         query_pos = jnp.where(row < QUERIES, row, row - QUERIES) - EXTRA
         column = lax.broadcasted_iota(jnp.int32, (2 * QUERIES, ALL_KEYS), 1)
-        key_pos = jnp.where(column < OWN_KEYS, column - HALO, column - (OWN_KEYS + HALO + EXTRA))
+        halo_pos = column - jnp.where(column >= column_at * ROWS, column_at * ROWS + HALO, column_at * ROWS)
+        key_pos = jnp.where(
+            column < HALO,
+            halo_pos,
+            jnp.where(column < OWN_KEYS, column - HALO, column - (OWN_KEYS + HALO + EXTRA)),
+        )
         gap = query_pos - key_pos
         allowed = (gap >= 0) & (gap < WINDOW) & (anchor + key_pos >= 0)
         bias[...] = jnp.where(allowed, 0.0, NEG)
         acc[...] = jnp.zeros_like(acc)
 
     width = q_ref.shape[1]
-    queries = plain(normed[HALO - EXTRA : OWN_KEYS, :], w_ref[0])
+    extra_at = pl.multiple_of(nearest * ROWS + (ROWS - EXTRA), EXTRA)
+    query_rows = jnp.concatenate([normed[pl.ds(extra_at, EXTRA), :], normed[HALO:OWN_KEYS, :]], axis=0)
+    queries = plain(query_rows, w_ref[0])
     both = plain(normed[...], jnp.concatenate([w_ref[1], w_ref[2]], axis=1))
     mixed = []
     for at in range(0, width, PAIR):
@@ -141,9 +151,9 @@
 
     @pl.when(step == pl.num_programs(0) - 1)
     def _():
-        before = t1[ROWS - EXTRA :, :].astype(F32) + acc[:EXTRA, :]
+        before = slots_ref[nearest, ROWS - EXTRA :, :].astype(F32) + acc[:EXTRA, :]
         before = jnp.where(anchor > 0, before, 0.0).astype(BF)
-        own = (t0[...].astype(F32) + acc[EXTRA:, :]).astype(BF)
+        own = (own_ref[...].astype(F32) + acc[EXTRA:, :]).astype(BF)
         hid_ref[...] = own
         chunk = lax.broadcasted_iota(jnp.int32, (COARSE, QUERIES), 0) * POOL
         row = lax.broadcasted_iota(jnp.int32, (COARSE, QUERIES), 1)
@@ -262,20 +272,21 @@
     send_ref[...] = jnp.concatenate([normed_grad, mixed], axis=1).astype(BF)
 
 
-def coarse_finish_kernel(got_ref, pooled_ref, cg_ref, spread_ref, state_ref):
+def coarse_finish_kernel(got_ref, message_ref, cg_ref, spread_ref, first_ref, state_ref):
     summed = jnp.sum(got_ref[...].astype(F32), axis=0)
-    pooled = pooled_ref[...].astype(F32)[:COARSE]
+    pooled = message_ref[0].astype(F32)[:COARSE]
     normed, factor = row_norm(pooled)
     pooled_grad = cg_ref[...] + row_norm_back(summed[:COARSE], normed, factor)
-    spread_ref[...] = pooled_grad * (1.0 / POOL)
+    spread = pooled_grad * (1.0 / POOL)
+    spread_ref[...] = spread
+    first_ref[...] = spread[:1]
     state_ref[...] = pooled + summed[COARSE:]
 
 
 def fine_backward_kernel(
     cot_ref, spread_ref, next_ref, out_w_ref, w_ref, q_ref, k_ref, v_ref, qf_ref, kf_ref, p_ref,
     att_ref,
-    h4, h3, h2, h1, own_ref, hg_ref,
-    hidden_grad, acc,
+    halo_ref, own_ref, hg_ref, hidden_grad, acc,
 ):
     step = pl.program_id(0)
     low = low_lanes()
@@ -330,15 +341,24 @@
 
     @pl.when(step == pl.num_programs(0) - 1)
     def _():
-        for at, ref in enumerate((h4, h3, h2, h1)):
-            ref[...] = acc[at * ROWS : (at + 1) * ROWS, :].astype(BF)
+        for slot in range(halo_ref.shape[0]):
+            halo_ref[slot] = acc[slot * ROWS : (slot + 1) * ROWS, :].astype(BF)
         own_ref[...] = acc[HALO:, :]
 
 
-def fine_finish_kernel(own_ref, a1, a2, a3, a4, hg_ref, tokens_ref, out_ref):
-    total = own_ref[...]
-    for ref in (a1, a2, a3, a4):
-        total = total + ref[...].astype(F32)
+def halo_sum_kernel(place_ref, got_ref, back_ref):
+    column_at = place_ref[1]
+    total = got_ref[0].astype(F32)
+    for slot in range(1, got_ref.shape[0]):
+        total = total + jnp.where(column_at >= slot, got_ref[slot].astype(F32), 0.0)
+    back_ref[...] = total.astype(BF)
+
+
+def fine_finish_kernel(place_ref, own_ref, got_ref, arrived_ref, hg_ref, tokens_ref, out_ref):
+    column_at = place_ref[1]
+    total = own_ref[...] + arrived_ref[...].astype(F32)
+    for slot in range(1, got_ref.shape[0]):
+        total = total + jnp.where(column_at < slot, got_ref[slot].astype(F32), 0.0)
     normed, factor = row_norm(tokens_ref[...].astype(F32))
     out_ref[...] = (hg_ref[...] + row_norm_back(total, normed, factor)).astype(BF)
 
@@ -373,13 +393,13 @@
     return pltpu.with_memory_space_constraint(x, pltpu.HBM)
 
 
-def fine_forward(anchor, t5, t4, t3, t2, t1, tokens, cotangent, weights, fine_out, peers):
+def fine_forward(place, tail, slots, tokens, cotangent, weights, fine_out, peers):
     width = FORWARD_WIDTH
     return pl.pallas_call(
         fine_forward_kernel,
         grid=(D // width,),
-        in_specs=[SCALAR, whole((EXTRA, D))]
-        + [whole((ROWS, D))] * 6
+        in_specs=[SCALAR, whole((EXTRA, D)), whole(slots.shape)]
+        + [whole((ROWS, D))] * 2
         + [
             pl.BlockSpec((3, D, width), lambda p: (0, 0, p)),
             pl.BlockSpec((width, D), lambda p: (p, 0)),
@@ -417,8 +437,7 @@
         cost_estimate=cost(4_500_000_000, 20_000_000, 1_600_000),
         name="fine_forward",
     )(
-        anchor, t5, t4, t3, t2, t1, in_hbm(tokens), in_hbm(cotangent), in_hbm(weights),
-        in_hbm(fine_out),
+        place, tail, slots, in_hbm(tokens), in_hbm(cotangent), in_hbm(weights), in_hbm(fine_out)
     )
 
 
@@ -446,14 +465,17 @@
     )(own_start, everyone, factor, coarse_in, coarse_back)
 
 
-def coarse_finish(returned, pooled, coarse_grad):
+def coarse_finish(returned, message, coarse_grad):
     return pl.pallas_call(
         coarse_finish_kernel,
-        out_shape=[shaped((COARSE, D), F32), shaped((COARSE, D), F32)],
+        grid=(1,),
+        in_specs=[whole(returned.shape), whole((1, 2 * COARSE, D)), whole((COARSE, D))],
+        out_specs=[whole((COARSE, D)), whole((1, D)), whole((COARSE, D))],
+        out_shape=[shaped((COARSE, D), F32), shaped((1, D), F32), shaped((COARSE, D), F32)],
         compiler_params=params(VMEM_MIB),
         cost_estimate=cost(1_000_000, 1_000_000),
         name="coarse_finish",
-    )(returned, pooled, coarse_grad)
+    )(returned, message, coarse_grad)
 
 
 def fine_backward(
@@ -478,8 +500,8 @@
             pl.BlockSpec((width // HEAD_DIM, ROWS, OWN_KEYS), lambda p: (p, 0, 0)),
             columns(ROWS, width),
         ],
-        out_specs=[whole((ROWS, D))] * 6,
-        out_shape=[shaped((ROWS, D), BF)] * 4 + [shaped((ROWS, D), F32)] * 2,
+        out_specs=[whole((HALO // ROWS, ROWS, D)), whole((ROWS, D)), whole((ROWS, D))],
+        out_shape=[shaped((HALO // ROWS, ROWS, D), BF)] + [shaped((ROWS, D), F32)] * 2,
         scratch_shapes=[pltpu.VMEM((ROWS, D), BF), pltpu.VMEM((OWN_KEYS, D), F32)],
         compiler_params=params(VMEM_MIB),
         cost_estimate=cost(5_000_000_000, 20_000_000),
@@ -491,14 +513,26 @@
     )
 
 
-def fine_finish(own, arrived, hidden_grad, tokens):
+def halo_sum(place, got):
+    return pl.pallas_call(
+        halo_sum_kernel,
+        in_specs=[SCALAR, IN_VMEM],
+        out_shape=shaped((ROWS, D), BF),
+        compiler_params=params(VMEM_MIB),
+        cost_estimate=cost(1_000_000, 1_500_000),
+        name="halo_sum",
+    )(place, got)
+
+
+def fine_finish(place, own, got, arrived, hidden_grad, tokens):
     return pl.pallas_call(
         fine_finish_kernel,
+        in_specs=[SCALAR] + [IN_VMEM] * 5,
         out_shape=shaped((ROWS, D), BF),
         compiler_params=params(VMEM_MIB),
         cost_estimate=cost(1_000_000, 3_000_000),
         name="fine_finish",
-    )(own, *arrived, hidden_grad, tokens)
+    )(place, own, got, arrived, hidden_grad, tokens)
 
 
 def per_device(tokens, cotangent, fine_qkv, fine_out, coarse_qkv, coarse_out):
@@ -517,12 +551,16 @@
     picked_out = jnp.where(core == 0, coarse_out[:HEAD_DIM], coarse_out[HEAD_DIM:])
     coarse_back = jnp.pad(picked_out, ((HEAD_DIM, PAIR), (0, 0)))
 
-    t1, t2, t3, t4 = (shifted_by(tokens, steps) for steps in (1, 2, 3, 4))
-    t5 = shifted_by(tokens[ROWS - EXTRA :], 5)
-    anchor = (lax.axis_index(LINE) * ROWS).astype(jnp.int32).reshape(1)
+    column_at = lax.axis_index("x")
+    columns_along = lax.axis_size("x")
+    tail = shifted_by(tokens[ROWS - EXTRA :], columns_along + 1)
+    row_before = shifted_by(tokens, columns_along)
+    later = (jnp.arange(columns_along) > column_at)[:, None, None]
+    slots = exchanged(jnp.where(later, tokens[None], row_before[None]), "x")
+    place = jnp.stack([lax.axis_index(LINE) * ROWS, column_at]).astype(jnp.int32)
 
     query, key, value, q_factor, k_factor, probs, attended, hidden, message, coarse_grad = (
-        fine_forward(anchor, t5, t4, t3, t2, t1, tokens, cotangent, weights, fine_out, peers)
+        fine_forward(place, tail, slots, tokens, cotangent, weights, fine_out, peers)
     )
     gathered = exchanged(message, GROUP)
     coarse_send, coarse_factor = coarse_project(gathered, coarse_in, coarse_back, groups)
@@ -531,17 +569,18 @@
     own_start = (lax.axis_index(FAR) * group_rows).astype(jnp.int32).reshape(1)
     partial = coarse_attention(own_start, everyone, coarse_factor, coarse_in, coarse_back)
     returned = exchanged(partial, GROUP)
-    spread, state = coarse_finish(returned, message[0], coarse_grad)
-    after = shifted_by(spread[0:1], -1)
+    spread, first, state = coarse_finish(returned, message, coarse_grad)
+    after = shifted_by(first, -1)
     output = (
         hidden.astype(F32) + jnp.repeat(state.astype(BF), POOL, axis=0).astype(F32)
     ).astype(BF)
-    h4, h3, h2, h1, own, hidden_grad = fine_backward(
+    halo, own, hidden_grad = fine_backward(
         cotangent, spread, after, fine_out, weights, query, key, value, q_factor, k_factor, probs,
         attended,
     )
-    arrived = [shifted_by(rows, -steps) for rows, steps in ((h1, 1), (h2, 2), (h3, 3), (h4, 4))]
-    return (output, fine_finish(own, arrived, hidden_grad, tokens))
+    got = exchanged(halo, "x")
+    arrived = shifted_by(halo_sum(place, got), -columns_along)
+    return (output, fine_finish(place, own, got, arrived, hidden_grad, tokens))
 
 
 def solution(mesh):

time: 171 us -> 172 us (level)
  blocking collectives: 0 us -> 31 us
  starting transfers between devices: 52.2 us -> 32.8 us
  waiting for transfers between devices: 75.1 us -> 62.8 us
  other arithmetic: 1.28 us -> 3.45 us
    all_to_all x0 -> x2, blocking collectives: none -> 31 us  [exchanged(): return lax.all_to_all(pieces, axes, 0, 0, tiled=True)]
    ppermute x10 -> x4, starting transfers between devices: 33.4 us -> 14.7 us  [shifted_by(): lax.ppermute(value, LINE, [(source, source + steps) for source in range(f...]
    ppermute x10 -> x4, waiting for transfers between devices: 27.2 us -> 19.1 us  [shifted_by(): lax.ppermute(value, LINE, [(source, source + steps) for source in range(f...]
    all_to_all x3, waiting for transfers between devices: 47.9 us -> 43.7 us  [exchanged(): return lax.all_to_all(pieces, axes, 0, 0, tiled=True)]
    pallas_call x2 -> x3, Pallas kernels: 1.22 us -> 3.32 us  [the longest x1 1.65 us: fine_finish(): pl.pallas_call(fine_finish_kernel, in_specs=[SCALAR] + [IN_VMEM] * 5, out...]
    select_n x0 -> x1, other arithmetic: none -> 2.09 us  [per_device(): slots = exchanged(jnp.where(later, tokens[None], row_before[None]), 'x')]
  transfers between devices with their start and end apart: 13 -> 7, of which waited for: 8 -> 7; matrix products, arithmetic and copies ran while one was open for 2% -> 1% of each run, Pallas kernels for 0% -> 0%
where the time goes in v3:
time: 172 us; the launch traced here: 171 us
  waiting for transfers between devices  62.8 us (37%)
  Pallas kernels  38.9 us (23%)
  starting transfers between devices  32.8 us (19%)
  blocking collectives  31 us (18%)
  other arithmetic  3.45 us (2%)
    all_to_all x3, waiting for transfers between devices, exchanged(): return lax.all_to_all(pieces, axes, 0, 0, tiled=True)  43.7 us
    all_to_all x2, blocking collectives, exchanged(): return lax.all_to_all(pieces, axes, 0, 0, tiled=True)  31 us
    ppermute x4, waiting for transfers between devices, shifted_by(): lax.ppermute(value, LINE, [(source, source + steps) for source in range(f...  19.1 us
    all_to_all x3, starting transfers between devices, exchanged(): return lax.all_to_all(pieces, axes, 0, 0, tiled=True)  18.1 us
    ppermute x4, starting transfers between devices, shifted_by(): lax.ppermute(value, LINE, [(source, source + steps) for source in range(f...  14.7 us
    pallas_call x1, Pallas kernels, fine_forward(): pl.pallas_call(fine_forward_kernel, grid=(D // width,), in_specs=[SCALAR,...  13.1 us
    pallas_call x1, Pallas kernels, fine_backward(): pl.pallas_call(fine_backward_kernel, grid=(D // width,), in_specs=[whole(...  12.8 us
    pallas_call x1, Pallas kernels, coarse_attention(): pl.pallas_call(coarse_attention_kernel, in_specs=[SCALAR] + [IN_VMEM] * 4...  8 us
  transfers between devices with their start and end apart: 7, of which 7 were waited for; matrix products, arithmetic and copies ran while one was open for 1% of the time, Pallas kernels for 0%

profile of v3, /device:TPU:64, one launch (start us, length us, event | category | flops | bytes accessed | tf_op | source)
XLA Modules:
  0.0 170.7 jit_solution(230458726753193596)
XLA Ops:
  0.6 3.8 %collective-permute-start.1 = (bf16[128,1024]{1,0:T(8,128)(2,1)}, bf16[128,1024]{1,0:T(8,128)(2,1)S(1)}, u32[]{:S(2)}, u32[]{:S(2)}) collective-permute-start(bf16[128,1024]{1,0:T(8,128)(2,1)} %tokens_ref.1), channel_id=1, source_target_pairs={{0,4},{1,5},{2,6},{3,7},{4,8},{5,9},{6,10},{7,11},{8,12},{9,13},{1... | collective-permute-start | bytes 786440 | tf_op jit(solution)/shard_map/ppermute | solution.py:41
  4.5 5.8 %collective-permute-done.1 = bf16[128,1024]{1,0:T(8,128)(2,1)S(1)} collective-permute-done((bf16[128,1024]{1,0:T(8,128)(2,1)}, bf16[128,1024]{1,0:T(8,128)(2,1)S(1)}, u32[]{:S(2)}, u32[]{:S(2)}) %collective-permute-start.1) | collective-permute-done | bytes 262176 | tf_op jit(solution)/shard_map/ppermute | solution.py:41
  10.3 2.1 %broadcast_select_fusion = bf16[4,128,1024]{2,1,0:T(8,128)(2,1)} fusion(pred[4]{0:T(512)(128)(4,1)S(1)} %iota_compare_fusion, bf16[128,1024]{1,0:T(8,128)(2,1)S(1)} %collective-permute-done.1, bf16[128,1024]{1,0:T(8,128)(2,1)} %tokens_ref.1), kind=kLoop, calls=%fused_computation | loop fusion | flops 524288 | bytes 1572868 | tf_op jit(solution)/shard_map/jit(_where)/select_n | solution.py:559
  12.4 4.3 %all-to-all-start = ((bf16[4,128,1024]{2,1,0:T(8,128)(2,1)}), bf16[4,128,1024]{2,1,0:T(8,128)(2,1)S(1)}, u32[]{:S(2)}, u32[]{:S(2)}) async-start(bf16[4,128,1024]{2,1,0:T(8,128)(2,1)} %broadcast_select_fusion), calls=%async_computation | async-start | bytes 2097152 | tf_op jit(solution)/shard_map/all_to_all | solution.py:45
  16.7 0.8 slice.24
  17.5 5.7 %collective-permute-start = (bf16[16,1024]{1,0:T(8,128)(2,1)S(1)}, bf16[16,1024]{1,0:T(8,128)(2,1)S(1)}, u32[]{:S(2)}, u32[]{:S(2)}) collective-permute-start(bf16[16,1024]{1,0:T(8,128)(2,1)S(1)} %slice.24), channel_id=1, source_target_pairs={{0,5},{1,6},{2,7},{3,8},{4,9},{5,10},{6,11},{7,12},{8,13},{9,14},{... | collective-permute-start | bytes 98312 | tf_op jit(solution)/shard_map/ppermute | solution.py:41
  23.2 0.1 pad_add_fusion.place_ref
  23.3 2.7 %collective-permute-done.tail_ref = bf16[16,1024]{1,0:T(8,128)(2,1)S(1)} collective-permute-done((bf16[16,1024]{1,0:T(8,128)(2,1)S(1)}, bf16[16,1024]{1,0:T(8,128)(2,1)S(1)}, u32[]{:S(2)}, u32[]{:S(2)}) %collective-permute-start) | collective-permute-done | bytes 32800 | tf_op jit(solution)/shard_map/ppermute | solution.py:41
  26.0 5.7 %all-to-all-done.slots_ref = bf16[4,128,1024]{2,1,0:T(8,128)(2,1)S(1)} async-done(((bf16[4,128,1024]{2,1,0:T(8,128)(2,1)}), bf16[4,128,1024]{2,1,0:T(8,128)(2,1)S(1)}, u32[]{:S(2)}, u32[]{:S(2)}) %all-to-all-start) | async-done | bytes 1048608 | tf_op jit(solution)/shard_map/all_to_all | solution.py:45
  31.6 13.1 %fine_forward.1 = (bf16[128,1024]{1,0:T(8,128)(2,1)}, bf16[640,1024]{1,0:T(8,128)(2,1)}, bf16[640,1024]{1,0:T(8,128)(2,1)}, f32[128,1024]{1,0:T(8,128)}, f32[640...) custom-call(s32[2]{0:T(128)S(1)} %pad_add_fusion.place_ref, ...), custom_call_target="tpu_custom_call" | custom-call | flops 4499999744 | bytes 20000000 | tf_op jit(solution)/shard_map/fine_forward/pallas_call | solution.py:398
  44.8 0.0 copy-start.1
  44.8 3.9 %all-to-all-start.1 = ((bf16[16,16,1024]{2,1,0:T(8,128)(2,1)}), bf16[16,16,1024]{2,1,0:T(8,128)(2,1)S(1)}, u32[]{:S(2)}, u32[]{:S(2)}) async-start(bf16[16,16,1024]{2,1,0:T(8,128)(2,1)} %get-tuple-element.21.message_ref), calls=%async_computation.1 | async-start | bytes 1048576 | tf_op jit(solution)/shard_map/all_to_all | solution.py:45
  48.8 0.1 pad.6.clone
  48.9 0.3 slice_select_fusion
  49.1 0.1 slice_bitcast_fusion.2
  49.2 0.2 pad_maximum_fusion.in_w_ref
  49.4 9.9 %all-to-all-done.1.got_ref = bf16[16,16,1024]{2,1,0:T(8,128)(2,1)S(1)} async-done(((bf16[16,16,1024]{2,1,0:T(8,128)(2,1)}), bf16[16,16,1024]{2,1,0:T(8,128)(2,1)S(1)}, u32[]{:S(2)}, u32[]{:S(2)}) %all-to-all-start.1) | async-done | bytes 524320 | tf_op jit(solution)/shard_map/all_to_all | solution.py:45
  59.4 1.6 coarse_project.1
  61.0 9.9 %all-to-all-start.2 = ((bf16[16,128,256]{2,1,0:T(8,128)(2,1)}), bf16[16,128,256]{2,1,0:T(8,128)(2,1)S(1)}, u32[]{:S(2)}, u32[]{:S(2)}) async-start(bf16[16,128,256]{2,1,0:T(8,128)(2,1)} %get-tuple-element.22), calls=%async_computation.2 | async-start | bytes 2097152 | tf_op jit(solution)/shard_map/all_to_all | solution.py:45
  70.9 28.1 %all-to-all-done.2 = bf16[16,128,256]{2,1,0:T(8,128)(2,1)S(1)} async-done(((bf16[16,128,256]{2,1,0:T(8,128)(2,1)}), bf16[16,128,256]{2,1,0:T(8,128)(2,1)S(1)}, u32[]{:S(2)}, u32[]{:S(2)}) %all-to-all-start.2) | async-done | bytes 1048608 | tf_op jit(solution)/shard_map/all_to_all | solution.py:45
  99.0 8.0 %coarse_attention.1 = bf16[16,16,1024]{2,1,0:T(8,128)(2,1)S(1)} custom-call(s32[1]{0:T(128)} %bitcast.3.start_ref, bf16[2048,256]{1,0:T(8,128)(2,1)S(1)} %bitcast.16, f32[128,256]{1,0:T(8,128)S(1)} %get-tuple-element.23.factor_ref, bf16[1024,256]{1,0:T(8,128)(2,1)S(1)} %pad_maximum_fusion.in_w_ref, bf16[256,1024]{1,0:T(8,128)(2,1)S(1)} %pad.4.out_w_ref), custom_call_target="tpu_custom_call" | custom-call | flops 1500000000 | bytes 3000000 | tf_op jit(solution)/shard_map/coarse_attention/pallas_call | solution.py:457
  107.0 13.3 %all_to_all.25.got_ref = bf16[16,16,1024]{2,1,0:T(8,128)(2,1)S(1)} all-to-all(bf16[16,16,1024]{2,1,0:T(8,128)(2,1)S(1)} %coarse_attention.1), channel_id=1, replica_groups=mesh['y'=4,'z_hi'=4,'core'=2,'z_lo'=2,'x'=4] {'core','z_lo','x'}, dimensions={0} | all-to-all | bytes 1048576 | tf_op jit(solution)/shard_map/all_to_all | solution.py:45
  120.3 0.9 coarse_finish.1
  121.2 3.1 %collective-permute-start.2 = (f32[1,1024]{1,0:T(1,128)S(1)}, f32[1,1024]{1,0:T(1,128)S(1)}, u32[]{:S(2)}, u32[]{:S(2)}) collective-permute-start(f32[1,1024]{1,0:T(1,128)S(1)} %get-tuple-element.27), channel_id=1, source_target_pairs={{1,0},{2,1},{3,2},{4,3},{5,4},{6,5},{7,6},{8,7},{9,8},{10,9},{11,1... | collective-permute-start | bytes 12296 | tf_op jit(solution)/shard_map/ppermute | solution.py:41
  124.4 2.4 %collective-permute-done.2.next_ref = f32[1,1024]{1,0:T(1,128)S(1)} collective-permute-done((f32[1,1024]{1,0:T(1,128)S(1)}, f32[1,1024]{1,0:T(1,128)S(1)}, u32[]{:S(2)}, u32[]{:S(2)}) %collective-permute-start.2) | collective-permute-done | bytes 4128 | tf_op jit(solution)/shard_map/ppermute | solution.py:41
  126.7 12.8 %fine_backward.1 = (bf16[4,128,1024]{2,1,0:T(8,128)(2,1)S(1)}, f32[128,1024]{1,0:T(8,128)S(1)}, f32[128,1024]{1,0:T(8,128)S(1)}) custom-call(bf16[128,1024]{1,0:T(8,128)(2,1)} %cot_ref.3, f32[8,1024]{1,0:T(8,128)S(1)} %get-tuple-element.26.spread_ref, f32[1,1024]{1,0:T(1,128)S(1)} %collective-permute-done.2.next_ref, bf16[1024,1024]{1,0:T(8,128)(2,1)} %out_w_ref.3, ...), custom_call_target="tpu_custom_call" | custom-call | flops 5000000000 | bytes 20000000 | tf_op jit(solution)/shard_map/fine_backward/pallas_call | solution.py:486
  139.6 17.7 %all_to_all.26.got_ref = bf16[4,128,1024]{2,1,0:T(8,128)(2,1)S(1)} all-to-all(bf16[4,128,1024]{2,1,0:T(8,128)(2,1)S(1)} %get-tuple-element.36), channel_id=1, replica_groups=mesh['y'=4,'z_hi'=4,'core'=2,'z_lo'=2,'x'=4] {'x'}, dimensions={0} | all-to-all | bytes 2097152 | tf_op jit(solution)/shard_map/all_to_all | solution.py:45
  157.3 0.7 halo_sum.1
  158.1 2.0 %collective-permute-start.3 = (bf16[128,1024]{1,0:T(8,128)(2,1)S(1)}, bf16[128,1024]{1,0:T(8,128)(2,1)S(1)}, u32[]{:S(2)}, u32[]{:S(2)}) collective-permute-start(bf16[128,1024]{1,0:T(8,128)(2,1)S(1)} %halo_sum.1), channel_id=1, source_target_pairs={{4,0},{5,1},{6,2},{7,3},{8,4},{9,5},{10,6},{11,7},{12,8},{13,9},{1... | collective-permute-start | bytes 786440 | tf_op jit(solution)/shard_map/ppermute | solution.py:41
  160.1 0.8 fusion
  160.9 8.2 %collective-permute-done.3.arrived_ref = bf16[128,1024]{1,0:T(8,128)(2,1)S(1)} collective-permute-done((bf16[128,1024]{1,0:T(8,128)(2,1)S(1)}, bf16[128,1024]{1,0:T(8,128)(2,1)S(1)}, u32[]{:S(2)}, u32[]{:S(2)}) %collective-permute-start.3) | collective-permute-done | bytes 262176 | tf_op jit(solution)/shard_map/ppermute | solution.py:41
  169.1 1.7 fine_finish.1
  (12 shorter events, 0.1 us)
Async XLA Ops:
  0.6 9.7 %collective-permute-start.1 = (bf16[128,1024]{1,0:T(8,128)(2,1)}, bf16[128,1024]{1,0:T(8,128)(2,1)S(1)}, u32[]{:S(2)}, u32[]{:S(2)}) collective-permute-start(bf16[128,1024]{1,0:T(8,128)(2,1)} %tokens_ref.1), channel_id=1, source_target_pairs={{0,4},{1,5},{2,6},{3,7},{4,8},{5,9},{6,10},{7,11},{8,12},{9,13},{1... | collective-permute-start | bytes 786440 | tf_op jit(solution)/shard_map/ppermute | solution.py:41
  12.4 19.2 %all-to-all-start = ((bf16[4,128,1024]{2,1,0:T(8,128)(2,1)}), bf16[4,128,1024]{2,1,0:T(8,128)(2,1)S(1)}, u32[]{:S(2)}, u32[]{:S(2)}) async-start(bf16[4,128,1024]{2,1,0:T(8,128)(2,1)} %broadcast_select_fusion), calls=%async_computation | async-start | bytes 2097152 | tf_op jit(solution)/shard_map/all_to_all | solution.py:45
  17.5 8.5 %collective-permute-start = (bf16[16,1024]{1,0:T(8,128)(2,1)S(1)}, bf16[16,1024]{1,0:T(8,128)(2,1)S(1)}, u32[]{:S(2)}, u32[]{:S(2)}) collective-permute-start(bf16[16,1024]{1,0:T(8,128)(2,1)S(1)} %slice.24), channel_id=1, source_target_pairs={{0,5},{1,6},{2,7},{3,8},{4,9},{5,10},{6,11},{7,12},{8,13},{9,14},{... | collective-permute-start | bytes 98312 | tf_op jit(solution)/shard_map/ppermute | solution.py:41
  31.6 17.1 %copy-start.2 = (bf16[128,1024]{1,0:T(8,128)(2,1)S(1)}, bf16[128,1024]{1,0:T(8,128)(2,1)}, u32[]{:S(2)}) copy-start(bf16[128,1024]{1,0:T(8,128)(2,1)} %param.11) | copy-start | bytes 786436
  44.8 4.1 %copy-start.1 = (bf16[1024,3,128]{2,0,1:T(8,128)(2,1)S(1)}, bf16[1024,3,128]{2,0,1:T(8,128)(2,1)}, u32[]{:S(2)}) copy-start(bf16[1024,3,128]{2,0,1:T(8,128)(2,1)} %param.10) | copy-start | bytes 2359300
  44.8 14.6 %all-to-all-start.1 = ((bf16[16,16,1024]{2,1,0:T(8,128)(2,1)}), bf16[16,16,1024]{2,1,0:T(8,128)(2,1)S(1)}, u32[]{:S(2)}, u32[]{:S(2)}) async-start(bf16[16,16,1024]{2,1,0:T(8,128)(2,1)} %get-tuple-element.21.message_ref), calls=%async_computation.1 | async-start | bytes 1048576 | tf_op jit(solution)/shard_map/all_to_all | solution.py:45
  61.0 38.0 %all-to-all-start.2 = ((bf16[16,128,256]{2,1,0:T(8,128)(2,1)}), bf16[16,128,256]{2,1,0:T(8,128)(2,1)S(1)}, u32[]{:S(2)}, u32[]{:S(2)}) async-start(bf16[16,128,256]{2,1,0:T(8,128)(2,1)} %get-tuple-element.22), calls=%async_computation.2 | async-start | bytes 2097152 | tf_op jit(solution)/shard_map/all_to_all | solution.py:45
  121.2 5.5 %collective-permute-start.2 = (f32[1,1024]{1,0:T(1,128)S(1)}, f32[1,1024]{1,0:T(1,128)S(1)}, u32[]{:S(2)}, u32[]{:S(2)}) collective-permute-start(f32[1,1024]{1,0:T(1,128)S(1)} %get-tuple-element.27), channel_id=1, source_target_pairs={{1,0},{2,1},{3,2},{4,3},{5,4},{6,5},{7,6},{8,7},{9,8},{10,9},{11,1... | collective-permute-start | bytes 12296 | tf_op jit(solution)/shard_map/ppermute | solution.py:41
  139.6 20.5 %copy-start.3 = (bf16[128,1024]{1,0:T(8,128)(2,1)S(1)}, bf16[128,1024]{1,0:T(8,128)(2,1)}, u32[]{:S(2)}) copy-start(bf16[128,1024]{1,0:T(8,128)(2,1)} %get-tuple-element.20) | copy-start | bytes 786436
  139.6 29.5 %copy-start = (bf16[128,1024]{1,0:T(8,128)(2,1)S(1)}, bf16[128,1024]{1,0:T(8,128)(2,1)}, u32[]{:S(2)}) copy-start(bf16[128,1024]{1,0:T(8,128)(2,1)} %tokens_ref.1) | copy-start | bytes 786436
  158.1 11.0 %collective-permute-start.3 = (bf16[128,1024]{1,0:T(8,128)(2,1)S(1)}, bf16[128,1024]{1,0:T(8,128)(2,1)S(1)}, u32[]{:S(2)}, u32[]{:S(2)}) collective-permute-start(bf16[128,1024]{1,0:T(8,128)(2,1)S(1)} %halo_sum.1), channel_id=1, source_target_pairs={{4,0},{5,1},{6,2},{7,3},{8,4},{9,5},{10,6},{11,7},{12,8},{13,9},{1... | collective-permute-start | bytes 786440 | tf_op jit(solution)/shard_map/ppermute | solution.py:41

commit v4 on v3

--- a/solution.py
+++ b/solution.py
@@ -344,6 +344,17 @@
         for slot in range(halo_ref.shape[0]):
             halo_ref[slot] = acc[slot * ROWS : (slot + 1) * ROWS, :].astype(BF)
         own_ref[...] = acc[HALO:, :]
+
+
+def halo_send_kernel(place_ref, own_ref, before_ref, send_ref):
+    column_at = place_ref[1]
+    for slot in range(send_ref.shape[0]):
+        send_ref[slot] = jnp.where(column_at < slot, own_ref[...], before_ref[...])
+
+
+def repeated_kernel(block_ref, send_ref):
+    for peer in range(send_ref.shape[0]):
+        send_ref[peer] = block_ref[...]
 
 
 def halo_sum_kernel(place_ref, got_ref, back_ref):
@@ -513,6 +524,27 @@
     )
 
 
+def halo_send(place, own, before, count):
+    return pl.pallas_call(
+        halo_send_kernel,
+        in_specs=[SCALAR] + [IN_VMEM] * 2,
+        out_shape=shaped((count, ROWS, D), BF),
+        compiler_params=params(VMEM_MIB),
+        cost_estimate=cost(1_000_000, 1_500_000),
+        name="halo_send",
+    )(place, own, before)
+
+
+def repeated(block, count):
+    return pl.pallas_call(
+        repeated_kernel,
+        out_shape=shaped((count, *block.shape), BF),
+        compiler_params=params(VMEM_MIB),
+        cost_estimate=cost(1_000_000, 1_300_000),
+        name="repeated",
+    )(block)
+
+
 def halo_sum(place, got):
     return pl.pallas_call(
         halo_sum_kernel,
@@ -555,17 +587,19 @@
     columns_along = lax.axis_size("x")
     tail = shifted_by(tokens[ROWS - EXTRA :], columns_along + 1)
     row_before = shifted_by(tokens, columns_along)
-    later = (jnp.arange(columns_along) > column_at)[:, None, None]
-    slots = exchanged(jnp.where(later, tokens[None], row_before[None]), "x")
+    tail, row_before = lax.optimization_barrier((tail, row_before))
     place = jnp.stack([lax.axis_index(LINE) * ROWS, column_at]).astype(jnp.int32)
+    slots = exchanged(halo_send(place, tokens, row_before, columns_along), "x")
 
     query, key, value, q_factor, k_factor, probs, attended, hidden, message, coarse_grad = (
         fine_forward(place, tail, slots, tokens, cotangent, weights, fine_out, peers)
     )
     gathered = exchanged(message, GROUP)
-    coarse_send, coarse_factor = coarse_project(gathered, coarse_in, coarse_back, groups)
+    near, further = lax.axis_size("z_hi"), lax.axis_size("y")
+    coarse_send, coarse_factor = coarse_project(gathered, coarse_in, coarse_back, near)
     group_rows = coarse_factor.shape[0]
-    everyone = exchanged(coarse_send, FAR).reshape(groups * group_rows, 2 * PAIR)
+    nearby = exchanged(coarse_send, "z_hi").reshape(near * group_rows, 2 * PAIR)
+    everyone = exchanged(repeated(nearby, further), "y").reshape(groups * group_rows, 2 * PAIR)
     own_start = (lax.axis_index(FAR) * group_rows).astype(jnp.int32).reshape(1)
     partial = coarse_attention(own_start, everyone, coarse_factor, coarse_in, coarse_back)
     returned = exchanged(partial, GROUP)

time: 172 us -> 171 us (level)
  blocking collectives: 31 us -> 46.1 us
  starting transfers between devices: 32.8 us -> 23.1 us
  waiting for transfers between devices: 62.8 us -> 56.2 us
  other arithmetic: 3.45 us -> 1.35 us
    all_to_all x2 -> x3, blocking collectives: 31 us -> 46.1 us  [exchanged(): return lax.all_to_all(pieces, axes, 0, 0, tiled=True)]
    all_to_all x3, starting transfers between devices: 18.1 us -> 12.6 us  [exchanged(): return lax.all_to_all(pieces, axes, 0, 0, tiled=True)]
    all_to_all x3, waiting for transfers between devices: 43.7 us -> 39 us  [exchanged(): return lax.all_to_all(pieces, axes, 0, 0, tiled=True)]
    ppermute x4, starting transfers between devices: 14.7 us -> 10.5 us  [shifted_by(): lax.ppermute(value, LINE, [(source, source + steps) for source in range(f...]
    pallas_call x0 -> x2, Pallas kernels: none -> 2.68 us  [the longest x1 1.59 us: halo_send(): pl.pallas_call(halo_send_kernel, in_specs=[SCALAR] + [IN_VMEM] * 2, out_s...]
    select_n x1 -> x0, other arithmetic: 2.09 us -> none  [per_device(): slots = exchanged(jnp.where(later, tokens[None], row_before[None]), 'x')]
    ppermute x4, waiting for transfers between devices: 19.1 us -> 17.2 us  [shifted_by(): lax.ppermute(value, LINE, [(source, source + steps) for source in range(f...]
  transfers between devices with their start and end apart: 7 -> 7, of which waited for: 7 -> 6; matrix products, arithmetic and copies ran while one was open for 1% -> 1% of each run, Pallas kernels for 0% -> 0%
where the time goes in v4:
time: 171 us; the launch traced here: 170 us
  waiting for transfers between devices  56.2 us (33%)
  blocking collectives  46.1 us (27%)
  Pallas kernels  40.5 us (24%)
  starting transfers between devices  23.1 us (14%)
  local copies, waits for them, and re-layouts  1.92 us (1%)
    all_to_all x3, blocking collectives, exchanged(): return lax.all_to_all(pieces, axes, 0, 0, tiled=True)  46.1 us
    all_to_all x3, waiting for transfers between devices, exchanged(): return lax.all_to_all(pieces, axes, 0, 0, tiled=True)  39 us
    ppermute x4, waiting for transfers between devices, shifted_by(): lax.ppermute(value, LINE, [(source, source + steps) for source in range(f...  17.2 us
    pallas_call x1, Pallas kernels, fine_forward(): pl.pallas_call(fine_forward_kernel, grid=(D // width,), in_specs=[SCALAR,...  13.1 us
    pallas_call x1, Pallas kernels, fine_backward(): pl.pallas_call(fine_backward_kernel, grid=(D // width,), in_specs=[whole(...  12.8 us
    all_to_all x3, starting transfers between devices, exchanged(): return lax.all_to_all(pieces, axes, 0, 0, tiled=True)  12.6 us
    ppermute x4, starting transfers between devices, shifted_by(): lax.ppermute(value, LINE, [(source, source + steps) for source in range(f...  10.5 us
    pallas_call x1, Pallas kernels, coarse_attention(): pl.pallas_call(coarse_attention_kernel, in_specs=[SCALAR] + [IN_VMEM] * 4...  8 us
  transfers between devices with their start and end apart: 7, of which 6 were waited for; matrix products, arithmetic and copies ran while one was open for 1% of the time, Pallas kernels for 0%

profile of v4, /device:TPU:64, one launch (start us, length us, event | category | flops | bytes accessed | tf_op | source)
XLA Modules:
  0.0 169.9 jit_solution(2733336161405280234)
XLA Ops:
  0.6 3.8 %collective-permute-start.1 = (bf16[128,1024]{1,0:T(8,128)(2,1)}, bf16[128,1024]{1,0:T(8,128)(2,1)S(1)}, u32[]{:S(2)}, u32[]{:S(2)}) collective-permute-start(bf16[128,1024]{1,0:T(8,128)(2,1)} %tokens_ref.1), channel_id=1, source_target_pairs={{0,4},{1,5},{2,6},{3,7},{4,8},{5,9},{6,10},{7,11},{8,12},{9,13},{1... | collective-permute-start | bytes 786440 | tf_op jit(solution)/shard_map/ppermute | solution.py:41
  4.5 0.8 slice.24
  5.2 2.8 %collective-permute-start = (bf16[16,1024]{1,0:T(8,128)(2,1)S(1)}, bf16[16,1024]{1,0:T(8,128)(2,1)S(1)}, u32[]{:S(2)}, u32[]{:S(2)}) collective-permute-start(bf16[16,1024]{1,0:T(8,128)(2,1)S(1)} %slice.24), channel_id=1, source_target_pairs={{0,5},{1,6},{2,7},{3,8},{4,9},{5,10},{6,11},{7,12},{8,13},{9,14},{... | collective-permute-start | bytes 98312 | tf_op jit(solution)/shard_map/ppermute | solution.py:41
  8.1 0.1 pad_add_fusion.place_ref
  8.2 5.3 %collective-permute-done.tail_ref = bf16[16,1024]{1,0:T(8,128)(2,1)S(1)} collective-permute-done((bf16[16,1024]{1,0:T(8,128)(2,1)S(1)}, bf16[16,1024]{1,0:T(8,128)(2,1)S(1)}, u32[]{:S(2)}, u32[]{:S(2)}) %collective-permute-start) | collective-permute-done | bytes 32800 | tf_op jit(solution)/shard_map/ppermute | solution.py:41
  13.5 0.9 copy-done
  14.4 1.6 halo_send.1
  16.0 3.5 %all-to-all-start = ((bf16[4,128,1024]{2,1,0:T(8,128)(2,1)}), bf16[4,128,1024]{2,1,0:T(8,128)(2,1)S(1)}, u32[]{:S(2)}, u32[]{:S(2)}) async-start(bf16[4,128,1024]{2,1,0:T(8,128)(2,1)} %halo_send.1), calls=%async_computation | async-start | bytes 2097152 | tf_op jit(solution)/shard_map/all_to_all | solution.py:45
  19.6 14.3 %all-to-all-done.slots_ref = bf16[4,128,1024]{2,1,0:T(8,128)(2,1)S(1)} async-done(((bf16[4,128,1024]{2,1,0:T(8,128)(2,1)}), bf16[4,128,1024]{2,1,0:T(8,128)(2,1)S(1)}, u32[]{:S(2)}, u32[]{:S(2)}) %all-to-all-start) | async-done | bytes 1048608 | tf_op jit(solution)/shard_map/all_to_all | solution.py:45
  33.8 13.1 %fine_forward.1 = (bf16[128,1024]{1,0:T(8,128)(2,1)}, bf16[640,1024]{1,0:T(8,128)(2,1)}, bf16[640,1024]{1,0:T(8,128)(2,1)}, f32[128,1024]{1,0:T(8,128)}, f32[640...) custom-call(s32[2]{0:T(128)S(1)} %pad_add_fusion.place_ref, ...), custom_call_target="tpu_custom_call" | custom-call | flops 4499999744 | bytes 20000000 | tf_op jit(solution)/shard_map/fine_forward/pallas_call | solution.py:409
  47.0 4.6 %all-to-all-start.1 = ((bf16[16,16,1024]{2,1,0:T(8,128)(2,1)}), bf16[16,16,1024]{2,1,0:T(8,128)(2,1)S(1)}, u32[]{:S(2)}, u32[]{:S(2)}) async-start(bf16[16,16,1024]{2,1,0:T(8,128)(2,1)} %get-tuple-element.25.message_ref), calls=%async_computation.1 | async-start | bytes 1048576 | tf_op jit(solution)/shard_map/all_to_all | solution.py:45
  51.7 0.1 pad.6.clone
  51.8 0.3 slice_select_fusion
  52.1 0.2 pad_maximum_fusion.in_w_ref
  52.3 9.9 %all-to-all-done.1.got_ref = bf16[16,16,1024]{2,1,0:T(8,128)(2,1)S(1)} async-done(((bf16[16,16,1024]{2,1,0:T(8,128)(2,1)}), bf16[16,16,1024]{2,1,0:T(8,128)(2,1)S(1)}, u32[]{:S(2)}, u32[]{:S(2)}) %all-to-all-start.1) | async-done | bytes 524320 | tf_op jit(solution)/shard_map/all_to_all | solution.py:45
  62.3 0.5 coarse_project.1
  62.8 15.0 %all_to_all.30 = bf16[4,128,256]{2,1,0:T(8,128)(2,1)S(1)} all-to-all(bf16[4,128,256]{2,1,0:T(8,128)(2,1)S(1)} %get-tuple-element.26), channel_id=1, replica_groups=mesh['y'=4,'z_hi'=4,'core'=2,'z_lo'=2,'x'=4] {'z_hi'}, dimensions={0} | all-to-all | bytes 524288 | tf_op jit(solution)/shard_map/all_to_all | solution.py:45
  77.8 1.1 repeated.1
  78.9 4.5 %all-to-all-start.3 = ((bf16[4,512,256]{2,1,0:T(8,128)(2,1)}), bf16[4,512,256]{2,1,0:T(8,128)(2,1)S(1)}, u32[]{:S(2)}, u32[]{:S(2)}) async-start(bf16[4,512,256]{2,1,0:T(8,128)(2,1)} %repeated.1), calls=%async_computation.3 | async-start | bytes 2097152 | tf_op jit(solution)/shard_map/all_to_all | solution.py:45
  83.4 14.8 %all-to-all-done.3 = bf16[4,512,256]{2,1,0:T(8,128)(2,1)S(1)} async-done(((bf16[4,512,256]{2,1,0:T(8,128)(2,1)}), bf16[4,512,256]{2,1,0:T(8,128)(2,1)S(1)}, u32[]{:S(2)}, u32[]{:S(2)}) %all-to-all-start.3) | async-done | bytes 1048608 | tf_op jit(solution)/shard_map/all_to_all | solution.py:45
  98.2 8.0 %coarse_attention.1 = bf16[16,16,1024]{2,1,0:T(8,128)(2,1)S(1)} custom-call(s32[1]{0:T(128)} %bitcast.3.start_ref, bf16[2048,256]{1,0:T(8,128)(2,1)S(1)} %bitcast.18, f32[128,256]{1,0:T(8,128)S(1)} %get-tuple-element.27.factor_ref, bf16[1024,256]{1,0:T(8,128)(2,1)S(1)} %pad_maximum_fusion.in_w_ref, bf16[256,1024]{1,0:T(8,128)(2,1)S(1)} %pad.4.out_w_ref), custom_call_target="tpu_custom_call" | custom-call | flops 1500000000 | bytes 3000000 | tf_op jit(solution)/shard_map/coarse_attention/pallas_call | solution.py:468
  106.2 13.3 %all_to_all.31.got_ref = bf16[16,16,1024]{2,1,0:T(8,128)(2,1)S(1)} all-to-all(bf16[16,16,1024]{2,1,0:T(8,128)(2,1)S(1)} %coarse_attention.1), channel_id=1, replica_groups=mesh['y'=4,'z_hi'=4,'core'=2,'z_lo'=2,'x'=4] {'core','z_lo','x'}, dimensions={0} | all-to-all | bytes 1048576 | tf_op jit(solution)/shard_map/all_to_all | solution.py:45
  119.5 0.9 coarse_finish.1
  120.4 1.9 %collective-permute-start.2 = (f32[1,1024]{1,0:T(1,128)S(1)}, f32[1,1024]{1,0:T(1,128)S(1)}, u32[]{:S(2)}, u32[]{:S(2)}) collective-permute-start(f32[1,1024]{1,0:T(1,128)S(1)} %get-tuple-element.31), channel_id=1, source_target_pairs={{1,0},{2,1},{3,2},{4,3},{5,4},{6,5},{7,6},{8,7},{9,8},{10,9},{11,1... | collective-permute-start | bytes 12296 | tf_op jit(solution)/shard_map/ppermute | solution.py:41
  122.4 3.6 %collective-permute-done.2.next_ref = f32[1,1024]{1,0:T(1,128)S(1)} collective-permute-done((f32[1,1024]{1,0:T(1,128)S(1)}, f32[1,1024]{1,0:T(1,128)S(1)}, u32[]{:S(2)}, u32[]{:S(2)}) %collective-permute-start.2) | collective-permute-done | bytes 4128 | tf_op jit(solution)/shard_map/ppermute | solution.py:41
  125.9 12.8 %fine_backward.1 = (bf16[4,128,1024]{2,1,0:T(8,128)(2,1)S(1)}, f32[128,1024]{1,0:T(8,128)S(1)}, f32[128,1024]{1,0:T(8,128)S(1)}) custom-call(bf16[128,1024]{1,0:T(8,128)(2,1)} %cot_ref.3, f32[8,1024]{1,0:T(8,128)S(1)} %get-tuple-element.30.spread_ref, f32[1,1024]{1,0:T(1,128)S(1)} %collective-permute-done.2.next_ref, bf16[1024,1024]{1,0:T(8,128)(2,1)} %out_w_ref.3, ...), custom_call_target="tpu_custom_call" | custom-call | flops 5000000000 | bytes 20000000 | tf_op jit(solution)/shard_map/fine_backward/pallas_call | solution.py:497
  138.8 17.7 %all_to_all.32.got_ref = bf16[4,128,1024]{2,1,0:T(8,128)(2,1)S(1)} all-to-all(bf16[4,128,1024]{2,1,0:T(8,128)(2,1)S(1)} %get-tuple-element.40), channel_id=1, replica_groups=mesh['y'=4,'z_hi'=4,'core'=2,'z_lo'=2,'x'=4] {'x'}, dimensions={0} | all-to-all | bytes 2097152 | tf_op jit(solution)/shard_map/all_to_all | solution.py:45
  156.6 0.7 halo_sum.1
  157.3 1.9 %collective-permute-start.3 = (bf16[128,1024]{1,0:T(8,128)(2,1)S(1)}, bf16[128,1024]{1,0:T(8,128)(2,1)S(1)}, u32[]{:S(2)}, u32[]{:S(2)}) collective-permute-start(bf16[128,1024]{1,0:T(8,128)(2,1)S(1)} %halo_sum.1), channel_id=1, source_target_pairs={{4,0},{5,1},{6,2},{7,3},{8,4},{9,5},{10,6},{11,7},{12,8},{13,9},{1... | collective-permute-start | bytes 786440 | tf_op jit(solution)/shard_map/ppermute | solution.py:41
  159.2 0.8 fusion
  160.0 8.3 %collective-permute-done.3.arrived_ref = bf16[128,1024]{1,0:T(8,128)(2,1)S(1)} collective-permute-done((bf16[128,1024]{1,0:T(8,128)(2,1)S(1)}, bf16[128,1024]{1,0:T(8,128)(2,1)S(1)}, u32[]{:S(2)}, u32[]{:S(2)}) %collective-permute-start.3) | collective-permute-done | bytes 262176 | tf_op jit(solution)/shard_map/ppermute | solution.py:41
  168.3 1.7 fine_finish.1
  (15 shorter events, 0.1 us)
Async XLA Ops:
  0.6 12.9 %collective-permute-start.1 = (bf16[128,1024]{1,0:T(8,128)(2,1)}, bf16[128,1024]{1,0:T(8,128)(2,1)S(1)}, u32[]{:S(2)}, u32[]{:S(2)}) collective-permute-start(bf16[128,1024]{1,0:T(8,128)(2,1)} %tokens_ref.1), channel_id=1, source_target_pairs={{0,4},{1,5},{2,6},{3,7},{4,8},{5,9},{6,10},{7,11},{8,12},{9,13},{1... | collective-permute-start | bytes 786440 | tf_op jit(solution)/shard_map/ppermute | solution.py:41
  5.2 8.2 %collective-permute-start = (bf16[16,1024]{1,0:T(8,128)(2,1)S(1)}, bf16[16,1024]{1,0:T(8,128)(2,1)S(1)}, u32[]{:S(2)}, u32[]{:S(2)}) collective-permute-start(bf16[16,1024]{1,0:T(8,128)(2,1)S(1)} %slice.24), channel_id=1, source_target_pairs={{0,5},{1,6},{2,7},{3,8},{4,9},{5,10},{6,11},{7,12},{8,13},{9,14},{... | collective-permute-start | bytes 98312 | tf_op jit(solution)/shard_map/ppermute | solution.py:41
  13.5 1.0 copy-start
  16.0 17.8 %all-to-all-start = ((bf16[4,128,1024]{2,1,0:T(8,128)(2,1)}), bf16[4,128,1024]{2,1,0:T(8,128)(2,1)S(1)}, u32[]{:S(2)}, u32[]{:S(2)}) async-start(bf16[4,128,1024]{2,1,0:T(8,128)(2,1)} %halo_send.1), calls=%async_computation | async-start | bytes 2097152 | tf_op jit(solution)/shard_map/all_to_all | solution.py:45
  33.8 17.7 %copy-start.3 = (bf16[128,1024]{1,0:T(8,128)(2,1)S(1)}, bf16[128,1024]{1,0:T(8,128)(2,1)}, u32[]{:S(2)}) copy-start(bf16[128,1024]{1,0:T(8,128)(2,1)} %param.11) | copy-start | bytes 786436
  47.0 4.8 %copy-start.2 = (bf16[1024,3,128]{2,0,1:T(8,128)(2,1)S(1)}, bf16[1024,3,128]{2,0,1:T(8,128)(2,1)}, u32[]{:S(2)}) copy-start(bf16[1024,3,128]{2,0,1:T(8,128)(2,1)} %param.10) | copy-start | bytes 2359300
  47.0 15.3 %all-to-all-start.1 = ((bf16[16,16,1024]{2,1,0:T(8,128)(2,1)}), bf16[16,16,1024]{2,1,0:T(8,128)(2,1)S(1)}, u32[]{:S(2)}, u32[]{:S(2)}) async-start(bf16[16,16,1024]{2,1,0:T(8,128)(2,1)} %get-tuple-element.25.message_ref), calls=%async_computation.1 | async-start | bytes 1048576 | tf_op jit(solution)/shard_map/all_to_all | solution.py:45
  78.9 19.3 %all-to-all-start.3 = ((bf16[4,512,256]{2,1,0:T(8,128)(2,1)}), bf16[4,512,256]{2,1,0:T(8,128)(2,1)S(1)}, u32[]{:S(2)}, u32[]{:S(2)}) async-start(bf16[4,512,256]{2,1,0:T(8,128)(2,1)} %repeated.1), calls=%async_computation.3 | async-start | bytes 2097152 | tf_op jit(solution)/shard_map/all_to_all | solution.py:45
  120.4 5.5 %collective-permute-start.2 = (f32[1,1024]{1,0:T(1,128)S(1)}, f32[1,1024]{1,0:T(1,128)S(1)}, u32[]{:S(2)}, u32[]{:S(2)}) collective-permute-start(f32[1,1024]{1,0:T(1,128)S(1)} %get-tuple-element.31), channel_id=1, source_target_pairs={{1,0},{2,1},{3,2},{4,3},{5,4},{6,5},{7,6},{8,7},{9,8},{10,9},{11,1... | collective-permute-start | bytes 12296 | tf_op jit(solution)/shard_map/ppermute | solution.py:41
  138.8 20.4 %copy-start.4 = (bf16[128,1024]{1,0:T(8,128)(2,1)S(1)}, bf16[128,1024]{1,0:T(8,128)(2,1)}, u32[]{:S(2)}) copy-start(bf16[128,1024]{1,0:T(8,128)(2,1)} %get-tuple-element.24) | copy-start | bytes 786436
  138.8 29.5 %copy-start.1 = (bf16[128,1024]{1,0:T(8,128)(2,1)S(1)}, bf16[128,1024]{1,0:T(8,128)(2,1)}, u32[]{:S(2)}) copy-start(bf16[128,1024]{1,0:T(8,128)(2,1)} %tokens_ref.1) | copy-start | bytes 786436
  157.3 11.0 %collective-permute-start.3 = (bf16[128,1024]{1,0:T(8,128)(2,1)S(1)}, bf16[128,1024]{1,0:T(8,128)(2,1)S(1)}, u32[]{:S(2)}, u32[]{:S(2)}) collective-permute-start(bf16[128,1024]{1,0:T(8,128)(2,1)S(1)} %halo_sum.1), channel_id=1, source_target_pairs={{4,0},{5,1},{6,2},{7,3},{8,4},{9,5},{10,6},{11,7},{12,8},{13,9},{1... | collective-permute-start | bytes 786440 | tf_op jit(solution)/shard_map/ppermute | solution.py:41

commit v5 on v4

v5 whole, which is shorter than its diff:
```python
import jax
import jax.numpy as jnp
from jax import lax
from jax.experimental import pallas as pl
from jax.experimental.pallas import tpu as pltpu
from jax.sharding import Mesh
from jax.sharding import PartitionSpec as P

D = 1024
HEADS = 16
HEAD_DIM = 64
WINDOW = 512
POOL = 16
EPS = 1e-06

LINE = ("y", "z_hi", "core", "z_lo", "x")
GROUP = ("core", "z_lo", "x")
FAR = ("y", "z_hi")

ROWS = 128
HALO = WINDOW
OWN_KEYS = HALO + ROWS
EXTRA = 16
ALL_KEYS = OWN_KEYS + EXTRA
QUERIES = EXTRA + ROWS
PAIR = 2 * HEAD_DIM
COARSE = ROWS // POOL
SCALE = HEAD_DIM ** (-0.5)
NEG = -1e30
VMEM_MIB = 16

BF = jnp.bfloat16
F32 = jnp.float32


def shifted_by(value, steps):
    count = 1
    for name in LINE:
        count *= lax.axis_size(name)
    first, last = (max(0, -steps), min(count, count - steps))
    return lax.ppermute(value, LINE, [(source, source + steps) for source in range(first, last)])


def exchanged(pieces, axes):
    return lax.all_to_all(pieces, axes, 0, 0, tiled=True)


def last_last(left, right):
    return lax.dot_general(left, right, (((1,), (1,)), ((), ())), preferred_element_type=F32)


def first_first(left, right):
    return lax.dot_general(left, right, (((0,), (0,)), ((), ())), preferred_element_type=F32)


def plain(left, right):
    return jnp.dot(left, right, preferred_element_type=F32)


def low_lanes():
    return lax.broadcasted_iota(jnp.int32, (1, PAIR), 1) < HEAD_DIM


def pair_sums(values, low):
    low_sum = jnp.sum(jnp.where(low, values, 0.0), axis=-1, keepdims=True)
    high_sum = jnp.sum(jnp.where(low, 0.0, values), axis=-1, keepdims=True)
    return jnp.where(low, low_sum, high_sum)


def pair_norm(values, low):
    factor = lax.rsqrt(pair_sums(values * values, low) * (1.0 / HEAD_DIM) + EPS)
    return values * factor, factor


def pair_norm_back(grad, unit, factor, low):
    return factor * (grad - unit * (pair_sums(unit * grad, low) * (1.0 / HEAD_DIM)))


def row_norm(rows):
    factor = lax.rsqrt(jnp.mean(rows * rows, axis=-1, keepdims=True) + EPS)
    return rows * factor, factor


def row_norm_back(grad, normed, factor):
    return factor * (grad - normed * jnp.mean(normed * grad, axis=-1, keepdims=True))


def fine_prepare_kernel(
    place_ref, own_hbm, cot_hbm, w_hbm, out_w_hbm,
    own_ref, w_ref, out_w_ref, q_ref, k_ref, v_ref, qf_ref, kf_ref, bias_ref, cg_ref,
    cot, copied,
):
    anchor = place_ref[0]
    column_at = place_ref[1]
    low = low_lanes()
    copies = [
        pltpu.make_async_copy(source, target, copied.at[at])
        for at, (source, target) in enumerate(
            ((own_hbm, own_ref), (cot_hbm, cot), (w_hbm, w_ref), (out_w_hbm, out_w_ref))
        )
    ]
    for copy in copies:
        copy.start()

    row = lax.broadcasted_iota(jnp.int32, (2 * QUERIES, ALL_KEYS), 0)
    query_pos = jnp.where(row < QUERIES, row, row - QUERIES) - EXTRA
    column = lax.broadcasted_iota(jnp.int32, (2 * QUERIES, ALL_KEYS), 1)
    turned = column_at * ROWS
    halo_pos = column - jnp.where(column >= turned, turned + HALO, turned)
    key_pos = jnp.where(
        column < HALO,
        halo_pos,
        jnp.where(column < OWN_KEYS, column - HALO, column - (OWN_KEYS + HALO + EXTRA)),
    )
    gap = query_pos - key_pos
    allowed = (gap >= 0) & (gap < WINDOW) & (anchor + key_pos >= 0)
    bias_ref[...] = jnp.where(allowed, 0.0, NEG)

    copies[0].wait()
    normed = row_norm(own_ref[...].astype(F32))[0].astype(BF)
    copies[1].wait()
    chunk = lax.broadcasted_iota(jnp.int32, (COARSE, ROWS), 0) * POOL
    row = lax.broadcasted_iota(jnp.int32, (COARSE, ROWS), 1)
    member = jnp.where((row >= chunk) & (row < chunk + POOL), 1.0, 0.0).astype(BF)
    cg_ref[...] = plain(member, cot[...])
    copies[2].wait()
    for at in range(0, D, WIDTH):
        here = slice(at, at + WIDTH)
        queries = plain(normed, w_ref[0, :, here])
        keys = plain(normed, w_ref[1, :, here])
        v_ref[:, here] = plain(normed, w_ref[2, :, here]).astype(BF)
        for part in range(0, WIDTH, PAIR):
            inner = slice(part, part + PAIR)
            outer = slice(at + part, at + part + PAIR)
            query, q_factor = pair_norm(queries[:, inner], low)
            key, k_factor = pair_norm(keys[:, inner], low)
            q_ref[:, outer] = query.astype(BF)
            k_ref[:, outer] = key.astype(BF)
            qf_ref[:, outer] = q_factor
            kf_ref[:, outer] = k_factor
    copies[3].wait()


def fine_forward_kernel(
    place_ref, tail_ref, slots_ref, own_ref, w_ref, out_w_ref, own_q_ref, own_k_ref, own_v_ref,
    own_kf_ref, bias, cg_ref,
    k_ref, v_ref, kf_ref, p_ref, att_ref, hid_ref, send_ref,
    normed, acc,
):
    anchor = place_ref[0]
    column_at = place_ref[1]
    low = low_lanes()
    slots = slots_ref.shape[0]
    nearest = lax.rem(column_at + (slots - 1), slots)
    for slot in range(slots):
        at = slot * ROWS
        normed[at : at + ROWS, :] = row_norm(slots_ref[slot].astype(F32))[0].astype(BF)
    normed[HALO:, :] = row_norm(tail_ref[...].astype(F32))[0].astype(BF)
    acc[...] = jnp.zeros_like(acc)
    extra_at = pl.multiple_of(nearest * ROWS + (ROWS - EXTRA), EXTRA)

    def one_step(step, carry):
        first = pl.multiple_of(step * WIDTH, WIDTH)
        here = pl.ds(first, WIDTH)
        extra = plain(normed[pl.ds(extra_at, EXTRA), :], w_ref[0, :, here])
        both = plain(
            normed[...], jnp.concatenate([w_ref[1, :, here], w_ref[2, :, here]], axis=1)
        )
        own_q, own_k, own_v = own_q_ref[:, here], own_k_ref[:, here], own_v_ref[:, here]
        own_kf = own_kf_ref[:, here]
        mixed = []
        for part in range(0, WIDTH, PAIR):
            inner = slice(part, part + PAIR)
            outer = pl.ds(pl.multiple_of(first + part, PAIR), PAIR)
            key, k_factor = pair_norm(both[:, inner], low)
            key = key.astype(BF)
            value = both[:, WIDTH + part : WIDTH + part + PAIR].astype(BF)
            k_ref[:HALO, outer] = key[:HALO]
            k_ref[HALO:, outer] = own_k[:, inner]
            v_ref[:HALO, outer] = value[:HALO]
            v_ref[HALO:, outer] = own_v[:, inner]
            kf_ref[:HALO, outer] = k_factor[:HALO]
            kf_ref[HALO:, outer] = own_kf[:, inner]
            key = jnp.concatenate([key[:HALO], own_k[:, inner], key[HALO:]], axis=0)
            value = jnp.concatenate([value[:HALO], own_v[:, inner], value[HALO:]], axis=0)
            before = pair_norm(extra[:, inner], low)[0].astype(BF).astype(F32)
            scaled = jnp.concatenate([before, own_q[:, inner].astype(F32)], axis=0) * SCALE
            stacked = jnp.concatenate(
                [jnp.where(low, scaled, 0.0), jnp.where(low, 0.0, scaled)], axis=0
            )
            numer = jnp.exp(last_last(stacked.astype(BF), key) + bias[...])
            total = jnp.sum(numer, axis=-1, keepdims=True)
            prob = (numer * (1.0 / jnp.where(total > 0.0, total, 1.0))).astype(BF)
            head = (first + part) // HEAD_DIM
            p_ref[head] = prob[EXTRA:QUERIES, :OWN_KEYS]
            p_ref[head + 1] = prob[QUERIES + EXTRA :, :OWN_KEYS]
            twice = plain(prob, value)
            attended = jnp.where(low, twice[:QUERIES], twice[QUERIES:]).astype(BF)
            att_ref[:, outer] = attended[EXTRA:]
            mixed.append(attended)
        acc[...] += plain(jnp.concatenate(mixed, axis=1), out_w_ref[here, :])
        return carry

    lax.fori_loop(0, D // WIDTH, one_step, 0)
    before = slots_ref[nearest, ROWS - EXTRA :, :].astype(F32) + acc[:EXTRA, :]
    before = jnp.where(anchor > 0, before, 0.0).astype(BF)
    own = (own_ref[...].astype(F32) + acc[EXTRA:, :]).astype(BF)
    hid_ref[...] = own
    chunk = lax.broadcasted_iota(jnp.int32, (COARSE, QUERIES), 0) * POOL
    row = lax.broadcasted_iota(jnp.int32, (COARSE, QUERIES), 1)
    member = jnp.where((row > chunk) & (row <= chunk + POOL), 1.0, 0.0).astype(BF)
    pooled = plain(member, jnp.concatenate([before, own], axis=0)) * (1.0 / POOL)
    message = jnp.concatenate([pooled, cg_ref[...]], axis=0).astype(BF)
    for peer in range(send_ref.shape[0]):
        send_ref[peer] = message


def coarse_prepare_kernel(core_ref, w_ref, back_ref, in_ref, out_ref):
    low = low_lanes()
    second = core_ref[0] > 0
    parts = [w_ref[at].astype(F32) for at in range(3)]
    turned = [pltpu.roll(part, HEAD_DIM, 1) for part in parts]
    query = jnp.where(second, turned[0], parts[0])
    key = jnp.where(second, turned[1], parts[1])
    value = jnp.where(second, parts[2], turned[2])
    in_ref[:, :PAIR] = jnp.where(low, query, 0.0).astype(BF)
    in_ref[:, PAIR:] = jnp.where(low, key, value).astype(BF)
    out_ref[...] = jnp.zeros_like(out_ref)
    out_ref[HEAD_DIM:PAIR, :] = jnp.where(second, back_ref[HEAD_DIM:, :], back_ref[:HEAD_DIM, :])


def coarse_project_kernel(got_ref, in_w_ref, out_w_ref, send_ref, factor_ref):
    low = low_lanes()
    rows = got_ref[...].astype(F32)
    count = rows.shape[0] * COARSE
    pooled = rows[:, :COARSE, :].reshape(count, D)
    coarse_grad = rows[:, COARSE:, :].reshape(count, D)
    normed = row_norm(pooled)[0].astype(BF)
    raw = plain(normed, in_w_ref[...]) + last_last(coarse_grad.astype(BF), out_w_ref[...])
    units, factors = [], []
    for tile in (raw[:, :PAIR], raw[:, PAIR:]):
        unit, factor = pair_norm(tile, low)
        units.append(jnp.where(low, unit, tile))
        factors.append(factor)
    message = jnp.concatenate(units, axis=1).astype(BF)
    factor_ref[...] = jnp.concatenate(factors, axis=1)
    for peer in range(send_ref.shape[0]):
        send_ref[peer] = message


def coarse_attention_kernel(place_ref, got_ref, factor_ref, in_w_ref, out_w_ref, send_ref, own_grad):
    low = low_lanes()
    own_start = pl.multiple_of(place_ref[2], ROWS)
    length = got_ref.shape[0]
    block = 512
    own_left = got_ref[pl.ds(own_start, ROWS), :PAIR]
    own_right = got_ref[pl.ds(own_start, ROWS), PAIR:]
    own_grad[...] = jnp.zeros_like(own_grad)

    def masked_halves(tile):
        wide = tile.astype(F32)
        return (
            jnp.where(low, wide * SCALE, 0.0).astype(BF),
            jnp.where(low, 0.0, wide).astype(BF),
        )

    def lane_partials(values):
        total = values[:, :PAIR]
        for at in range(PAIR, values.shape[1], PAIR):
            total = total + values[:, at : at + PAIR]
        return total

    def one_block(index, carry):
        first = pl.multiple_of(index * block, block)
        query, grad = masked_halves(got_ref[pl.ds(first, block), :PAIR])
        stacked = jnp.concatenate([query, grad], axis=0)

        def scored(keys):
            both = last_last(stacked, keys)
            return jnp.exp(both[:block]), both[block:]

        def one_chunk(at, sums):
            total, product = sums
            numer, prob_grad = scored(got_ref[pl.ds(pl.multiple_of(at * block, block), block), PAIR:])
            return total + lane_partials(numer), product + lane_partials(numer * prob_grad)

        nothing = jnp.zeros((block, PAIR), F32)
        total, product = lax.fori_loop(0, index, one_chunk, (nothing, nothing))
        numer, prob_grad = scored(got_ref[pl.ds(first, block), PAIR:])
        query_at = lax.broadcasted_iota(jnp.int32, (block, 1), 0)
        numer = jnp.where(lax.broadcasted_iota(jnp.int32, (1, block), 1) <= query_at, numer, 0.0)
        total = jnp.sum(total + lane_partials(numer), axis=-1, keepdims=True)
        product = jnp.sum(product + lane_partials(numer * prob_grad), axis=-1, keepdims=True)
        inverse = 1.0 / total
        delta = product * inverse
        own_pos = own_start + lax.broadcasted_iota(jnp.int32, (1, ROWS), 1)
        numer, prob_grad = scored(own_right)
        numer = jnp.where(own_pos <= query_at + first, numer, 0.0)
        prob = numer * inverse
        score_grad = (prob * (prob_grad - delta)).astype(BF)
        own_grad[...] += first_first(
            jnp.concatenate([score_grad, prob.astype(BF)], axis=0), stacked
        )
        return carry

    lax.fori_loop(own_start // block, length // block, one_block, 0)

    query, grad = masked_halves(own_left)
    query_pos = own_start + lax.broadcasted_iota(jnp.int32, (ROWS, 1), 0)
    key_pos = lax.broadcasted_iota(jnp.int32, (1, length), 1)
    keys = got_ref[:, PAIR:]
    key_scaled, value = masked_halves(keys)
    numer = jnp.where(key_pos <= query_pos, jnp.exp(last_last(query, keys)), 0.0)
    prob_grad = last_last(grad, keys)
    inverse = 1.0 / jnp.sum(numer, axis=-1, keepdims=True)
    delta = jnp.sum(numer * prob_grad, axis=-1, keepdims=True) * inverse
    prob = numer * inverse
    score_grad = (prob * (prob_grad - delta)).astype(BF)
    mine = plain(score_grad, key_scaled) + plain(prob.astype(BF), value)

    parts = []
    for tile, unit, factor in (
        (mine, own_left, factor_ref[:, :PAIR]),
        (own_grad[...], own_right, factor_ref[:, PAIR:]),
    ):
        back = pair_norm_back(tile, unit.astype(F32), factor, low)
        parts.append(jnp.where(low, back, tile))
    parts = jnp.concatenate(parts, axis=1).astype(BF)
    peers = send_ref.shape[0]
    normed_grad = last_last(parts, in_w_ref[...]).reshape(peers, COARSE, D)
    mixed = plain(parts, out_w_ref[...]).reshape(peers, COARSE, D)
    send_ref[...] = jnp.concatenate([normed_grad, mixed], axis=1).astype(BF)


def coarse_finish_kernel(got_ref, message_ref, cg_ref, spread_ref, first_ref, state_ref):
    summed = jnp.sum(got_ref[...].astype(F32), axis=0)
    pooled = message_ref[0].astype(F32)[:COARSE]
    normed, factor = row_norm(pooled)
    pooled_grad = cg_ref[...] + row_norm_back(summed[:COARSE], normed, factor)
    spread = pooled_grad * (1.0 / POOL)
    spread_ref[...] = spread
    first_ref[...] = spread[:1]
    state_ref[...] = pooled + summed[COARSE:]


def fine_backward_kernel(
    cot_ref, spread_ref, next_ref, out_w_ref, w_ref, q_ref, k_ref, v_ref, qf_ref, kf_ref, p_ref,
    att_ref,
    halo_ref, own_ref, hg_ref, hidden_grad, acc,
):
    low = low_lanes()
    block = (lax.broadcasted_iota(jnp.int32, (ROWS, 1), 0) + (POOL - 1)) // POOL
    added = jnp.zeros((ROWS, D), F32)
    for at in range(COARSE):
        added = jnp.where(block == at, spread_ref[at : at + 1, :], added)
    added = jnp.where(block == COARSE, next_ref[0:1, :], added)
    total = cot_ref[...].astype(F32) + added
    hg_ref[...] = total
    hidden_grad[...] = total.astype(BF)
    acc[...] = jnp.zeros_like(acc)

    def one_step(step, carry):
        first = pl.multiple_of(step * WIDTH, WIDTH)
        here = pl.ds(first, WIDTH)
        att_grads = last_last(hidden_grad[...], out_w_ref[here, :]).astype(BF).astype(F32)
        query_grads, key_grads, value_grads = [], [], []
        for part in range(0, WIDTH, PAIR):
            outer = pl.ds(pl.multiple_of(first + part, PAIR), PAIR)
            att_grad = att_grads[:, part : part + PAIR]
            delta_all = att_grad * att_ref[:, outer].astype(F32)
            value = v_ref[:, outer]
            key_wide = k_ref[:, outer].astype(F32)
            query_wide = q_ref[:, outer].astype(F32)
            grad = jnp.concatenate(
                [jnp.where(low, att_grad, 0.0), jnp.where(low, 0.0, att_grad)], axis=0
            ).astype(BF)
            delta = jnp.sum(
                jnp.concatenate(
                    [jnp.where(low, delta_all, 0.0), jnp.where(low, 0.0, delta_all)], axis=0
                ),
                axis=-1,
                keepdims=True,
            )
            scaled = query_wide * SCALE
            query = jnp.concatenate(
                [jnp.where(low, scaled, 0.0), jnp.where(low, 0.0, scaled)], axis=0
            ).astype(BF)
            head = (first + part) // HEAD_DIM
            prob = p_ref[pl.ds(head, 2)].reshape(2 * ROWS, OWN_KEYS)
            score_grad = (prob.astype(F32) * (last_last(grad, value) - delta)).astype(BF)
            twice = plain(score_grad, (key_wide * SCALE).astype(BF))
            query_grad = jnp.where(low, twice[:ROWS], twice[ROWS:])
            key_grad = first_first(score_grad, query)
            value_grad = first_first(prob, grad)
            query_grads.append(pair_norm_back(query_grad, query_wide, qf_ref[:, outer], low).astype(BF))
            key_grads.append(pair_norm_back(key_grad, key_wide, kf_ref[:, outer], low).astype(BF))
            value_grads.append(value_grad.astype(BF))
        both = jnp.concatenate(key_grads + value_grads, axis=1)
        acc[...] += last_last(
            both, jnp.concatenate([w_ref[1, :, here], w_ref[2, :, here]], axis=1)
        )
        acc[HALO:, :] += last_last(jnp.concatenate(query_grads, axis=1), w_ref[0, :, here])
        return carry

    lax.fori_loop(0, D // WIDTH, one_step, 0)
    for slot in range(halo_ref.shape[0]):
        halo_ref[slot] = acc[slot * ROWS : (slot + 1) * ROWS, :].astype(BF)
    own_ref[...] = acc[HALO:, :]


def halo_send_kernel(place_ref, own_ref, before_ref, send_ref):
    send_ref[0] = jnp.where(place_ref[1] < pl.program_id(0), own_ref[...], before_ref[...])


def repeated_kernel(block_ref, send_ref):
    for peer in range(send_ref.shape[0]):
        send_ref[peer] = block_ref[...]


def halo_sum_kernel(place_ref, got_ref, back_ref):
    column_at = place_ref[1]
    total = got_ref[0].astype(F32)
    for slot in range(1, got_ref.shape[0]):
        total = total + jnp.where(column_at >= slot, got_ref[slot].astype(F32), 0.0)
    back_ref[...] = total.astype(BF)


def fine_finish_kernel(place_ref, own_ref, got_ref, arrived_ref, hg_ref, tokens_ref, out_ref):
    column_at = place_ref[1]
    total = own_ref[...] + arrived_ref[...].astype(F32)
    for slot in range(1, got_ref.shape[0]):
        total = total + jnp.where(column_at < slot, got_ref[slot].astype(F32), 0.0)
    normed, factor = row_norm(tokens_ref[...].astype(F32))
    out_ref[...] = (hg_ref[...] + row_norm_back(total, normed, factor)).astype(BF)


def whole(shape):
    return pl.BlockSpec(shape, lambda *_: (0,) * len(shape))


def columns(rows, width):
    return pl.BlockSpec((rows, width), lambda p: (0, p))


def shaped(shape, kind):
    return jax.ShapeDtypeStruct(shape, kind)


def params(mib):
    return pltpu.CompilerParams(vmem_limit_bytes=mib << 20)


def cost(flops, moved, exps=0):
    return pl.CostEstimate(flops=flops, bytes_accessed=moved, transcendentals=exps)


SCALAR = pl.BlockSpec(memory_space=pltpu.SMEM)
IN_VMEM = pl.BlockSpec(memory_space=pltpu.VMEM)
WIDTH = 2 * PAIR


def in_hbm(x):
    return pltpu.with_memory_space_constraint(x, pltpu.HBM)


def fine_prepare(place, tokens, cotangent, weights, fine_out):
    anywhere = pl.BlockSpec(memory_space=pltpu.HBM)
    return pl.pallas_call(
        fine_prepare_kernel,
        in_specs=[SCALAR] + [anywhere] * 4,
        out_specs=[IN_VMEM] * 10,
        out_shape=[
            pltpu.VMEM((ROWS, D), BF),
            pltpu.VMEM((3, D, D), BF),
            pltpu.VMEM((D, D), BF),
            pltpu.VMEM((ROWS, D), BF),
            pltpu.VMEM((ROWS, D), BF),
            pltpu.VMEM((ROWS, D), BF),
            pltpu.VMEM((ROWS, D), F32),
            pltpu.VMEM((ROWS, D), F32),
            pltpu.VMEM((2 * QUERIES, ALL_KEYS), F32),
            pltpu.VMEM((COARSE, D), F32),
        ],
        scratch_shapes=[pltpu.VMEM((ROWS, D), BF), pltpu.SemaphoreType.DMA((4,))],
        compiler_params=params(16),
        cost_estimate=cost(900_000_000, 17_000_000),
        name="fine_prepare",
    )(place, *(in_hbm(x) for x in (tokens, cotangent, weights, fine_out)))


def fine_forward(place, tail, slots, own, weights, fine_out, own_q, own_k, own_v, own_kf, bias, cg, peers):
    return pl.pallas_call(
        fine_forward_kernel,
        in_specs=[SCALAR] + [IN_VMEM] * 11,
        out_specs=[IN_VMEM] * 7,
        out_shape=[
            pltpu.VMEM((OWN_KEYS, D), BF),
            pltpu.VMEM((OWN_KEYS, D), BF),
            pltpu.VMEM((OWN_KEYS, D), F32),
            pltpu.VMEM((HEADS, ROWS, OWN_KEYS), BF),
            pltpu.VMEM((ROWS, D), BF),
            shaped((ROWS, D), BF),
            shaped((peers, 2 * COARSE, D), BF),
        ],
        scratch_shapes=[pltpu.VMEM((HALO + EXTRA, D), BF), pltpu.VMEM((QUERIES, D), F32)],
        compiler_params=params(16),
        cost_estimate=cost(4_500_000_000, 20_000_000, 1_600_000),
        name="fine_forward",
    )(place, tail, slots, own, weights, fine_out, own_q, own_k, own_v, own_kf, bias, cg)


def coarse_prepare(core, weights, back):
    return pl.pallas_call(
        coarse_prepare_kernel,
        in_specs=[SCALAR, IN_VMEM, IN_VMEM],
        out_specs=[IN_VMEM] * 2,
        out_shape=[shaped((D, 2 * PAIR), BF), shaped((2 * PAIR, D), BF)],
        compiler_params=params(8),
        cost_estimate=cost(1_000_000, 2_500_000),
        name="coarse_prepare",
    )(core, weights, back)


def coarse_project(gathered, coarse_in, coarse_back, groups):
    rows = gathered.shape[0] * COARSE
    return pl.pallas_call(
        coarse_project_kernel,
        out_shape=[shaped((groups, rows, 2 * PAIR), BF), shaped((rows, 2 * PAIR), F32)],
        compiler_params=params(VMEM_MIB),
        cost_estimate=cost(140_000_000, 3_000_000),
        name="coarse_project",
    )(gathered, coarse_in, coarse_back)


def coarse_attention(place, everyone, factor, coarse_in, coarse_back):
    rows = factor.shape[0]
    return pl.pallas_call(
        coarse_attention_kernel,
        in_specs=[SCALAR] + [IN_VMEM] * 4,
        out_shape=shaped((rows // COARSE, 2 * COARSE, D), BF),
        scratch_shapes=[pltpu.VMEM((rows, PAIR), F32)],
        compiler_params=params(VMEM_MIB),
        cost_estimate=cost(1_500_000_000, 3_000_000, 3_000_000),
        name="coarse_attention",
    )(place, everyone, factor, coarse_in, coarse_back)


def coarse_finish(returned, message, coarse_grad):
    return pl.pallas_call(
        coarse_finish_kernel,
        grid=(1,),
        in_specs=[whole(returned.shape), whole((1, 2 * COARSE, D)), whole((COARSE, D))],
        out_specs=[whole((COARSE, D)), whole((1, D)), whole((COARSE, D))],
        out_shape=[shaped((COARSE, D), F32), shaped((1, D), F32), shaped((COARSE, D), F32)],
        compiler_params=params(VMEM_MIB),
        cost_estimate=cost(1_000_000, 1_000_000),
        name="coarse_finish",
    )(returned, message, coarse_grad)


def fine_backward(
    cotangent, spread, after, fine_out, weights, query, key, value, q_factor, k_factor, probs,
    attended,
):
    return pl.pallas_call(
        fine_backward_kernel,
        in_specs=[IN_VMEM] * 12,
        out_specs=[IN_VMEM] * 3,
        out_shape=[shaped((HALO // ROWS, ROWS, D), BF)] + [shaped((ROWS, D), F32)] * 2,
        scratch_shapes=[pltpu.VMEM((ROWS, D), BF), pltpu.VMEM((OWN_KEYS, D), F32)],
        compiler_params=params(16),
        cost_estimate=cost(5_000_000_000, 20_000_000),
        name="fine_backward",
    )(
        cotangent, spread, after, fine_out, weights, query, key, value, q_factor, k_factor, probs,
        attended,
    )


def halo_send(place, own, before, count):
    return pl.pallas_call(
        halo_send_kernel,
        grid=(count,),
        in_specs=[SCALAR, whole((ROWS, D)), whole((ROWS, D))],
        out_specs=pl.BlockSpec((1, ROWS, D), lambda p: (p, 0, 0)),
        out_shape=shaped((count, ROWS, D), BF),
        compiler_params=params(8),
        cost_estimate=cost(1_000_000, 1_500_000),
        name="halo_send",
    )(place, own, before)


def repeated(block, count):
    return pl.pallas_call(
        repeated_kernel,
        out_shape=shaped((count, *block.shape), BF),
        compiler_params=params(VMEM_MIB),
        cost_estimate=cost(1_000_000, 1_300_000),
        name="repeated",
    )(block)


def halo_sum(place, got):
    return pl.pallas_call(
        halo_sum_kernel,
        in_specs=[SCALAR, IN_VMEM],
        out_shape=shaped((ROWS, D), BF),
        compiler_params=params(VMEM_MIB),
        cost_estimate=cost(1_000_000, 1_500_000),
        name="halo_sum",
    )(place, got)


def fine_finish(place, own, got, arrived, hidden_grad, tokens):
    return pl.pallas_call(
        fine_finish_kernel,
        in_specs=[SCALAR] + [IN_VMEM] * 5,
        out_shape=shaped((ROWS, D), BF),
        compiler_params=params(VMEM_MIB),
        cost_estimate=cost(1_000_000, 3_000_000),
        name="fine_finish",
    )(place, own, got, arrived, hidden_grad, tokens)


def per_device(tokens, cotangent, fine_qkv, fine_out, coarse_qkv, coarse_out):
    peers = 1
    for name in GROUP:
        peers *= lax.axis_size(name)
    groups = 1
    for name in FAR:
        groups *= lax.axis_size(name)
    weights = jnp.transpose(fine_qkv, (1, 0, 2))
    core = lax.axis_index("core").astype(jnp.int32).reshape(1)
    column_at = lax.axis_index("x")
    columns_along = lax.axis_size("x")
    tail = shifted_by(tokens[ROWS - EXTRA :], columns_along + 1)
    row_before = shifted_by(tokens, columns_along)
    group_start = lax.axis_index(FAR) * (peers * COARSE)
    place = jnp.stack([lax.axis_index(LINE) * ROWS, column_at, group_start]).astype(jnp.int32)
    prepared = fine_prepare(place, tokens, cotangent, weights, fine_out)
    coarse_weights = coarse_prepare(core, jnp.transpose(coarse_qkv, (1, 0, 2)), coarse_out)
    tail, row_before, prepared, coarse_weights, place = lax.optimization_barrier(
        (tail, row_before, prepared, coarse_weights, place)
    )
    own, weights, fine_out, query, own_key, own_value, q_factor, own_k_factor, bias, coarse_grad = prepared
    coarse_in, coarse_back = coarse_weights
    slots = exchanged(halo_send(place, own, row_before, columns_along), "x")
    key, value, k_factor, probs, attended, hidden, message = fine_forward(
        place, tail, slots, own, weights, fine_out, query, own_key, own_value, own_k_factor, bias,
        coarse_grad, peers,
    )
    gathered = exchanged(message, GROUP)
    near, further = lax.axis_size("z_hi"), lax.axis_size("y")
    coarse_send, coarse_factor = coarse_project(gathered, coarse_in, coarse_back, near)
    group_rows = coarse_factor.shape[0]
    nearby = exchanged(coarse_send, "z_hi").reshape(near * group_rows, 2 * PAIR)
    everyone = exchanged(repeated(nearby, further), "y").reshape(groups * group_rows, 2 * PAIR)
    partial = coarse_attention(place, everyone, coarse_factor, coarse_in, coarse_back)
    returned = exchanged(partial, GROUP)
    spread, first, state = coarse_finish(returned, message, coarse_grad)
    after = shifted_by(first, -1)
    output = (
        hidden.astype(F32) + jnp.repeat(state.astype(BF), POOL, axis=0).astype(F32)
    ).astype(BF)
    halo, own_grad, hidden_grad = fine_backward(
        cotangent, spread, after, fine_out, weights, query, key, value, q_factor, k_factor, probs,
        attended,
    )
    got = exchanged(halo, "x")
    arrived = shifted_by(halo_sum(place, got), -columns_along)
    return (output, fine_finish(place, own_grad, got, arrived, hidden_grad, own))


def solution(mesh):
    sizes = (4, 4, 2, 2, 4)
    fine_mesh = Mesh(mesh.devices.reshape(sizes), LINE)
    placed = (
        P(LINE, None),
        P(LINE, None),
        P(),
        P(),
        P(None, None, ("z_lo", "x")),
        P(("z_lo", "x"), None),
    )
    return jax.shard_map(
        per_device,
        mesh=fine_mesh,
        in_specs=placed,
        out_specs=(P(LINE, None), P(LINE, None)),
        check_vma=False,
    )
```

time: 171 us -> 162 us (0.947)
  blocking collectives: 46.1 us -> 100 us
  waiting for transfers between devices: 56.2 us -> 12 us
  starting transfers between devices: 23.1 us -> 10.5 us
  Pallas kernels: 40.5 us -> 36.6 us
    all_to_all x3 -> x6, blocking collectives: 46.1 us -> 100 us  [exchanged(): return lax.all_to_all(pieces, axes, 0, 0, tiled=True)]
    all_to_all x3 -> x0, waiting for transfers between devices: 39 us -> none  [exchanged(): return lax.all_to_all(pieces, axes, 0, 0, tiled=True)]
    all_to_all x3 -> x0, starting transfers between devices: 12.6 us -> none  [exchanged(): return lax.all_to_all(pieces, axes, 0, 0, tiled=True)]
    ppermute x4, waiting for transfers between devices: 17.2 us -> 12 us  [shifted_by(): lax.ppermute(value, LINE, [(source, source + steps) for source in range(f...]
    pallas_call x3 -> x5, Pallas kernels: 27.6 us -> 24.8 us  [the longest x1 9.7 us: fine_backward(): pl.pallas_call(fine_backward_kernel, in_specs=[IN_VMEM] * 12, out_specs=[...]
  transfers between devices with their start and end apart: 7 -> 4, of which waited for: 6 -> 3; matrix products, arithmetic and copies ran while one was open for 1% -> 1% of each run, Pallas kernels for 0% -> 3%
where the time goes in v5:
time: 162 us
  blocking collectives  100 us (62%)
  Pallas kernels  36.6 us (23%)
  waiting for transfers between devices  12 us (7%)
  starting transfers between devices  10.5 us (6%)
    all_to_all x6, blocking collectives, exchanged(): return lax.all_to_all(pieces, axes, 0, 0, tiled=True)  100 us
    ppermute x4, waiting for transfers between devices, shifted_by(): lax.ppermute(value, LINE, [(source, source + steps) for source in range(f...  12 us
    ppermute x4, starting transfers between devices, shifted_by(): lax.ppermute(value, LINE, [(source, source + steps) for source in range(f...  10.5 us
    pallas_call x1, Pallas kernels, fine_backward(): pl.pallas_call(fine_backward_kernel, in_specs=[IN_VMEM] * 12, out_specs=[...  9.7 us
    pallas_call x1, Pallas kernels, fine_forward(): pl.pallas_call(fine_forward_kernel, in_specs=[SCALAR] + [IN_VMEM] * 11, o...  9.3 us
    pallas_call x1, Pallas kernels, coarse_attention(): pl.pallas_call(coarse_attention_kernel, in_specs=[SCALAR] + [IN_VMEM] * 4...  8.59 us
    pallas_call x1, Pallas kernels, fine_prepare(): pl.pallas_call(fine_prepare_kernel, in_specs=[SCALAR] + [anywhere] * 4, o...  4.73 us
  transfers between devices with their start and end apart: 4, of which 3 were waited for; matrix products, arithmetic and copies ran while one was open for 1% of the time, Pallas kernels for 3%

profile of v5, /device:TPU:64, one launch (start us, length us, event | category | flops | bytes accessed | tf_op | source)
XLA Modules:
  0.0 161.6 jit_solution(17078054474740049900)
XLA Ops:
  0.6 3.8 %collective-permute-start.1 = (bf16[128,1024]{1,0:T(8,128)(2,1)}, bf16[128,1024]{1,0:T(8,128)(2,1)S(1)}, u32[]{:S(2)}, u32[]{:S(2)}) collective-permute-start(bf16[128,1024]{1,0:T(8,128)(2,1)} %own_hbm.1), channel_id=1, source_target_pairs={{0,4},{1,5},{2,6},{3,7},{4,8},{5,9},{6,10},{7,11},{8,12},{9,13},{1... | collective-permute-start | bytes 786440 | tf_op jit(solution)/shard_map/ppermute | solution.py:41
  4.5 0.8 slice.3
  5.2 2.8 %collective-permute-start = (bf16[16,1024]{1,0:T(8,128)(2,1)S(1)}, bf16[16,1024]{1,0:T(8,128)(2,1)S(1)}, u32[]{:S(2)}, u32[]{:S(2)}) collective-permute-start(bf16[16,1024]{1,0:T(8,128)(2,1)S(1)} %slice.3), channel_id=1, source_target_pairs={{0,5},{1,6},{2,7},{3,8},{4,9},{5,10},{6,11},{7,12},{8,13},{9,14},{... | collective-permute-start | bytes 98312 | tf_op jit(solution)/shard_map/ppermute | solution.py:41
  8.1 0.1 pad_add_fusion.place_ref
  8.2 0.0 copy-start
  8.2 4.7 %fine_prepare.1 = (bf16[128,1024]{1,0:T(8,128)(2,1)S(1)}, bf16[3,1024,1024]{2,1,0:T(8,128)(2,1)S(1)}, bf16[1024,1024]{1,0:T(8,128)(2,1)S(1)}, bf16[128,1024]{1,0...) custom-call(s32[3]{0:T(128)S(1)} %pad_add_fusion.place_ref, ...), custom_call_target="tpu_custom_call" | custom-call | flops 900000000 | bytes 17000000 | tf_op jit(solution)/shard_map/fine_prepare/pallas_call | solution.py:468
  12.9 0.0 copy-done
  12.9 0.0 copy-done.2
  12.9 0.4 coarse_prepare.1
  13.3 0.2 collective-permute-done.tail_ref
  13.5 0.0 collective-permute-done.1.before_ref
  13.5 0.7 halo_send.1
  14.2 18.4 %all_to_all.30.slots_ref = bf16[4,128,1024]{2,1,0:T(8,128)(2,1)S(1)} all-to-all(bf16[4,128,1024]{2,1,0:T(8,128)(2,1)S(1)} %halo_send.1), channel_id=1, replica_groups=mesh['y'=4,'z_hi'=4,'core'=2,'z_lo'=2,'x'=4] {'x'}, dimensions={0} | all-to-all | bytes 2097152 | tf_op jit(solution)/shard_map/all_to_all | solution.py:45
  32.6 9.3 %fine_forward.1 = (bf16[640,1024]{1,0:T(8,128)(2,1)S(1)}, bf16[640,1024]{1,0:T(8,128)(2,1)S(1)}, f32[640,1024]{1,0:T(8,128)S(1)}, bf16[16,128,640]{2,1,0:T(8,128...) custom-call(s32[3]{0:T(128)S(1)} %pad_add_fusion.place_ref, ...), custom_call_target="tpu_custom_call" | custom-call | flops 4499999744 | bytes 20000000 | tf_op jit(solution)/shard_map/fine_forward/pallas_call | solution.py:492
  41.9 16.1 %all_to_all.31.got_ref = bf16[16,16,1024]{2,1,0:T(8,128)(2,1)S(1)} all-to-all(bf16[16,16,1024]{2,1,0:T(8,128)(2,1)S(1)} %get-tuple-element.69.message_ref), channel_id=1, replica_groups=mesh['y'=4,'z_hi'=4,'core'=2,'z_lo'=2,'x'=4] {'core','z_lo','x'}, dimensions={0} | all-to-all | bytes 1048576 | tf_op jit(solution)/shard_map/all_to_all | solution.py:45
  58.1 0.5 coarse_project.1
  58.6 15.6 %all_to_all.32 = bf16[4,128,256]{2,1,0:T(8,128)(2,1)S(1)} all-to-all(bf16[4,128,256]{2,1,0:T(8,128)(2,1)S(1)} %get-tuple-element.72), channel_id=1, replica_groups=mesh['y'=4,'z_hi'=4,'core'=2,'z_lo'=2,'x'=4] {'z_hi'}, dimensions={0} | all-to-all | bytes 524288 | tf_op jit(solution)/shard_map/all_to_all | solution.py:45
  74.2 0.1 repeated.1
  74.3 19.1 %all_to_all.33 = bf16[4,512,256]{2,1,0:T(8,128)(2,1)S(1)} all-to-all(bf16[4,512,256]{2,1,0:T(8,128)(2,1)S(1)} %repeated.1), channel_id=1, replica_groups=mesh['y'=4,'z_hi'=4,'core'=2,'z_lo'=2,'x'=4] {'y'}, dimensions={0} | all-to-all | bytes 2097152 | tf_op jit(solution)/shard_map/all_to_all | solution.py:45
  93.4 8.6 %coarse_attention.1 = bf16[16,16,1024]{2,1,0:T(8,128)(2,1)S(1)} custom-call(s32[3]{0:T(128)S(1)} %pad_add_fusion.place_ref, bf16[2048,256]{1,0:T(8,128)(2,1)S(1)} %bitcast.13, f32[128,256]{1,0:T(8,128)S(1)} %get-tuple-element.73.factor_ref, bf16[1024,256]{1,0:T(8,128)(2,1)S(1)} %get-tuple-element.70.in_w_ref, bf16[256,1024]{1,0:T(8,128)(2,1)S(1)} %get-tuple-element.71.out_w_ref), custom_call_target="tpu_custom_call" | custom-call | flops 1500000000 | bytes 3000000 | tf_op jit(solution)/shard_map/coarse_attention/pallas_call | solution.py:537
  102.0 13.3 %all_to_all.34.got_ref = bf16[16,16,1024]{2,1,0:T(8,128)(2,1)S(1)} all-to-all(bf16[16,16,1024]{2,1,0:T(8,128)(2,1)S(1)} %coarse_attention.1), channel_id=1, replica_groups=mesh['y'=4,'z_hi'=4,'core'=2,'z_lo'=2,'x'=4] {'core','z_lo','x'}, dimensions={0} | all-to-all | bytes 1048576 | tf_op jit(solution)/shard_map/all_to_all | solution.py:45
  115.3 0.2 coarse_finish.1
  115.4 1.9 %collective-permute-start.2 = (f32[1,1024]{1,0:T(1,128)S(1)}, f32[1,1024]{1,0:T(1,128)S(1)}, u32[]{:S(2)}, u32[]{:S(2)}) collective-permute-start(f32[1,1024]{1,0:T(1,128)S(1)} %get-tuple-element.76), channel_id=1, source_target_pairs={{1,0},{2,1},{3,2},{4,3},{5,4},{6,5},{7,6},{8,7},{9,8},{10,9},{11,1... | collective-permute-start | bytes 12296 | tf_op jit(solution)/shard_map/ppermute | solution.py:41
  117.4 3.6 %collective-permute-done.2.next_ref = f32[1,1024]{1,0:T(1,128)S(1)} collective-permute-done((f32[1,1024]{1,0:T(1,128)S(1)}, f32[1,1024]{1,0:T(1,128)S(1)}, u32[]{:S(2)}, u32[]{:S(2)}) %collective-permute-start.2) | collective-permute-done | bytes 4128 | tf_op jit(solution)/shard_map/ppermute | solution.py:41
  120.9 0.0 copy-done.1
  120.9 9.7 %fine_backward.1 = (bf16[4,128,1024]{2,1,0:T(8,128)(2,1)S(1)}, f32[128,1024]{1,0:T(8,128)S(1)}, f32[128,1024]{1,0:T(8,128)S(1)}) custom-call(bf16[128,1024]{1,0:T(8,128)(2,1)S(1)} %copy-done.1, f32[8,1024]{1,0:T(8,128)S(1)} %get-tuple-element.75.spread_ref, f32[1,1024]{1,0:T(1,128)S(1)} %collective-permute-done.2.next_ref, ...), custom_call_target="tpu_custom_call" | custom-call | flops 5000000000 | bytes 20000000 | tf_op jit(solution)/shard_map/fine_backward/pallas_call | solution.py:565
  130.7 17.6 %all_to_all.35.got_ref = bf16[4,128,1024]{2,1,0:T(8,128)(2,1)S(1)} all-to-all(bf16[4,128,1024]{2,1,0:T(8,128)(2,1)S(1)} %get-tuple-element.84), channel_id=1, replica_groups=mesh['y'=4,'z_hi'=4,'core'=2,'z_lo'=2,'x'=4] {'x'}, dimensions={0} | all-to-all | bytes 2097152 | tf_op jit(solution)/shard_map/all_to_all | solution.py:45
  148.3 0.7 halo_sum.1
  149.0 1.9 %collective-permute-start.3 = (bf16[128,1024]{1,0:T(8,128)(2,1)S(1)}, bf16[128,1024]{1,0:T(8,128)(2,1)S(1)}, u32[]{:S(2)}, u32[]{:S(2)}) collective-permute-start(bf16[128,1024]{1,0:T(8,128)(2,1)S(1)} %halo_sum.1), channel_id=1, source_target_pairs={{4,0},{5,1},{6,2},{7,3},{8,4},{9,5},{10,6},{11,7},{12,8},{13,9},{1... | collective-permute-start | bytes 786440 | tf_op jit(solution)/shard_map/ppermute | solution.py:41
  150.9 0.8 fusion
  151.7 8.3 %collective-permute-done.3.arrived_ref = bf16[128,1024]{1,0:T(8,128)(2,1)S(1)} collective-permute-done((bf16[128,1024]{1,0:T(8,128)(2,1)S(1)}, bf16[128,1024]{1,0:T(8,128)(2,1)S(1)}, u32[]{:S(2)}, u32[]{:S(2)}) %collective-permute-start.3) | collective-permute-done | bytes 262176 | tf_op jit(solution)/shard_map/ppermute | solution.py:41
  160.0 1.7 %fine_finish.1 = bf16[128,1024]{1,0:T(8,128)(2,1)} custom-call(s32[3]{0:T(128)S(1)} %pad_add_fusion.place_ref, f32[128,1024]{1,0:T(8,128)S(1)} %get-tuple-element.83.own_ref, bf16[4,128,1024]{2,1,0:T(8,128)(2,1)S(1)} %all_to_all.35.got_ref, bf16[128,1024]{1,0:T(8,128)(2,1)S(1)} %collective-permute-done.3.arrived_ref, ...), custom_call_target="tpu_custom_call" | custom-call | flops 1000000 | bytes 3000000 | tf_op jit(solution)/shard_map/fine_finish/pallas_call | solution.py:615
  (3 shorter events, 0.0 us)
Async XLA Ops:
  0.6 12.9 %collective-permute-start.1 = (bf16[128,1024]{1,0:T(8,128)(2,1)}, bf16[128,1024]{1,0:T(8,128)(2,1)S(1)}, u32[]{:S(2)}, u32[]{:S(2)}) collective-permute-start(bf16[128,1024]{1,0:T(8,128)(2,1)} %own_hbm.1), channel_id=1, source_target_pairs={{0,4},{1,5},{2,6},{3,7},{4,8},{5,9},{6,10},{7,11},{8,12},{9,13},{1... | collective-permute-start | bytes 786440 | tf_op jit(solution)/shard_map/ppermute | solution.py:41
  5.2 8.2 %collective-permute-start = (bf16[16,1024]{1,0:T(8,128)(2,1)S(1)}, bf16[16,1024]{1,0:T(8,128)(2,1)S(1)}, u32[]{:S(2)}, u32[]{:S(2)}) collective-permute-start(bf16[16,1024]{1,0:T(8,128)(2,1)S(1)} %slice.3), channel_id=1, source_target_pairs={{0,5},{1,6},{2,7},{3,8},{4,9},{5,10},{6,11},{7,12},{8,13},{9,14},{... | collective-permute-start | bytes 98312 | tf_op jit(solution)/shard_map/ppermute | solution.py:41
  8.2 4.7 %copy-start = (bf16[1024,3,128]{2,0,1:T(8,128)(2,1)S(1)}, bf16[1024,3,128]{2,0,1:T(8,128)(2,1)}, u32[]{:S(2)}) copy-start(bf16[1024,3,128]{2,0,1:T(8,128)(2,1)} %param.10) | copy-start | bytes 2359300
  8.2 4.8 %copy-start.2 = (bf16[128,1024]{1,0:T(8,128)(2,1)S(1)}, bf16[128,1024]{1,0:T(8,128)(2,1)}, u32[]{:S(2)}) copy-start(bf16[128,1024]{1,0:T(8,128)(2,1)} %back_ref.1) | copy-start | bytes 786436
  93.4 27.6 %copy-start.1 = (bf16[128,1024]{1,0:T(8,128)(2,1)S(1)}, bf16[128,1024]{1,0:T(8,128)(2,1)}, u32[]{:S(2)}) copy-start(bf16[128,1024]{1,0:T(8,128)(2,1)} %cot_ref.1) | copy-start | bytes 786436
  115.4 5.5 %collective-permute-start.2 = (f32[1,1024]{1,0:T(1,128)S(1)}, f32[1,1024]{1,0:T(1,128)S(1)}, u32[]{:S(2)}, u32[]{:S(2)}) collective-permute-start(f32[1,1024]{1,0:T(1,128)S(1)} %get-tuple-element.76), channel_id=1, source_target_pairs={{1,0},{2,1},{3,2},{4,3},{5,4},{6,5},{7,6},{8,7},{9,8},{10,9},{11,1... | collective-permute-start | bytes 12296 | tf_op jit(solution)/shard_map/ppermute | solution.py:41
  149.0 11.0 %collective-permute-start.3 = (bf16[128,1024]{1,0:T(8,128)(2,1)S(1)}, bf16[128,1024]{1,0:T(8,128)(2,1)S(1)}, u32[]{:S(2)}, u32[]{:S(2)}) collective-permute-start(bf16[128,1024]{1,0:T(8,128)(2,1)S(1)} %halo_sum.1), channel_id=1, source_target_pairs={{4,0},{5,1},{6,2},{7,3},{8,4},{9,5},{10,6},{11,7},{12,8},{13,9},{1... | collective-permute-start | bytes 786440 | tf_op jit(solution)/shard_map/ppermute | solution.py:41

commit v6 on v5

--- a/solution.py
+++ b/solution.py
@@ -201,7 +201,7 @@
         acc[...] += plain(jnp.concatenate(mixed, axis=1), out_w_ref[here, :])
         return carry
 
-    lax.fori_loop(0, D // WIDTH, one_step, 0)
+    lax.fori_loop(0, D // WIDTH, one_step, 0, unroll=True)
     before = slots_ref[nearest, ROWS - EXTRA :, :].astype(F32) + acc[:EXTRA, :]
     before = jnp.where(anchor > 0, before, 0.0).astype(BF)
     own = (own_ref[...].astype(F32) + acc[EXTRA:, :]).astype(BF)
@@ -270,29 +270,26 @@
             total = total + values[:, at : at + PAIR]
         return total
 
-    def one_block(index, carry):
-        first = pl.multiple_of(index * block, block)
-        query, grad = masked_halves(got_ref[pl.ds(first, block), :PAIR])
+    def one_block(index):
+        first = index * block
+        query, grad = masked_halves(got_ref[first : first + block, :PAIR])
         stacked = jnp.concatenate([query, grad], axis=0)
 
         def scored(keys):
             both = last_last(stacked, keys)
             return jnp.exp(both[:block]), both[block:]
 
-        def one_chunk(at, sums):
-            total, product = sums
-            numer, prob_grad = scored(got_ref[pl.ds(pl.multiple_of(at * block, block), block), PAIR:])
-            return total + lane_partials(numer), product + lane_partials(numer * prob_grad)
-
-        nothing = jnp.zeros((block, PAIR), F32)
-        total, product = lax.fori_loop(0, index, one_chunk, (nothing, nothing))
-        numer, prob_grad = scored(got_ref[pl.ds(first, block), PAIR:])
         query_at = lax.broadcasted_iota(jnp.int32, (block, 1), 0)
-        numer = jnp.where(lax.broadcasted_iota(jnp.int32, (1, block), 1) <= query_at, numer, 0.0)
-        total = jnp.sum(total + lane_partials(numer), axis=-1, keepdims=True)
-        product = jnp.sum(product + lane_partials(numer * prob_grad), axis=-1, keepdims=True)
-        inverse = 1.0 / total
-        delta = product * inverse
+        total = product = None
+        for at in range(index + 1):
+            numer, prob_grad = scored(got_ref[at * block : (at + 1) * block, PAIR:])
+            if at == index:
+                key_at = lax.broadcasted_iota(jnp.int32, (1, block), 1)
+                numer = jnp.where(key_at <= query_at, numer, 0.0)
+            sums = lane_partials(numer), lane_partials(numer * prob_grad)
+            total, product = sums if at == 0 else (total + sums[0], product + sums[1])
+        inverse = 1.0 / jnp.sum(total, axis=-1, keepdims=True)
+        delta = jnp.sum(product, axis=-1, keepdims=True) * inverse
         own_pos = own_start + lax.broadcasted_iota(jnp.int32, (1, ROWS), 1)
         numer, prob_grad = scored(own_right)
         numer = jnp.where(own_pos <= query_at + first, numer, 0.0)
@@ -301,22 +298,39 @@
         own_grad[...] += first_first(
             jnp.concatenate([score_grad, prob.astype(BF)], axis=0), stacked
         )
-        return carry
-
-    lax.fori_loop(own_start // block, length // block, one_block, 0)
+
+    for index in range(length // block):
+        pl.when(own_start < (index + 1) * block)(lambda index=index: one_block(index))
 
     query, grad = masked_halves(own_left)
+    stacked = jnp.concatenate([query, grad], axis=0)
     query_pos = own_start + lax.broadcasted_iota(jnp.int32, (ROWS, 1), 0)
-    key_pos = lax.broadcasted_iota(jnp.int32, (1, length), 1)
-    keys = got_ref[:, PAIR:]
-    key_scaled, value = masked_halves(keys)
-    numer = jnp.where(key_pos <= query_pos, jnp.exp(last_last(query, keys)), 0.0)
-    prob_grad = last_last(grad, keys)
-    inverse = 1.0 / jnp.sum(numer, axis=-1, keepdims=True)
-    delta = jnp.sum(numer * prob_grad, axis=-1, keepdims=True) * inverse
-    prob = numer * inverse
-    score_grad = (prob * (prob_grad - delta)).astype(BF)
-    mine = plain(score_grad, key_scaled) + plain(prob.astype(BF), value)
+
+    def own_chunk(at):
+        key_start = pl.multiple_of(at * block, block)
+        keys = got_ref[pl.ds(key_start, block), PAIR:]
+        both = last_last(stacked, keys)
+        key_pos = key_start + lax.broadcasted_iota(jnp.int32, (1, block), 1)
+        return keys, jnp.where(key_pos <= query_pos, jnp.exp(both[:ROWS]), 0.0), both[ROWS:]
+
+    def own_sums(at, sums):
+        numer, prob_grad = own_chunk(at)[1:]
+        return sums[0] + lane_partials(numer), sums[1] + lane_partials(numer * prob_grad)
+
+    nothing = jnp.zeros((ROWS, PAIR), F32)
+    chunks = own_start // block + 1
+    total, product = lax.fori_loop(0, chunks, own_sums, (nothing, nothing))
+    inverse = 1.0 / jnp.sum(total, axis=-1, keepdims=True)
+    delta = jnp.sum(product, axis=-1, keepdims=True) * inverse
+
+    def own_results(at, mine):
+        keys, numer, prob_grad = own_chunk(at)
+        key_scaled, value = masked_halves(keys)
+        prob = numer * inverse
+        score_grad = (prob * (prob_grad - delta)).astype(BF)
+        return mine + plain(score_grad, key_scaled) + plain(prob.astype(BF), value)
+
+    mine = lax.fori_loop(0, chunks, own_results, nothing)
 
     parts = []
     for tile, unit, factor in (
@@ -402,7 +416,7 @@
         acc[HALO:, :] += last_last(jnp.concatenate(query_grads, axis=1), w_ref[0, :, here])
         return carry
 
-    lax.fori_loop(0, D // WIDTH, one_step, 0)
+    lax.fori_loop(0, D // WIDTH, one_step, 0, unroll=True)
     for slot in range(halo_ref.shape[0]):
         halo_ref[slot] = acc[slot * ROWS : (slot + 1) * ROWS, :].astype(BF)
     own_ref[...] = acc[HALO:, :]
@@ -425,11 +439,16 @@
     back_ref[...] = total.astype(BF)
 
 
-def fine_finish_kernel(place_ref, own_ref, got_ref, arrived_ref, hg_ref, tokens_ref, out_ref):
+def halo_keep_kernel(place_ref, own_ref, got_ref, kept_ref):
     column_at = place_ref[1]
-    total = own_ref[...] + arrived_ref[...].astype(F32)
+    total = own_ref[...]
     for slot in range(1, got_ref.shape[0]):
         total = total + jnp.where(column_at < slot, got_ref[slot].astype(F32), 0.0)
+    kept_ref[...] = total
+
+
+def fine_finish_kernel(kept_ref, arrived_ref, hg_ref, tokens_ref, out_ref):
+    total = kept_ref[...] + arrived_ref[...].astype(F32)
     normed, factor = row_norm(tokens_ref[...].astype(F32))
     out_ref[...] = (hg_ref[...] + row_norm_back(total, normed, factor)).astype(BF)
 
@@ -611,15 +630,25 @@
     )(place, got)
 
 
-def fine_finish(place, own, got, arrived, hidden_grad, tokens):
+def halo_keep(place, own, got):
+    return pl.pallas_call(
+        halo_keep_kernel,
+        in_specs=[SCALAR, IN_VMEM, IN_VMEM],
+        out_shape=shaped((ROWS, D), F32),
+        compiler_params=params(VMEM_MIB),
+        cost_estimate=cost(1_000_000, 1_500_000),
+        name="halo_keep",
+    )(place, own, got)
+
+
+def fine_finish(kept, arrived, hidden_grad, tokens):
     return pl.pallas_call(
         fine_finish_kernel,
-        in_specs=[SCALAR] + [IN_VMEM] * 5,
         out_shape=shaped((ROWS, D), BF),
         compiler_params=params(VMEM_MIB),
         cost_estimate=cost(1_000_000, 3_000_000),
         name="fine_finish",
-    )(place, own, got, arrived, hidden_grad, tokens)
+    )(kept, arrived, hidden_grad, tokens)
 
 
 def per_device(tokens, cotangent, fine_qkv, fine_out, coarse_qkv, coarse_out):
@@ -668,7 +697,8 @@
     )
     got = exchanged(halo, "x")
     arrived = shifted_by(halo_sum(place, got), -columns_along)
-    return (output, fine_finish(place, own_grad, got, arrived, hidden_grad, own))
+    kept = halo_keep(place, own_grad, got)
+    return (output, fine_finish(kept, arrived, hidden_grad, own))
 
 
 def solution(mesh):

time: 162 us -> 158 us (0.975)
  Pallas kernels: 36.6 us -> 32.9 us
    pallas_call x1, Pallas kernels: 8.59 us -> 6.95 us  [coarse_attention(): pl.pallas_call(coarse_attention_kernel, in_specs=[SCALAR] + [IN_VMEM] * 4...]
  transfers between devices with their start and end apart: 4 -> 4, of which waited for: 3 -> 3; matrix products, arithmetic and copies ran while one was open for 1% -> 1% of each run, Pallas kernels for 3% -> 4%
where the time goes in v6:
time: 158 us; the launch traced here: 157 us
  blocking collectives  100 us (63%)
  Pallas kernels  32.9 us (21%)
  waiting for transfers between devices  11.3 us (7%)
  starting transfers between devices  10.5 us (7%)
    all_to_all x6, blocking collectives, exchanged(): return lax.all_to_all(pieces, axes, 0, 0, tiled=True)  100 us
    ppermute x4, waiting for transfers between devices, shifted_by(): lax.ppermute(value, LINE, [(source, source + steps) for source in range(f...  11.3 us
    ppermute x4, starting transfers between devices, shifted_by(): lax.ppermute(value, LINE, [(source, source + steps) for source in range(f...  10.5 us
    pallas_call x1, Pallas kernels, fine_backward(): pl.pallas_call(fine_backward_kernel, in_specs=[IN_VMEM] * 12, out_specs=[...  8.82 us
    pallas_call x1, Pallas kernels, fine_forward(): pl.pallas_call(fine_forward_kernel, in_specs=[SCALAR] + [IN_VMEM] * 11, o...  8.11 us
    pallas_call x1, Pallas kernels, coarse_attention(): pl.pallas_call(coarse_attention_kernel, in_specs=[SCALAR] + [IN_VMEM] * 4...  6.95 us
    pallas_call x1, Pallas kernels, fine_prepare(): pl.pallas_call(fine_prepare_kernel, in_specs=[SCALAR] + [anywhere] * 4, o...  4.73 us
  transfers between devices with their start and end apart: 4, of which 3 were waited for; matrix products, arithmetic and copies ran while one was open for 1% of the time, Pallas kernels for 4%

profile of v6, /device:TPU:64, one launch (start us, length us, event | category | flops | bytes accessed | tf_op | source)
XLA Modules:
  0.0 157.3 jit_solution(14437602267034234297)
XLA Ops:
  0.6 3.8 %collective-permute-start.1 = (bf16[128,1024]{1,0:T(8,128)(2,1)}, bf16[128,1024]{1,0:T(8,128)(2,1)S(1)}, u32[]{:S(2)}, u32[]{:S(2)}) collective-permute-start(bf16[128,1024]{1,0:T(8,128)(2,1)} %own_hbm.1), channel_id=1, source_target_pairs={{0,4},{1,5},{2,6},{3,7},{4,8},{5,9},{6,10},{7,11},{8,12},{9,13},{1... | collective-permute-start | bytes 786440 | tf_op jit(solution)/shard_map/ppermute | solution.py:41
  4.5 0.8 slice.3
  5.2 2.8 %collective-permute-start = (bf16[16,1024]{1,0:T(8,128)(2,1)S(1)}, bf16[16,1024]{1,0:T(8,128)(2,1)S(1)}, u32[]{:S(2)}, u32[]{:S(2)}) collective-permute-start(bf16[16,1024]{1,0:T(8,128)(2,1)S(1)} %slice.3), channel_id=1, source_target_pairs={{0,5},{1,6},{2,7},{3,8},{4,9},{5,10},{6,11},{7,12},{8,13},{9,14},{... | collective-permute-start | bytes 98312 | tf_op jit(solution)/shard_map/ppermute | solution.py:41
  8.1 0.1 pad_add_fusion.place_ref
  8.2 4.7 %fine_prepare.1 = (bf16[128,1024]{1,0:T(8,128)(2,1)S(1)}, bf16[3,1024,1024]{2,1,0:T(8,128)(2,1)S(1)}, bf16[1024,1024]{1,0:T(8,128)(2,1)S(1)}, bf16[128,1024]{1,0...) custom-call(s32[3]{0:T(128)S(1)} %pad_add_fusion.place_ref, ...), custom_call_target="tpu_custom_call" | custom-call | flops 900000000 | bytes 17000000 | tf_op jit(solution)/shard_map/fine_prepare/pallas_call | solution.py:487
  12.9 0.0 copy-done
  12.9 0.0 copy-done.2
  12.9 0.4 coarse_prepare.1
  13.3 0.2 collective-permute-done.tail_ref
  13.5 0.0 collective-permute-done.1.before_ref
  13.5 0.7 halo_send.1
  14.2 18.4 %all_to_all.30.slots_ref = bf16[4,128,1024]{2,1,0:T(8,128)(2,1)S(1)} all-to-all(bf16[4,128,1024]{2,1,0:T(8,128)(2,1)S(1)} %halo_send.1), channel_id=1, replica_groups=mesh['y'=4,'z_hi'=4,'core'=2,'z_lo'=2,'x'=4] {'x'}, dimensions={0} | all-to-all | bytes 2097152 | tf_op jit(solution)/shard_map/all_to_all | solution.py:45
  32.6 8.1 %fine_forward.1 = (bf16[640,1024]{1,0:T(8,128)(2,1)S(1)}, bf16[640,1024]{1,0:T(8,128)(2,1)S(1)}, f32[640,1024]{1,0:T(8,128)S(1)}, bf16[16,128,640]{2,1,0:T(8,128...) custom-call(s32[3]{0:T(128)S(1)} %pad_add_fusion.place_ref, ...), custom_call_target="tpu_custom_call" | custom-call | flops 4499999744 | bytes 20000000 | tf_op jit(solution)/shard_map/fine_forward/pallas_call | solution.py:511
  40.7 16.1 %all_to_all.31.got_ref = bf16[16,16,1024]{2,1,0:T(8,128)(2,1)S(1)} all-to-all(bf16[16,16,1024]{2,1,0:T(8,128)(2,1)S(1)} %get-tuple-element.69.message_ref), channel_id=1, replica_groups=mesh['y'=4,'z_hi'=4,'core'=2,'z_lo'=2,'x'=4] {'core','z_lo','x'}, dimensions={0} | all-to-all | bytes 1048576 | tf_op jit(solution)/shard_map/all_to_all | solution.py:45
  56.9 0.5 coarse_project.1
  57.4 15.6 %all_to_all.32 = bf16[4,128,256]{2,1,0:T(8,128)(2,1)S(1)} all-to-all(bf16[4,128,256]{2,1,0:T(8,128)(2,1)S(1)} %get-tuple-element.72), channel_id=1, replica_groups=mesh['y'=4,'z_hi'=4,'core'=2,'z_lo'=2,'x'=4] {'z_hi'}, dimensions={0} | all-to-all | bytes 524288 | tf_op jit(solution)/shard_map/all_to_all | solution.py:45
  73.0 0.1 repeated.1
  73.1 19.1 %all_to_all.33 = bf16[4,512,256]{2,1,0:T(8,128)(2,1)S(1)} all-to-all(bf16[4,512,256]{2,1,0:T(8,128)(2,1)S(1)} %repeated.1), channel_id=1, replica_groups=mesh['y'=4,'z_hi'=4,'core'=2,'z_lo'=2,'x'=4] {'y'}, dimensions={0} | all-to-all | bytes 2097152 | tf_op jit(solution)/shard_map/all_to_all | solution.py:45
  92.2 6.9 %coarse_attention.1 = bf16[16,16,1024]{2,1,0:T(8,128)(2,1)S(1)} custom-call(s32[3]{0:T(128)S(1)} %pad_add_fusion.place_ref, bf16[2048,256]{1,0:T(8,128)(2,1)S(1)} %bitcast.13, f32[128,256]{1,0:T(8,128)S(1)} %get-tuple-element.73.factor_ref, bf16[1024,256]{1,0:T(8,128)(2,1)S(1)} %get-tuple-element.70.in_w_ref, bf16[256,1024]{1,0:T(8,128)(2,1)S(1)} %get-tuple-element.71.out_w_ref), custom_call_target="tpu_custom_call" | custom-call | flops 1500000000 | bytes 3000000 | tf_op jit(solution)/shard_map/coarse_attention/pallas_call | solution.py:556
  99.1 13.3 %all_to_all.34.got_ref = bf16[16,16,1024]{2,1,0:T(8,128)(2,1)S(1)} all-to-all(bf16[16,16,1024]{2,1,0:T(8,128)(2,1)S(1)} %coarse_attention.1), channel_id=1, replica_groups=mesh['y'=4,'z_hi'=4,'core'=2,'z_lo'=2,'x'=4] {'core','z_lo','x'}, dimensions={0} | all-to-all | bytes 1048576 | tf_op jit(solution)/shard_map/all_to_all | solution.py:45
  112.4 0.2 coarse_finish.1
  112.6 2.0 %collective-permute-start.2 = (f32[1,1024]{1,0:T(1,128)S(1)}, f32[1,1024]{1,0:T(1,128)S(1)}, u32[]{:S(2)}, u32[]{:S(2)}) collective-permute-start(f32[1,1024]{1,0:T(1,128)S(1)} %get-tuple-element.76), channel_id=1, source_target_pairs={{1,0},{2,1},{3,2},{4,3},{5,4},{6,5},{7,6},{8,7},{9,8},{10,9},{11,1... | collective-permute-start | bytes 12296 | tf_op jit(solution)/shard_map/ppermute | solution.py:41
  114.6 3.5 %collective-permute-done.2.next_ref = f32[1,1024]{1,0:T(1,128)S(1)} collective-permute-done((f32[1,1024]{1,0:T(1,128)S(1)}, f32[1,1024]{1,0:T(1,128)S(1)}, u32[]{:S(2)}, u32[]{:S(2)}) %collective-permute-start.2) | collective-permute-done | bytes 4128 | tf_op jit(solution)/shard_map/ppermute | solution.py:41
  118.1 0.0 copy-done.1
  118.1 8.8 %fine_backward.1 = (bf16[4,128,1024]{2,1,0:T(8,128)(2,1)S(1)}, f32[128,1024]{1,0:T(8,128)S(1)}, f32[128,1024]{1,0:T(8,128)S(1)}) custom-call(bf16[128,1024]{1,0:T(8,128)(2,1)S(1)} %copy-done.1, f32[8,1024]{1,0:T(8,128)S(1)} %get-tuple-element.75.spread_ref, f32[1,1024]{1,0:T(1,128)S(1)} %collective-permute-done.2.next_ref, ...), custom_call_target="tpu_custom_call" | custom-call | flops 5000000000 | bytes 20000000 | tf_op jit(solution)/shard_map/fine_backward/pallas_call | solution.py:584
  127.0 17.6 %all_to_all.35.got_ref = bf16[4,128,1024]{2,1,0:T(8,128)(2,1)S(1)} all-to-all(bf16[4,128,1024]{2,1,0:T(8,128)(2,1)S(1)} %get-tuple-element.84), channel_id=1, replica_groups=mesh['y'=4,'z_hi'=4,'core'=2,'z_lo'=2,'x'=4] {'x'}, dimensions={0} | all-to-all | bytes 2097152 | tf_op jit(solution)/shard_map/all_to_all | solution.py:45
  144.6 0.7 halo_sum.1
  145.3 1.9 %collective-permute-start.3 = (bf16[128,1024]{1,0:T(8,128)(2,1)S(1)}, bf16[128,1024]{1,0:T(8,128)(2,1)S(1)}, u32[]{:S(2)}, u32[]{:S(2)}) collective-permute-start(bf16[128,1024]{1,0:T(8,128)(2,1)S(1)} %halo_sum.1), channel_id=1, source_target_pairs={{4,0},{5,1},{6,2},{7,3},{8,4},{9,5},{10,6},{11,7},{12,8},{13,9},{1... | collective-permute-start | bytes 786440 | tf_op jit(solution)/shard_map/ppermute | solution.py:41
  147.2 0.8 fusion
  148.0 0.7 halo_keep.1.kept_ref
  148.7 7.6 %collective-permute-done.3.arrived_ref = bf16[128,1024]{1,0:T(8,128)(2,1)S(1)} collective-permute-done((bf16[128,1024]{1,0:T(8,128)(2,1)S(1)}, bf16[128,1024]{1,0:T(8,128)(2,1)S(1)}, u32[]{:S(2)}, u32[]{:S(2)}) %collective-permute-start.3) | collective-permute-done | bytes 262176 | tf_op jit(solution)/shard_map/ppermute | solution.py:41
  156.3 1.0 fine_finish.1
  (4 shorter events, 0.0 us)
Async XLA Ops:
  0.6 12.9 %collective-permute-start.1 = (bf16[128,1024]{1,0:T(8,128)(2,1)}, bf16[128,1024]{1,0:T(8,128)(2,1)S(1)}, u32[]{:S(2)}, u32[]{:S(2)}) collective-permute-start(bf16[128,1024]{1,0:T(8,128)(2,1)} %own_hbm.1), channel_id=1, source_target_pairs={{0,4},{1,5},{2,6},{3,7},{4,8},{5,9},{6,10},{7,11},{8,12},{9,13},{1... | collective-permute-start | bytes 786440 | tf_op jit(solution)/shard_map/ppermute | solution.py:41
  5.2 8.2 %collective-permute-start = (bf16[16,1024]{1,0:T(8,128)(2,1)S(1)}, bf16[16,1024]{1,0:T(8,128)(2,1)S(1)}, u32[]{:S(2)}, u32[]{:S(2)}) collective-permute-start(bf16[16,1024]{1,0:T(8,128)(2,1)S(1)} %slice.3), channel_id=1, source_target_pairs={{0,5},{1,6},{2,7},{3,8},{4,9},{5,10},{6,11},{7,12},{8,13},{9,14},{... | collective-permute-start | bytes 98312 | tf_op jit(solution)/shard_map/ppermute | solution.py:41
  8.2 4.7 %copy-start = (bf16[1024,3,128]{2,0,1:T(8,128)(2,1)S(1)}, bf16[1024,3,128]{2,0,1:T(8,128)(2,1)}, u32[]{:S(2)}) copy-start(bf16[1024,3,128]{2,0,1:T(8,128)(2,1)} %param.10) | copy-start | bytes 2359300
  8.2 4.8 %copy-start.2 = (bf16[128,1024]{1,0:T(8,128)(2,1)S(1)}, bf16[128,1024]{1,0:T(8,128)(2,1)}, u32[]{:S(2)}) copy-start(bf16[128,1024]{1,0:T(8,128)(2,1)} %back_ref.1) | copy-start | bytes 786436
  92.2 25.9 %copy-start.1 = (bf16[128,1024]{1,0:T(8,128)(2,1)S(1)}, bf16[128,1024]{1,0:T(8,128)(2,1)}, u32[]{:S(2)}) copy-start(bf16[128,1024]{1,0:T(8,128)(2,1)} %cot_ref.1) | copy-start | bytes 786436
  112.6 5.5 %collective-permute-start.2 = (f32[1,1024]{1,0:T(1,128)S(1)}, f32[1,1024]{1,0:T(1,128)S(1)}, u32[]{:S(2)}, u32[]{:S(2)}) collective-permute-start(f32[1,1024]{1,0:T(1,128)S(1)} %get-tuple-element.76), channel_id=1, source_target_pairs={{1,0},{2,1},{3,2},{4,3},{5,4},{6,5},{7,6},{8,7},{9,8},{10,9},{11,1... | collective-permute-start | bytes 12296 | tf_op jit(solution)/shard_map/ppermute | solution.py:41
  145.3 11.0 %collective-permute-start.3 = (bf16[128,1024]{1,0:T(8,128)(2,1)S(1)}, bf16[128,1024]{1,0:T(8,128)(2,1)S(1)}, u32[]{:S(2)}, u32[]{:S(2)}) collective-permute-start(bf16[128,1024]{1,0:T(8,128)(2,1)S(1)} %halo_sum.1), channel_id=1, source_target_pairs={{4,0},{5,1},{6,2},{7,3},{8,4},{9,5},{10,6},{11,7},{12,8},{13,9},{1... | collective-permute-start | bytes 786440 | tf_op jit(solution)/shard_map/ppermute | solution.py:41

commit v7 on v6

--- a/solution.py
+++ b/solution.py
@@ -358,9 +358,9 @@
 
 
 def fine_backward_kernel(
-    cot_ref, spread_ref, next_ref, out_w_ref, w_ref, q_ref, k_ref, v_ref, qf_ref, kf_ref, p_ref,
+    place_ref, cot_ref, spread_ref, next_ref, out_w_ref, w_ref, q_ref, k_ref, v_ref, qf_ref, kf_ref, p_ref,
     att_ref,
-    halo_ref, own_ref, hg_ref, hidden_grad, acc,
+    back1, back2, back3, back4, own_ref, hg_ref, hidden_grad, acc,
 ):
     low = low_lanes()
     block = (lax.broadcasted_iota(jnp.int32, (ROWS, 1), 0) + (POOL - 1)) // POOL
@@ -417,8 +417,10 @@
         return carry
 
     lax.fori_loop(0, D // WIDTH, one_step, 0, unroll=True)
-    for slot in range(halo_ref.shape[0]):
-        halo_ref[slot] = acc[slot * ROWS : (slot + 1) * ROWS, :].astype(BF)
+    backs = (back1, back2, back3, back4)
+    for distance, ref in enumerate(backs, 1):
+        slot = lax.rem(place_ref[1] + (len(backs) - distance), len(backs))
+        ref[...] = acc[pl.ds(pl.multiple_of(slot * ROWS, ROWS), ROWS), :].astype(BF)
     own_ref[...] = acc[HALO:, :]
 
 
@@ -431,24 +433,10 @@
         send_ref[peer] = block_ref[...]
 
 
-def halo_sum_kernel(place_ref, got_ref, back_ref):
-    column_at = place_ref[1]
-    total = got_ref[0].astype(F32)
-    for slot in range(1, got_ref.shape[0]):
-        total = total + jnp.where(column_at >= slot, got_ref[slot].astype(F32), 0.0)
-    back_ref[...] = total.astype(BF)
-
-
-def halo_keep_kernel(place_ref, own_ref, got_ref, kept_ref):
-    column_at = place_ref[1]
+def fine_finish_kernel(own_ref, a1, a2, a3, a4, hg_ref, tokens_ref, out_ref):
     total = own_ref[...]
-    for slot in range(1, got_ref.shape[0]):
-        total = total + jnp.where(column_at < slot, got_ref[slot].astype(F32), 0.0)
-    kept_ref[...] = total
-
-
-def fine_finish_kernel(kept_ref, arrived_ref, hg_ref, tokens_ref, out_ref):
-    total = kept_ref[...] + arrived_ref[...].astype(F32)
+    for ref in (a1, a2, a3, a4):
+        total = total + ref[...].astype(F32)
     normed, factor = row_norm(tokens_ref[...].astype(F32))
     out_ref[...] = (hg_ref[...] + row_norm_back(total, normed, factor)).astype(BF)
 
@@ -475,7 +463,7 @@
 
 SCALAR = pl.BlockSpec(memory_space=pltpu.SMEM)
 IN_VMEM = pl.BlockSpec(memory_space=pltpu.VMEM)
-WIDTH = 2 * PAIR
+WIDTH = 4 * PAIR
 
 
 def in_hbm(x):
@@ -578,20 +566,20 @@
 
 
 def fine_backward(
-    cotangent, spread, after, fine_out, weights, query, key, value, q_factor, k_factor, probs,
+    place, cotangent, spread, after, fine_out, weights, query, key, value, q_factor, k_factor, probs,
     attended,
 ):
     return pl.pallas_call(
         fine_backward_kernel,
-        in_specs=[IN_VMEM] * 12,
-        out_specs=[IN_VMEM] * 3,
-        out_shape=[shaped((HALO // ROWS, ROWS, D), BF)] + [shaped((ROWS, D), F32)] * 2,
+        in_specs=[SCALAR] + [IN_VMEM] * 12,
+        out_specs=[IN_VMEM] * 6,
+        out_shape=[shaped((ROWS, D), BF)] * 4 + [shaped((ROWS, D), F32)] * 2,
         scratch_shapes=[pltpu.VMEM((ROWS, D), BF), pltpu.VMEM((OWN_KEYS, D), F32)],
         compiler_params=params(16),
         cost_estimate=cost(5_000_000_000, 20_000_000),
         name="fine_backward",
     )(
-        cotangent, spread, after, fine_out, weights, query, key, value, q_factor, k_factor, probs,
+        place, cotangent, spread, after, fine_out, weights, query, key, value, q_factor, k_factor, probs,
         attended,
     )
 
@@ -619,36 +607,14 @@
     )(block)
 
 
-def halo_sum(place, got):
-    return pl.pallas_call(
-        halo_sum_kernel,
-        in_specs=[SCALAR, IN_VMEM],
-        out_shape=shaped((ROWS, D), BF),
-        compiler_params=params(VMEM_MIB),
-        cost_estimate=cost(1_000_000, 1_500_000),
-        name="halo_sum",
-    )(place, got)
-
-
-def halo_keep(place, own, got):
-    return pl.pallas_call(
-        halo_keep_kernel,
-        in_specs=[SCALAR, IN_VMEM, IN_VMEM],
-        out_shape=shaped((ROWS, D), F32),
-        compiler_params=params(VMEM_MIB),
-        cost_estimate=cost(1_000_000, 1_500_000),
-        name="halo_keep",
-    )(place, own, got)
-
-
-def fine_finish(kept, arrived, hidden_grad, tokens):
+def fine_finish(own, arrived, hidden_grad, tokens):
     return pl.pallas_call(
         fine_finish_kernel,
         out_shape=shaped((ROWS, D), BF),
         compiler_params=params(VMEM_MIB),
         cost_estimate=cost(1_000_000, 3_000_000),
         name="fine_finish",
-    )(kept, arrived, hidden_grad, tokens)
+    )(own, *arrived, hidden_grad, tokens)
 
 
 def per_device(tokens, cotangent, fine_qkv, fine_out, coarse_qkv, coarse_out):
@@ -691,14 +657,12 @@
     output = (
         hidden.astype(F32) + jnp.repeat(state.astype(BF), POOL, axis=0).astype(F32)
     ).astype(BF)
-    halo, own_grad, hidden_grad = fine_backward(
-        cotangent, spread, after, fine_out, weights, query, key, value, q_factor, k_factor, probs,
+    *backs, own_grad, hidden_grad = fine_backward(
+        place, cotangent, spread, after, fine_out, weights, query, key, value, q_factor, k_factor, probs,
         attended,
     )
-    got = exchanged(halo, "x")
-    arrived = shifted_by(halo_sum(place, got), -columns_along)
-    kept = halo_keep(place, own_grad, got)
-    return (output, fine_finish(kept, arrived, hidden_grad, own))
+    arrived = [shifted_by(rows, -steps) for steps, rows in enumerate(backs, 1)]
+    return (output, fine_finish(own_grad, arrived, hidden_grad, own))
 
 
 def solution(mesh):

time: 158 us -> 156 us (0.987)
  blocking collectives: 100 us -> 82.5 us
  starting transfers between devices: 10.5 us -> 20.4 us
  waiting for transfers between devices: 11.3 us -> 19.1 us
  Pallas kernels: 32.9 us -> 30.6 us
    all_to_all x6 -> x5, blocking collectives: 100 us -> 82.5 us  [exchanged(): return lax.all_to_all(pieces, axes, 0, 0, tiled=True)]
    ppermute x4 -> x7, starting transfers between devices: 10.5 us -> 20.4 us  [shifted_by(): lax.ppermute(value, LINE, [(source, source + steps) for source in range(f...]
    ppermute x4 -> x7, waiting for transfers between devices: 11.3 us -> 19.1 us  [shifted_by(): lax.ppermute(value, LINE, [(source, source + steps) for source in range(f...]
    pallas_call x3 -> x1, Pallas kernels: 10.2 us -> 8.79 us  [fine_backward(): pl.pallas_call(fine_backward_kernel, in_specs=[SCALAR] + [IN_VMEM] * 12,...]
  transfers between devices with their start and end apart: 4 -> 7, of which waited for: 3 -> 4; matrix products, arithmetic and copies ran while one was open for 1% -> 1% of each run, Pallas kernels for 4% -> 3%
where the time goes in v7:
time: 156 us; the launch traced here: 155 us
  blocking collectives  82.5 us (53%)
  Pallas kernels  30.6 us (20%)
  starting transfers between devices  20.4 us (13%)
  waiting for transfers between devices  19.1 us (12%)
    all_to_all x5, blocking collectives, exchanged(): return lax.all_to_all(pieces, axes, 0, 0, tiled=True)  82.5 us
    ppermute x7, starting transfers between devices, shifted_by(): lax.ppermute(value, LINE, [(source, source + steps) for source in range(f...  20.4 us
    ppermute x7, waiting for transfers between devices, shifted_by(): lax.ppermute(value, LINE, [(source, source + steps) for source in range(f...  19.1 us
    pallas_call x1, Pallas kernels, fine_backward(): pl.pallas_call(fine_backward_kernel, in_specs=[SCALAR] + [IN_VMEM] * 12,...  8.79 us
    pallas_call x1, Pallas kernels, fine_forward(): pl.pallas_call(fine_forward_kernel, in_specs=[SCALAR] + [IN_VMEM] * 11, o...  7.3 us
    pallas_call x1, Pallas kernels, coarse_attention(): pl.pallas_call(coarse_attention_kernel, in_specs=[SCALAR] + [IN_VMEM] * 4...  6.95 us
    pallas_call x1, Pallas kernels, fine_prepare(): pl.pallas_call(fine_prepare_kernel, in_specs=[SCALAR] + [anywhere] * 4, o...  4.64 us
  transfers between devices with their start and end apart: 7, of which 4 were waited for; matrix products, arithmetic and copies ran while one was open for 1% of the time, Pallas kernels for 3%

profile of v7, /device:TPU:64, one launch (start us, length us, event | category | flops | bytes accessed | tf_op | source)
XLA Modules:
  0.0 155.1 jit_solution(11568197459977923015)
XLA Ops:
  0.6 3.8 %collective-permute-start.1 = (bf16[128,1024]{1,0:T(8,128)(2,1)}, bf16[128,1024]{1,0:T(8,128)(2,1)S(1)}, u32[]{:S(2)}, u32[]{:S(2)}) collective-permute-start(bf16[128,1024]{1,0:T(8,128)(2,1)} %own_hbm.1), channel_id=1, source_target_pairs={{0,4},{1,5},{2,6},{3,7},{4,8},{5,9},{6,10},{7,11},{8,12},{9,13},{1... | collective-permute-start | bytes 786440 | tf_op jit(solution)/shard_map/ppermute | solution.py:41
  4.5 0.8 slice.3
  5.2 2.8 %collective-permute-start = (bf16[16,1024]{1,0:T(8,128)(2,1)S(1)}, bf16[16,1024]{1,0:T(8,128)(2,1)S(1)}, u32[]{:S(2)}, u32[]{:S(2)}) collective-permute-start(bf16[16,1024]{1,0:T(8,128)(2,1)S(1)} %slice.3), channel_id=1, source_target_pairs={{0,5},{1,6},{2,7},{3,8},{4,9},{5,10},{6,11},{7,12},{8,13},{9,14},{... | collective-permute-start | bytes 98312 | tf_op jit(solution)/shard_map/ppermute | solution.py:41
  8.1 0.1 pad_add_fusion.place_ref
  8.2 4.6 %fine_prepare.1 = (bf16[128,1024]{1,0:T(8,128)(2,1)S(1)}, bf16[3,1024,1024]{2,1,0:T(8,128)(2,1)S(1)}, bf16[1024,1024]{1,0:T(8,128)(2,1)S(1)}, bf16[128,1024]{1,0...) custom-call(s32[3]{0:T(128)S(1)} %pad_add_fusion.place_ref, ...), custom_call_target="tpu_custom_call" | custom-call | flops 900000000 | bytes 17000000 | tf_op jit(solution)/shard_map/fine_prepare/pallas_call | solution.py:475
  12.8 0.4 coarse_prepare.1
  13.2 0.3 collective-permute-done.tail_ref
  13.5 0.0 collective-permute-done.1.before_ref
  13.5 0.7 halo_send.1
  14.2 18.3 %all_to_all.25.slots_ref = bf16[4,128,1024]{2,1,0:T(8,128)(2,1)S(1)} all-to-all(bf16[4,128,1024]{2,1,0:T(8,128)(2,1)S(1)} %halo_send.1), channel_id=1, replica_groups=mesh['y'=4,'z_hi'=4,'core'=2,'z_lo'=2,'x'=4] {'x'}, dimensions={0} | all-to-all | bytes 2097152 | tf_op jit(solution)/shard_map/all_to_all | solution.py:45
  32.5 7.3 %fine_forward.1 = (bf16[640,1024]{1,0:T(8,128)(2,1)S(1)}, bf16[640,1024]{1,0:T(8,128)(2,1)S(1)}, f32[640,1024]{1,0:T(8,128)S(1)}, bf16[16,128,640]{2,1,0:T(8,128...) custom-call(s32[3]{0:T(128)S(1)} %pad_add_fusion.place_ref, ...), custom_call_target="tpu_custom_call" | custom-call | flops 4499999744 | bytes 20000000 | tf_op jit(solution)/shard_map/fine_forward/pallas_call | solution.py:499
  39.8 16.1 %all_to_all.26.got_ref = bf16[16,16,1024]{2,1,0:T(8,128)(2,1)S(1)} all-to-all(bf16[16,16,1024]{2,1,0:T(8,128)(2,1)S(1)} %get-tuple-element.72.message_ref), channel_id=1, replica_groups=mesh['y'=4,'z_hi'=4,'core'=2,'z_lo'=2,'x'=4] {'core','z_lo','x'}, dimensions={0} | all-to-all | bytes 1048576 | tf_op jit(solution)/shard_map/all_to_all | solution.py:45
  56.0 0.5 coarse_project.1
  56.5 15.6 %all_to_all.27 = bf16[4,128,256]{2,1,0:T(8,128)(2,1)S(1)} all-to-all(bf16[4,128,256]{2,1,0:T(8,128)(2,1)S(1)} %get-tuple-element.75), channel_id=1, replica_groups=mesh['y'=4,'z_hi'=4,'core'=2,'z_lo'=2,'x'=4] {'z_hi'}, dimensions={0} | all-to-all | bytes 524288 | tf_op jit(solution)/shard_map/all_to_all | solution.py:45
  72.1 0.1 repeated.1
  72.2 19.1 %all_to_all.28 = bf16[4,512,256]{2,1,0:T(8,128)(2,1)S(1)} all-to-all(bf16[4,512,256]{2,1,0:T(8,128)(2,1)S(1)} %repeated.1), channel_id=1, replica_groups=mesh['y'=4,'z_hi'=4,'core'=2,'z_lo'=2,'x'=4] {'y'}, dimensions={0} | all-to-all | bytes 2097152 | tf_op jit(solution)/shard_map/all_to_all | solution.py:45
  91.3 6.9 %coarse_attention.1 = bf16[16,16,1024]{2,1,0:T(8,128)(2,1)S(1)} custom-call(s32[3]{0:T(128)S(1)} %pad_add_fusion.place_ref, bf16[2048,256]{1,0:T(8,128)(2,1)S(1)} %bitcast.13, f32[128,256]{1,0:T(8,128)S(1)} %get-tuple-element.76.factor_ref, bf16[1024,256]{1,0:T(8,128)(2,1)S(1)} %get-tuple-element.73.in_w_ref, bf16[256,1024]{1,0:T(8,128)(2,1)S(1)} %get-tuple-element.74.out_w_ref), custom_call_target="tpu_custom_call" | custom-call | flops 1500000000 | bytes 3000000 | tf_op jit(solution)/shard_map/coarse_attention/pallas_call | solution.py:544
  98.3 13.3 %all_to_all.29.got_ref = bf16[16,16,1024]{2,1,0:T(8,128)(2,1)S(1)} all-to-all(bf16[16,16,1024]{2,1,0:T(8,128)(2,1)S(1)} %coarse_attention.1), channel_id=1, replica_groups=mesh['y'=4,'z_hi'=4,'core'=2,'z_lo'=2,'x'=4] {'core','z_lo','x'}, dimensions={0} | all-to-all | bytes 1048576 | tf_op jit(solution)/shard_map/all_to_all | solution.py:45
  111.5 0.2 coarse_finish.1
  111.7 2.0 %collective-permute-start.2 = (f32[1,1024]{1,0:T(1,128)S(1)}, f32[1,1024]{1,0:T(1,128)S(1)}, u32[]{:S(2)}, u32[]{:S(2)}) collective-permute-start(f32[1,1024]{1,0:T(1,128)S(1)} %get-tuple-element.79), channel_id=1, source_target_pairs={{1,0},{2,1},{3,2},{4,3},{5,4},{6,5},{7,6},{8,7},{9,8},{10,9},{11,1... | collective-permute-start | bytes 12296 | tf_op jit(solution)/shard_map/ppermute | solution.py:41
  113.7 3.5 %collective-permute-done.2.next_ref = f32[1,1024]{1,0:T(1,128)S(1)} collective-permute-done((f32[1,1024]{1,0:T(1,128)S(1)}, f32[1,1024]{1,0:T(1,128)S(1)}, u32[]{:S(2)}, u32[]{:S(2)}) %collective-permute-start.2) | collective-permute-done | bytes 4128 | tf_op jit(solution)/shard_map/ppermute | solution.py:41
  117.2 8.8 %fine_backward.1 = (bf16[128,1024]{1,0:T(8,128)(2,1)S(1)}, bf16[128,1024]{1,0:T(8,128)(2,1)S(1)}, bf16[128,1024]{1,0:T(8,128)(2,1)S(1)}, bf16[128,1024]{1,0:T(8,...) custom-call(s32[3]{0:T(128)S(1)} %pad_add_fusion.place_ref, bf16[128,1024]{1,0:T(8,128)(2,1)S(1)} %copy-done.1, ...), custom_call_target="tpu_custom_call" | custom-call | flops 5000000000 | bytes 20000000 | tf_op jit(solution)/shard_map/fine_backward/pallas_call | solution.py:572
  126.0 3.5 %collective-permute-start.3 = (bf16[128,1024]{1,0:T(8,128)(2,1)S(1)}, bf16[128,1024]{1,0:T(8,128)(2,1)S(1)}, u32[]{:S(2)}, u32[]{:S(2)}) collective-permute-start(bf16[128,1024]{1,0:T(8,128)(2,1)S(1)} %get-tuple-element.87), channel_id=1, source_target_pairs={{1,0},{2,1},{3,2},{4,3},{5,4},{6,5},{7,6},{8,7},{9,8},{10,9},{11,1... | collective-permute-start | bytes 786440 | tf_op jit(solution)/shard_map/ppermute | solution.py:41
  129.5 1.9 %collective-permute-start.4 = (bf16[128,1024]{1,0:T(8,128)(2,1)S(1)}, bf16[128,1024]{1,0:T(8,128)(2,1)S(1)}, u32[]{:S(2)}, u32[]{:S(2)}) collective-permute-start(bf16[128,1024]{1,0:T(8,128)(2,1)S(1)} %get-tuple-element.88), channel_id=1, source_target_pairs={{2,0},{3,1},{4,2},{5,3},{6,4},{7,5},{8,6},{9,7},{10,8},{11,9},{12,... | collective-permute-start | bytes 786440 | tf_op jit(solution)/shard_map/ppermute | solution.py:41
  131.5 2.0 %collective-permute-start.5 = (bf16[128,1024]{1,0:T(8,128)(2,1)S(1)}, bf16[128,1024]{1,0:T(8,128)(2,1)S(1)}, u32[]{:S(2)}, u32[]{:S(2)}) collective-permute-start(bf16[128,1024]{1,0:T(8,128)(2,1)S(1)} %get-tuple-element.89), channel_id=1, source_target_pairs={{3,0},{4,1},{5,2},{6,3},{7,4},{8,5},{9,6},{10,7},{11,8},{12,9},{13... | collective-permute-start | bytes 786440 | tf_op jit(solution)/shard_map/ppermute | solution.py:41
  133.4 4.5 %collective-permute-start.6 = (bf16[128,1024]{1,0:T(8,128)(2,1)S(1)}, bf16[128,1024]{1,0:T(8,128)(2,1)S(1)}, u32[]{:S(2)}, u32[]{:S(2)}) collective-permute-start(bf16[128,1024]{1,0:T(8,128)(2,1)S(1)} %get-tuple-element.90), channel_id=1, source_target_pairs={{4,0},{5,1},{6,2},{7,3},{8,4},{9,5},{10,6},{11,7},{12,8},{13,9},{1... | collective-permute-start | bytes 786440 | tf_op jit(solution)/shard_map/ppermute | solution.py:41
  137.9 0.8 fusion
  138.7 0.0 collective-permute-done.3.a1
  138.7 8.5 %collective-permute-done.4.a2 = bf16[128,1024]{1,0:T(8,128)(2,1)S(1)} collective-permute-done((bf16[128,1024]{1,0:T(8,128)(2,1)S(1)}, bf16[128,1024]{1,0:T(8,128)(2,1)S(1)}, u32[]{:S(2)}, u32[]{:S(2)}) %collective-permute-start.4) | collective-permute-done | bytes 262176 | tf_op jit(solution)/shard_map/ppermute | solution.py:41
  147.1 0.0 collective-permute-done.5.a3
  147.1 6.9 %collective-permute-done.6.a4 = bf16[128,1024]{1,0:T(8,128)(2,1)S(1)} collective-permute-done((bf16[128,1024]{1,0:T(8,128)(2,1)S(1)}, bf16[128,1024]{1,0:T(8,128)(2,1)S(1)}, u32[]{:S(2)}, u32[]{:S(2)}) %collective-permute-start.6) | collective-permute-done | bytes 262176 | tf_op jit(solution)/shard_map/ppermute | solution.py:41
  154.0 1.1 fine_finish.1
  (7 shorter events, 0.0 us)
Async XLA Ops:
  0.6 12.9 %collective-permute-start.1 = (bf16[128,1024]{1,0:T(8,128)(2,1)}, bf16[128,1024]{1,0:T(8,128)(2,1)S(1)}, u32[]{:S(2)}, u32[]{:S(2)}) collective-permute-start(bf16[128,1024]{1,0:T(8,128)(2,1)} %own_hbm.1), channel_id=1, source_target_pairs={{0,4},{1,5},{2,6},{3,7},{4,8},{5,9},{6,10},{7,11},{8,12},{9,13},{1... | collective-permute-start | bytes 786440 | tf_op jit(solution)/shard_map/ppermute | solution.py:41
  5.2 8.2 %collective-permute-start = (bf16[16,1024]{1,0:T(8,128)(2,1)S(1)}, bf16[16,1024]{1,0:T(8,128)(2,1)S(1)}, u32[]{:S(2)}, u32[]{:S(2)}) collective-permute-start(bf16[16,1024]{1,0:T(8,128)(2,1)S(1)} %slice.3), channel_id=1, source_target_pairs={{0,5},{1,6},{2,7},{3,8},{4,9},{5,10},{6,11},{7,12},{8,13},{9,14},{... | collective-permute-start | bytes 98312 | tf_op jit(solution)/shard_map/ppermute | solution.py:41
  8.2 4.7 %copy-start = (bf16[1024,3,128]{2,0,1:T(8,128)(2,1)S(1)}, bf16[1024,3,128]{2,0,1:T(8,128)(2,1)}, u32[]{:S(2)}) copy-start(bf16[1024,3,128]{2,0,1:T(8,128)(2,1)} %param.10) | copy-start | bytes 2359300
  8.2 4.7 %copy-start.2 = (bf16[128,1024]{1,0:T(8,128)(2,1)S(1)}, bf16[128,1024]{1,0:T(8,128)(2,1)}, u32[]{:S(2)}) copy-start(bf16[128,1024]{1,0:T(8,128)(2,1)} %back_ref.1) | copy-start | bytes 786436
  91.3 25.9 %copy-start.1 = (bf16[128,1024]{1,0:T(8,128)(2,1)S(1)}, bf16[128,1024]{1,0:T(8,128)(2,1)}, u32[]{:S(2)}) copy-start(bf16[128,1024]{1,0:T(8,128)(2,1)} %cot_ref.1) | copy-start | bytes 786436
  111.7 5.5 %collective-permute-start.2 = (f32[1,1024]{1,0:T(1,128)S(1)}, f32[1,1024]{1,0:T(1,128)S(1)}, u32[]{:S(2)}, u32[]{:S(2)}) collective-permute-start(f32[1,1024]{1,0:T(1,128)S(1)} %get-tuple-element.79), channel_id=1, source_target_pairs={{1,0},{2,1},{3,2},{4,3},{5,4},{6,5},{7,6},{8,7},{9,8},{10,9},{11,1... | collective-permute-start | bytes 12296 | tf_op jit(solution)/shard_map/ppermute | solution.py:41
  126.0 12.6 %collective-permute-start.3 = (bf16[128,1024]{1,0:T(8,128)(2,1)S(1)}, bf16[128,1024]{1,0:T(8,128)(2,1)S(1)}, u32[]{:S(2)}, u32[]{:S(2)}) collective-permute-start(bf16[128,1024]{1,0:T(8,128)(2,1)S(1)} %get-tuple-element.87), channel_id=1, source_target_pairs={{1,0},{2,1},{3,2},{4,3},{5,4},{6,5},{7,6},{8,7},{9,8},{10,9},{11,1... | collective-permute-start | bytes 786440 | tf_op jit(solution)/shard_map/ppermute | solution.py:41
  129.5 17.6 %collective-permute-start.4 = (bf16[128,1024]{1,0:T(8,128)(2,1)S(1)}, bf16[128,1024]{1,0:T(8,128)(2,1)S(1)}, u32[]{:S(2)}, u32[]{:S(2)}) collective-permute-start(bf16[128,1024]{1,0:T(8,128)(2,1)S(1)} %get-tuple-element.88), channel_id=1, source_target_pairs={{2,0},{3,1},{4,2},{5,3},{6,4},{7,5},{8,6},{9,7},{10,8},{11,9},{12,... | collective-permute-start | bytes 786440 | tf_op jit(solution)/shard_map/ppermute | solution.py:41
  131.5 15.7 %collective-permute-start.5 = (bf16[128,1024]{1,0:T(8,128)(2,1)S(1)}, bf16[128,1024]{1,0:T(8,128)(2,1)S(1)}, u32[]{:S(2)}, u32[]{:S(2)}) collective-permute-start(bf16[128,1024]{1,0:T(8,128)(2,1)S(1)} %get-tuple-element.89), channel_id=1, source_target_pairs={{3,0},{4,1},{5,2},{6,3},{7,4},{8,5},{9,6},{10,7},{11,8},{12,9},{13... | collective-permute-start | bytes 786440 | tf_op jit(solution)/shard_map/ppermute | solution.py:41
  133.4 20.6 %collective-permute-start.6 = (bf16[128,1024]{1,0:T(8,128)(2,1)S(1)}, bf16[128,1024]{1,0:T(8,128)(2,1)S(1)}, u32[]{:S(2)}, u32[]{:S(2)}) collective-permute-start(bf16[128,1024]{1,0:T(8,128)(2,1)S(1)} %get-tuple-element.90), channel_id=1, source_target_pairs={{4,0},{5,1},{6,2},{7,3},{8,4},{9,5},{10,6},{11,7},{12,8},{13,9},{1... | collective-permute-start | bytes 786440 | tf_op jit(solution)/shard_map/ppermute | solution.py:41

commit v8 on v7

--- a/solution.py
+++ b/solution.py
@@ -143,8 +143,8 @@
 
 def fine_forward_kernel(
     place_ref, tail_ref, slots_ref, own_ref, w_ref, out_w_ref, own_q_ref, own_k_ref, own_v_ref,
-    own_kf_ref, bias, cg_ref,
-    k_ref, v_ref, kf_ref, p_ref, att_ref, hid_ref, send_ref,
+    own_qf_ref, own_kf_ref, bias, cg_ref,
+    q_ref, k_ref, v_ref, qf_ref, kf_ref, p_ref, att_ref, hid_ref, send_ref,
     normed, acc,
 ):
     anchor = place_ref[0]
@@ -175,16 +175,19 @@
             key, k_factor = pair_norm(both[:, inner], low)
             key = key.astype(BF)
             value = both[:, WIDTH + part : WIDTH + part + PAIR].astype(BF)
-            k_ref[:HALO, outer] = key[:HALO]
-            k_ref[HALO:, outer] = own_k[:, inner]
-            v_ref[:HALO, outer] = value[:HALO]
-            v_ref[HALO:, outer] = own_v[:, inner]
-            kf_ref[:HALO, outer] = k_factor[:HALO]
-            kf_ref[HALO:, outer] = own_kf[:, inner]
             key = jnp.concatenate([key[:HALO], own_k[:, inner], key[HALO:]], axis=0)
             value = jnp.concatenate([value[:HALO], own_v[:, inner], value[HALO:]], axis=0)
-            before = pair_norm(extra[:, inner], low)[0].astype(BF).astype(F32)
-            scaled = jnp.concatenate([before, own_q[:, inner].astype(F32)], axis=0) * SCALE
+            k_ref[:, outer] = key
+            v_ref[:, outer] = value
+            kf_ref[:HALO, outer] = k_factor[:HALO]
+            kf_ref[HALO:OWN_KEYS, outer] = own_kf[:, inner]
+            kf_ref[OWN_KEYS:, outer] = k_factor[HALO:]
+            before, before_factor = pair_norm(extra[:, inner], low)
+            query = jnp.concatenate([before.astype(BF), own_q[:, inner]], axis=0)
+            q_ref[:, outer] = query
+            qf_ref[:EXTRA, outer] = before_factor
+            qf_ref[EXTRA:, outer] = own_qf_ref[:, outer]
+            scaled = query.astype(F32) * SCALE
             stacked = jnp.concatenate(
                 [jnp.where(low, scaled, 0.0), jnp.where(low, 0.0, scaled)], axis=0
             )
@@ -192,11 +195,11 @@
             total = jnp.sum(numer, axis=-1, keepdims=True)
             prob = (numer * (1.0 / jnp.where(total > 0.0, total, 1.0))).astype(BF)
             head = (first + part) // HEAD_DIM
-            p_ref[head] = prob[EXTRA:QUERIES, :OWN_KEYS]
-            p_ref[head + 1] = prob[QUERIES + EXTRA :, :OWN_KEYS]
+            p_ref[head] = prob[:QUERIES]
+            p_ref[head + 1] = prob[QUERIES:]
             twice = plain(prob, value)
             attended = jnp.where(low, twice[:QUERIES], twice[QUERIES:]).astype(BF)
-            att_ref[:, outer] = attended[EXTRA:]
+            att_ref[:, outer] = attended
             mixed.append(attended)
         acc[...] += plain(jnp.concatenate(mixed, axis=1), out_w_ref[here, :])
         return carry
@@ -358,19 +361,24 @@
 
 
 def fine_backward_kernel(
-    place_ref, cot_ref, spread_ref, next_ref, out_w_ref, w_ref, q_ref, k_ref, v_ref, qf_ref, kf_ref, p_ref,
+    place_ref, cot_ref, spread_ref, out_w_ref, w_ref, q_ref, k_ref, v_ref, qf_ref, kf_ref, p_ref,
     att_ref,
-    back1, back2, back3, back4, own_ref, hg_ref, hidden_grad, acc,
+    back1, back2, back3, back4, tail_ref, own_ref, hg_ref, hidden_grad, acc,
 ):
     low = low_lanes()
     block = (lax.broadcasted_iota(jnp.int32, (ROWS, 1), 0) + (POOL - 1)) // POOL
     added = jnp.zeros((ROWS, D), F32)
     for at in range(COARSE):
         added = jnp.where(block == at, spread_ref[at : at + 1, :], added)
-    added = jnp.where(block == COARSE, next_ref[0:1, :], added)
     total = cot_ref[...].astype(F32) + added
     hg_ref[...] = total
-    hidden_grad[...] = total.astype(BF)
+    counted = lax.broadcasted_iota(jnp.int32, (EXTRA, 1), 0) > EXTRA - POOL
+    hidden_grad[:EXTRA, :] = jnp.where(counted, spread_ref[0:1, :], 0.0).astype(BF)
+    hidden_grad[EXTRA:, :] = total.astype(BF)
+    backs = (back1, back2, back3, back4)
+    slots = len(backs)
+    nearest = lax.rem(place_ref[1] + (slots - 1), slots)
+    extra_at = pl.multiple_of(nearest * ROWS + (ROWS - EXTRA), EXTRA)
     acc[...] = jnp.zeros_like(acc)
 
     def one_step(step, carry):
@@ -400,10 +408,10 @@
                 [jnp.where(low, scaled, 0.0), jnp.where(low, 0.0, scaled)], axis=0
             ).astype(BF)
             head = (first + part) // HEAD_DIM
-            prob = p_ref[pl.ds(head, 2)].reshape(2 * ROWS, OWN_KEYS)
+            prob = p_ref[pl.ds(head, 2)].reshape(2 * QUERIES, ALL_KEYS)
             score_grad = (prob.astype(F32) * (last_last(grad, value) - delta)).astype(BF)
             twice = plain(score_grad, (key_wide * SCALE).astype(BF))
-            query_grad = jnp.where(low, twice[:ROWS], twice[ROWS:])
+            query_grad = jnp.where(low, twice[:QUERIES], twice[QUERIES:])
             key_grad = first_first(score_grad, query)
             value_grad = first_first(prob, grad)
             query_grads.append(pair_norm_back(query_grad, query_wide, qf_ref[:, outer], low).astype(BF))
@@ -413,15 +421,17 @@
         acc[...] += last_last(
             both, jnp.concatenate([w_ref[1, :, here], w_ref[2, :, here]], axis=1)
         )
-        acc[HALO:, :] += last_last(jnp.concatenate(query_grads, axis=1), w_ref[0, :, here])
+        from_query = last_last(jnp.concatenate(query_grads, axis=1), w_ref[0, :, here])
+        acc[pl.ds(extra_at, EXTRA), :] += from_query[:EXTRA]
+        acc[HALO:OWN_KEYS, :] += from_query[EXTRA:]
         return carry
 
     lax.fori_loop(0, D // WIDTH, one_step, 0, unroll=True)
-    backs = (back1, back2, back3, back4)
     for distance, ref in enumerate(backs, 1):
-        slot = lax.rem(place_ref[1] + (len(backs) - distance), len(backs))
+        slot = lax.rem(place_ref[1] + (slots - distance), slots)
         ref[...] = acc[pl.ds(pl.multiple_of(slot * ROWS, ROWS), ROWS), :].astype(BF)
-    own_ref[...] = acc[HALO:, :]
+    tail_ref[...] = acc[OWN_KEYS:, :].astype(BF)
+    own_ref[...] = acc[HALO:OWN_KEYS, :]
 
 
 def halo_send_kernel(place_ref, own_ref, before_ref, send_ref):
@@ -433,12 +443,16 @@
         send_ref[peer] = block_ref[...]
 
 
-def fine_finish_kernel(own_ref, a1, a2, a3, a4, hg_ref, tokens_ref, out_ref):
+def fine_finish_kernel(own_ref, a1, a2, a3, a4, tail_ref, next_ref, hg_ref, tokens_ref, out_ref):
     total = own_ref[...]
     for ref in (a1, a2, a3, a4):
         total = total + ref[...].astype(F32)
+    split = ROWS - EXTRA
+    total = jnp.concatenate([total[:split], total[split:] + tail_ref[...].astype(F32)], axis=0)
     normed, factor = row_norm(tokens_ref[...].astype(F32))
-    out_ref[...] = (hg_ref[...] + row_norm_back(total, normed, factor)).astype(BF)
+    after = lax.broadcasted_iota(jnp.int32, (ROWS, 1), 0) > ROWS - POOL
+    hidden_grad = hg_ref[...] + jnp.where(after, next_ref[...], 0.0)
+    out_ref[...] = (hidden_grad + row_norm_back(total, normed, factor)).astype(BF)
 
 
 def whole(shape):
@@ -495,17 +509,19 @@
     )(place, *(in_hbm(x) for x in (tokens, cotangent, weights, fine_out)))
 
 
-def fine_forward(place, tail, slots, own, weights, fine_out, own_q, own_k, own_v, own_kf, bias, cg, peers):
+def fine_forward(place, tail, slots, prepared, peers):
     return pl.pallas_call(
         fine_forward_kernel,
-        in_specs=[SCALAR] + [IN_VMEM] * 11,
-        out_specs=[IN_VMEM] * 7,
+        in_specs=[SCALAR] + [IN_VMEM] * 12,
+        out_specs=[IN_VMEM] * 9,
         out_shape=[
-            pltpu.VMEM((OWN_KEYS, D), BF),
-            pltpu.VMEM((OWN_KEYS, D), BF),
-            pltpu.VMEM((OWN_KEYS, D), F32),
-            pltpu.VMEM((HEADS, ROWS, OWN_KEYS), BF),
-            pltpu.VMEM((ROWS, D), BF),
+            pltpu.VMEM((QUERIES, D), BF),
+            pltpu.VMEM((ALL_KEYS, D), BF),
+            pltpu.VMEM((ALL_KEYS, D), BF),
+            pltpu.VMEM((QUERIES, D), F32),
+            pltpu.VMEM((ALL_KEYS, D), F32),
+            pltpu.VMEM((HEADS, QUERIES, ALL_KEYS), BF),
+            pltpu.VMEM((QUERIES, D), BF),
             shaped((ROWS, D), BF),
             shaped((peers, 2 * COARSE, D), BF),
         ],
@@ -513,7 +529,7 @@
         compiler_params=params(16),
         cost_estimate=cost(4_500_000_000, 20_000_000, 1_600_000),
         name="fine_forward",
-    )(place, tail, slots, own, weights, fine_out, own_q, own_k, own_v, own_kf, bias, cg)
+    )(place, tail, slots, *prepared)
 
 
 def coarse_prepare(core, weights, back):
@@ -566,20 +582,22 @@
 
 
 def fine_backward(
-    place, cotangent, spread, after, fine_out, weights, query, key, value, q_factor, k_factor, probs,
+    place, cotangent, spread, fine_out, weights, query, key, value, q_factor, k_factor, probs,
     attended,
 ):
     return pl.pallas_call(
         fine_backward_kernel,
-        in_specs=[SCALAR] + [IN_VMEM] * 12,
-        out_specs=[IN_VMEM] * 6,
-        out_shape=[shaped((ROWS, D), BF)] * 4 + [shaped((ROWS, D), F32)] * 2,
-        scratch_shapes=[pltpu.VMEM((ROWS, D), BF), pltpu.VMEM((OWN_KEYS, D), F32)],
+        in_specs=[SCALAR] + [IN_VMEM] * 11,
+        out_specs=[IN_VMEM] * 7,
+        out_shape=[shaped((ROWS, D), BF)] * 4
+        + [shaped((EXTRA, D), BF)]
+        + [shaped((ROWS, D), F32)] * 2,
+        scratch_shapes=[pltpu.VMEM((QUERIES, D), BF), pltpu.VMEM((ALL_KEYS, D), F32)],
         compiler_params=params(16),
         cost_estimate=cost(5_000_000_000, 20_000_000),
         name="fine_backward",
     )(
-        place, cotangent, spread, after, fine_out, weights, query, key, value, q_factor, k_factor, probs,
+        place, cotangent, spread, fine_out, weights, query, key, value, q_factor, k_factor, probs,
         attended,
     )
 
@@ -607,14 +625,14 @@
     )(block)
 
 
-def fine_finish(own, arrived, hidden_grad, tokens):
+def fine_finish(own, arrived, tail, after, hidden_grad, tokens):
     return pl.pallas_call(
         fine_finish_kernel,
         out_shape=shaped((ROWS, D), BF),
         compiler_params=params(VMEM_MIB),
         cost_estimate=cost(1_000_000, 3_000_000),
         name="fine_finish",
-    )(own, *arrived, hidden_grad, tokens)
+    )(own, *arrived, tail, after, hidden_grad, tokens)
 
 
 def per_device(tokens, cotangent, fine_qkv, fine_out, coarse_qkv, coarse_out):
@@ -637,13 +655,10 @@
     tail, row_before, prepared, coarse_weights, place = lax.optimization_barrier(
         (tail, row_before, prepared, coarse_weights, place)
     )
-    own, weights, fine_out, query, own_key, own_value, q_factor, own_k_factor, bias, coarse_grad = prepared
+    own, weights, fine_out, *_, coarse_grad = prepared
     coarse_in, coarse_back = coarse_weights
     slots = exchanged(halo_send(place, own, row_before, columns_along), "x")
-    key, value, k_factor, probs, attended, hidden, message = fine_forward(
-        place, tail, slots, own, weights, fine_out, query, own_key, own_value, own_k_factor, bias,
-        coarse_grad, peers,
-    )
+    *kept, hidden, message = fine_forward(place, tail, slots, prepared, peers)
     gathered = exchanged(message, GROUP)
     near, further = lax.axis_size("z_hi"), lax.axis_size("y")
     coarse_send, coarse_factor = coarse_project(gathered, coarse_in, coarse_back, near)
@@ -653,16 +668,17 @@
     partial = coarse_attention(place, everyone, coarse_factor, coarse_in, coarse_back)
     returned = exchanged(partial, GROUP)
     spread, first, state = coarse_finish(returned, message, coarse_grad)
-    after = shifted_by(first, -1)
     output = (
         hidden.astype(F32) + jnp.repeat(state.astype(BF), POOL, axis=0).astype(F32)
     ).astype(BF)
-    *backs, own_grad, hidden_grad = fine_backward(
-        place, cotangent, spread, after, fine_out, weights, query, key, value, q_factor, k_factor, probs,
-        attended,
+    *backs, tail_back, own_grad, hidden_grad = fine_backward(
+        place, cotangent, spread, fine_out, weights, *kept
     )
     arrived = [shifted_by(rows, -steps) for steps, rows in enumerate(backs, 1)]
-    return (output, fine_finish(own_grad, arrived, hidden_grad, own))
+    tail_back, first, _ = lax.optimization_barrier((tail_back, first, own_grad))
+    tail_arrived = shifted_by(tail_back, -(columns_along + 1))
+    after = shifted_by(first, -1)
+    return (output, fine_finish(own_grad, arrived, tail_arrived, after, hidden_grad, own))
 
 
 def solution(mesh):

time: 156 us -> 162 us (1.038)
  the two profiles are of different devices: /device:TPU:64 before, /device:TPU:71 now
where the time goes in v8:
time: 162 us; the launch traced here: 161 us
  blocking collectives  77.6 us (48%)
  Pallas kernels  33.5 us (21%)
  starting transfers between devices  28.7 us (18%)
  waiting for transfers between devices  18.9 us (12%)
    all_to_all x5, blocking collectives, exchanged(): return lax.all_to_all(pieces, axes, 0, 0, tiled=True)  77.6 us
    ppermute x8, starting transfers between devices, shifted_by(): lax.ppermute(value, LINE, [(source, source + steps) for source in range(f...  28.7 us
    ppermute x8, waiting for transfers between devices, shifted_by(): lax.ppermute(value, LINE, [(source, source + steps) for source in range(f...  18.9 us
    pallas_call x1, Pallas kernels, fine_backward(): pl.pallas_call(fine_backward_kernel, in_specs=[SCALAR] + [IN_VMEM] * 11,...  11.5 us
    pallas_call x1, Pallas kernels, fine_forward(): pl.pallas_call(fine_forward_kernel, in_specs=[SCALAR] + [IN_VMEM] * 12, o...  7.42 us
    pallas_call x1, Pallas kernels, coarse_attention(): pl.pallas_call(coarse_attention_kernel, in_specs=[SCALAR] + [IN_VMEM] * 4...  6.95 us
    pallas_call x1, Pallas kernels, fine_prepare(): pl.pallas_call(fine_prepare_kernel, in_specs=[SCALAR] + [anywhere] * 4, o...  4.64 us
  transfers between devices with their start and end apart: 8, of which 2 were waited for; matrix products, arithmetic and copies ran while one was open for 1% of the time, Pallas kernels for 3%

profile of v8, /device:TPU:71, one launch (start us, length us, event | category | flops | bytes accessed | tf_op | source)
XLA Modules:
  0.0 161.0 jit_solution(11392575636967003854)
XLA Ops:
  0.6 3.5 %collective-permute-start.1 = (bf16[128,1024]{1,0:T(8,128)(2,1)}, bf16[128,1024]{1,0:T(8,128)(2,1)S(1)}, u32[]{:S(2)}, u32[]{:S(2)}) collective-permute-start(bf16[128,1024]{1,0:T(8,128)(2,1)} %own_hbm.1), channel_id=1, source_target_pairs={{0,4},{1,5},{2,6},{3,7},{4,8},{5,9},{6,10},{7,11},{8,12},{9,13},{1... | collective-permute-start | bytes 786440 | tf_op jit(solution)/shard_map/ppermute | solution.py:41
  4.2 0.8 slice.3
  5.0 6.0 %collective-permute-start = (bf16[16,1024]{1,0:T(8,128)(2,1)S(1)}, bf16[16,1024]{1,0:T(8,128)(2,1)S(1)}, u32[]{:S(2)}, u32[]{:S(2)}) collective-permute-start(bf16[16,1024]{1,0:T(8,128)(2,1)S(1)} %slice.3), channel_id=1, source_target_pairs={{0,5},{1,6},{2,7},{3,8},{4,9},{5,10},{6,11},{7,12},{8,13},{9,14},{... | collective-permute-start | bytes 98312 | tf_op jit(solution)/shard_map/ppermute | solution.py:41
  10.9 0.1 pad_add_fusion.place_ref
  11.0 4.6 %fine_prepare.1 = (bf16[128,1024]{1,0:T(8,128)(2,1)S(1)}, bf16[3,1024,1024]{2,1,0:T(8,128)(2,1)S(1)}, bf16[1024,1024]{1,0:T(8,128)(2,1)S(1)}, bf16[128,1024]{1,0...) custom-call(s32[3]{0:T(128)S(1)} %pad_add_fusion.place_ref, ...), custom_call_target="tpu_custom_call" | custom-call | flops 900000000 | bytes 17000000 | tf_op jit(solution)/shard_map/fine_prepare/pallas_call | solution.py:489
  15.7 0.4 coarse_prepare.1
  16.1 0.0 collective-permute-done.tail_ref
  16.1 0.0 collective-permute-done.1.before_ref
  16.1 0.7 halo_send.1
  16.8 15.9 %all_to_all.25.slots_ref = bf16[4,128,1024]{2,1,0:T(8,128)(2,1)S(1)} all-to-all(bf16[4,128,1024]{2,1,0:T(8,128)(2,1)S(1)} %halo_send.1), channel_id=1, replica_groups=mesh['y'=4,'z_hi'=4,'core'=2,'z_lo'=2,'x'=4] {'x'}, dimensions={0} | all-to-all | bytes 2097152 | tf_op jit(solution)/shard_map/all_to_all | solution.py:45
  32.7 7.4 %fine_forward.1 = (bf16[144,1024]{1,0:T(8,128)(2,1)S(1)}, bf16[656,1024]{1,0:T(8,128)(2,1)S(1)}, bf16[656,1024]{1,0:T(8,128)(2,1)S(1)}, f32[144,1024]{1,0:T(8,12...) custom-call(s32[3]{0:T(128)S(1)} %pad_add_fusion.place_ref, ...), custom_call_target="tpu_custom_call" | custom-call | flops 4499999744 | bytes 20000000 | tf_op jit(solution)/shard_map/fine_forward/pallas_call | solution.py:513
  40.1 13.8 %all_to_all.26.got_ref = bf16[16,16,1024]{2,1,0:T(8,128)(2,1)S(1)} all-to-all(bf16[16,16,1024]{2,1,0:T(8,128)(2,1)S(1)} %get-tuple-element.78.message_ref), channel_id=1, replica_groups=mesh['y'=4,'z_hi'=4,'core'=2,'z_lo'=2,'x'=4] {'core','z_lo','x'}, dimensions={0} | all-to-all | bytes 1048576 | tf_op jit(solution)/shard_map/all_to_all | solution.py:45
  53.9 0.5 coarse_project.1
  54.4 11.9 %all_to_all.27 = bf16[4,128,256]{2,1,0:T(8,128)(2,1)S(1)} all-to-all(bf16[4,128,256]{2,1,0:T(8,128)(2,1)S(1)} %get-tuple-element.81), channel_id=1, replica_groups=mesh['y'=4,'z_hi'=4,'core'=2,'z_lo'=2,'x'=4] {'z_hi'}, dimensions={0} | all-to-all | bytes 524288 | tf_op jit(solution)/shard_map/all_to_all | solution.py:45
  66.3 0.1 repeated.1
  66.3 14.5 %all_to_all.28 = bf16[4,512,256]{2,1,0:T(8,128)(2,1)S(1)} all-to-all(bf16[4,512,256]{2,1,0:T(8,128)(2,1)S(1)} %repeated.1), channel_id=1, replica_groups=mesh['y'=4,'z_hi'=4,'core'=2,'z_lo'=2,'x'=4] {'y'}, dimensions={0} | all-to-all | bytes 2097152 | tf_op jit(solution)/shard_map/all_to_all | solution.py:45
  80.8 6.9 %coarse_attention.1 = bf16[16,16,1024]{2,1,0:T(8,128)(2,1)S(1)} custom-call(s32[3]{0:T(128)S(1)} %pad_add_fusion.place_ref, bf16[2048,256]{1,0:T(8,128)(2,1)S(1)} %bitcast.13, f32[128,256]{1,0:T(8,128)S(1)} %get-tuple-element.82.factor_ref, bf16[1024,256]{1,0:T(8,128)(2,1)S(1)} %get-tuple-element.79.in_w_ref, bf16[256,1024]{1,0:T(8,128)(2,1)S(1)} %get-tuple-element.80.out_w_ref), custom_call_target="tpu_custom_call" | custom-call | flops 1500000000 | bytes 3000000 | tf_op jit(solution)/shard_map/coarse_attention/pallas_call | solution.py:560
  87.8 21.6 %all_to_all.29.got_ref = bf16[16,16,1024]{2,1,0:T(8,128)(2,1)S(1)} all-to-all(bf16[16,16,1024]{2,1,0:T(8,128)(2,1)S(1)} %coarse_attention.1), channel_id=1, replica_groups=mesh['y'=4,'z_hi'=4,'core'=2,'z_lo'=2,'x'=4] {'core','z_lo','x'}, dimensions={0} | all-to-all | bytes 1048576 | tf_op jit(solution)/shard_map/all_to_all | solution.py:45
  109.4 0.2 coarse_finish.1
  109.6 11.5 %fine_backward.1 = (bf16[128,1024]{1,0:T(8,128)(2,1)S(1)}, bf16[128,1024]{1,0:T(8,128)(2,1)S(1)}, bf16[128,1024]{1,0:T(8,128)(2,1)S(1)}, bf16[128,1024]{1,0:T(8,...) custom-call(s32[3]{0:T(128)S(1)} %pad_add_fusion.place_ref, ...), custom_call_target="tpu_custom_call" | custom-call | flops 5000000000 | bytes 20000000 | tf_op jit(solution)/shard_map/fine_backward/pallas_call | solution.py:588
  121.1 2.2 %collective-permute-start.2 = (bf16[128,1024]{1,0:T(8,128)(2,1)S(1)}, bf16[128,1024]{1,0:T(8,128)(2,1)S(1)}, u32[]{:S(2)}, u32[]{:S(2)}) collective-permute-start(bf16[128,1024]{1,0:T(8,128)(2,1)S(1)} %get-tuple-element.93), channel_id=1, source_target_pairs={{1,0},{2,1},{3,2},{4,3},{5,4},{6,5},{7,6},{8,7},{9,8},{10,9},{11,1... | collective-permute-start | bytes 786440 | tf_op jit(solution)/shard_map/ppermute | solution.py:41
  123.4 5.7 %collective-permute-start.3 = (bf16[128,1024]{1,0:T(8,128)(2,1)S(1)}, bf16[128,1024]{1,0:T(8,128)(2,1)S(1)}, u32[]{:S(2)}, u32[]{:S(2)}) collective-permute-start(bf16[128,1024]{1,0:T(8,128)(2,1)S(1)} %get-tuple-element.94), channel_id=1, source_target_pairs={{2,0},{3,1},{4,2},{5,3},{6,4},{7,5},{8,6},{9,7},{10,8},{11,9},{12,... | collective-permute-start | bytes 786440 | tf_op jit(solution)/shard_map/ppermute | solution.py:41
  129.0 3.7 %collective-permute-start.4 = (bf16[128,1024]{1,0:T(8,128)(2,1)S(1)}, bf16[128,1024]{1,0:T(8,128)(2,1)S(1)}, u32[]{:S(2)}, u32[]{:S(2)}) collective-permute-start(bf16[128,1024]{1,0:T(8,128)(2,1)S(1)} %get-tuple-element.95), channel_id=1, source_target_pairs={{3,0},{4,1},{5,2},{6,3},{7,4},{8,5},{9,6},{10,7},{11,8},{12,9},{13... | collective-permute-start | bytes 786440 | tf_op jit(solution)/shard_map/ppermute | solution.py:41
  132.7 3.2 %collective-permute-start.5 = (bf16[128,1024]{1,0:T(8,128)(2,1)S(1)}, bf16[128,1024]{1,0:T(8,128)(2,1)S(1)}, u32[]{:S(2)}, u32[]{:S(2)}) collective-permute-start(bf16[128,1024]{1,0:T(8,128)(2,1)S(1)} %get-tuple-element.96), channel_id=1, source_target_pairs={{4,0},{5,1},{6,2},{7,3},{8,4},{9,5},{10,6},{11,7},{12,8},{13,9},{1... | collective-permute-start | bytes 786440 | tf_op jit(solution)/shard_map/ppermute | solution.py:41
  135.9 2.5 %collective-permute-start.7 = (f32[1,1024]{1,0:T(1,128)S(1)}, f32[1,1024]{1,0:T(1,128)S(1)}, u32[]{:S(2)}, u32[]{:S(2)}) collective-permute-start(f32[1,1024]{1,0:T(1,128)S(1)} %get-tuple-element.100), channel_id=1, source_target_pairs={{1,0},{2,1},{3,2},{4,3},{5,4},{6,5},{7,6},{8,7},{9,8},{10,9},{11,1... | collective-permute-start | bytes 12296 | tf_op jit(solution)/shard_map/ppermute | solution.py:41
  138.4 12.1 %collective-permute-done.7.next_ref = f32[1,1024]{1,0:T(1,128)S(1)} collective-permute-done((f32[1,1024]{1,0:T(1,128)S(1)}, f32[1,1024]{1,0:T(1,128)S(1)}, u32[]{:S(2)}, u32[]{:S(2)}) %collective-permute-start.7) | collective-permute-done | bytes 4128 | tf_op jit(solution)/shard_map/ppermute | solution.py:41
  150.5 1.9 %collective-permute-start.6 = (bf16[16,1024]{1,0:T(8,128)(2,1)S(1)}, bf16[16,1024]{1,0:T(8,128)(2,1)S(1)}, u32[]{:S(2)}, u32[]{:S(2)}) collective-permute-start(bf16[16,1024]{1,0:T(8,128)(2,1)S(1)} %get-tuple-element.99), channel_id=1, source_target_pairs={{5,0},{6,1},{7,2},{8,3},{9,4},{10,5},{11,6},{12,7},{13,8},{14,9},{... | collective-permute-start | bytes 98312 | tf_op jit(solution)/shard_map/ppermute | solution.py:41
  152.4 0.8 fusion
  153.2 6.8 %collective-permute-done.6.tail_ref = bf16[16,1024]{1,0:T(8,128)(2,1)S(1)} collective-permute-done((bf16[16,1024]{1,0:T(8,128)(2,1)S(1)}, bf16[16,1024]{1,0:T(8,128)(2,1)S(1)}, u32[]{:S(2)}, u32[]{:S(2)}) %collective-permute-start.6) | collective-permute-done | bytes 32800 | tf_op jit(solution)/shard_map/ppermute | solution.py:41
  159.9 0.0 collective-permute-done.2.a1
  159.9 0.0 collective-permute-done.3.a2
  160.0 1.1 fine_finish.1
  (9 shorter events, 0.0 us)
Async XLA Ops:
  0.6 15.4 %collective-permute-start.1 = (bf16[128,1024]{1,0:T(8,128)(2,1)}, bf16[128,1024]{1,0:T(8,128)(2,1)S(1)}, u32[]{:S(2)}, u32[]{:S(2)}) collective-permute-start(bf16[128,1024]{1,0:T(8,128)(2,1)} %own_hbm.1), channel_id=1, source_target_pairs={{0,4},{1,5},{2,6},{3,7},{4,8},{5,9},{6,10},{7,11},{8,12},{9,13},{1... | collective-permute-start | bytes 786440 | tf_op jit(solution)/shard_map/ppermute | solution.py:41
  5.0 11.1 %collective-permute-start = (bf16[16,1024]{1,0:T(8,128)(2,1)S(1)}, bf16[16,1024]{1,0:T(8,128)(2,1)S(1)}, u32[]{:S(2)}, u32[]{:S(2)}) collective-permute-start(bf16[16,1024]{1,0:T(8,128)(2,1)S(1)} %slice.3), channel_id=1, source_target_pairs={{0,5},{1,6},{2,7},{3,8},{4,9},{5,10},{6,11},{7,12},{8,13},{9,14},{... | collective-permute-start | bytes 98312 | tf_op jit(solution)/shard_map/ppermute | solution.py:41
  11.0 4.7 %copy-start.1 = (bf16[1024,3,128]{2,0,1:T(8,128)(2,1)S(1)}, bf16[1024,3,128]{2,0,1:T(8,128)(2,1)}, u32[]{:S(2)}) copy-start(bf16[1024,3,128]{2,0,1:T(8,128)(2,1)} %param.10) | copy-start | bytes 2359300
  11.0 4.7 %copy-start.2 = (bf16[128,1024]{1,0:T(8,128)(2,1)S(1)}, bf16[128,1024]{1,0:T(8,128)(2,1)}, u32[]{:S(2)}) copy-start(bf16[128,1024]{1,0:T(8,128)(2,1)} %back_ref.1) | copy-start | bytes 786436
  80.8 28.7 %copy-start = (bf16[128,1024]{1,0:T(8,128)(2,1)S(1)}, bf16[128,1024]{1,0:T(8,128)(2,1)}, u32[]{:S(2)}) copy-start(bf16[128,1024]{1,0:T(8,128)(2,1)} %cot_ref.1) | copy-start | bytes 786436
  121.1 38.8 %collective-permute-start.2 = (bf16[128,1024]{1,0:T(8,128)(2,1)S(1)}, bf16[128,1024]{1,0:T(8,128)(2,1)S(1)}, u32[]{:S(2)}, u32[]{:S(2)}) collective-permute-start(bf16[128,1024]{1,0:T(8,128)(2,1)S(1)} %get-tuple-element.93), channel_id=1, source_target_pairs={{1,0},{2,1},{3,2},{4,3},{5,4},{6,5},{7,6},{8,7},{9,8},{10,9},{11,1... | collective-permute-start | bytes 786440 | tf_op jit(solution)/shard_map/ppermute | solution.py:41
  123.4 36.6 %collective-permute-start.3 = (bf16[128,1024]{1,0:T(8,128)(2,1)S(1)}, bf16[128,1024]{1,0:T(8,128)(2,1)S(1)}, u32[]{:S(2)}, u32[]{:S(2)}) collective-permute-start(bf16[128,1024]{1,0:T(8,128)(2,1)S(1)} %get-tuple-element.94), channel_id=1, source_target_pairs={{2,0},{3,1},{4,2},{5,3},{6,4},{7,5},{8,6},{9,7},{10,8},{11,9},{12,... | collective-permute-start | bytes 786440 | tf_op jit(solution)/shard_map/ppermute | solution.py:41
  129.0 30.9 %collective-permute-start.4 = (bf16[128,1024]{1,0:T(8,128)(2,1)S(1)}, bf16[128,1024]{1,0:T(8,128)(2,1)S(1)}, u32[]{:S(2)}, u32[]{:S(2)}) collective-permute-start(bf16[128,1024]{1,0:T(8,128)(2,1)S(1)} %get-tuple-element.95), channel_id=1, source_target_pairs={{3,0},{4,1},{5,2},{6,3},{7,4},{8,5},{9,6},{10,7},{11,8},{12,9},{13... | collective-permute-start | bytes 786440 | tf_op jit(solution)/shard_map/ppermute | solution.py:41
  132.7 27.2 %collective-permute-start.5 = (bf16[128,1024]{1,0:T(8,128)(2,1)S(1)}, bf16[128,1024]{1,0:T(8,128)(2,1)S(1)}, u32[]{:S(2)}, u32[]{:S(2)}) collective-permute-start(bf16[128,1024]{1,0:T(8,128)(2,1)S(1)} %get-tuple-element.96), channel_id=1, source_target_pairs={{4,0},{5,1},{6,2},{7,3},{8,4},{9,5},{10,6},{11,7},{12,8},{13,9},{1... | collective-permute-start | bytes 786440 | tf_op jit(solution)/shard_map/ppermute | solution.py:41
  135.9 14.6 %collective-permute-start.7 = (f32[1,1024]{1,0:T(1,128)S(1)}, f32[1,1024]{1,0:T(1,128)S(1)}, u32[]{:S(2)}, u32[]{:S(2)}) collective-permute-start(f32[1,1024]{1,0:T(1,128)S(1)} %get-tuple-element.100), channel_id=1, source_target_pairs={{1,0},{2,1},{3,2},{4,3},{5,4},{6,5},{7,6},{8,7},{9,8},{10,9},{11,1... | collective-permute-start | bytes 12296 | tf_op jit(solution)/shard_map/ppermute | solution.py:41
  150.5 9.4 %collective-permute-start.6 = (bf16[16,1024]{1,0:T(8,128)(2,1)S(1)}, bf16[16,1024]{1,0:T(8,128)(2,1)S(1)}, u32[]{:S(2)}, u32[]{:S(2)}) collective-permute-start(bf16[16,1024]{1,0:T(8,128)(2,1)S(1)} %get-tuple-element.99), channel_id=1, source_target_pairs={{5,0},{6,1},{7,2},{8,3},{9,4},{10,5},{11,6},{12,7},{13,8},{14,9},{... | collective-permute-start | bytes 98312 | tf_op jit(solution)/shard_map/ppermute | solution.py:41

commit v9 on v8

--- a/solution.py
+++ b/solution.py
@@ -349,14 +349,12 @@
     send_ref[...] = jnp.concatenate([normed_grad, mixed], axis=1).astype(BF)
 
 
-def coarse_finish_kernel(got_ref, message_ref, cg_ref, spread_ref, first_ref, state_ref):
+def coarse_finish_kernel(got_ref, message_ref, cg_ref, spread_ref, state_ref):
     summed = jnp.sum(got_ref[...].astype(F32), axis=0)
     pooled = message_ref[0].astype(F32)[:COARSE]
     normed, factor = row_norm(pooled)
     pooled_grad = cg_ref[...] + row_norm_back(summed[:COARSE], normed, factor)
-    spread = pooled_grad * (1.0 / POOL)
-    spread_ref[...] = spread
-    first_ref[...] = spread[:1]
+    spread_ref[...] = pooled_grad * (1.0 / POOL)
     state_ref[...] = pooled + summed[COARSE:]
 
 
@@ -429,7 +427,8 @@
     lax.fori_loop(0, D // WIDTH, one_step, 0, unroll=True)
     for distance, ref in enumerate(backs, 1):
         slot = lax.rem(place_ref[1] + (slots - distance), slots)
-        ref[...] = acc[pl.ds(pl.multiple_of(slot * ROWS, ROWS), ROWS), :].astype(BF)
+        ref[:ROWS, :] = acc[pl.ds(pl.multiple_of(slot * ROWS, ROWS), ROWS), :].astype(BF)
+    back1[ROWS:, :] = jnp.broadcast_to(spread_ref[0:1, :], (EXTRA, D)).astype(BF)
     tail_ref[...] = acc[OWN_KEYS:, :].astype(BF)
     own_ref[...] = acc[HALO:OWN_KEYS, :]
 
@@ -443,15 +442,15 @@
         send_ref[peer] = block_ref[...]
 
 
-def fine_finish_kernel(own_ref, a1, a2, a3, a4, tail_ref, next_ref, hg_ref, tokens_ref, out_ref):
+def fine_finish_kernel(own_ref, a1, a2, a3, a4, tail_ref, hg_ref, tokens_ref, out_ref):
     total = own_ref[...]
     for ref in (a1, a2, a3, a4):
-        total = total + ref[...].astype(F32)
+        total = total + ref[:ROWS, :].astype(F32)
     split = ROWS - EXTRA
     total = jnp.concatenate([total[:split], total[split:] + tail_ref[...].astype(F32)], axis=0)
     normed, factor = row_norm(tokens_ref[...].astype(F32))
     after = lax.broadcasted_iota(jnp.int32, (ROWS, 1), 0) > ROWS - POOL
-    hidden_grad = hg_ref[...] + jnp.where(after, next_ref[...], 0.0)
+    hidden_grad = hg_ref[...] + jnp.where(after, a1[ROWS:, :].astype(F32)[:1], 0.0)
     out_ref[...] = (hidden_grad + row_norm_back(total, normed, factor)).astype(BF)
 
 
@@ -573,8 +572,8 @@
         coarse_finish_kernel,
         grid=(1,),
         in_specs=[whole(returned.shape), whole((1, 2 * COARSE, D)), whole((COARSE, D))],
-        out_specs=[whole((COARSE, D)), whole((1, D)), whole((COARSE, D))],
-        out_shape=[shaped((COARSE, D), F32), shaped((1, D), F32), shaped((COARSE, D), F32)],
+        out_specs=[whole((COARSE, D))] * 2,
+        out_shape=[shaped((COARSE, D), F32)] * 2,
         compiler_params=params(VMEM_MIB),
         cost_estimate=cost(1_000_000, 1_000_000),
         name="coarse_finish",
@@ -589,7 +588,8 @@
         fine_backward_kernel,
         in_specs=[SCALAR] + [IN_VMEM] * 11,
         out_specs=[IN_VMEM] * 7,
-        out_shape=[shaped((ROWS, D), BF)] * 4
+        out_shape=[shaped((ROWS + EXTRA, D), BF)]
+        + [shaped((ROWS, D), BF)] * 3
         + [shaped((EXTRA, D), BF)]
         + [shaped((ROWS, D), F32)] * 2,
         scratch_shapes=[pltpu.VMEM((QUERIES, D), BF), pltpu.VMEM((ALL_KEYS, D), F32)],
@@ -625,14 +625,14 @@
     )(block)
 
 
-def fine_finish(own, arrived, tail, after, hidden_grad, tokens):
+def fine_finish(own, arrived, tail, hidden_grad, tokens):
     return pl.pallas_call(
         fine_finish_kernel,
         out_shape=shaped((ROWS, D), BF),
         compiler_params=params(VMEM_MIB),
         cost_estimate=cost(1_000_000, 3_000_000),
         name="fine_finish",
-    )(own, *arrived, tail, after, hidden_grad, tokens)
+    )(own, *arrived, tail, hidden_grad, tokens)
 
 
 def per_device(tokens, cotangent, fine_qkv, fine_out, coarse_qkv, coarse_out):
@@ -667,7 +667,7 @@
     everyone = exchanged(repeated(nearby, further), "y").reshape(groups * group_rows, 2 * PAIR)
     partial = coarse_attention(place, everyone, coarse_factor, coarse_in, coarse_back)
     returned = exchanged(partial, GROUP)
-    spread, first, state = coarse_finish(returned, message, coarse_grad)
+    spread, state = coarse_finish(returned, message, coarse_grad)
     output = (
         hidden.astype(F32) + jnp.repeat(state.astype(BF), POOL, axis=0).astype(F32)
     ).astype(BF)
@@ -675,10 +675,8 @@
         place, cotangent, spread, fine_out, weights, *kept
     )
     arrived = [shifted_by(rows, -steps) for steps, rows in enumerate(backs, 1)]
-    tail_back, first, _ = lax.optimization_barrier((tail_back, first, own_grad))
     tail_arrived = shifted_by(tail_back, -(columns_along + 1))
-    after = shifted_by(first, -1)
-    return (output, fine_finish(own_grad, arrived, tail_arrived, after, hidden_grad, own))
+    return (output, fine_finish(own_grad, arrived, tail_arrived, hidden_grad, own))
 
 
 def solution(mesh):

time: 162 us -> 157 us (0.969)
  the two profiles are of different devices: /device:TPU:71 before, /device:TPU:64 now
where the time goes in v9:
time: 157 us; the launch traced here: 155 us
  blocking collectives  82.5 us (53%)
  Pallas kernels  33.5 us (21%)
  starting transfers between devices  23.4 us (15%)
  waiting for transfers between devices  13.4 us (9%)
    all_to_all x5, blocking collectives, exchanged(): return lax.all_to_all(pieces, axes, 0, 0, tiled=True)  82.5 us
    ppermute x7, starting transfers between devices, shifted_by(): lax.ppermute(value, LINE, [(source, source + steps) for source in range(f...  23.4 us
    ppermute x7, waiting for transfers between devices, shifted_by(): lax.ppermute(value, LINE, [(source, source + steps) for source in range(f...  13.4 us
    pallas_call x1, Pallas kernels, fine_backward(): pl.pallas_call(fine_backward_kernel, in_specs=[SCALAR] + [IN_VMEM] * 11,...  11.5 us
    pallas_call x1, Pallas kernels, fine_forward(): pl.pallas_call(fine_forward_kernel, in_specs=[SCALAR] + [IN_VMEM] * 12, o...  7.42 us
    pallas_call x1, Pallas kernels, coarse_attention(): pl.pallas_call(coarse_attention_kernel, in_specs=[SCALAR] + [IN_VMEM] * 4...  6.94 us
    pallas_call x1, Pallas kernels, fine_prepare(): pl.pallas_call(fine_prepare_kernel, in_specs=[SCALAR] + [anywhere] * 4, o...  4.64 us
  transfers between devices with their start and end apart: 7, of which 3 were waited for; matrix products, arithmetic and copies ran while one was open for 1% of the time, Pallas kernels for 3%

profile of v9, /device:TPU:64, one launch (start us, length us, event | category | flops | bytes accessed | tf_op | source)
XLA Modules:
  0.0 155.2 jit_solution(7336001285885168005)
XLA Ops:
  0.6 3.8 %collective-permute-start.1 = (bf16[128,1024]{1,0:T(8,128)(2,1)}, bf16[128,1024]{1,0:T(8,128)(2,1)S(1)}, u32[]{:S(2)}, u32[]{:S(2)}) collective-permute-start(bf16[128,1024]{1,0:T(8,128)(2,1)} %own_hbm.1), channel_id=1, source_target_pairs={{0,4},{1,5},{2,6},{3,7},{4,8},{5,9},{6,10},{7,11},{8,12},{9,13},{1... | collective-permute-start | bytes 786440 | tf_op jit(solution)/shard_map/ppermute | solution.py:41
  4.5 0.8 slice.3
  5.2 2.8 %collective-permute-start = (bf16[16,1024]{1,0:T(8,128)(2,1)S(1)}, bf16[16,1024]{1,0:T(8,128)(2,1)S(1)}, u32[]{:S(2)}, u32[]{:S(2)}) collective-permute-start(bf16[16,1024]{1,0:T(8,128)(2,1)S(1)} %slice.3), channel_id=1, source_target_pairs={{0,5},{1,6},{2,7},{3,8},{4,9},{5,10},{6,11},{7,12},{8,13},{9,14},{... | collective-permute-start | bytes 98312 | tf_op jit(solution)/shard_map/ppermute | solution.py:41
  8.1 0.1 pad_add_fusion.place_ref
  8.2 4.6 %fine_prepare.1 = (bf16[128,1024]{1,0:T(8,128)(2,1)S(1)}, bf16[3,1024,1024]{2,1,0:T(8,128)(2,1)S(1)}, bf16[1024,1024]{1,0:T(8,128)(2,1)S(1)}, bf16[128,1024]{1,0...) custom-call(s32[3]{0:T(128)S(1)} %pad_add_fusion.place_ref, ...), custom_call_target="tpu_custom_call" | custom-call | flops 900000000 | bytes 17000000 | tf_op jit(solution)/shard_map/fine_prepare/pallas_call | solution.py:488
  12.8 0.4 coarse_prepare.1
  13.2 0.3 collective-permute-done.tail_ref
  13.5 0.0 collective-permute-done.1.before_ref
  13.5 0.7 halo_send.1
  14.2 18.3 %all_to_all.25.slots_ref = bf16[4,128,1024]{2,1,0:T(8,128)(2,1)S(1)} all-to-all(bf16[4,128,1024]{2,1,0:T(8,128)(2,1)S(1)} %halo_send.1), channel_id=1, replica_groups=mesh['y'=4,'z_hi'=4,'core'=2,'z_lo'=2,'x'=4] {'x'}, dimensions={0} | all-to-all | bytes 2097152 | tf_op jit(solution)/shard_map/all_to_all | solution.py:45
  32.5 7.4 %fine_forward.1 = (bf16[144,1024]{1,0:T(8,128)(2,1)S(1)}, bf16[656,1024]{1,0:T(8,128)(2,1)S(1)}, bf16[656,1024]{1,0:T(8,128)(2,1)S(1)}, f32[144,1024]{1,0:T(8,12...) custom-call(s32[3]{0:T(128)S(1)} %pad_add_fusion.place_ref, ...), custom_call_target="tpu_custom_call" | custom-call | flops 4499999744 | bytes 20000000 | tf_op jit(solution)/shard_map/fine_forward/pallas_call | solution.py:512
  40.0 16.1 %all_to_all.26.got_ref = bf16[16,16,1024]{2,1,0:T(8,128)(2,1)S(1)} all-to-all(bf16[16,16,1024]{2,1,0:T(8,128)(2,1)S(1)} %get-tuple-element.75.message_ref), channel_id=1, replica_groups=mesh['y'=4,'z_hi'=4,'core'=2,'z_lo'=2,'x'=4] {'core','z_lo','x'}, dimensions={0} | all-to-all | bytes 1048576 | tf_op jit(solution)/shard_map/all_to_all | solution.py:45
  56.1 0.5 coarse_project.1
  56.6 15.6 %all_to_all.27 = bf16[4,128,256]{2,1,0:T(8,128)(2,1)S(1)} all-to-all(bf16[4,128,256]{2,1,0:T(8,128)(2,1)S(1)} %get-tuple-element.78), channel_id=1, replica_groups=mesh['y'=4,'z_hi'=4,'core'=2,'z_lo'=2,'x'=4] {'z_hi'}, dimensions={0} | all-to-all | bytes 524288 | tf_op jit(solution)/shard_map/all_to_all | solution.py:45
  72.3 0.1 repeated.1
  72.3 19.1 %all_to_all.28 = bf16[4,512,256]{2,1,0:T(8,128)(2,1)S(1)} all-to-all(bf16[4,512,256]{2,1,0:T(8,128)(2,1)S(1)} %repeated.1), channel_id=1, replica_groups=mesh['y'=4,'z_hi'=4,'core'=2,'z_lo'=2,'x'=4] {'y'}, dimensions={0} | all-to-all | bytes 2097152 | tf_op jit(solution)/shard_map/all_to_all | solution.py:45
  91.4 6.9 %coarse_attention.1 = bf16[16,16,1024]{2,1,0:T(8,128)(2,1)S(1)} custom-call(s32[3]{0:T(128)S(1)} %pad_add_fusion.place_ref, bf16[2048,256]{1,0:T(8,128)(2,1)S(1)} %bitcast.13, f32[128,256]{1,0:T(8,128)S(1)} %get-tuple-element.79.factor_ref, bf16[1024,256]{1,0:T(8,128)(2,1)S(1)} %get-tuple-element.76.in_w_ref, bf16[256,1024]{1,0:T(8,128)(2,1)S(1)} %get-tuple-element.77.out_w_ref), custom_call_target="tpu_custom_call" | custom-call | flops 1500000000 | bytes 3000000 | tf_op jit(solution)/shard_map/coarse_attention/pallas_call | solution.py:559
  98.4 13.3 %all_to_all.29.got_ref = bf16[16,16,1024]{2,1,0:T(8,128)(2,1)S(1)} all-to-all(bf16[16,16,1024]{2,1,0:T(8,128)(2,1)S(1)} %coarse_attention.1), channel_id=1, replica_groups=mesh['y'=4,'z_hi'=4,'core'=2,'z_lo'=2,'x'=4] {'core','z_lo','x'}, dimensions={0} | all-to-all | bytes 1048576 | tf_op jit(solution)/shard_map/all_to_all | solution.py:45
  111.7 0.2 coarse_finish.1
  111.9 11.5 %fine_backward.1 = (bf16[144,1024]{1,0:T(8,128)(2,1)S(1)}, bf16[128,1024]{1,0:T(8,128)(2,1)S(1)}, bf16[128,1024]{1,0:T(8,128)(2,1)S(1)}, bf16[128,1024]{1,0:T(8,...) custom-call(s32[3]{0:T(128)S(1)} %pad_add_fusion.place_ref, ...), custom_call_target="tpu_custom_call" | custom-call | flops 5000000000 | bytes 20000000 | tf_op jit(solution)/shard_map/fine_backward/pallas_call | solution.py:587
  123.4 2.0 %collective-permute-start.2 = (bf16[144,1024]{1,0:T(8,128)(2,1)S(1)}, bf16[144,1024]{1,0:T(8,128)(2,1)S(1)}, u32[]{:S(2)}, u32[]{:S(2)}) collective-permute-start(bf16[144,1024]{1,0:T(8,128)(2,1)S(1)} %get-tuple-element.90), channel_id=1, source_target_pairs={{1,0},{2,1},{3,2},{4,3},{5,4},{6,5},{7,6},{8,7},{9,8},{10,9},{11,1... | collective-permute-start | bytes 884744 | tf_op jit(solution)/shard_map/ppermute | solution.py:41
  125.3 2.9 %collective-permute-start.3 = (bf16[128,1024]{1,0:T(8,128)(2,1)S(1)}, bf16[128,1024]{1,0:T(8,128)(2,1)S(1)}, u32[]{:S(2)}, u32[]{:S(2)}) collective-permute-start(bf16[128,1024]{1,0:T(8,128)(2,1)S(1)} %get-tuple-element.91), channel_id=1, source_target_pairs={{2,0},{3,1},{4,2},{5,3},{6,4},{7,5},{8,6},{9,7},{10,8},{11,9},{12,... | collective-permute-start | bytes 786440 | tf_op jit(solution)/shard_map/ppermute | solution.py:41
  128.3 1.9 %collective-permute-start.4 = (bf16[128,1024]{1,0:T(8,128)(2,1)S(1)}, bf16[128,1024]{1,0:T(8,128)(2,1)S(1)}, u32[]{:S(2)}, u32[]{:S(2)}) collective-permute-start(bf16[128,1024]{1,0:T(8,128)(2,1)S(1)} %get-tuple-element.92), channel_id=1, source_target_pairs={{3,0},{4,1},{5,2},{6,3},{7,4},{8,5},{9,6},{10,7},{11,8},{12,9},{13... | collective-permute-start | bytes 786440 | tf_op jit(solution)/shard_map/ppermute | solution.py:41
  130.2 4.1 %collective-permute-start.5 = (bf16[128,1024]{1,0:T(8,128)(2,1)S(1)}, bf16[128,1024]{1,0:T(8,128)(2,1)S(1)}, u32[]{:S(2)}, u32[]{:S(2)}) collective-permute-start(bf16[128,1024]{1,0:T(8,128)(2,1)S(1)} %get-tuple-element.93), channel_id=1, source_target_pairs={{4,0},{5,1},{6,2},{7,3},{8,4},{9,5},{10,6},{11,7},{12,8},{13,9},{1... | collective-permute-start | bytes 786440 | tf_op jit(solution)/shard_map/ppermute | solution.py:41
  134.3 5.9 %collective-permute-start.6 = (bf16[16,1024]{1,0:T(8,128)(2,1)S(1)}, bf16[16,1024]{1,0:T(8,128)(2,1)S(1)}, u32[]{:S(2)}, u32[]{:S(2)}) collective-permute-start(bf16[16,1024]{1,0:T(8,128)(2,1)S(1)} %get-tuple-element.94), channel_id=1, source_target_pairs={{5,0},{6,1},{7,2},{8,3},{9,4},{10,5},{11,6},{12,7},{13,8},{14,9},{... | collective-permute-start | bytes 98312 | tf_op jit(solution)/shard_map/ppermute | solution.py:41
  140.2 0.8 fusion
  141.0 10.1 %collective-permute-done.6.tail_ref = bf16[16,1024]{1,0:T(8,128)(2,1)S(1)} collective-permute-done((bf16[16,1024]{1,0:T(8,128)(2,1)S(1)}, bf16[16,1024]{1,0:T(8,128)(2,1)S(1)}, u32[]{:S(2)}, u32[]{:S(2)}) %collective-permute-start.6) | collective-permute-done | bytes 32800 | tf_op jit(solution)/shard_map/ppermute | solution.py:41
  151.1 0.0 collective-permute-done.3.a2
  151.1 0.0 collective-permute-done.4.a3
  151.1 3.0 %collective-permute-done.5.a4 = bf16[128,1024]{1,0:T(8,128)(2,1)S(1)} collective-permute-done((bf16[128,1024]{1,0:T(8,128)(2,1)S(1)}, bf16[128,1024]{1,0:T(8,128)(2,1)S(1)}, u32[]{:S(2)}, u32[]{:S(2)}) %collective-permute-start.5) | collective-permute-done | bytes 262176 | tf_op jit(solution)/shard_map/ppermute | solution.py:41
  154.1 0.0 collective-permute-done.2.a1
  154.1 1.1 fine_finish.1
  (7 shorter events, 0.0 us)
Async XLA Ops:
  0.6 12.9 %collective-permute-start.1 = (bf16[128,1024]{1,0:T(8,128)(2,1)}, bf16[128,1024]{1,0:T(8,128)(2,1)S(1)}, u32[]{:S(2)}, u32[]{:S(2)}) collective-permute-start(bf16[128,1024]{1,0:T(8,128)(2,1)} %own_hbm.1), channel_id=1, source_target_pairs={{0,4},{1,5},{2,6},{3,7},{4,8},{5,9},{6,10},{7,11},{8,12},{9,13},{1... | collective-permute-start | bytes 786440 | tf_op jit(solution)/shard_map/ppermute | solution.py:41
  5.2 8.2 %collective-permute-start = (bf16[16,1024]{1,0:T(8,128)(2,1)S(1)}, bf16[16,1024]{1,0:T(8,128)(2,1)S(1)}, u32[]{:S(2)}, u32[]{:S(2)}) collective-permute-start(bf16[16,1024]{1,0:T(8,128)(2,1)S(1)} %slice.3), channel_id=1, source_target_pairs={{0,5},{1,6},{2,7},{3,8},{4,9},{5,10},{6,11},{7,12},{8,13},{9,14},{... | collective-permute-start | bytes 98312 | tf_op jit(solution)/shard_map/ppermute | solution.py:41
  8.2 4.7 %copy-start.1 = (bf16[1024,3,128]{2,0,1:T(8,128)(2,1)S(1)}, bf16[1024,3,128]{2,0,1:T(8,128)(2,1)}, u32[]{:S(2)}) copy-start(bf16[1024,3,128]{2,0,1:T(8,128)(2,1)} %param.10) | copy-start | bytes 2359300
  8.2 4.7 %copy-start.2 = (bf16[128,1024]{1,0:T(8,128)(2,1)S(1)}, bf16[128,1024]{1,0:T(8,128)(2,1)}, u32[]{:S(2)}) copy-start(bf16[128,1024]{1,0:T(8,128)(2,1)} %back_ref.1) | copy-start | bytes 786436
  91.4 20.4 %copy-start = (bf16[128,1024]{1,0:T(8,128)(2,1)S(1)}, bf16[128,1024]{1,0:T(8,128)(2,1)}, u32[]{:S(2)}) copy-start(bf16[128,1024]{1,0:T(8,128)(2,1)} %cot_ref.1) | copy-start | bytes 786436
  123.4 30.8 %collective-permute-start.2 = (bf16[144,1024]{1,0:T(8,128)(2,1)S(1)}, bf16[144,1024]{1,0:T(8,128)(2,1)S(1)}, u32[]{:S(2)}, u32[]{:S(2)}) collective-permute-start(bf16[144,1024]{1,0:T(8,128)(2,1)S(1)} %get-tuple-element.90), channel_id=1, source_target_pairs={{1,0},{2,1},{3,2},{4,3},{5,4},{6,5},{7,6},{8,7},{9,8},{10,9},{11,1... | collective-permute-start | bytes 884744 | tf_op jit(solution)/shard_map/ppermute | solution.py:41
  125.3 25.7 %collective-permute-start.3 = (bf16[128,1024]{1,0:T(8,128)(2,1)S(1)}, bf16[128,1024]{1,0:T(8,128)(2,1)S(1)}, u32[]{:S(2)}, u32[]{:S(2)}) collective-permute-start(bf16[128,1024]{1,0:T(8,128)(2,1)S(1)} %get-tuple-element.91), channel_id=1, source_target_pairs={{2,0},{3,1},{4,2},{5,3},{6,4},{7,5},{8,6},{9,7},{10,8},{11,9},{12,... | collective-permute-start | bytes 786440 | tf_op jit(solution)/shard_map/ppermute | solution.py:41
  128.3 22.8 %collective-permute-start.4 = (bf16[128,1024]{1,0:T(8,128)(2,1)S(1)}, bf16[128,1024]{1,0:T(8,128)(2,1)S(1)}, u32[]{:S(2)}, u32[]{:S(2)}) collective-permute-start(bf16[128,1024]{1,0:T(8,128)(2,1)S(1)} %get-tuple-element.92), channel_id=1, source_target_pairs={{3,0},{4,1},{5,2},{6,3},{7,4},{8,5},{9,6},{10,7},{11,8},{12,9},{13... | collective-permute-start | bytes 786440 | tf_op jit(solution)/shard_map/ppermute | solution.py:41
  130.2 23.9 %collective-permute-start.5 = (bf16[128,1024]{1,0:T(8,128)(2,1)S(1)}, bf16[128,1024]{1,0:T(8,128)(2,1)S(1)}, u32[]{:S(2)}, u32[]{:S(2)}) collective-permute-start(bf16[128,1024]{1,0:T(8,128)(2,1)S(1)} %get-tuple-element.93), channel_id=1, source_target_pairs={{4,0},{5,1},{6,2},{7,3},{8,4},{9,5},{10,6},{11,7},{12,8},{13,9},{1... | collective-permute-start | bytes 786440 | tf_op jit(solution)/shard_map/ppermute | solution.py:41
  134.3 16.8 %collective-permute-start.6 = (bf16[16,1024]{1,0:T(8,128)(2,1)S(1)}, bf16[16,1024]{1,0:T(8,128)(2,1)S(1)}, u32[]{:S(2)}, u32[]{:S(2)}) collective-permute-start(bf16[16,1024]{1,0:T(8,128)(2,1)S(1)} %get-tuple-element.94), channel_id=1, source_target_pairs={{5,0},{6,1},{7,2},{8,3},{9,4},{10,5},{11,6},{12,7},{13,8},{14,9},{... | collective-permute-start | bytes 98312 | tf_op jit(solution)/shard_map/ppermute | solution.py:41

commit v10 on v7

--- a/solution.py
+++ b/solution.py
@@ -661,7 +661,7 @@
         place, cotangent, spread, after, fine_out, weights, query, key, value, q_factor, k_factor, probs,
         attended,
     )
-    arrived = [shifted_by(rows, -steps) for steps, rows in enumerate(backs, 1)]
+    arrived = [shifted_by(backs[steps - 1], -steps) for steps in range(len(backs), 0, -1)]
     return (output, fine_finish(own_grad, arrived, hidden_grad, own))
 
 

time: 156 us -> 155 us (level)
  waiting for transfers between devices: 19.1 us -> 16.2 us
    ppermute x7, waiting for transfers between devices: 19.1 us -> 16.2 us  [shifted_by(): lax.ppermute(value, LINE, [(source, source + steps) for source in range(f...]
  transfers between devices with their start and end apart: 7 -> 7, of which waited for: 4 -> 5; matrix products, arithmetic and copies ran while one was open for 1% -> 1% of each run, Pallas kernels for 3% -> 3%
where the time goes in v10:
time: 155 us; the launch traced here: 153 us
  blocking collectives  82.5 us (53%)
  Pallas kernels  30.6 us (20%)
  starting transfers between devices  21 us (14%)
  waiting for transfers between devices  16.2 us (10%)
    all_to_all x5, blocking collectives, exchanged(): return lax.all_to_all(pieces, axes, 0, 0, tiled=True)  82.5 us
    ppermute x7, starting transfers between devices, shifted_by(): lax.ppermute(value, LINE, [(source, source + steps) for source in range(f...  21 us
    ppermute x7, waiting for transfers between devices, shifted_by(): lax.ppermute(value, LINE, [(source, source + steps) for source in range(f...  16.2 us
    pallas_call x1, Pallas kernels, fine_backward(): pl.pallas_call(fine_backward_kernel, in_specs=[SCALAR] + [IN_VMEM] * 12,...  8.79 us
    pallas_call x1, Pallas kernels, fine_forward(): pl.pallas_call(fine_forward_kernel, in_specs=[SCALAR] + [IN_VMEM] * 11, o...  7.3 us
    pallas_call x1, Pallas kernels, coarse_attention(): pl.pallas_call(coarse_attention_kernel, in_specs=[SCALAR] + [IN_VMEM] * 4...  6.95 us
    pallas_call x1, Pallas kernels, fine_prepare(): pl.pallas_call(fine_prepare_kernel, in_specs=[SCALAR] + [anywhere] * 4, o...  4.64 us
  transfers between devices with their start and end apart: 7, of which 5 were waited for; matrix products, arithmetic and copies ran while one was open for 1% of the time, Pallas kernels for 3%

profile of v10, /device:TPU:64, one launch (start us, length us, event | category | flops | bytes accessed | tf_op | source)
XLA Modules:
  0.0 152.8 jit_solution(5695463269178048992)
XLA Ops:
  0.6 3.8 %collective-permute-start.1 = (bf16[128,1024]{1,0:T(8,128)(2,1)}, bf16[128,1024]{1,0:T(8,128)(2,1)S(1)}, u32[]{:S(2)}, u32[]{:S(2)}) collective-permute-start(bf16[128,1024]{1,0:T(8,128)(2,1)} %own_hbm.1), channel_id=1, source_target_pairs={{0,4},{1,5},{2,6},{3,7},{4,8},{5,9},{6,10},{7,11},{8,12},{9,13},{1... | collective-permute-start | bytes 786440 | tf_op jit(solution)/shard_map/ppermute | solution.py:41
  4.5 0.8 slice.3
  5.2 2.8 %collective-permute-start = (bf16[16,1024]{1,0:T(8,128)(2,1)S(1)}, bf16[16,1024]{1,0:T(8,128)(2,1)S(1)}, u32[]{:S(2)}, u32[]{:S(2)}) collective-permute-start(bf16[16,1024]{1,0:T(8,128)(2,1)S(1)} %slice.3), channel_id=1, source_target_pairs={{0,5},{1,6},{2,7},{3,8},{4,9},{5,10},{6,11},{7,12},{8,13},{9,14},{... | collective-permute-start | bytes 98312 | tf_op jit(solution)/shard_map/ppermute | solution.py:41
  8.1 0.1 pad_add_fusion.place_ref
  8.2 4.6 %fine_prepare.1 = (bf16[128,1024]{1,0:T(8,128)(2,1)S(1)}, bf16[3,1024,1024]{2,1,0:T(8,128)(2,1)S(1)}, bf16[1024,1024]{1,0:T(8,128)(2,1)S(1)}, bf16[128,1024]{1,0...) custom-call(s32[3]{0:T(128)S(1)} %pad_add_fusion.place_ref, ...), custom_call_target="tpu_custom_call" | custom-call | flops 900000000 | bytes 17000000 | tf_op jit(solution)/shard_map/fine_prepare/pallas_call | solution.py:475
  12.8 0.4 coarse_prepare.1
  13.2 0.3 collective-permute-done.tail_ref
  13.5 0.0 collective-permute-done.1.before_ref
  13.5 0.7 halo_send.1
  14.2 18.3 %all_to_all.25.slots_ref = bf16[4,128,1024]{2,1,0:T(8,128)(2,1)S(1)} all-to-all(bf16[4,128,1024]{2,1,0:T(8,128)(2,1)S(1)} %halo_send.1), channel_id=1, replica_groups=mesh['y'=4,'z_hi'=4,'core'=2,'z_lo'=2,'x'=4] {'x'}, dimensions={0} | all-to-all | bytes 2097152 | tf_op jit(solution)/shard_map/all_to_all | solution.py:45
  32.5 7.3 %fine_forward.1 = (bf16[640,1024]{1,0:T(8,128)(2,1)S(1)}, bf16[640,1024]{1,0:T(8,128)(2,1)S(1)}, f32[640,1024]{1,0:T(8,128)S(1)}, bf16[16,128,640]{2,1,0:T(8,128...) custom-call(s32[3]{0:T(128)S(1)} %pad_add_fusion.place_ref, ...), custom_call_target="tpu_custom_call" | custom-call | flops 4499999744 | bytes 20000000 | tf_op jit(solution)/shard_map/fine_forward/pallas_call | solution.py:499
  39.8 16.1 %all_to_all.26.got_ref = bf16[16,16,1024]{2,1,0:T(8,128)(2,1)S(1)} all-to-all(bf16[16,16,1024]{2,1,0:T(8,128)(2,1)S(1)} %get-tuple-element.72.message_ref), channel_id=1, replica_groups=mesh['y'=4,'z_hi'=4,'core'=2,'z_lo'=2,'x'=4] {'core','z_lo','x'}, dimensions={0} | all-to-all | bytes 1048576 | tf_op jit(solution)/shard_map/all_to_all | solution.py:45
  56.0 0.5 coarse_project.1
  56.5 15.6 %all_to_all.27 = bf16[4,128,256]{2,1,0:T(8,128)(2,1)S(1)} all-to-all(bf16[4,128,256]{2,1,0:T(8,128)(2,1)S(1)} %get-tuple-element.75), channel_id=1, replica_groups=mesh['y'=4,'z_hi'=4,'core'=2,'z_lo'=2,'x'=4] {'z_hi'}, dimensions={0} | all-to-all | bytes 524288 | tf_op jit(solution)/shard_map/all_to_all | solution.py:45
  72.1 0.1 repeated.1
  72.2 19.1 %all_to_all.28 = bf16[4,512,256]{2,1,0:T(8,128)(2,1)S(1)} all-to-all(bf16[4,512,256]{2,1,0:T(8,128)(2,1)S(1)} %repeated.1), channel_id=1, replica_groups=mesh['y'=4,'z_hi'=4,'core'=2,'z_lo'=2,'x'=4] {'y'}, dimensions={0} | all-to-all | bytes 2097152 | tf_op jit(solution)/shard_map/all_to_all | solution.py:45
  91.3 6.9 %coarse_attention.1 = bf16[16,16,1024]{2,1,0:T(8,128)(2,1)S(1)} custom-call(s32[3]{0:T(128)S(1)} %pad_add_fusion.place_ref, bf16[2048,256]{1,0:T(8,128)(2,1)S(1)} %bitcast.13, f32[128,256]{1,0:T(8,128)S(1)} %get-tuple-element.76.factor_ref, bf16[1024,256]{1,0:T(8,128)(2,1)S(1)} %get-tuple-element.73.in_w_ref, bf16[256,1024]{1,0:T(8,128)(2,1)S(1)} %get-tuple-element.74.out_w_ref), custom_call_target="tpu_custom_call" | custom-call | flops 1500000000 | bytes 3000000 | tf_op jit(solution)/shard_map/coarse_attention/pallas_call | solution.py:544
  98.3 13.3 %all_to_all.29.got_ref = bf16[16,16,1024]{2,1,0:T(8,128)(2,1)S(1)} all-to-all(bf16[16,16,1024]{2,1,0:T(8,128)(2,1)S(1)} %coarse_attention.1), channel_id=1, replica_groups=mesh['y'=4,'z_hi'=4,'core'=2,'z_lo'=2,'x'=4] {'core','z_lo','x'}, dimensions={0} | all-to-all | bytes 1048576 | tf_op jit(solution)/shard_map/all_to_all | solution.py:45
  111.5 0.2 coarse_finish.1
  111.7 2.0 %collective-permute-start.2 = (f32[1,1024]{1,0:T(1,128)S(1)}, f32[1,1024]{1,0:T(1,128)S(1)}, u32[]{:S(2)}, u32[]{:S(2)}) collective-permute-start(f32[1,1024]{1,0:T(1,128)S(1)} %get-tuple-element.79), channel_id=1, source_target_pairs={{1,0},{2,1},{3,2},{4,3},{5,4},{6,5},{7,6},{8,7},{9,8},{10,9},{11,1... | collective-permute-start | bytes 12296 | tf_op jit(solution)/shard_map/ppermute | solution.py:41
  113.7 3.5 %collective-permute-done.2.next_ref = f32[1,1024]{1,0:T(1,128)S(1)} collective-permute-done((f32[1,1024]{1,0:T(1,128)S(1)}, f32[1,1024]{1,0:T(1,128)S(1)}, u32[]{:S(2)}, u32[]{:S(2)}) %collective-permute-start.2) | collective-permute-done | bytes 4128 | tf_op jit(solution)/shard_map/ppermute | solution.py:41
  117.2 8.8 %fine_backward.1 = (bf16[128,1024]{1,0:T(8,128)(2,1)S(1)}, bf16[128,1024]{1,0:T(8,128)(2,1)S(1)}, bf16[128,1024]{1,0:T(8,128)(2,1)S(1)}, bf16[128,1024]{1,0:T(8,...) custom-call(s32[3]{0:T(128)S(1)} %pad_add_fusion.place_ref, bf16[128,1024]{1,0:T(8,128)(2,1)S(1)} %copy-done.1, ...), custom_call_target="tpu_custom_call" | custom-call | flops 5000000000 | bytes 20000000 | tf_op jit(solution)/shard_map/fine_backward/pallas_call | solution.py:572
  126.0 1.9 %collective-permute-start.3 = (bf16[128,1024]{1,0:T(8,128)(2,1)S(1)}, bf16[128,1024]{1,0:T(8,128)(2,1)S(1)}, u32[]{:S(2)}, u32[]{:S(2)}) collective-permute-start(bf16[128,1024]{1,0:T(8,128)(2,1)S(1)} %get-tuple-element.87), channel_id=1, source_target_pairs={{4,0},{5,1},{6,2},{7,3},{8,4},{9,5},{10,6},{11,7},{12,8},{13,9},{1... | collective-permute-start | bytes 786440 | tf_op jit(solution)/shard_map/ppermute | solution.py:41
  128.0 1.9 %collective-permute-start.4 = (bf16[128,1024]{1,0:T(8,128)(2,1)S(1)}, bf16[128,1024]{1,0:T(8,128)(2,1)S(1)}, u32[]{:S(2)}, u32[]{:S(2)}) collective-permute-start(bf16[128,1024]{1,0:T(8,128)(2,1)S(1)} %get-tuple-element.88), channel_id=1, source_target_pairs={{3,0},{4,1},{5,2},{6,3},{7,4},{8,5},{9,6},{10,7},{11,8},{12,9},{13... | collective-permute-start | bytes 786440 | tf_op jit(solution)/shard_map/ppermute | solution.py:41
  129.9 6.7 %collective-permute-start.5 = (bf16[128,1024]{1,0:T(8,128)(2,1)S(1)}, bf16[128,1024]{1,0:T(8,128)(2,1)S(1)}, u32[]{:S(2)}, u32[]{:S(2)}) collective-permute-start(bf16[128,1024]{1,0:T(8,128)(2,1)S(1)} %get-tuple-element.89), channel_id=1, source_target_pairs={{2,0},{3,1},{4,2},{5,3},{6,4},{7,5},{8,6},{9,7},{10,8},{11,9},{12,... | collective-permute-start | bytes 786440 | tf_op jit(solution)/shard_map/ppermute | solution.py:41
  136.6 1.9 %collective-permute-start.6 = (bf16[128,1024]{1,0:T(8,128)(2,1)S(1)}, bf16[128,1024]{1,0:T(8,128)(2,1)S(1)}, u32[]{:S(2)}, u32[]{:S(2)}) collective-permute-start(bf16[128,1024]{1,0:T(8,128)(2,1)S(1)} %get-tuple-element.90), channel_id=1, source_target_pairs={{1,0},{2,1},{3,2},{4,3},{5,4},{6,5},{7,6},{8,7},{9,8},{10,9},{11,1... | collective-permute-start | bytes 786440 | tf_op jit(solution)/shard_map/ppermute | solution.py:41
  138.5 0.8 fusion
  139.3 0.0 collective-permute-done.3.a1
  139.3 0.9 collective-permute-done.4.a2
  140.2 7.5 %collective-permute-done.5.a3 = bf16[128,1024]{1,0:T(8,128)(2,1)S(1)} collective-permute-done((bf16[128,1024]{1,0:T(8,128)(2,1)S(1)}, bf16[128,1024]{1,0:T(8,128)(2,1)S(1)}, u32[]{:S(2)}, u32[]{:S(2)}) %collective-permute-start.5) | collective-permute-done | bytes 262176 | tf_op jit(solution)/shard_map/ppermute | solution.py:41
  147.7 4.0 %collective-permute-done.6.a4 = bf16[128,1024]{1,0:T(8,128)(2,1)S(1)} collective-permute-done((bf16[128,1024]{1,0:T(8,128)(2,1)S(1)}, bf16[128,1024]{1,0:T(8,128)(2,1)S(1)}, u32[]{:S(2)}, u32[]{:S(2)}) %collective-permute-start.6) | collective-permute-done | bytes 262176 | tf_op jit(solution)/shard_map/ppermute | solution.py:41
  151.7 1.1 fine_finish.1
  (7 shorter events, 0.0 us)
Async XLA Ops:
  0.6 12.9 %collective-permute-start.1 = (bf16[128,1024]{1,0:T(8,128)(2,1)}, bf16[128,1024]{1,0:T(8,128)(2,1)S(1)}, u32[]{:S(2)}, u32[]{:S(2)}) collective-permute-start(bf16[128,1024]{1,0:T(8,128)(2,1)} %own_hbm.1), channel_id=1, source_target_pairs={{0,4},{1,5},{2,6},{3,7},{4,8},{5,9},{6,10},{7,11},{8,12},{9,13},{1... | collective-permute-start | bytes 786440 | tf_op jit(solution)/shard_map/ppermute | solution.py:41
  5.2 8.2 %collective-permute-start = (bf16[16,1024]{1,0:T(8,128)(2,1)S(1)}, bf16[16,1024]{1,0:T(8,128)(2,1)S(1)}, u32[]{:S(2)}, u32[]{:S(2)}) collective-permute-start(bf16[16,1024]{1,0:T(8,128)(2,1)S(1)} %slice.3), channel_id=1, source_target_pairs={{0,5},{1,6},{2,7},{3,8},{4,9},{5,10},{6,11},{7,12},{8,13},{9,14},{... | collective-permute-start | bytes 98312 | tf_op jit(solution)/shard_map/ppermute | solution.py:41
  8.2 4.7 %copy-start = (bf16[1024,3,128]{2,0,1:T(8,128)(2,1)S(1)}, bf16[1024,3,128]{2,0,1:T(8,128)(2,1)}, u32[]{:S(2)}) copy-start(bf16[1024,3,128]{2,0,1:T(8,128)(2,1)} %param.10) | copy-start | bytes 2359300
  8.2 4.7 %copy-start.2 = (bf16[128,1024]{1,0:T(8,128)(2,1)S(1)}, bf16[128,1024]{1,0:T(8,128)(2,1)}, u32[]{:S(2)}) copy-start(bf16[128,1024]{1,0:T(8,128)(2,1)} %back_ref.1) | copy-start | bytes 786436
  91.3 25.9 %copy-start.1 = (bf16[128,1024]{1,0:T(8,128)(2,1)S(1)}, bf16[128,1024]{1,0:T(8,128)(2,1)}, u32[]{:S(2)}) copy-start(bf16[128,1024]{1,0:T(8,128)(2,1)} %cot_ref.1) | copy-start | bytes 786436
  111.7 5.5 %collective-permute-start.2 = (f32[1,1024]{1,0:T(1,128)S(1)}, f32[1,1024]{1,0:T(1,128)S(1)}, u32[]{:S(2)}, u32[]{:S(2)}) collective-permute-start(f32[1,1024]{1,0:T(1,128)S(1)} %get-tuple-element.79), channel_id=1, source_target_pairs={{1,0},{2,1},{3,2},{4,3},{5,4},{6,5},{7,6},{8,7},{9,8},{10,9},{11,1... | collective-permute-start | bytes 12296 | tf_op jit(solution)/shard_map/ppermute | solution.py:41
  126.0 13.2 %collective-permute-start.3 = (bf16[128,1024]{1,0:T(8,128)(2,1)S(1)}, bf16[128,1024]{1,0:T(8,128)(2,1)S(1)}, u32[]{:S(2)}, u32[]{:S(2)}) collective-permute-start(bf16[128,1024]{1,0:T(8,128)(2,1)S(1)} %get-tuple-element.87), channel_id=1, source_target_pairs={{4,0},{5,1},{6,2},{7,3},{8,4},{9,5},{10,6},{11,7},{12,8},{13,9},{1... | collective-permute-start | bytes 786440 | tf_op jit(solution)/shard_map/ppermute | solution.py:41
  128.0 12.2 %collective-permute-start.4 = (bf16[128,1024]{1,0:T(8,128)(2,1)S(1)}, bf16[128,1024]{1,0:T(8,128)(2,1)S(1)}, u32[]{:S(2)}, u32[]{:S(2)}) collective-permute-start(bf16[128,1024]{1,0:T(8,128)(2,1)S(1)} %get-tuple-element.88), channel_id=1, source_target_pairs={{3,0},{4,1},{5,2},{6,3},{7,4},{8,5},{9,6},{10,7},{11,8},{12,9},{13... | collective-permute-start | bytes 786440 | tf_op jit(solution)/shard_map/ppermute | solution.py:41
  129.9 17.8 %collective-permute-start.5 = (bf16[128,1024]{1,0:T(8,128)(2,1)S(1)}, bf16[128,1024]{1,0:T(8,128)(2,1)S(1)}, u32[]{:S(2)}, u32[]{:S(2)}) collective-permute-start(bf16[128,1024]{1,0:T(8,128)(2,1)S(1)} %get-tuple-element.89), channel_id=1, source_target_pairs={{2,0},{3,1},{4,2},{5,3},{6,4},{7,5},{8,6},{9,7},{10,8},{11,9},{12,... | collective-permute-start | bytes 786440 | tf_op jit(solution)/shard_map/ppermute | solution.py:41
  136.6 15.1 %collective-permute-start.6 = (bf16[128,1024]{1,0:T(8,128)(2,1)S(1)}, bf16[128,1024]{1,0:T(8,128)(2,1)S(1)}, u32[]{:S(2)}, u32[]{:S(2)}) collective-permute-start(bf16[128,1024]{1,0:T(8,128)(2,1)S(1)} %get-tuple-element.90), channel_id=1, source_target_pairs={{1,0},{2,1},{3,2},{4,3},{5,4},{6,5},{7,6},{8,7},{9,8},{10,9},{11,1... | collective-permute-start | bytes 786440 | tf_op jit(solution)/shard_map/ppermute | solution.py:41

commit v11 on v9

--- a/solution.py
+++ b/solution.py
@@ -674,9 +674,9 @@
     *backs, tail_back, own_grad, hidden_grad = fine_backward(
         place, cotangent, spread, fine_out, weights, *kept
     )
-    arrived = [shifted_by(rows, -steps) for steps, rows in enumerate(backs, 1)]
+    arrived = [shifted_by(backs[steps - 1], -steps) for steps in range(len(backs), 0, -1)]
     tail_arrived = shifted_by(tail_back, -(columns_along + 1))
-    return (output, fine_finish(own_grad, arrived, tail_arrived, hidden_grad, own))
+    return (output, fine_finish(own_grad, arrived[::-1], tail_arrived, hidden_grad, own))
 
 
 def solution(mesh):

time: 157 us -> 157 us (level)
  no operation moved by 1% of the time
where the time goes in v11:
time: 157 us; the launch traced here: 155 us
  blocking collectives  82.5 us (53%)
  Pallas kernels  33.5 us (21%)
  starting transfers between devices  23.4 us (15%)
  waiting for transfers between devices  13.4 us (9%)
    all_to_all x5, blocking collectives, exchanged(): return lax.all_to_all(pieces, axes, 0, 0, tiled=True)  82.5 us
    ppermute x7, starting transfers between devices, shifted_by(): lax.ppermute(value, LINE, [(source, source + steps) for source in range(f...  23.4 us
    ppermute x7, waiting for transfers between devices, shifted_by(): lax.ppermute(value, LINE, [(source, source + steps) for source in range(f...  13.4 us
    pallas_call x1, Pallas kernels, fine_backward(): pl.pallas_call(fine_backward_kernel, in_specs=[SCALAR] + [IN_VMEM] * 11,...  11.5 us
    pallas_call x1, Pallas kernels, fine_forward(): pl.pallas_call(fine_forward_kernel, in_specs=[SCALAR] + [IN_VMEM] * 12, o...  7.42 us
    pallas_call x1, Pallas kernels, coarse_attention(): pl.pallas_call(coarse_attention_kernel, in_specs=[SCALAR] + [IN_VMEM] * 4...  6.94 us
    pallas_call x1, Pallas kernels, fine_prepare(): pl.pallas_call(fine_prepare_kernel, in_specs=[SCALAR] + [anywhere] * 4, o...  4.64 us
  transfers between devices with their start and end apart: 7, of which 3 were waited for; matrix products, arithmetic and copies ran while one was open for 1% of the time, Pallas kernels for 3%

profile of v11, /device:TPU:64, one launch (start us, length us, event | category | flops | bytes accessed | tf_op | source)
XLA Modules:
  0.0 155.2 jit_solution(7336001285885168005)
XLA Ops:
  0.6 3.8 %collective-permute-start.1 = (bf16[128,1024]{1,0:T(8,128)(2,1)}, bf16[128,1024]{1,0:T(8,128)(2,1)S(1)}, u32[]{:S(2)}, u32[]{:S(2)}) collective-permute-start(bf16[128,1024]{1,0:T(8,128)(2,1)} %own_hbm.1), channel_id=1, source_target_pairs={{0,4},{1,5},{2,6},{3,7},{4,8},{5,9},{6,10},{7,11},{8,12},{9,13},{1... | collective-permute-start | bytes 786440 | tf_op jit(solution)/shard_map/ppermute | solution.py:41
  4.5 0.8 slice.3
  5.2 2.8 %collective-permute-start = (bf16[16,1024]{1,0:T(8,128)(2,1)S(1)}, bf16[16,1024]{1,0:T(8,128)(2,1)S(1)}, u32[]{:S(2)}, u32[]{:S(2)}) collective-permute-start(bf16[16,1024]{1,0:T(8,128)(2,1)S(1)} %slice.3), channel_id=1, source_target_pairs={{0,5},{1,6},{2,7},{3,8},{4,9},{5,10},{6,11},{7,12},{8,13},{9,14},{... | collective-permute-start | bytes 98312 | tf_op jit(solution)/shard_map/ppermute | solution.py:41
  8.1 0.1 pad_add_fusion.place_ref
  8.2 4.6 %fine_prepare.1 = (bf16[128,1024]{1,0:T(8,128)(2,1)S(1)}, bf16[3,1024,1024]{2,1,0:T(8,128)(2,1)S(1)}, bf16[1024,1024]{1,0:T(8,128)(2,1)S(1)}, bf16[128,1024]{1,0...) custom-call(s32[3]{0:T(128)S(1)} %pad_add_fusion.place_ref, ...), custom_call_target="tpu_custom_call" | custom-call | flops 900000000 | bytes 17000000 | tf_op jit(solution)/shard_map/fine_prepare/pallas_call | solution.py:488
  12.8 0.4 coarse_prepare.1
  13.2 0.3 collective-permute-done.tail_ref
  13.5 0.0 collective-permute-done.1.before_ref
  13.5 0.7 halo_send.1
  14.2 18.3 %all_to_all.25.slots_ref = bf16[4,128,1024]{2,1,0:T(8,128)(2,1)S(1)} all-to-all(bf16[4,128,1024]{2,1,0:T(8,128)(2,1)S(1)} %halo_send.1), channel_id=1, replica_groups=mesh['y'=4,'z_hi'=4,'core'=2,'z_lo'=2,'x'=4] {'x'}, dimensions={0} | all-to-all | bytes 2097152 | tf_op jit(solution)/shard_map/all_to_all | solution.py:45
  32.5 7.4 %fine_forward.1 = (bf16[144,1024]{1,0:T(8,128)(2,1)S(1)}, bf16[656,1024]{1,0:T(8,128)(2,1)S(1)}, bf16[656,1024]{1,0:T(8,128)(2,1)S(1)}, f32[144,1024]{1,0:T(8,12...) custom-call(s32[3]{0:T(128)S(1)} %pad_add_fusion.place_ref, ...), custom_call_target="tpu_custom_call" | custom-call | flops 4499999744 | bytes 20000000 | tf_op jit(solution)/shard_map/fine_forward/pallas_call | solution.py:512
  40.0 16.1 %all_to_all.26.got_ref = bf16[16,16,1024]{2,1,0:T(8,128)(2,1)S(1)} all-to-all(bf16[16,16,1024]{2,1,0:T(8,128)(2,1)S(1)} %get-tuple-element.75.message_ref), channel_id=1, replica_groups=mesh['y'=4,'z_hi'=4,'core'=2,'z_lo'=2,'x'=4] {'core','z_lo','x'}, dimensions={0} | all-to-all | bytes 1048576 | tf_op jit(solution)/shard_map/all_to_all | solution.py:45
  56.1 0.5 coarse_project.1
  56.6 15.6 %all_to_all.27 = bf16[4,128,256]{2,1,0:T(8,128)(2,1)S(1)} all-to-all(bf16[4,128,256]{2,1,0:T(8,128)(2,1)S(1)} %get-tuple-element.78), channel_id=1, replica_groups=mesh['y'=4,'z_hi'=4,'core'=2,'z_lo'=2,'x'=4] {'z_hi'}, dimensions={0} | all-to-all | bytes 524288 | tf_op jit(solution)/shard_map/all_to_all | solution.py:45
  72.3 0.1 repeated.1
  72.3 19.1 %all_to_all.28 = bf16[4,512,256]{2,1,0:T(8,128)(2,1)S(1)} all-to-all(bf16[4,512,256]{2,1,0:T(8,128)(2,1)S(1)} %repeated.1), channel_id=1, replica_groups=mesh['y'=4,'z_hi'=4,'core'=2,'z_lo'=2,'x'=4] {'y'}, dimensions={0} | all-to-all | bytes 2097152 | tf_op jit(solution)/shard_map/all_to_all | solution.py:45
  91.4 6.9 %coarse_attention.1 = bf16[16,16,1024]{2,1,0:T(8,128)(2,1)S(1)} custom-call(s32[3]{0:T(128)S(1)} %pad_add_fusion.place_ref, bf16[2048,256]{1,0:T(8,128)(2,1)S(1)} %bitcast.13, f32[128,256]{1,0:T(8,128)S(1)} %get-tuple-element.79.factor_ref, bf16[1024,256]{1,0:T(8,128)(2,1)S(1)} %get-tuple-element.76.in_w_ref, bf16[256,1024]{1,0:T(8,128)(2,1)S(1)} %get-tuple-element.77.out_w_ref), custom_call_target="tpu_custom_call" | custom-call | flops 1500000000 | bytes 3000000 | tf_op jit(solution)/shard_map/coarse_attention/pallas_call | solution.py:559
  98.4 13.3 %all_to_all.29.got_ref = bf16[16,16,1024]{2,1,0:T(8,128)(2,1)S(1)} all-to-all(bf16[16,16,1024]{2,1,0:T(8,128)(2,1)S(1)} %coarse_attention.1), channel_id=1, replica_groups=mesh['y'=4,'z_hi'=4,'core'=2,'z_lo'=2,'x'=4] {'core','z_lo','x'}, dimensions={0} | all-to-all | bytes 1048576 | tf_op jit(solution)/shard_map/all_to_all | solution.py:45
  111.7 0.2 coarse_finish.1
  111.9 11.5 %fine_backward.1 = (bf16[144,1024]{1,0:T(8,128)(2,1)S(1)}, bf16[128,1024]{1,0:T(8,128)(2,1)S(1)}, bf16[128,1024]{1,0:T(8,128)(2,1)S(1)}, bf16[128,1024]{1,0:T(8,...) custom-call(s32[3]{0:T(128)S(1)} %pad_add_fusion.place_ref, ...), custom_call_target="tpu_custom_call" | custom-call | flops 5000000000 | bytes 20000000 | tf_op jit(solution)/shard_map/fine_backward/pallas_call | solution.py:587
  123.4 2.0 %collective-permute-start.2 = (bf16[144,1024]{1,0:T(8,128)(2,1)S(1)}, bf16[144,1024]{1,0:T(8,128)(2,1)S(1)}, u32[]{:S(2)}, u32[]{:S(2)}) collective-permute-start(bf16[144,1024]{1,0:T(8,128)(2,1)S(1)} %get-tuple-element.90), channel_id=1, source_target_pairs={{1,0},{2,1},{3,2},{4,3},{5,4},{6,5},{7,6},{8,7},{9,8},{10,9},{11,1... | collective-permute-start | bytes 884744 | tf_op jit(solution)/shard_map/ppermute | solution.py:41
  125.3 2.9 %collective-permute-start.3 = (bf16[128,1024]{1,0:T(8,128)(2,1)S(1)}, bf16[128,1024]{1,0:T(8,128)(2,1)S(1)}, u32[]{:S(2)}, u32[]{:S(2)}) collective-permute-start(bf16[128,1024]{1,0:T(8,128)(2,1)S(1)} %get-tuple-element.91), channel_id=1, source_target_pairs={{2,0},{3,1},{4,2},{5,3},{6,4},{7,5},{8,6},{9,7},{10,8},{11,9},{12,... | collective-permute-start | bytes 786440 | tf_op jit(solution)/shard_map/ppermute | solution.py:41
  128.3 1.9 %collective-permute-start.4 = (bf16[128,1024]{1,0:T(8,128)(2,1)S(1)}, bf16[128,1024]{1,0:T(8,128)(2,1)S(1)}, u32[]{:S(2)}, u32[]{:S(2)}) collective-permute-start(bf16[128,1024]{1,0:T(8,128)(2,1)S(1)} %get-tuple-element.92), channel_id=1, source_target_pairs={{3,0},{4,1},{5,2},{6,3},{7,4},{8,5},{9,6},{10,7},{11,8},{12,9},{13... | collective-permute-start | bytes 786440 | tf_op jit(solution)/shard_map/ppermute | solution.py:41
  130.2 4.1 %collective-permute-start.5 = (bf16[128,1024]{1,0:T(8,128)(2,1)S(1)}, bf16[128,1024]{1,0:T(8,128)(2,1)S(1)}, u32[]{:S(2)}, u32[]{:S(2)}) collective-permute-start(bf16[128,1024]{1,0:T(8,128)(2,1)S(1)} %get-tuple-element.93), channel_id=1, source_target_pairs={{4,0},{5,1},{6,2},{7,3},{8,4},{9,5},{10,6},{11,7},{12,8},{13,9},{1... | collective-permute-start | bytes 786440 | tf_op jit(solution)/shard_map/ppermute | solution.py:41
  134.3 5.9 %collective-permute-start.6 = (bf16[16,1024]{1,0:T(8,128)(2,1)S(1)}, bf16[16,1024]{1,0:T(8,128)(2,1)S(1)}, u32[]{:S(2)}, u32[]{:S(2)}) collective-permute-start(bf16[16,1024]{1,0:T(8,128)(2,1)S(1)} %get-tuple-element.94), channel_id=1, source_target_pairs={{5,0},{6,1},{7,2},{8,3},{9,4},{10,5},{11,6},{12,7},{13,8},{14,9},{... | collective-permute-start | bytes 98312 | tf_op jit(solution)/shard_map/ppermute | solution.py:41
  140.2 0.8 fusion
  141.0 10.1 %collective-permute-done.6.tail_ref = bf16[16,1024]{1,0:T(8,128)(2,1)S(1)} collective-permute-done((bf16[16,1024]{1,0:T(8,128)(2,1)S(1)}, bf16[16,1024]{1,0:T(8,128)(2,1)S(1)}, u32[]{:S(2)}, u32[]{:S(2)}) %collective-permute-start.6) | collective-permute-done | bytes 32800 | tf_op jit(solution)/shard_map/ppermute | solution.py:41
  151.1 0.0 collective-permute-done.3.a2
  151.1 0.0 collective-permute-done.4.a3
  151.1 3.0 %collective-permute-done.5.a4 = bf16[128,1024]{1,0:T(8,128)(2,1)S(1)} collective-permute-done((bf16[128,1024]{1,0:T(8,128)(2,1)S(1)}, bf16[128,1024]{1,0:T(8,128)(2,1)S(1)}, u32[]{:S(2)}, u32[]{:S(2)}) %collective-permute-start.5) | collective-permute-done | bytes 262176 | tf_op jit(solution)/shard_map/ppermute | solution.py:41
  154.1 0.0 collective-permute-done.2.a1
  154.1 1.1 fine_finish.1
  (7 shorter events, 0.0 us)
Async XLA Ops:
  0.6 12.9 %collective-permute-start.1 = (bf16[128,1024]{1,0:T(8,128)(2,1)}, bf16[128,1024]{1,0:T(8,128)(2,1)S(1)}, u32[]{:S(2)}, u32[]{:S(2)}) collective-permute-start(bf16[128,1024]{1,0:T(8,128)(2,1)} %own_hbm.1), channel_id=1, source_target_pairs={{0,4},{1,5},{2,6},{3,7},{4,8},{5,9},{6,10},{7,11},{8,12},{9,13},{1... | collective-permute-start | bytes 786440 | tf_op jit(solution)/shard_map/ppermute | solution.py:41
  5.2 8.2 %collective-permute-start = (bf16[16,1024]{1,0:T(8,128)(2,1)S(1)}, bf16[16,1024]{1,0:T(8,128)(2,1)S(1)}, u32[]{:S(2)}, u32[]{:S(2)}) collective-permute-start(bf16[16,1024]{1,0:T(8,128)(2,1)S(1)} %slice.3), channel_id=1, source_target_pairs={{0,5},{1,6},{2,7},{3,8},{4,9},{5,10},{6,11},{7,12},{8,13},{9,14},{... | collective-permute-start | bytes 98312 | tf_op jit(solution)/shard_map/ppermute | solution.py:41
  8.2 4.7 %copy-start.1 = (bf16[1024,3,128]{2,0,1:T(8,128)(2,1)S(1)}, bf16[1024,3,128]{2,0,1:T(8,128)(2,1)}, u32[]{:S(2)}) copy-start(bf16[1024,3,128]{2,0,1:T(8,128)(2,1)} %param.10) | copy-start | bytes 2359300
  8.2 4.7 %copy-start.2 = (bf16[128,1024]{1,0:T(8,128)(2,1)S(1)}, bf16[128,1024]{1,0:T(8,128)(2,1)}, u32[]{:S(2)}) copy-start(bf16[128,1024]{1,0:T(8,128)(2,1)} %back_ref.1) | copy-start | bytes 786436
  91.4 20.4 %copy-start = (bf16[128,1024]{1,0:T(8,128)(2,1)S(1)}, bf16[128,1024]{1,0:T(8,128)(2,1)}, u32[]{:S(2)}) copy-start(bf16[128,1024]{1,0:T(8,128)(2,1)} %cot_ref.1) | copy-start | bytes 786436
  123.4 30.8 %collective-permute-start.2 = (bf16[144,1024]{1,0:T(8,128)(2,1)S(1)}, bf16[144,1024]{1,0:T(8,128)(2,1)S(1)}, u32[]{:S(2)}, u32[]{:S(2)}) collective-permute-start(bf16[144,1024]{1,0:T(8,128)(2,1)S(1)} %get-tuple-element.90), channel_id=1, source_target_pairs={{1,0},{2,1},{3,2},{4,3},{5,4},{6,5},{7,6},{8,7},{9,8},{10,9},{11,1... | collective-permute-start | bytes 884744 | tf_op jit(solution)/shard_map/ppermute | solution.py:41
  125.3 25.7 %collective-permute-start.3 = (bf16[128,1024]{1,0:T(8,128)(2,1)S(1)}, bf16[128,1024]{1,0:T(8,128)(2,1)S(1)}, u32[]{:S(2)}, u32[]{:S(2)}) collective-permute-start(bf16[128,1024]{1,0:T(8,128)(2,1)S(1)} %get-tuple-element.91), channel_id=1, source_target_pairs={{2,0},{3,1},{4,2},{5,3},{6,4},{7,5},{8,6},{9,7},{10,8},{11,9},{12,... | collective-permute-start | bytes 786440 | tf_op jit(solution)/shard_map/ppermute | solution.py:41
  128.3 22.8 %collective-permute-start.4 = (bf16[128,1024]{1,0:T(8,128)(2,1)S(1)}, bf16[128,1024]{1,0:T(8,128)(2,1)S(1)}, u32[]{:S(2)}, u32[]{:S(2)}) collective-permute-start(bf16[128,1024]{1,0:T(8,128)(2,1)S(1)} %get-tuple-element.92), channel_id=1, source_target_pairs={{3,0},{4,1},{5,2},{6,3},{7,4},{8,5},{9,6},{10,7},{11,8},{12,9},{13... | collective-permute-start | bytes 786440 | tf_op jit(solution)/shard_map/ppermute | solution.py:41
  130.2 23.9 %collective-permute-start.5 = (bf16[128,1024]{1,0:T(8,128)(2,1)S(1)}, bf16[128,1024]{1,0:T(8,128)(2,1)S(1)}, u32[]{:S(2)}, u32[]{:S(2)}) collective-permute-start(bf16[128,1024]{1,0:T(8,128)(2,1)S(1)} %get-tuple-element.93), channel_id=1, source_target_pairs={{4,0},{5,1},{6,2},{7,3},{8,4},{9,5},{10,6},{11,7},{12,8},{13,9},{1... | collective-permute-start | bytes 786440 | tf_op jit(solution)/shard_map/ppermute | solution.py:41
  134.3 16.8 %collective-permute-start.6 = (bf16[16,1024]{1,0:T(8,128)(2,1)S(1)}, bf16[16,1024]{1,0:T(8,128)(2,1)S(1)}, u32[]{:S(2)}, u32[]{:S(2)}) collective-permute-start(bf16[16,1024]{1,0:T(8,128)(2,1)S(1)} %get-tuple-element.94), channel_id=1, source_target_pairs={{5,0},{6,1},{7,2},{8,3},{9,4},{10,5},{11,6},{12,7},{13,8},{14,9},{... | collective-permute-start | bytes 98312 | tf_op jit(solution)/shard_map/ppermute | solution.py:41

commit v12 on v10

--- a/solution.py
+++ b/solution.py
@@ -661,7 +661,7 @@
         place, cotangent, spread, after, fine_out, weights, query, key, value, q_factor, k_factor, probs,
         attended,
     )
-    arrived = [shifted_by(backs[steps - 1], -steps) for steps in range(len(backs), 0, -1)]
+    arrived = [shifted_by(backs[steps - 1], -steps) for steps in (4, 2, 3, 1)]
     return (output, fine_finish(own_grad, arrived, hidden_grad, own))
 
 

time: 155 us -> 155 us (level)
  the two profiles are of different devices: /device:TPU:64 before, /device:TPU:6 now
where the time goes in v12:
time: 155 us; the launch traced here: 154 us
  blocking collectives  83 us (54%)
  Pallas kernels  30.6 us (20%)
  waiting for transfers between devices  22 us (14%)
  starting transfers between devices  16 us (10%)
    all_to_all x5, blocking collectives, exchanged(): return lax.all_to_all(pieces, axes, 0, 0, tiled=True)  83 us
    ppermute x7, waiting for transfers between devices, shifted_by(): lax.ppermute(value, LINE, [(source, source + steps) for source in range(f...  22 us
    ppermute x7, starting transfers between devices, shifted_by(): lax.ppermute(value, LINE, [(source, source + steps) for source in range(f...  16 us
    pallas_call x1, Pallas kernels, fine_backward(): pl.pallas_call(fine_backward_kernel, in_specs=[SCALAR] + [IN_VMEM] * 12,...  8.79 us
    pallas_call x1, Pallas kernels, fine_forward(): pl.pallas_call(fine_forward_kernel, in_specs=[SCALAR] + [IN_VMEM] * 11, o...  7.3 us
    pallas_call x1, Pallas kernels, coarse_attention(): pl.pallas_call(coarse_attention_kernel, in_specs=[SCALAR] + [IN_VMEM] * 4...  6.94 us
    pallas_call x1, Pallas kernels, fine_prepare(): pl.pallas_call(fine_prepare_kernel, in_specs=[SCALAR] + [anywhere] * 4, o...  4.64 us
  transfers between devices with their start and end apart: 7, of which 5 were waited for; matrix products, arithmetic and copies ran while one was open for 1% of the time, Pallas kernels for 3%

profile of v12, /device:TPU:6, one launch (start us, length us, event | category | flops | bytes accessed | tf_op | source)
XLA Modules:
  0.0 154.2 jit_solution(12637547990389714634)
XLA Ops:
  0.6 3.8 %collective-permute-start.1 = (bf16[128,1024]{1,0:T(8,128)(2,1)}, bf16[128,1024]{1,0:T(8,128)(2,1)S(1)}, u32[]{:S(2)}, u32[]{:S(2)}) collective-permute-start(bf16[128,1024]{1,0:T(8,128)(2,1)} %own_hbm.1), channel_id=1, source_target_pairs={{0,4},{1,5},{2,6},{3,7},{4,8},{5,9},{6,10},{7,11},{8,12},{9,13},{1... | collective-permute-start | bytes 786440 | tf_op jit(solution)/shard_map/ppermute | solution.py:41
  4.5 0.8 slice.3
  5.3 1.5 collective-permute-start
  6.8 0.1 pad_add_fusion.place_ref
  6.9 4.6 %fine_prepare.1 = (bf16[128,1024]{1,0:T(8,128)(2,1)S(1)}, bf16[3,1024,1024]{2,1,0:T(8,128)(2,1)S(1)}, bf16[1024,1024]{1,0:T(8,128)(2,1)S(1)}, bf16[128,1024]{1,0...) custom-call(s32[3]{0:T(128)S(1)} %pad_add_fusion.place_ref, ...), custom_call_target="tpu_custom_call" | custom-call | flops 900000000 | bytes 17000000 | tf_op jit(solution)/shard_map/fine_prepare/pallas_call | solution.py:475
  11.5 0.4 coarse_prepare.1
  11.9 0.0 collective-permute-done.tail_ref
  11.9 0.0 collective-permute-done.1.before_ref
  11.9 0.7 halo_send.1
  12.7 18.9 %all_to_all.25.slots_ref = bf16[4,128,1024]{2,1,0:T(8,128)(2,1)S(1)} all-to-all(bf16[4,128,1024]{2,1,0:T(8,128)(2,1)S(1)} %halo_send.1), channel_id=1, replica_groups=mesh['y'=4,'z_hi'=4,'core'=2,'z_lo'=2,'x'=4] {'x'}, dimensions={0} | all-to-all | bytes 2097152 | tf_op jit(solution)/shard_map/all_to_all | solution.py:45
  31.6 7.3 %fine_forward.1 = (bf16[640,1024]{1,0:T(8,128)(2,1)S(1)}, bf16[640,1024]{1,0:T(8,128)(2,1)S(1)}, f32[640,1024]{1,0:T(8,128)S(1)}, bf16[16,128,640]{2,1,0:T(8,128...) custom-call(s32[3]{0:T(128)S(1)} %pad_add_fusion.place_ref, ...), custom_call_target="tpu_custom_call" | custom-call | flops 4499999744 | bytes 20000000 | tf_op jit(solution)/shard_map/fine_forward/pallas_call | solution.py:499
  38.9 13.8 %all_to_all.26.got_ref = bf16[16,16,1024]{2,1,0:T(8,128)(2,1)S(1)} all-to-all(bf16[16,16,1024]{2,1,0:T(8,128)(2,1)S(1)} %get-tuple-element.72.message_ref), channel_id=1, replica_groups=mesh['y'=4,'z_hi'=4,'core'=2,'z_lo'=2,'x'=4] {'core','z_lo','x'}, dimensions={0} | all-to-all | bytes 1048576 | tf_op jit(solution)/shard_map/all_to_all | solution.py:45
  52.7 0.5 coarse_project.1
  53.2 18.6 %all_to_all.27 = bf16[4,128,256]{2,1,0:T(8,128)(2,1)S(1)} all-to-all(bf16[4,128,256]{2,1,0:T(8,128)(2,1)S(1)} %get-tuple-element.75), channel_id=1, replica_groups=mesh['y'=4,'z_hi'=4,'core'=2,'z_lo'=2,'x'=4] {'z_hi'}, dimensions={0} | all-to-all | bytes 524288 | tf_op jit(solution)/shard_map/all_to_all | solution.py:45
  71.8 0.1 repeated.1
  71.9 16.5 %all_to_all.28 = bf16[4,512,256]{2,1,0:T(8,128)(2,1)S(1)} all-to-all(bf16[4,512,256]{2,1,0:T(8,128)(2,1)S(1)} %repeated.1), channel_id=1, replica_groups=mesh['y'=4,'z_hi'=4,'core'=2,'z_lo'=2,'x'=4] {'y'}, dimensions={0} | all-to-all | bytes 2097152 | tf_op jit(solution)/shard_map/all_to_all | solution.py:45
  88.4 6.9 %coarse_attention.1 = bf16[16,16,1024]{2,1,0:T(8,128)(2,1)S(1)} custom-call(s32[3]{0:T(128)S(1)} %pad_add_fusion.place_ref, bf16[2048,256]{1,0:T(8,128)(2,1)S(1)} %bitcast.13, f32[128,256]{1,0:T(8,128)S(1)} %get-tuple-element.76.factor_ref, bf16[1024,256]{1,0:T(8,128)(2,1)S(1)} %get-tuple-element.73.in_w_ref, bf16[256,1024]{1,0:T(8,128)(2,1)S(1)} %get-tuple-element.74.out_w_ref), custom_call_target="tpu_custom_call" | custom-call | flops 1500000000 | bytes 3000000 | tf_op jit(solution)/shard_map/coarse_attention/pallas_call | solution.py:544
  95.3 15.2 %all_to_all.29.got_ref = bf16[16,16,1024]{2,1,0:T(8,128)(2,1)S(1)} all-to-all(bf16[16,16,1024]{2,1,0:T(8,128)(2,1)S(1)} %coarse_attention.1), channel_id=1, replica_groups=mesh['y'=4,'z_hi'=4,'core'=2,'z_lo'=2,'x'=4] {'core','z_lo','x'}, dimensions={0} | all-to-all | bytes 1048576 | tf_op jit(solution)/shard_map/all_to_all | solution.py:45
  110.6 0.2 coarse_finish.1
  110.8 3.0 %collective-permute-start.2 = (f32[1,1024]{1,0:T(1,128)S(1)}, f32[1,1024]{1,0:T(1,128)S(1)}, u32[]{:S(2)}, u32[]{:S(2)}) collective-permute-start(f32[1,1024]{1,0:T(1,128)S(1)} %get-tuple-element.79), channel_id=1, source_target_pairs={{1,0},{2,1},{3,2},{4,3},{5,4},{6,5},{7,6},{8,7},{9,8},{10,9},{11,1... | collective-permute-start | bytes 12296 | tf_op jit(solution)/shard_map/ppermute | solution.py:41
  113.8 4.6 %collective-permute-done.2.next_ref = f32[1,1024]{1,0:T(1,128)S(1)} collective-permute-done((f32[1,1024]{1,0:T(1,128)S(1)}, f32[1,1024]{1,0:T(1,128)S(1)}, u32[]{:S(2)}, u32[]{:S(2)}) %collective-permute-start.2) | collective-permute-done | bytes 4128 | tf_op jit(solution)/shard_map/ppermute | solution.py:41
  118.4 8.8 %fine_backward.1 = (bf16[128,1024]{1,0:T(8,128)(2,1)S(1)}, bf16[128,1024]{1,0:T(8,128)(2,1)S(1)}, bf16[128,1024]{1,0:T(8,128)(2,1)S(1)}, bf16[128,1024]{1,0:T(8,...) custom-call(s32[3]{0:T(128)S(1)} %pad_add_fusion.place_ref, bf16[128,1024]{1,0:T(8,128)(2,1)S(1)} %copy-done.1, ...), custom_call_target="tpu_custom_call" | custom-call | flops 5000000000 | bytes 20000000 | tf_op jit(solution)/shard_map/fine_backward/pallas_call | solution.py:572
  127.2 1.3 collective-permute-start.3
  128.5 2.3 %collective-permute-start.4 = (bf16[128,1024]{1,0:T(8,128)(2,1)S(1)}, bf16[128,1024]{1,0:T(8,128)(2,1)S(1)}, u32[]{:S(2)}, u32[]{:S(2)}) collective-permute-start(bf16[128,1024]{1,0:T(8,128)(2,1)S(1)} %get-tuple-element.88), channel_id=1, source_target_pairs={{2,0},{3,1},{4,2},{5,3},{6,4},{7,5},{8,6},{9,7},{10,8},{11,9},{12,... | collective-permute-start | bytes 786440 | tf_op jit(solution)/shard_map/ppermute | solution.py:41
  130.8 1.9 %collective-permute-start.5 = (bf16[128,1024]{1,0:T(8,128)(2,1)S(1)}, bf16[128,1024]{1,0:T(8,128)(2,1)S(1)}, u32[]{:S(2)}, u32[]{:S(2)}) collective-permute-start(bf16[128,1024]{1,0:T(8,128)(2,1)S(1)} %get-tuple-element.89), channel_id=1, source_target_pairs={{3,0},{4,1},{5,2},{6,3},{7,4},{8,5},{9,6},{10,7},{11,8},{12,9},{13... | collective-permute-start | bytes 786440 | tf_op jit(solution)/shard_map/ppermute | solution.py:41
  132.7 2.1 %collective-permute-start.6 = (bf16[128,1024]{1,0:T(8,128)(2,1)S(1)}, bf16[128,1024]{1,0:T(8,128)(2,1)S(1)}, u32[]{:S(2)}, u32[]{:S(2)}) collective-permute-start(bf16[128,1024]{1,0:T(8,128)(2,1)S(1)} %get-tuple-element.90), channel_id=1, source_target_pairs={{1,0},{2,1},{3,2},{4,3},{5,4},{6,5},{7,6},{8,7},{9,8},{10,9},{11,1... | collective-permute-start | bytes 786440 | tf_op jit(solution)/shard_map/ppermute | solution.py:41
  134.9 0.8 fusion
  135.7 0.3 collective-permute-done.3.a1
  136.0 5.4 %collective-permute-done.4.a2 = bf16[128,1024]{1,0:T(8,128)(2,1)S(1)} collective-permute-done((bf16[128,1024]{1,0:T(8,128)(2,1)S(1)}, bf16[128,1024]{1,0:T(8,128)(2,1)S(1)}, u32[]{:S(2)}, u32[]{:S(2)}) %collective-permute-start.4) | collective-permute-done | bytes 262176 | tf_op jit(solution)/shard_map/ppermute | solution.py:41
  141.4 1.0 collective-permute-done.5.a3
  142.5 10.6 %collective-permute-done.6.a4 = bf16[128,1024]{1,0:T(8,128)(2,1)S(1)} collective-permute-done((bf16[128,1024]{1,0:T(8,128)(2,1)S(1)}, bf16[128,1024]{1,0:T(8,128)(2,1)S(1)}, u32[]{:S(2)}, u32[]{:S(2)}) %collective-permute-start.6) | collective-permute-done | bytes 262176 | tf_op jit(solution)/shard_map/ppermute | solution.py:41
  153.1 1.1 fine_finish.1
  (7 shorter events, 0.0 us)
Async XLA Ops:
  0.6 11.3 %collective-permute-start.1 = (bf16[128,1024]{1,0:T(8,128)(2,1)}, bf16[128,1024]{1,0:T(8,128)(2,1)S(1)}, u32[]{:S(2)}, u32[]{:S(2)}) collective-permute-start(bf16[128,1024]{1,0:T(8,128)(2,1)} %own_hbm.1), channel_id=1, source_target_pairs={{0,4},{1,5},{2,6},{3,7},{4,8},{5,9},{6,10},{7,11},{8,12},{9,13},{1... | collective-permute-start | bytes 786440 | tf_op jit(solution)/shard_map/ppermute | solution.py:41
  5.3 6.6 %collective-permute-start = (bf16[16,1024]{1,0:T(8,128)(2,1)S(1)}, bf16[16,1024]{1,0:T(8,128)(2,1)S(1)}, u32[]{:S(2)}, u32[]{:S(2)}) collective-permute-start(bf16[16,1024]{1,0:T(8,128)(2,1)S(1)} %slice.3), channel_id=1, source_target_pairs={{0,5},{1,6},{2,7},{3,8},{4,9},{5,10},{6,11},{7,12},{8,13},{9,14},{... | collective-permute-start | bytes 98312 | tf_op jit(solution)/shard_map/ppermute | solution.py:41
  6.9 4.7 %copy-start = (bf16[1024,3,128]{2,0,1:T(8,128)(2,1)S(1)}, bf16[1024,3,128]{2,0,1:T(8,128)(2,1)}, u32[]{:S(2)}) copy-start(bf16[1024,3,128]{2,0,1:T(8,128)(2,1)} %param.10) | copy-start | bytes 2359300
  6.9 4.7 %copy-start.2 = (bf16[128,1024]{1,0:T(8,128)(2,1)S(1)}, bf16[128,1024]{1,0:T(8,128)(2,1)}, u32[]{:S(2)}) copy-start(bf16[128,1024]{1,0:T(8,128)(2,1)} %back_ref.1) | copy-start | bytes 786436
  88.4 30.0 %copy-start.1 = (bf16[128,1024]{1,0:T(8,128)(2,1)S(1)}, bf16[128,1024]{1,0:T(8,128)(2,1)}, u32[]{:S(2)}) copy-start(bf16[128,1024]{1,0:T(8,128)(2,1)} %cot_ref.1) | copy-start | bytes 786436
  110.8 7.6 %collective-permute-start.2 = (f32[1,1024]{1,0:T(1,128)S(1)}, f32[1,1024]{1,0:T(1,128)S(1)}, u32[]{:S(2)}, u32[]{:S(2)}) collective-permute-start(f32[1,1024]{1,0:T(1,128)S(1)} %get-tuple-element.79), channel_id=1, source_target_pairs={{1,0},{2,1},{3,2},{4,3},{5,4},{6,5},{7,6},{8,7},{9,8},{10,9},{11,1... | collective-permute-start | bytes 12296 | tf_op jit(solution)/shard_map/ppermute | solution.py:41
  127.2 8.8 %collective-permute-start.3 = (bf16[128,1024]{1,0:T(8,128)(2,1)S(1)}, bf16[128,1024]{1,0:T(8,128)(2,1)S(1)}, u32[]{:S(2)}, u32[]{:S(2)}) collective-permute-start(bf16[128,1024]{1,0:T(8,128)(2,1)S(1)} %get-tuple-element.87), channel_id=1, source_target_pairs={{4,0},{5,1},{6,2},{7,3},{8,4},{9,5},{10,6},{11,7},{12,8},{13,9},{1... | collective-permute-start | bytes 786440 | tf_op jit(solution)/shard_map/ppermute | solution.py:41
  128.5 13.0 %collective-permute-start.4 = (bf16[128,1024]{1,0:T(8,128)(2,1)S(1)}, bf16[128,1024]{1,0:T(8,128)(2,1)S(1)}, u32[]{:S(2)}, u32[]{:S(2)}) collective-permute-start(bf16[128,1024]{1,0:T(8,128)(2,1)S(1)} %get-tuple-element.88), channel_id=1, source_target_pairs={{2,0},{3,1},{4,2},{5,3},{6,4},{7,5},{8,6},{9,7},{10,8},{11,9},{12,... | collective-permute-start | bytes 786440 | tf_op jit(solution)/shard_map/ppermute | solution.py:41
  130.8 11.7 %collective-permute-start.5 = (bf16[128,1024]{1,0:T(8,128)(2,1)S(1)}, bf16[128,1024]{1,0:T(8,128)(2,1)S(1)}, u32[]{:S(2)}, u32[]{:S(2)}) collective-permute-start(bf16[128,1024]{1,0:T(8,128)(2,1)S(1)} %get-tuple-element.89), channel_id=1, source_target_pairs={{3,0},{4,1},{5,2},{6,3},{7,4},{8,5},{9,6},{10,7},{11,8},{12,9},{13... | collective-permute-start | bytes 786440 | tf_op jit(solution)/shard_map/ppermute | solution.py:41
  132.7 20.4 %collective-permute-start.6 = (bf16[128,1024]{1,0:T(8,128)(2,1)S(1)}, bf16[128,1024]{1,0:T(8,128)(2,1)S(1)}, u32[]{:S(2)}, u32[]{:S(2)}) collective-permute-start(bf16[128,1024]{1,0:T(8,128)(2,1)S(1)} %get-tuple-element.90), channel_id=1, source_target_pairs={{1,0},{2,1},{3,2},{4,3},{5,4},{6,5},{7,6},{8,7},{9,8},{10,9},{11,1... | collective-permute-start | bytes 786440 | tf_op jit(solution)/shard_map/ppermute | solution.py:41
